TPU v7x, 32 devices: a whole 2x2x4 slice. The times are simulated.
32 devices in a mesh: groups: 2 (over y), assets: 8 (over z, x), tm: 2 (over core).
Axes of the slice: x: 2, y: 2, z: 4, core: 2. Of those that a mesh axis runs over, the one named last changes fastest.
Arguments:
- returns: bfloat16 [1536, 16384], P('tm', ('groups', 'assets')), parts along dimension 1, may hold values from -24 to 24
- prior: float32 [16384, 8192], P(('groups', 'assets')), parts along dimension 0, may hold values from -3 to 3
Outputs:
- covariance: float32 [2, 16384, 8192], P('tm', ('groups', 'assets')), parts along dimension 1
There are 2 independent parts, one for each index of `groups`. A program takes and returns all parts, laid end to end along the dimension named above; each array names one. Nothing has to cross between parts.
All inputs are finite; a program needn't handle non-finite values.
Results may differ from a plain program's by a relative error of at most 0.0045.
Values may be sent and summed in bfloat16 or wider, within the bound.
No kernel may reach another device: no remote copies, remote signals or barrier semaphores. Data moves between devices by JAX's collectives and lax.ppermute only.
A program may use at most 256 MiB of HBM per device.

v0:
```python
import functools

import jax
import jax.numpy as jnp
from jax import lax
from jax.experimental import pallas as pl
from jax.experimental.pallas import tpu as pltpu
from jax.sharding import PartitionSpec as P


LANES = 128


def weights(minutes):
    lam = jnp.float32(0.9995)
    position = jnp.arange(minutes, dtype=jnp.float32)
    weight = jnp.sqrt(
        (jnp.float32(1.0) - lam) * jnp.power(lam, jnp.float32(minutes - 1) - position)
    )
    return weight, jnp.power(lam, jnp.float32(minutes))


def scale(part, weight):
    return (part.astype(jnp.float32) * weight[:, None]).astype(jnp.bfloat16)


def prefix(shard, axis, combine, identity):
    length, mine = (lax.axis_size(axis), lax.axis_index(axis))
    everything = jax.tree.map(
        lambda part: lax.all_gather(part.astype(jnp.bfloat16), axis), shard
    )
    start = jax.tree.map(
        lambda part, zero: jnp.broadcast_to(jnp.asarray(zero, part.dtype), part.shape),
        shard,
        identity,
    )

    def turn(k, before):
        reached = k < mine
        new = combine(
            before, jax.tree.map(lambda part, own: part[k].astype(own.dtype), everything, shard)
        )
        return jax.tree.map(lambda a, b: jnp.where(reached, a, b), new, before)

    return lax.fori_loop(0, length, turn, start)


def combine_carry(earlier, later):
    return (later[1] * earlier[0] + later[0], earlier[1] * later[1])


def local_any(returns, prior):
    weight, factor = weights(returns.shape[0])
    scaled = scale(returns, weight)
    tile = lax.dot_general(
        scaled,
        lax.all_gather(scaled, "assets", axis=1, tiled=True),
        (((0,), (0,)), ((), ())),
        preferred_element_type=jnp.float32,
    )
    decay = jnp.full((1,), factor, jnp.float32)
    identity = (jnp.zeros_like(tile), jnp.ones((1,), jnp.float32))
    before, reach = prefix((tile, decay), "tm", combine_carry, identity)
    return (factor * (before + reach[0] * prior) + tile)[None]


def tile_kernel(count, rows, columns, coef, *refs):
    own, other = refs[:count], refs[count : 2 * count]
    weight, left_own, left_other, prior = refs[2 * count : 2 * count + 4]
    out, x_own, x_other, box, x_sem, in_sem, out_sem = refs[-7:]
    width = own[0].shape[1]
    tiles = prior.shape[0] // rows
    earlier = coef[1] != 0.0
    copy = pltpu.make_async_copy

    def place(k):
        return pl.ds(pl.multiple_of(columns[k] * LANES, LANES), width)

    def inside(k):
        return pl.ds(k * width, width)

    def take(part, x, side, k):
        return copy(part[k], x.at[:, inside(k)], x_sem.at[side, k])

    def fetch(k, i):
        at = pl.ds(i * rows, rows)
        return copy(prior.at[at, place(k)], box.at[at, inside(k)], in_sem.at[k, i])

    def flush(k, i):
        at = pl.ds(i * rows, rows)
        return copy(box.at[at, inside(k)], out.at[0, at, place(k)], out_sem.at[k, i])

    def scale_in_place(ref, k):
        for lane in range(k * width, (k + 1) * width, LANES):
            at = slice(lane, lane + LANES)
            ref[:, at] = (ref[:, at].astype(jnp.float32) * weight[...]).astype(jnp.bfloat16)

    for k in range(count):
        take(own, x_own, 0, k).start()

        @pl.when(earlier)
        def _():
            take(other, x_other, 1, k).start()

    for i in range(tiles):
        for k in range(count):
            fetch(k, i).start()

    for k in range(count):
        take(own, x_own, 0, k).wait()
        scale_in_place(x_own, k)

        @pl.when(earlier)
        def _():
            take(other, x_other, 1, k).wait()
            scale_in_place(x_other, k)

    @pl.loop(0, tiles)
    def _(i):
        at = pl.ds(pl.multiple_of(i * rows, rows), rows)
        for k in range(count):
            fetch(k, i).wait()
        base = coef[0] * box[at] + jnp.dot(
            left_own[at], x_own[...], preferred_element_type=jnp.float32
        )

        @pl.when(earlier)
        def _():
            box[at] = base + coef[1] * jnp.dot(
                left_other[at], x_other[...], preferred_element_type=jnp.float32
            )

        @pl.when(jnp.logical_not(earlier))
        def _():
            box[at] = base

        for k in range(count):
            flush(k, i).start()

    for i in range(tiles):
        for k in range(count):
            flush(k, i).wait()


def turn_kernel(count, *refs):
    weight, out = refs[count], refs[-1]
    for k in range(count):

        @pl.when(pl.program_id(0) == k)
        def _():
            for lane in range(0, refs[k].shape[1], LANES):
                part = refs[k][:, lane : lane + LANES].astype(jnp.float32) * weight[...]
                out[lane : lane + LANES, :] = part.T.astype(jnp.bfloat16)


def turn_call(pieces, weight):
    count = len(pieces)
    minutes, width = pieces[0].shape
    return pl.pallas_call(
        functools.partial(turn_kernel, count),
        out_shape=jax.ShapeDtypeStruct((count * width, minutes), jnp.bfloat16),
        grid=(count,),
        in_specs=[pl.BlockSpec((minutes, width), lambda k: (0, 0))] * count
        + [pl.BlockSpec((minutes, LANES), lambda k: (0, 0))],
        out_specs=pl.BlockSpec((width, minutes), lambda k: (k, 0)),
        cost_estimate=pl.CostEstimate(
            flops=count * minutes * width,
            bytes_accessed=4 * count * minutes * width,
            transcendentals=0,
        ),
    )(*pieces, weight)


def tile_call(out, columns, coef, own, other, weight, left_own, left_other, prior, rows):
    count = len(own)
    minutes, width = own[0].shape
    height, total = prior.shape
    tiles = height // rows
    near = pl.BlockSpec(memory_space=pltpu.VMEM)
    far = pl.BlockSpec(memory_space=pl.ANY)
    scalar = pl.BlockSpec(memory_space=pltpu.SMEM)
    args = [columns, coef, *own, *other, weight, left_own, left_other, prior]
    in_specs = [scalar] * 2 + [far] * (2 * count) + [near] * 3 + [far]
    aliases = {}
    if out is not None:
        aliases = {len(args): 0}
        in_specs.append(far)
        args.append(out)
    return pl.pallas_call(
        functools.partial(tile_kernel, count, rows),
        out_shape=jax.ShapeDtypeStruct((1, height, total), jnp.float32),
        in_specs=in_specs,
        out_specs=far,
        scratch_shapes=[
            pltpu.VMEM((minutes, count * width), jnp.bfloat16),
            pltpu.VMEM((minutes, count * width), jnp.bfloat16),
            pltpu.VMEM((height, count * width), jnp.float32),
            pltpu.SemaphoreType.DMA((2, count)),
            pltpu.SemaphoreType.DMA((count, tiles)),
            pltpu.SemaphoreType.DMA((count, tiles)),
        ],
        input_output_aliases=aliases,
        compiler_params=pltpu.CompilerParams(vmem_limit_bytes=24 * 2**20),
        cost_estimate=pl.CostEstimate(
            flops=4 * count * minutes * width * height,
            bytes_accessed=count * (8 * width * height + 4 * width * minutes),
            transcendentals=0,
        ),
    )(*args)


def last_cuts(half):
    return (half // 2, half // 4, half // 4)


def local_ring(returns, prior):
    minutes, width = returns.shape
    n = lax.axis_size("assets")
    me, slab = lax.axis_index("assets"), lax.axis_index("tm")
    half = width // 2
    rows = min(prior.shape[0], 512)

    cycle = list(range(0, n, 2)) + list(range(n - 1, 0, -2))
    forward = [(cycle[k], cycle[(k + 1) % n]) for k in range(n)]
    backward = [(b, a) for a, b in forward]
    place = jnp.where(me % 2 == 0, me // 2, n - 1 - me // 2)

    def owner(step):
        at = lax.rem(place - step + 2 * n, n)
        return jnp.where(at < n // 2, 2 * at, 2 * (n - 1 - at) + 1)

    def swap(pieces):
        moved = []
        for part in pieces:
            moved.append(lax.ppermute(part, "tm", [(0, 1), (1, 0)]))
        return moved

    weight, factor = weights(minutes)
    wide = jnp.broadcast_to(weight[:, None], (minutes, LANES))
    coef = jnp.where(slab == 0, jnp.stack([factor, 0.0]), jnp.stack([factor * factor, factor]))

    def hop(parts):
        moved = []
        for way, pairs in enumerate((forward, backward)):
            moved.append(lax.ppermute(parts[way], "assets", pairs))
        return moved

    halves = [returns[:, :half], returns[:, half:]]
    flight = [halves, halves[::-1]]
    arrived = []
    for k in range(n - 2):
        flight[k % 2] = hop(flight[k % 2])
        arrived.append((flight[k % 2], k // 2 + 1, (k % 2, 1 - k % 2), 0))
    start = 0
    for part in last_cuts(half):
        cut = slice(start, start + part)
        arrived.append((hop([f[:, cut] for f in flight[0]]), n // 2, (0, 1), start))
        start = start + part

    own_other = swap(halves)
    left_own = turn_call(halves, wide)
    left_other = turn_call(own_other, wide)

    common = (wide, left_own, left_other, prior, rows)
    unit = half // LANES
    columns = (2 * me + jnp.arange(2, dtype=jnp.int32)) * unit
    out = tile_call(None, columns, coef, halves, own_other, *common)
    for pair, step, sides, start in arrived:
        block = owner(jnp.array([step, -step], jnp.int32))
        columns = (2 * block + jnp.array(sides, jnp.int32)) * unit + start // LANES
        other = swap(pair)
        out = tile_call(out, columns, coef, pair, other, *common)
    return out


def solution(mesh):
    n, slabs = mesh.shape["assets"], mesh.shape["tm"]

    def rings(width):
        return slabs == 2 and n % 2 == 0 and 4 <= n <= 16 and width % (8 * LANES) == 0

    def local(returns, prior):
        if not rings(returns.shape[1]):
            return local_any(returns, prior)
        return local_ring(returns, prior)

    placed = (P("tm", ("groups", "assets")), P(("groups", "assets"), None))
    return jax.shard_map(
        local,
        mesh=mesh,
        in_specs=placed,
        out_specs=P("tm", ("groups", "assets"), None),
        check_vma=False,
    )
```

profile of v0, /device:TPU:0, one launch (start us, length us, event | category | flops | bytes accessed | tf_op | source)
XLA Modules:
  0.0 180.3 jit_solution(2416214351050572206)
XLA Ops:
  0.0 1.5 fusion.16
  1.5 0.6 collective-permute-start.10
  2.1 2.6 %collective-permute-start = (bf16[768,512]{1,0:T(8,128)(2,1)S(1)}, bf16[768,512]{1,0:T(8,128)(2,1)S(1)}, u32[]{:S(2)}, u32[]{:S(2)}) collective-permute-start(bf16[768,512]{1,0:T(8,128)(2,1)S(1)} %get-tuple-element.14.refs_0_), channel_id=1, source_target_pairs={{0,4},{4,8},{8,12},{12,14},{14,10},{10,6},{6,2},{2,0},{1,5},{5,9},... | collective-permute-start | bytes 2359304 | tf_op jit(solution)/shard_map/ppermute | solution.py:245
  5.0 1.8 %collective-permute-start.20 = (bf16[768,512]{1,0:T(8,128)(2,1)S(1)}, bf16[768,512]{1,0:T(8,128)(2,1)}, u32[]{:S(2)}, u32[]{:S(2)}) collective-permute-start(bf16[768,512]{1,0:T(8,128)(2,1)S(1)} %get-tuple-element.13.refs_1_), channel_id=1, source_target_pairs={{0,4},{4,8},{8,12},{12,14},{14,10},{10,6},{6,2},{2,0},{1,5},{5,9},... | collective-permute-start | bytes 2359304 | tf_op jit(solution)/shard_map/ppermute | solution.py:245
  6.9 0.2 collective-permute-start.23
  7.1 15.9 %collective-permute-done.refs_0_ = bf16[768,512]{1,0:T(8,128)(2,1)S(1)} collective-permute-done((bf16[768,512]{1,0:T(8,128)(2,1)S(1)}, bf16[768,512]{1,0:T(8,128)(2,1)S(1)}, u32[]{:S(2)}, u32[]{:S(2)}) %collective-permute-start) | collective-permute-done | bytes 786464 | tf_op jit(solution)/shard_map/ppermute | solution.py:245
  23.0 2.2 %collective-permute-start.1 = (bf16[768,512]{1,0:T(8,128)(2,1)S(1)}, bf16[768,512]{1,0:T(8,128)(2,1)}, u32[]{:S(2)}, u32[]{:S(2)}) collective-permute-start(bf16[768,512]{1,0:T(8,128)(2,1)S(1)} %collective-permute-done.refs_0_), channel_id=1, source_target_pairs={{0,4},{4,8},{8,12},{12,14},{14,10},{10,6},{6,2},{2,0},{1,5},{5,9},... | collective-permute-start | bytes 2359304 | tf_op jit(solution)/shard_map/ppermute | solution.py:245
  25.4 14.6 %collective-permute-done.20.refs_0_ = bf16[768,512]{1,0:T(8,128)(2,1)} collective-permute-done((bf16[768,512]{1,0:T(8,128)(2,1)S(1)}, bf16[768,512]{1,0:T(8,128)(2,1)}, u32[]{:S(2)}, u32[]{:S(2)}) %collective-permute-start.20) | collective-permute-done | bytes 786464 | tf_op jit(solution)/shard_map/ppermute | solution.py:245
  39.9 2.0 %collective-permute-start.5 = (bf16[768,512]{1,0:T(8,128)(2,1)}, bf16[768,512]{1,0:T(8,128)(2,1)}, u32[]{:S(2)}, u32[]{:S(2)}) collective-permute-start(bf16[768,512]{1,0:T(8,128)(2,1)} %collective-permute-done.4.refs_1_), channel_id=1, source_target_pairs={{4,0},{8,4},{12,8},{14,12},{10,14},{6,10},{2,6},{0,2},{5,1},{9,5},... | collective-permute-start | bytes 2359304 | tf_op jit(solution)/shard_map/ppermute | solution.py:245
  42.0 0.5 collective-permute-start.35
  42.5 0.7 broadcast_add_fusion.1
  43.2 0.6 copy-done.21
  43.7 0.7 fusion.1
  44.4 0.7 fusion
  45.1 0.9 copy-done.19
  46.0 1.2 collective-permute-start.21
  47.2 0.9 copy-done.15
  48.1 0.8 collective-permute-start.24
  48.9 7.9 %collective-permute-done.1.refs_0_ = bf16[768,512]{1,0:T(8,128)(2,1)} collective-permute-done((bf16[768,512]{1,0:T(8,128)(2,1)S(1)}, bf16[768,512]{1,0:T(8,128)(2,1)}, u32[]{:S(2)}, u32[]{:S(2)}) %collective-permute-start.1) | collective-permute-done | bytes 786464 | tf_op jit(solution)/shard_map/ppermute | solution.py:245
  56.8 0.9 copy-done.17
  57.7 2.1 %collective-permute-start.2 = (bf16[768,512]{1,0:T(8,128)(2,1)}, bf16[768,512]{1,0:T(8,128)(2,1)}, u32[]{:S(2)}, u32[]{:S(2)}) collective-permute-start(bf16[768,512]{1,0:T(8,128)(2,1)} %collective-permute-done.1.refs_0_), channel_id=1, source_target_pairs={{0,4},{4,8},{8,12},{12,14},{14,10},{10,6},{6,2},{2,0},{1,5},{5,9},... | collective-permute-start | bytes 2359304 | tf_op jit(solution)/shard_map/ppermute | solution.py:245
  59.8 1.0 collective-permute-done.5.refs_1_
  60.8 0.9 broadcast_in_dim.28.refs_2_.refs_4_
  61.7 3.0 %shard_map.190.refs_5_ = bf16[1024,768]{1,0:T(8,128)(2,1)} custom-call(bf16[768,512]{1,0:T(8,128)(2,1)} %copy-done.7, bf16[768,512]{1,0:T(8,128)(2,1)} %copy-done.5, f32[768,128]{1,0:T(8,128)} %broadcast_in_dim.28.refs_2_.refs_4_), custom_call_target="tpu_custom_call" | custom-call | flops 786432 | bytes 3145728 | tf_op jit(solution)/shard_map/pallas_call | solution.py:159
  64.7 0.7 fusion.3
  65.4 0.7 broadcast_select_fusion.coef
  66.0 0.7 add_multiply_fusion.1
  66.7 3.1 %shard_map.191.refs_6_ = bf16[1024,768]{1,0:T(8,128)(2,1)} custom-call(bf16[768,512]{1,0:T(8,128)(2,1)} %copy-done.9, bf16[768,512]{1,0:T(8,128)(2,1)} %copy-done.11, f32[768,128]{1,0:T(8,128)} %broadcast_in_dim.28.refs_2_.refs_4_), custom_call_target="tpu_custom_call" | custom-call | flops 786432 | bytes 3145728 | tf_op jit(solution)/shard_map/pallas_call | solution.py:159
  69.8 3.8 %collective-permute-done.21.refs_0_ = bf16[768,512]{1,0:T(8,128)(2,1)} collective-permute-done((bf16[768,512]{1,0:T(8,128)(2,1)}, bf16[768,512]{1,0:T(8,128)(2,1)}, u32[]{:S(2)}, u32[]{:S(2)}) %collective-permute-start.21) | collective-permute-done | bytes 786464 | tf_op jit(solution)/shard_map/ppermute | solution.py:245
  73.7 2.0 %collective-permute-start.6 = (bf16[768,512]{1,0:T(8,128)(2,1)}, bf16[768,512]{1,0:T(8,128)(2,1)S(1)}, u32[]{:S(2)}, u32[]{:S(2)}) collective-permute-start(bf16[768,512]{1,0:T(8,128)(2,1)} %collective-permute-done.5.refs_1_), channel_id=1, source_target_pairs={{4,0},{8,4},{12,8},{14,12},{10,14},{6,10},{2,6},{0,2},{5,1},{9,5},... | collective-permute-start | bytes 2359304 | tf_op jit(solution)/shard_map/ppermute | solution.py:245
  75.7 0.5 collective-permute-done.24.refs_1_
  76.2 1.6 collective-permute-start.22
  77.7 0.2 collective-permute-start.31
  78.0 12.5 %collective-permute-done.2.refs_0_ = bf16[768,512]{1,0:T(8,128)(2,1)} collective-permute-done((bf16[768,512]{1,0:T(8,128)(2,1)}, bf16[768,512]{1,0:T(8,128)(2,1)}, u32[]{:S(2)}, u32[]{:S(2)}) %collective-permute-start.2) | collective-permute-done | bytes 786464 | tf_op jit(solution)/shard_map/ppermute | solution.py:245
  90.5 2.0 %collective-permute-start.25 = (bf16[768,512]{1,0:T(8,128)(2,1)}, bf16[768,512]{1,0:T(8,128)(2,1)S(1)}, u32[]{:S(2)}, u32[]{:S(2)}) collective-permute-start(bf16[768,512]{1,0:T(8,128)(2,1)} %collective-permute-done.24.refs_1_), channel_id=1, source_target_pairs={{4,0},{8,4},{12,8},{14,12},{10,14},{6,10},{2,6},{0,2},{5,1},{9,5},... | collective-permute-start | bytes 2359304 | tf_op jit(solution)/shard_map/ppermute | solution.py:245
  92.5 1.4 copy-done
  93.9 1.4 copy-done.2
  95.3 1.0 copy-done.4
  96.3 1.1 copy-done.6
  97.5 1.1 copy-done.8
  98.6 1.1 copy-done.10
  99.7 1.1 copy-done.12
  100.9 6.0 %shard_map.192.refs_8_ = f32[1,1024,8192]{2,1,0:T(8,128)} custom-call(s32[2]{0:T(128)S(1)} %add_multiply_fusion.columns, f32[2]{0:T(128)S(1)} %broadcast_select_fusion.coef, bf16[768,512]{1,0:T(8,128)(2,1)S(1)} %copy-done.8, bf16[768,512]{1,0:T(8,128)(2,1)S(1)} %copy-done.6, bf16[768,512]{1,0:T(8,128)(2,1)S(1)} %copy-done.10, ...), custom_call_target="tpu_custom_call" | custom-call | flops 3221225472 | bytes 11534336 | tf_op jit(solution)/shard_map/pallas_call | solution.py:189
  106.9 6.1 %shard_map.193.refs_8_ = f32[1,1024,8192]{2,1,0:T(8,128)} custom-call(s32[2]{0:T(128)S(1)} %get-tuple-element.5.columns, f32[2]{0:T(128)S(1)} %broadcast_select_fusion.coef, bf16[768,512]{1,0:T(8,128)(2,1)S(1)} %copy-done.14, bf16[768,512]{1,0:T(8,128)(2,1)} %collective-permute-done.4.refs_1_, ...), custom_call_target="tpu_custom_call", output_to_operand_aliasing={{}: (10, {})} | custom-call | flops 3221225472 | bytes 11534336 | tf_op jit(solution)/shard_map/pallas_call | solution.py:189
  113.1 1.0 slice.36
  114.1 1.1 fusion.18
  115.4 2.1 %collective-permute-start.12 = (bf16[768,128]{1,0:T(8,128)(2,1)S(1)}, bf16[768,128]{1,0:T(8,128)(2,1)S(1)}, u32[]{:S(2)}, u32[]{:S(2)}) collective-permute-start(bf16[768,128]{1,0:T(8,128)(2,1)S(1)} %get-tuple-element.17), channel_id=1, source_target_pairs={{0,4},{4,8},{8,12},{12,14},{14,10},{10,6},{6,2},{2,0},{1,5},{5,9},... | collective-permute-start | bytes 589832 | tf_op jit(solution)/shard_map/ppermute | solution.py:245
  117.4 2.4 %collective-permute-start.28 = (bf16[768,512]{1,0:T(8,128)(2,1)}, bf16[768,512]{1,0:T(8,128)(2,1)S(1)}, u32[]{:S(2)}, u32[]{:S(2)}) collective-permute-start(bf16[768,512]{1,0:T(8,128)(2,1)} %collective-permute-done.2.refs_0_), channel_id=1, source_target_pairs={{0,1},{1,0},{2,3},{3,2},{4,5},{5,4},{6,7},{7,6},{8,9},{9,8},{10,11... | collective-permute-start | bytes 2359304 | tf_op jit(solution)/shard_map/ppermute | solution.py:235
  119.9 6.2 %shard_map.194.refs_8_ = f32[1,1024,8192]{2,1,0:T(8,128)} custom-call(s32[2]{0:T(128)S(1)} %get-tuple-element.19.columns, f32[2]{0:T(128)S(1)} %broadcast_select_fusion.coef, bf16[768,512]{1,0:T(8,128)(2,1)} %collective-permute-done.20.refs_0_, bf16[768,512]{1,0:T(8,128)(2,1)} %collective-permute-done.23.refs_1_, ...), custom_call_target="tpu_custom_call", output_to_operand_aliasing={{}: (10, {})} | custom-call | flops 3221225472 | bytes 11534336 | tf_op jit(solution)/shard_map/pallas_call | solution.py:189
  126.2 3.5 %collective-permute-done.12.refs_0_ = bf16[768,128]{1,0:T(8,128)(2,1)S(1)} collective-permute-done((bf16[768,128]{1,0:T(8,128)(2,1)S(1)}, bf16[768,128]{1,0:T(8,128)(2,1)S(1)}, u32[]{:S(2)}, u32[]{:S(2)}) %collective-permute-start.12) | collective-permute-done | bytes 196640 | tf_op jit(solution)/shard_map/ppermute | solution.py:245
  129.6 1.6 collective-permute-start.17
  131.2 1.3 collective-permute-start.26
  132.6 6.5 %shard_map.195.refs_8_ = f32[1,1024,8192]{2,1,0:T(8,128)} custom-call(s32[2]{0:T(128)S(1)} %get-tuple-element.7.columns, f32[2]{0:T(128)S(1)} %broadcast_select_fusion.coef, bf16[768,512]{1,0:T(8,128)(2,1)} %collective-permute-done.1.refs_0_, bf16[768,512]{1,0:T(8,128)(2,1)} %collective-permute-done.5.refs_1_, ...), custom_call_target="tpu_custom_call", output_to_operand_aliasing={{}: (10, {})} | custom-call | flops 3221225472 | bytes 11534336 | tf_op jit(solution)/shard_map/pallas_call | solution.py:189
  139.1 6.2 %shard_map.196.refs_8_ = f32[1,1024,8192]{2,1,0:T(8,128)} custom-call(s32[2]{0:T(128)S(1)} %get-tuple-element.21.columns, f32[2]{0:T(128)S(1)} %broadcast_select_fusion.coef, bf16[768,512]{1,0:T(8,128)(2,1)} %collective-permute-done.21.refs_0_, bf16[768,512]{1,0:T(8,128)(2,1)} %collective-permute-done.24.refs_1_, ...), custom_call_target="tpu_custom_call", output_to_operand_aliasing={{}: (10, {})} | custom-call | flops 3221225472 | bytes 11534336 | tf_op jit(solution)/shard_map/pallas_call | solution.py:189
  145.4 0.5 collective-permute-start.3
  145.9 4.6 %collective-permute-start.18 = (bf16[768,256]{1,0:T(8,128)(2,1)S(1)}, bf16[768,256]{1,0:T(8,128)(2,1)S(1)}, u32[]{:S(2)}, u32[]{:S(2)}) collective-permute-start(bf16[768,256]{1,0:T(8,128)(2,1)S(1)} %collective-permute-done.16.refs_0_), channel_id=1, source_target_pairs={{0,1},{1,0},{2,3},{3,2},{4,5},{5,4},{6,7},{7,6},{8,9},{9,8},{10,11... | collective-permute-start | bytes 1179656 | tf_op jit(solution)/shard_map/ppermute | solution.py:235
  150.5 6.0 %shard_map.197.refs_8_ = f32[1,1024,8192]{2,1,0:T(8,128)} custom-call(s32[2]{0:T(128)S(1)} %get-tuple-element.9.columns, f32[2]{0:T(128)S(1)} %broadcast_select_fusion.coef, bf16[768,512]{1,0:T(8,128)(2,1)} %collective-permute-done.2.refs_0_, bf16[768,512]{1,0:T(8,128)(2,1)S(1)} %collective-permute-done.6.refs_1_, ...), custom_call_target="tpu_custom_call", output_to_operand_aliasing={{}: (10, {})} | custom-call | flops 3221225472 | bytes 11534336 | tf_op jit(solution)/shard_map/pallas_call | solution.py:189
  156.6 1.6 collective-permute-start.7
  158.2 2.3 %collective-permute-start.14 = (bf16[768,128]{1,0:T(8,128)(2,1)S(1)}, bf16[768,128]{1,0:T(8,128)(2,1)S(1)}, u32[]{:S(2)}, u32[]{:S(2)}) collective-permute-start(bf16[768,128]{1,0:T(8,128)(2,1)S(1)} %collective-permute-done.12.refs_0_), channel_id=1, source_target_pairs={{0,1},{1,0},{2,3},{3,2},{4,5},{5,4},{6,7},{7,6},{8,9},{9,8},{10,11... | collective-permute-start | bytes 589832 | tf_op jit(solution)/shard_map/ppermute | solution.py:235
  160.5 6.0 %shard_map.198.refs_8_ = f32[1,1024,8192]{2,1,0:T(8,128)} custom-call(s32[2]{0:T(128)S(1)} %get-tuple-element.20.columns, f32[2]{0:T(128)S(1)} %broadcast_select_fusion.coef, bf16[768,512]{1,0:T(8,128)(2,1)S(1)} %collective-permute-done.22.refs_0_, bf16[768,512]{1,0:T(8,128)(2,1)S(1)} %collective-permute-done.25.refs_1_, ...), custom_call_target="tpu_custom_call", output_to_operand_aliasing={{}: (10, {})} | custom-call | flops 3221225472 | bytes 11534336 | tf_op jit(solution)/shard_map/pallas_call | solution.py:189
  166.6 2.5 %collective-permute-start.8 = (bf16[768,128]{1,0:T(8,128)(2,1)S(1)}, bf16[768,128]{1,0:T(8,128)(2,1)S(1)}, u32[]{:S(2)}, u32[]{:S(2)}) collective-permute-start(bf16[768,128]{1,0:T(8,128)(2,1)S(1)} %collective-permute-done.3.refs_0_), channel_id=1, source_target_pairs={{0,1},{1,0},{2,3},{3,2},{4,5},{5,4},{6,7},{7,6},{8,9},{9,8},{10,11... | collective-permute-start | bytes 589832 | tf_op jit(solution)/shard_map/ppermute | solution.py:235
  169.2 4.2 %shard_map.199.refs_8_ = f32[1,1024,8192]{2,1,0:T(8,128)} custom-call(s32[2]{0:T(128)S(1)} %copy-done.22, f32[2]{0:T(128)S(1)} %broadcast_select_fusion.coef, bf16[768,256]{1,0:T(8,128)(2,1)S(1)} %collective-permute-done.16.refs_0_, bf16[768,256]{1,0:T(8,128)(2,1)S(1)} %collective-permute-done.17.refs_1_, ...), custom_call_target="tpu_custom_call", output_to_operand_aliasing={{}: (10, {})} | custom-call | flops 1610612736 | bytes 5767168 | tf_op jit(solution)/shard_map/pallas_call | solution.py:189
  173.4 3.4 %shard_map.200.refs_8_ = f32[1,1024,8192]{2,1,0:T(8,128)} custom-call(s32[2]{0:T(128)S(1)} %get-tuple-element.11.columns, f32[2]{0:T(128)S(1)} %broadcast_select_fusion.coef, bf16[768,128]{1,0:T(8,128)(2,1)S(1)} %collective-permute-done.12.refs_0_, bf16[768,128]{1,0:T(8,128)(2,1)S(1)} %collective-permute-done.13.refs_1_, ...), custom_call_target="tpu_custom_call", output_to_operand_aliasing={{}: (10, {})} | custom-call | flops 805306368 | bytes 2883584 | tf_op jit(solution)/shard_map/pallas_call | solution.py:189
  176.8 3.4 %shard_map.201 = f32[1,1024,8192]{2,1,0:T(8,128)} custom-call(s32[2]{0:T(128)S(1)} %broadcast_add_fusion.columns, f32[2]{0:T(128)S(1)} %broadcast_select_fusion.coef, bf16[768,128]{1,0:T(8,128)(2,1)S(1)} %collective-permute-done.3.refs_0_, bf16[768,128]{1,0:T(8,128)(2,1)S(1)} %collective-permute-done.7.refs_1_, ...), custom_call_target="tpu_custom_call", output_to_operand_aliasing={{}: (10, {})} | custom-call | flops 805306368 | bytes 2883584 | tf_op jit(solution)/shard_map/pallas_call | solution.py:189
  (85 shorter events, 1.3 us)
Async XLA Ops:
  1.5 60.2 %copy-start.5 = (bf16[768,512]{1,0:T(8,128)(2,1)}, bf16[768,512]{1,0:T(8,128)(2,1)S(1)}, u32[]{:S(2)}) copy-start(bf16[768,512]{1,0:T(8,128)(2,1)S(1)} %get-tuple-element.13.refs_1_) | copy-start | bytes 2359300
  1.5 60.2 %copy-start.7 = (bf16[768,512]{1,0:T(8,128)(2,1)}, bf16[768,512]{1,0:T(8,128)(2,1)S(1)}, u32[]{:S(2)}) copy-start(bf16[768,512]{1,0:T(8,128)(2,1)S(1)} %get-tuple-element.14.refs_0_) | copy-start | bytes 2359300
  1.5 5.4 %collective-permute-start.10 = (bf16[768,512]{1,0:T(8,128)(2,1)S(1)}, bf16[768,512]{1,0:T(8,128)(2,1)S(1)}, u32[]{:S(2)}, u32[]{:S(2)}) collective-permute-start(bf16[768,512]{1,0:T(8,128)(2,1)S(1)} %get-tuple-element.14.refs_0_), channel_id=1, source_target_pairs={{0,1},{1,0},{2,3},{3,2},{4,5},{5,4},{6,7},{7,6},{8,9},{9,8},{10,11... | collective-permute-start | bytes 2359304 | tf_op jit(solution)/shard_map/ppermute | solution.py:235
  2.1 20.9 %collective-permute-start = (bf16[768,512]{1,0:T(8,128)(2,1)S(1)}, bf16[768,512]{1,0:T(8,128)(2,1)S(1)}, u32[]{:S(2)}, u32[]{:S(2)}) collective-permute-start(bf16[768,512]{1,0:T(8,128)(2,1)S(1)} %get-tuple-element.14.refs_0_), channel_id=1, source_target_pairs={{0,4},{4,8},{8,12},{12,14},{14,10},{10,6},{6,2},{2,0},{1,5},{5,9},... | collective-permute-start | bytes 2359304 | tf_op jit(solution)/shard_map/ppermute | solution.py:245
  4.7 18.3 %collective-permute-start.11 = (bf16[768,512]{1,0:T(8,128)(2,1)S(1)}, bf16[768,512]{1,0:T(8,128)(2,1)S(1)}, u32[]{:S(2)}, u32[]{:S(2)}) collective-permute-start(bf16[768,512]{1,0:T(8,128)(2,1)S(1)} %get-tuple-element.13.refs_1_), channel_id=1, source_target_pairs={{0,1},{1,0},{2,3},{3,2},{4,5},{5,4},{6,7},{7,6},{8,9},{9,8},{10,11... | collective-permute-start | bytes 2359304 | tf_op jit(solution)/shard_map/ppermute | solution.py:235
  4.8 20.5 %collective-permute-start.4 = (bf16[768,512]{1,0:T(8,128)(2,1)S(1)}, bf16[768,512]{1,0:T(8,128)(2,1)}, u32[]{:S(2)}, u32[]{:S(2)}) collective-permute-start(bf16[768,512]{1,0:T(8,128)(2,1)S(1)} %get-tuple-element.13.refs_1_), channel_id=1, source_target_pairs={{4,0},{8,4},{12,8},{14,12},{10,14},{6,10},{2,6},{0,2},{5,1},{9,5},... | collective-permute-start | bytes 2359304 | tf_op jit(solution)/shard_map/ppermute | solution.py:245
  5.0 34.9 %collective-permute-start.20 = (bf16[768,512]{1,0:T(8,128)(2,1)S(1)}, bf16[768,512]{1,0:T(8,128)(2,1)}, u32[]{:S(2)}, u32[]{:S(2)}) collective-permute-start(bf16[768,512]{1,0:T(8,128)(2,1)S(1)} %get-tuple-element.13.refs_1_), channel_id=1, source_target_pairs={{0,4},{4,8},{8,12},{12,14},{14,10},{10,6},{6,2},{2,0},{1,5},{5,9},... | collective-permute-start | bytes 2359304 | tf_op jit(solution)/shard_map/ppermute | solution.py:245
  6.9 16.1 %copy-start.9 = (bf16[768,512]{1,0:T(8,128)(2,1)}, bf16[768,512]{1,0:T(8,128)(2,1)S(1)}, u32[]{:S(2)}) copy-start(bf16[768,512]{1,0:T(8,128)(2,1)S(1)} %collective-permute-done.10.refs_0_.refs_2_) | copy-start | bytes 2359300
  6.9 35.1 %collective-permute-start.23 = (bf16[768,512]{1,0:T(8,128)(2,1)S(1)}, bf16[768,512]{1,0:T(8,128)(2,1)}, u32[]{:S(2)}, u32[]{:S(2)}) collective-permute-start(bf16[768,512]{1,0:T(8,128)(2,1)S(1)} %get-tuple-element.14.refs_0_), channel_id=1, source_target_pairs={{4,0},{8,4},{12,8},{14,12},{10,14},{6,10},{2,6},{0,2},{5,1},{9,5},... | collective-permute-start | bytes 2359304 | tf_op jit(solution)/shard_map/ppermute | solution.py:245
  23.0 43.0 %copy-start.13 = (bf16[768,512]{1,0:T(8,128)(2,1)}, bf16[768,512]{1,0:T(8,128)(2,1)S(1)}, u32[]{:S(2)}) copy-start(bf16[768,512]{1,0:T(8,128)(2,1)S(1)} %collective-permute-done.refs_0_) | copy-start | bytes 2359300
  23.0 19.0 %collective-permute-start.36 = (bf16[768,512]{1,0:T(8,128)(2,1)S(1)}, bf16[768,512]{1,0:T(8,128)(2,1)}, u32[]{:S(2)}, u32[]{:S(2)}) collective-permute-start(bf16[768,512]{1,0:T(8,128)(2,1)S(1)} %collective-permute-done.refs_0_), channel_id=1, source_target_pairs={{0,1},{1,0},{2,3},{3,2},{4,5},{5,4},{6,7},{7,6},{8,9},{9,8},{10,11... | collective-permute-start | bytes 2359304 | tf_op jit(solution)/shard_map/ppermute | solution.py:235
  23.0 43.0 %copy-start.11 = (bf16[768,512]{1,0:T(8,128)(2,1)}, bf16[768,512]{1,0:T(8,128)(2,1)S(1)}, u32[]{:S(2)}) copy-start(bf16[768,512]{1,0:T(8,128)(2,1)S(1)} %collective-permute-done.11.refs_1_.refs_3_) | copy-start | bytes 2359300
  23.0 33.8 %collective-permute-start.1 = (bf16[768,512]{1,0:T(8,128)(2,1)S(1)}, bf16[768,512]{1,0:T(8,128)(2,1)}, u32[]{:S(2)}, u32[]{:S(2)}) collective-permute-start(bf16[768,512]{1,0:T(8,128)(2,1)S(1)} %collective-permute-done.refs_0_), channel_id=1, source_target_pairs={{0,4},{4,8},{8,12},{12,14},{14,10},{10,6},{6,2},{2,0},{1,5},{5,9},... | collective-permute-start | bytes 2359304 | tf_op jit(solution)/shard_map/ppermute | solution.py:245
  25.4 19.7 %collective-permute-start.37 = (bf16[768,512]{1,0:T(8,128)(2,1)}, bf16[768,512]{1,0:T(8,128)(2,1)S(1)}, u32[]{:S(2)}, u32[]{:S(2)}) collective-permute-start(bf16[768,512]{1,0:T(8,128)(2,1)} %collective-permute-done.4.refs_1_), channel_id=1, source_target_pairs={{0,1},{1,0},{2,3},{3,2},{4,5},{5,4},{6,7},{7,6},{8,9},{9,8},{10,11... | collective-permute-start | bytes 2359304 | tf_op jit(solution)/shard_map/ppermute | solution.py:235
  39.9 20.8 %collective-permute-start.5 = (bf16[768,512]{1,0:T(8,128)(2,1)}, bf16[768,512]{1,0:T(8,128)(2,1)}, u32[]{:S(2)}, u32[]{:S(2)}) collective-permute-start(bf16[768,512]{1,0:T(8,128)(2,1)} %collective-permute-done.4.refs_1_), channel_id=1, source_target_pairs={{4,0},{8,4},{12,8},{14,12},{10,14},{6,10},{2,6},{0,2},{5,1},{9,5},... | collective-permute-start | bytes 2359304 | tf_op jit(solution)/shard_map/ppermute | solution.py:245
  42.0 5.2 %collective-permute-start.34 = (bf16[768,512]{1,0:T(8,128)(2,1)}, bf16[768,512]{1,0:T(8,128)(2,1)S(1)}, u32[]{:S(2)}, u32[]{:S(2)}) collective-permute-start(bf16[768,512]{1,0:T(8,128)(2,1)} %collective-permute-done.20.refs_0_), channel_id=1, source_target_pairs={{0,1},{1,0},{2,3},{3,2},{4,5},{5,4},{6,7},{7,6},{8,9},{9,8},{10,11... | collective-permute-start | bytes 2359304 | tf_op jit(solution)/shard_map/ppermute | solution.py:235
  42.0 14.8 %collective-permute-start.35 = (bf16[768,512]{1,0:T(8,128)(2,1)}, bf16[768,512]{1,0:T(8,128)(2,1)S(1)}, u32[]{:S(2)}, u32[]{:S(2)}) collective-permute-start(bf16[768,512]{1,0:T(8,128)(2,1)} %collective-permute-done.23.refs_1_), channel_id=1, source_target_pairs={{0,1},{1,0},{2,3},{3,2},{4,5},{5,4},{6,7},{7,6},{8,9},{9,8},{10,11... | collective-permute-start | bytes 2359304 | tf_op jit(solution)/shard_map/ppermute | solution.py:235
  43.2 0.6 copy-start.21
  45.1 0.9 copy-start.19
  46.0 27.7 %collective-permute-start.21 = (bf16[768,512]{1,0:T(8,128)(2,1)}, bf16[768,512]{1,0:T(8,128)(2,1)}, u32[]{:S(2)}, u32[]{:S(2)}) collective-permute-start(bf16[768,512]{1,0:T(8,128)(2,1)} %collective-permute-done.20.refs_0_), channel_id=1, source_target_pairs={{0,4},{4,8},{8,12},{12,14},{14,10},{10,6},{6,2},{2,0},{1,5},{5,9},... | collective-permute-start | bytes 2359304 | tf_op jit(solution)/shard_map/ppermute | solution.py:245
  47.2 0.9 copy-start.15
  48.1 28.1 %collective-permute-start.24 = (bf16[768,512]{1,0:T(8,128)(2,1)}, bf16[768,512]{1,0:T(8,128)(2,1)}, u32[]{:S(2)}, u32[]{:S(2)}) collective-permute-start(bf16[768,512]{1,0:T(8,128)(2,1)} %collective-permute-done.23.refs_1_), channel_id=1, source_target_pairs={{4,0},{8,4},{12,8},{14,12},{10,14},{6,10},{2,6},{0,2},{5,1},{9,5},... | collective-permute-start | bytes 2359304 | tf_op jit(solution)/shard_map/ppermute | solution.py:245
  56.8 19.4 %collective-permute-start.32 = (bf16[768,512]{1,0:T(8,128)(2,1)}, bf16[768,512]{1,0:T(8,128)(2,1)}, u32[]{:S(2)}, u32[]{:S(2)}) collective-permute-start(bf16[768,512]{1,0:T(8,128)(2,1)} %collective-permute-done.1.refs_0_), channel_id=1, source_target_pairs={{0,1},{1,0},{2,3},{3,2},{4,5},{5,4},{6,7},{7,6},{8,9},{9,8},{10,11... | collective-permute-start | bytes 2359304 | tf_op jit(solution)/shard_map/ppermute | solution.py:235
  56.8 0.9 copy-start.17
  57.7 32.8 %collective-permute-start.2 = (bf16[768,512]{1,0:T(8,128)(2,1)}, bf16[768,512]{1,0:T(8,128)(2,1)}, u32[]{:S(2)}, u32[]{:S(2)}) collective-permute-start(bf16[768,512]{1,0:T(8,128)(2,1)} %collective-permute-done.1.refs_0_), channel_id=1, source_target_pairs={{0,4},{4,8},{8,12},{12,14},{14,10},{10,6},{6,2},{2,0},{1,5},{5,9},... | collective-permute-start | bytes 2359304 | tf_op jit(solution)/shard_map/ppermute | solution.py:245
  60.8 17.0 %collective-permute-start.33 = (bf16[768,512]{1,0:T(8,128)(2,1)}, bf16[768,512]{1,0:T(8,128)(2,1)}, u32[]{:S(2)}, u32[]{:S(2)}) collective-permute-start(bf16[768,512]{1,0:T(8,128)(2,1)} %collective-permute-done.5.refs_1_), channel_id=1, source_target_pairs={{0,1},{1,0},{2,3},{3,2},{4,5},{5,4},{6,7},{7,6},{8,9},{9,8},{10,11... | collective-permute-start | bytes 2359304 | tf_op jit(solution)/shard_map/ppermute | solution.py:235
  66.7 40.2 %copy-start.1 = (bf16[1024,768]{1,0:T(8,128)(2,1)S(1)}, bf16[1024,768]{1,0:T(8,128)(2,1)}, u32[]{:S(2)}) copy-start(bf16[1024,768]{1,0:T(8,128)(2,1)} %shard_map.190.refs_5_) | copy-start | bytes 4718596
  66.7 40.2 %copy-start.14 = (bf16[768,512]{1,0:T(8,128)(2,1)S(1)}, bf16[768,512]{1,0:T(8,128)(2,1)}, u32[]{:S(2)}) copy-start(bf16[768,512]{1,0:T(8,128)(2,1)} %copy-done.13) | copy-start | bytes 2359300
  66.7 40.2 %copy-start.20 = (bf16[768,512]{1,0:T(8,128)(2,1)S(1)}, bf16[768,512]{1,0:T(8,128)(2,1)}, u32[]{:S(2)}) copy-start(bf16[768,512]{1,0:T(8,128)(2,1)} %copy-done.19) | copy-start | bytes 2359300
  73.7 41.5 %collective-permute-start.6 = (bf16[768,512]{1,0:T(8,128)(2,1)}, bf16[768,512]{1,0:T(8,128)(2,1)S(1)}, u32[]{:S(2)}, u32[]{:S(2)}) collective-permute-start(bf16[768,512]{1,0:T(8,128)(2,1)} %collective-permute-done.5.refs_1_), channel_id=1, source_target_pairs={{4,0},{8,4},{12,8},{14,12},{10,14},{6,10},{2,6},{0,2},{5,1},{9,5},... | collective-permute-start | bytes 2359304 | tf_op jit(solution)/shard_map/ppermute | solution.py:245
  76.2 39.2 %collective-permute-start.30 = (bf16[768,512]{1,0:T(8,128)(2,1)}, bf16[768,512]{1,0:T(8,128)(2,1)S(1)}, u32[]{:S(2)}, u32[]{:S(2)}) collective-permute-start(bf16[768,512]{1,0:T(8,128)(2,1)} %collective-permute-done.21.refs_0_), channel_id=1, source_target_pairs={{0,1},{1,0},{2,3},{3,2},{4,5},{5,4},{6,7},{7,6},{8,9},{9,8},{10,11... | collective-permute-start | bytes 2359304 | tf_op jit(solution)/shard_map/ppermute | solution.py:235
  76.2 41.3 %collective-permute-start.22 = (bf16[768,512]{1,0:T(8,128)(2,1)}, bf16[768,512]{1,0:T(8,128)(2,1)S(1)}, u32[]{:S(2)}, u32[]{:S(2)}) collective-permute-start(bf16[768,512]{1,0:T(8,128)(2,1)} %collective-permute-done.21.refs_0_), channel_id=1, source_target_pairs={{0,4},{4,8},{8,12},{12,14},{14,10},{10,6},{6,2},{2,0},{1,5},{5,9},... | collective-permute-start | bytes 2359304 | tf_op jit(solution)/shard_map/ppermute | solution.py:245
  77.7 39.7 %collective-permute-start.31 = (bf16[768,512]{1,0:T(8,128)(2,1)}, bf16[768,512]{1,0:T(8,128)(2,1)S(1)}, u32[]{:S(2)}, u32[]{:S(2)}) collective-permute-start(bf16[768,512]{1,0:T(8,128)(2,1)} %collective-permute-done.24.refs_1_), channel_id=1, source_target_pairs={{0,1},{1,0},{2,3},{3,2},{4,5},{5,4},{6,7},{7,6},{8,9},{9,8},{10,11... | collective-permute-start | bytes 2359304 | tf_op jit(solution)/shard_map/ppermute | solution.py:235
  90.5 29.3 %collective-permute-start.25 = (bf16[768,512]{1,0:T(8,128)(2,1)}, bf16[768,512]{1,0:T(8,128)(2,1)S(1)}, u32[]{:S(2)}, u32[]{:S(2)}) collective-permute-start(bf16[768,512]{1,0:T(8,128)(2,1)} %collective-permute-done.24.refs_1_), channel_id=1, source_target_pairs={{4,0},{8,4},{12,8},{14,12},{10,14},{6,10},{2,6},{0,2},{5,1},{9,5},... | collective-permute-start | bytes 2359304 | tf_op jit(solution)/shard_map/ppermute | solution.py:245
  92.5 1.4 copy-start
  93.9 1.4 copy-start.2
  95.3 1.0 copy-start.4
  96.3 1.1 copy-start.6
  97.5 1.1 copy-start.8
  98.6 1.1 copy-start.10
  99.7 1.1 copy-start.12
  100.9 6.0 %copy-start.3 = (bf16[1024,768]{1,0:T(8,128)(2,1)S(1)}, bf16[1024,768]{1,0:T(8,128)(2,1)}, u32[]{:S(2)}) copy-start(bf16[1024,768]{1,0:T(8,128)(2,1)} %shard_map.191.refs_6_) | copy-start | bytes 4718596
  106.9 13.0 %copy-start.16 = (bf16[768,512]{1,0:T(8,128)(2,1)S(1)}, bf16[768,512]{1,0:T(8,128)(2,1)}, u32[]{:S(2)}) copy-start(bf16[768,512]{1,0:T(8,128)(2,1)} %copy-done.15) | copy-start | bytes 2359300
  106.9 13.0 %copy-start.18 = (bf16[768,512]{1,0:T(8,128)(2,1)S(1)}, bf16[768,512]{1,0:T(8,128)(2,1)}, u32[]{:S(2)}) copy-start(bf16[768,512]{1,0:T(8,128)(2,1)} %copy-done.17) | copy-start | bytes 2359300
  115.2 17.4 %collective-permute-start.16 = (bf16[768,256]{1,0:T(8,128)(2,1)S(1)}, bf16[768,256]{1,0:T(8,128)(2,1)S(1)}, u32[]{:S(2)}, u32[]{:S(2)}) collective-permute-start(bf16[768,256]{1,0:T(8,128)(2,1)S(1)} %slice.36), channel_id=1, source_target_pairs={{0,4},{4,8},{8,12},{12,14},{14,10},{10,6},{6,2},{2,0},{1,5},{5,9},... | collective-permute-start | bytes 1179656 | tf_op jit(solution)/shard_map/ppermute | solution.py:245
  115.4 14.3 %collective-permute-start.12 = (bf16[768,128]{1,0:T(8,128)(2,1)S(1)}, bf16[768,128]{1,0:T(8,128)(2,1)S(1)}, u32[]{:S(2)}, u32[]{:S(2)}) collective-permute-start(bf16[768,128]{1,0:T(8,128)(2,1)S(1)} %get-tuple-element.17), channel_id=1, source_target_pairs={{0,4},{4,8},{8,12},{12,14},{14,10},{10,6},{6,2},{2,0},{1,5},{5,9},... | collective-permute-start | bytes 589832 | tf_op jit(solution)/shard_map/ppermute | solution.py:245
  117.4 13.8 %collective-permute-start.13 = (bf16[768,128]{1,0:T(8,128)(2,1)S(1)}, bf16[768,128]{1,0:T(8,128)(2,1)S(1)}, u32[]{:S(2)}, u32[]{:S(2)}) collective-permute-start(bf16[768,128]{1,0:T(8,128)(2,1)S(1)} %get-tuple-element.15), channel_id=1, source_target_pairs={{4,0},{8,4},{12,8},{14,12},{10,14},{6,10},{2,6},{0,2},{5,1},{9,5},... | collective-permute-start | bytes 589832 | tf_op jit(solution)/shard_map/ppermute | solution.py:245
  117.4 28.4 %collective-permute-start.28 = (bf16[768,512]{1,0:T(8,128)(2,1)}, bf16[768,512]{1,0:T(8,128)(2,1)S(1)}, u32[]{:S(2)}, u32[]{:S(2)}) collective-permute-start(bf16[768,512]{1,0:T(8,128)(2,1)} %collective-permute-done.2.refs_0_), channel_id=1, source_target_pairs={{0,1},{1,0},{2,3},{3,2},{4,5},{5,4},{6,7},{7,6},{8,9},{9,8},{10,11... | collective-permute-start | bytes 2359304 | tf_op jit(solution)/shard_map/ppermute | solution.py:235
  119.8 30.6 %collective-permute-start.29 = (bf16[768,512]{1,0:T(8,128)(2,1)S(1)}, bf16[768,512]{1,0:T(8,128)(2,1)S(1)}, u32[]{:S(2)}, u32[]{:S(2)}) collective-permute-start(bf16[768,512]{1,0:T(8,128)(2,1)S(1)} %collective-permute-done.6.refs_1_), channel_id=1, source_target_pairs={{0,1},{1,0},{2,3},{3,2},{4,5},{5,4},{6,7},{7,6},{8,9},{9,8},{10,11... | collective-permute-start | bytes 2359304 | tf_op jit(solution)/shard_map/ppermute | solution.py:235
  129.6 15.7 %collective-permute-start.17 = (bf16[768,256]{1,0:T(8,128)(2,1)S(1)}, bf16[768,256]{1,0:T(8,128)(2,1)S(1)}, u32[]{:S(2)}, u32[]{:S(2)}) collective-permute-start(bf16[768,256]{1,0:T(8,128)(2,1)S(1)} %slice.37), channel_id=1, source_target_pairs={{4,0},{8,4},{12,8},{14,12},{10,14},{6,10},{2,6},{0,2},{5,1},{9,5},... | collective-permute-start | bytes 1179656 | tf_op jit(solution)/shard_map/ppermute | solution.py:245
  131.2 27.0 %collective-permute-start.26 = (bf16[768,512]{1,0:T(8,128)(2,1)S(1)}, bf16[768,512]{1,0:T(8,128)(2,1)S(1)}, u32[]{:S(2)}, u32[]{:S(2)}) collective-permute-start(bf16[768,512]{1,0:T(8,128)(2,1)S(1)} %collective-permute-done.22.refs_0_), channel_id=1, source_target_pairs={{0,1},{1,0},{2,3},{3,2},{4,5},{5,4},{6,7},{7,6},{8,9},{9,8},{10,11... | collective-permute-start | bytes 2359304 | tf_op jit(solution)/shard_map/ppermute | solution.py:235
  132.6 27.9 %collective-permute-start.27 = (bf16[768,512]{1,0:T(8,128)(2,1)S(1)}, bf16[768,512]{1,0:T(8,128)(2,1)S(1)}, u32[]{:S(2)}, u32[]{:S(2)}) collective-permute-start(bf16[768,512]{1,0:T(8,128)(2,1)S(1)} %collective-permute-done.25.refs_1_), channel_id=1, source_target_pairs={{0,1},{1,0},{2,3},{3,2},{4,5},{5,4},{6,7},{7,6},{8,9},{9,8},{10,11... | collective-permute-start | bytes 2359304 | tf_op jit(solution)/shard_map/ppermute | solution.py:235
  145.4 11.2 %collective-permute-start.3 = (bf16[768,128]{1,0:T(8,128)(2,1)S(1)}, bf16[768,128]{1,0:T(8,128)(2,1)S(1)}, u32[]{:S(2)}, u32[]{:S(2)}) collective-permute-start(bf16[768,128]{1,0:T(8,128)(2,1)S(1)} %get-tuple-element.18), channel_id=1, source_target_pairs={{0,4},{4,8},{8,12},{12,14},{14,10},{10,6},{6,2},{2,0},{1,5},{5,9},... | collective-permute-start | bytes 589832 | tf_op jit(solution)/shard_map/ppermute | solution.py:245
  145.9 23.2 %collective-permute-start.18 = (bf16[768,256]{1,0:T(8,128)(2,1)S(1)}, bf16[768,256]{1,0:T(8,128)(2,1)S(1)}, u32[]{:S(2)}, u32[]{:S(2)}) collective-permute-start(bf16[768,256]{1,0:T(8,128)(2,1)S(1)} %collective-permute-done.16.refs_0_), channel_id=1, source_target_pairs={{0,1},{1,0},{2,3},{3,2},{4,5},{5,4},{6,7},{7,6},{8,9},{9,8},{10,11... | collective-permute-start | bytes 1179656 | tf_op jit(solution)/shard_map/ppermute | solution.py:235
  150.5 18.7 %collective-permute-start.19 = (bf16[768,256]{1,0:T(8,128)(2,1)S(1)}, bf16[768,256]{1,0:T(8,128)(2,1)S(1)}, u32[]{:S(2)}, u32[]{:S(2)}) collective-permute-start(bf16[768,256]{1,0:T(8,128)(2,1)S(1)} %collective-permute-done.17.refs_1_), channel_id=1, source_target_pairs={{0,1},{1,0},{2,3},{3,2},{4,5},{5,4},{6,7},{7,6},{8,9},{9,8},{10,11... | collective-permute-start | bytes 1179656 | tf_op jit(solution)/shard_map/ppermute | solution.py:235
  156.6 10.0 %collective-permute-start.7 = (bf16[768,128]{1,0:T(8,128)(2,1)S(1)}, bf16[768,128]{1,0:T(8,128)(2,1)S(1)}, u32[]{:S(2)}, u32[]{:S(2)}) collective-permute-start(bf16[768,128]{1,0:T(8,128)(2,1)S(1)} %get-tuple-element.16), channel_id=1, source_target_pairs={{4,0},{8,4},{12,8},{14,12},{10,14},{6,10},{2,6},{0,2},{5,1},{9,5},... | collective-permute-start | bytes 589832 | tf_op jit(solution)/shard_map/ppermute | solution.py:245
  158.2 15.1 %collective-permute-start.14 = (bf16[768,128]{1,0:T(8,128)(2,1)S(1)}, bf16[768,128]{1,0:T(8,128)(2,1)S(1)}, u32[]{:S(2)}, u32[]{:S(2)}) collective-permute-start(bf16[768,128]{1,0:T(8,128)(2,1)S(1)} %collective-permute-done.12.refs_0_), channel_id=1, source_target_pairs={{0,1},{1,0},{2,3},{3,2},{4,5},{5,4},{6,7},{7,6},{8,9},{9,8},{10,11... | collective-permute-start | bytes 589832 | tf_op jit(solution)/shard_map/ppermute | solution.py:235
  160.5 12.9 %collective-permute-start.15 = (bf16[768,128]{1,0:T(8,128)(2,1)S(1)}, bf16[768,128]{1,0:T(8,128)(2,1)S(1)}, u32[]{:S(2)}, u32[]{:S(2)}) collective-permute-start(bf16[768,128]{1,0:T(8,128)(2,1)S(1)} %collective-permute-done.13.refs_1_), channel_id=1, source_target_pairs={{0,1},{1,0},{2,3},{3,2},{4,5},{5,4},{6,7},{7,6},{8,9},{9,8},{10,11... | collective-permute-start | bytes 589832 | tf_op jit(solution)/shard_map/ppermute | solution.py:235
  160.5 8.6 %copy-start.22 = (s32[2]{0:T(128)S(1)}, s32[2]{0:T(128)}, u32[]{:S(2)}) copy-start(s32[2]{0:T(128)} %copy-done.21) | copy-start | bytes 28
  166.6 10.2 %collective-permute-start.8 = (bf16[768,128]{1,0:T(8,128)(2,1)S(1)}, bf16[768,128]{1,0:T(8,128)(2,1)S(1)}, u32[]{:S(2)}, u32[]{:S(2)}) collective-permute-start(bf16[768,128]{1,0:T(8,128)(2,1)S(1)} %collective-permute-done.3.refs_0_), channel_id=1, source_target_pairs={{0,1},{1,0},{2,3},{3,2},{4,5},{5,4},{6,7},{7,6},{8,9},{9,8},{10,11... | collective-permute-start | bytes 589832 | tf_op jit(solution)/shard_map/ppermute | solution.py:235
  169.1 7.7 %collective-permute-start.9 = (bf16[768,128]{1,0:T(8,128)(2,1)S(1)}, bf16[768,128]{1,0:T(8,128)(2,1)S(1)}, u32[]{:S(2)}, u32[]{:S(2)}) collective-permute-start(bf16[768,128]{1,0:T(8,128)(2,1)S(1)} %collective-permute-done.7.refs_1_), channel_id=1, source_target_pairs={{0,1},{1,0},{2,3},{3,2},{4,5},{5,4},{6,7},{7,6},{8,9},{9,8},{10,11... | collective-permute-start | bytes 589832 | tf_op jit(solution)/shard_map/ppermute | solution.py:235
where the time goes:
time: 183 us; the launch traced here: 180 us
  Pallas kernels  60.2 us (33%)
  waiting for transfers between devices  59.9 us (33%)
  starting transfers between devices  39.5 us (22%)
  local copies, waits for them, and re-layouts  16.2 us (9%)
  other arithmetic  4.03 us (2%)
    ppermute x18, waiting for transfers between devices, hop(): moved.append(lax.ppermute(parts[way], 'assets', pairs))  59.8 us
    pallas_call x10, Pallas kernels, tile_call(): pl.pallas_call(functools.partial(tile_kernel, count, rows), out_shape=jax...  54.1 us
    ppermute x18, starting transfers between devices, hop(): moved.append(lax.ppermute(parts[way], 'assets', pairs))  24.7 us
    ppermute x20, starting transfers between devices, swap(): moved.append(lax.ppermute(part, 'tm', [(0, 1), (1, 0)]))  14.9 us
    unnamed x46, local copies, waits for them, and re-layouts  11.7 us
    pallas_call x2, Pallas kernels, turn_call(): pl.pallas_call(functools.partial(turn_kernel, count), out_shape=jax.Shape...  6.1 us
  transfers between devices with their start and end apart: 38, of which 9 were waited for; matrix products, arithmetic and copies ran while one was open for 4% of the time, Pallas kernels for 31%

commit v1 on v0

--- a/solution.py
+++ b/solution.py
@@ -9,6 +9,7 @@
 
 
 LANES = 128
+LAST_HOPS = 2
 
 
 def weights(minutes):
@@ -64,82 +65,89 @@
     return (factor * (before + reach[0] * prior) + tile)[None]
 
 
-def tile_kernel(count, rows, columns, coef, *refs):
+def tile_kernel(count, group, rows, columns, coef, *refs):
     own, other = refs[:count], refs[count : 2 * count]
     weight, left_own, left_other, prior = refs[2 * count : 2 * count + 4]
-    out, x_own, x_other, box, x_sem, in_sem, out_sem = refs[-7:]
+    out, box, rhs, in_sem, out_sem = refs[-5:]
     width = own[0].shape[1]
-    tiles = prior.shape[0] // rows
+    height = prior.shape[0]
     earlier = coef[1] != 0.0
     copy = pltpu.make_async_copy
-
-    def place(k):
-        return pl.ds(pl.multiple_of(columns[k] * LANES, LANES), width)
-
-    def inside(k):
-        return pl.ds(k * width, width)
-
-    def take(part, x, side, k):
-        return copy(part[k], x.at[:, inside(k)], x_sem.at[side, k])
-
-    def fetch(k, i):
-        at = pl.ds(i * rows, rows)
-        return copy(prior.at[at, place(k)], box.at[at, inside(k)], in_sem.at[k, i])
-
-    def flush(k, i):
-        at = pl.ds(i * rows, rows)
-        return copy(box.at[at, inside(k)], out.at[0, at, place(k)], out_sem.at[k, i])
-
-    def scale_in_place(ref, k):
-        for lane in range(k * width, (k + 1) * width, LANES):
-            at = slice(lane, lane + LANES)
-            ref[:, at] = (ref[:, at].astype(jnp.float32) * weight[...]).astype(jnp.bfloat16)
-
-    for k in range(count):
-        take(own, x_own, 0, k).start()
+    joined = width < group
+    turns = 1 if joined else count * (width // group)
+    part = width if joined else group
+    parts = count if joined else 1
+
+    def where(turn, j):
+        if joined:
+            return j, 0
+        return turn // (width // group), (turn % (width // group)) * group
+
+    def place(turn, j):
+        k, start = where(turn, j)
+        return pl.ds(pl.multiple_of(columns[k] * LANES + start, part), part)
+
+    def fetch(turn, j):
+        at = pl.ds(j * part, part)
+        return copy(prior.at[:, place(turn, j)], box.at[turn, :, at], in_sem.at[turn, j])
+
+    def flush(turn, j, i):
+        at, down = pl.ds(j * part, part), pl.ds(i * rows, rows)
+        return copy(
+            box.at[turn, down, at], out.at[0, down, place(turn, j)], out_sem.at[turn, j, i]
+        )
+
+    def scaled(source, turn, j):
+        k, start = where(turn, j)
+        parts = [
+            (source[k][:, start + lane : start + lane + LANES].astype(jnp.float32) * weight[...])
+            .astype(jnp.bfloat16)
+            for lane in range(0, part, LANES)
+        ]
+        return parts
+
+    for turn in range(turns):
+        for j in range(parts):
+            fetch(turn, j).start()
+
+    for turn in range(turns):
+        for j in range(parts):
+            for lane, piece in enumerate(scaled(own, turn, j)):
+                rhs[0, :, j * part + lane * LANES : j * part + (lane + 1) * LANES] = piece
 
         @pl.when(earlier)
         def _():
-            take(other, x_other, 1, k).start()
-
-    for i in range(tiles):
-        for k in range(count):
-            fetch(k, i).start()
-
-    for k in range(count):
-        take(own, x_own, 0, k).wait()
-        scale_in_place(x_own, k)
-
-        @pl.when(earlier)
-        def _():
-            take(other, x_other, 1, k).wait()
-            scale_in_place(x_other, k)
-
-    @pl.loop(0, tiles)
-    def _(i):
-        at = pl.ds(pl.multiple_of(i * rows, rows), rows)
-        for k in range(count):
-            fetch(k, i).wait()
-        base = coef[0] * box[at] + jnp.dot(
-            left_own[at], x_own[...], preferred_element_type=jnp.float32
-        )
-
-        @pl.when(earlier)
-        def _():
-            box[at] = base + coef[1] * jnp.dot(
-                left_other[at], x_other[...], preferred_element_type=jnp.float32
+            for j in range(parts):
+                for lane, piece in enumerate(scaled(other, turn, j)):
+                    rhs[1, :, j * part + lane * LANES : j * part + (lane + 1) * LANES] = piece
+
+        for j in range(parts):
+            fetch(turn, j).wait()
+
+        @pl.loop(0, height // rows)
+        def _(i):
+            at = pl.ds(pl.multiple_of(i * rows, rows), rows)
+            base = coef[0] * box[turn, at] + jnp.dot(
+                left_own[at], rhs[0], preferred_element_type=jnp.float32
             )
 
-        @pl.when(jnp.logical_not(earlier))
-        def _():
-            box[at] = base
-
-        for k in range(count):
-            flush(k, i).start()
-
-    for i in range(tiles):
-        for k in range(count):
-            flush(k, i).wait()
+            @pl.when(earlier)
+            def _():
+                box[turn, at] = base + coef[1] * jnp.dot(
+                    left_other[at], rhs[1], preferred_element_type=jnp.float32
+                )
+
+            @pl.when(jnp.logical_not(earlier))
+            def _():
+                box[turn, at] = base
+
+            for j in range(parts):
+                flush(turn, j, i).start()
+
+    for turn in range(turns):
+        for j in range(parts):
+            for i in range(height // rows):
+                flush(turn, j, i).wait()
 
 
 def turn_kernel(count, *refs):
@@ -163,6 +171,7 @@
         in_specs=[pl.BlockSpec((minutes, width), lambda k: (0, 0))] * count
         + [pl.BlockSpec((minutes, LANES), lambda k: (0, 0))],
         out_specs=pl.BlockSpec((width, minutes), lambda k: (k, 0)),
+        compiler_params=pltpu.CompilerParams(vmem_limit_bytes=34 * 2**20),
         cost_estimate=pl.CostEstimate(
             flops=count * minutes * width,
             bytes_accessed=4 * count * minutes * width,
@@ -171,36 +180,35 @@
     )(*pieces, weight)
 
 
-def tile_call(out, columns, coef, own, other, weight, left_own, left_other, prior, rows):
+def tile_call(out, columns, coef, own, other, weight, left_own, left_other, prior, rows, group):
     count = len(own)
     minutes, width = own[0].shape
     height, total = prior.shape
-    tiles = height // rows
+    group = min(group, count * width)
+    turns, parts = max(1, count * width // group), (count if width < group else 1)
     near = pl.BlockSpec(memory_space=pltpu.VMEM)
-    far = pl.BlockSpec(memory_space=pl.ANY)
+    far = pl.BlockSpec(memory_space=pltpu.HBM)
     scalar = pl.BlockSpec(memory_space=pltpu.SMEM)
     args = [columns, coef, *own, *other, weight, left_own, left_other, prior]
-    in_specs = [scalar] * 2 + [far] * (2 * count) + [near] * 3 + [far]
+    in_specs = [scalar] * 2 + [near] * (2 * count + 3) + [far]
     aliases = {}
     if out is not None:
         aliases = {len(args): 0}
         in_specs.append(far)
         args.append(out)
     return pl.pallas_call(
-        functools.partial(tile_kernel, count, rows),
+        functools.partial(tile_kernel, count, group, rows),
         out_shape=jax.ShapeDtypeStruct((1, height, total), jnp.float32),
         in_specs=in_specs,
         out_specs=far,
         scratch_shapes=[
-            pltpu.VMEM((minutes, count * width), jnp.bfloat16),
-            pltpu.VMEM((minutes, count * width), jnp.bfloat16),
-            pltpu.VMEM((height, count * width), jnp.float32),
-            pltpu.SemaphoreType.DMA((2, count)),
-            pltpu.SemaphoreType.DMA((count, tiles)),
-            pltpu.SemaphoreType.DMA((count, tiles)),
+            pltpu.VMEM((turns, height, group), jnp.float32),
+            pltpu.VMEM((2, minutes, group), jnp.bfloat16),
+            pltpu.SemaphoreType.DMA((turns, parts)),
+            pltpu.SemaphoreType.DMA((turns, parts, height // rows)),
         ],
         input_output_aliases=aliases,
-        compiler_params=pltpu.CompilerParams(vmem_limit_bytes=24 * 2**20),
+        compiler_params=pltpu.CompilerParams(vmem_limit_bytes=34 * 2**20),
         cost_estimate=pl.CostEstimate(
             flops=4 * count * minutes * width * height,
             bytes_accessed=count * (8 * width * height + 4 * width * minutes),
@@ -210,7 +218,7 @@
 
 
 def last_cuts(half):
-    return (half // 2, half // 4, half // 4)
+    return (half // LAST_HOPS,) * LAST_HOPS
 
 
 def local_ring(returns, prior):
@@ -261,7 +269,7 @@
     left_own = turn_call(halves, wide)
     left_other = turn_call(own_other, wide)
 
-    common = (wide, left_own, left_other, prior, rows)
+    common = (wide, left_own, left_other, prior, rows, 512)
     unit = half // LANES
     columns = (2 * me + jnp.arange(2, dtype=jnp.int32)) * unit
     out = tile_call(None, columns, coef, halves, own_other, *common)

time: 183 us -> 174 us (0.951)
  the two profiles are of different devices: /device:TPU:0 before, /device:TPU:1 now
where the time goes in v1:
time: 174 us
  Pallas kernels  74.3 us (43%)
  waiting for transfers between devices  60.4 us (35%)
  starting transfers between devices  30.7 us (18%)
  other arithmetic  4.04 us (2%)
  local copies, waits for them, and re-layouts  3.96 us (2%)
    pallas_call x9, Pallas kernels, tile_call(): pl.pallas_call(functools.partial(tile_kernel, count, group, rows), out_sh...  73 us
    ppermute x16, waiting for transfers between devices, hop(): moved.append(lax.ppermute(parts[way], 'assets', pairs))  60.4 us
    ppermute x18, starting transfers between devices, swap(): moved.append(lax.ppermute(part, 'tm', [(0, 1), (1, 0)]))  16.8 us
    ppermute x16, starting transfers between devices, hop(): moved.append(lax.ppermute(parts[way], 'assets', pairs))  13.8 us
  transfers between devices with their start and end apart: 34, of which 8 were waited for; matrix products, arithmetic and copies ran while one was open for 4% of the time, Pallas kernels for 40%

profile of v1, /device:TPU:1, one launch (start us, length us, event | category | flops | bytes accessed | tf_op | source)
XLA Modules:
  0.0 173.9 jit_solution(15606323490407575233)
XLA Ops:
  0.0 1.5 fusion.16
  1.5 0.1 collective-permute-start.10
  1.6 2.8 %collective-permute-start = (bf16[768,512]{1,0:T(8,128)(2,1)S(1)}, bf16[768,512]{1,0:T(8,128)(2,1)}, u32[]{:S(2)}, u32[]{:S(2)}) collective-permute-start(bf16[768,512]{1,0:T(8,128)(2,1)S(1)} %get-tuple-element.14.refs_0_), channel_id=1, source_target_pairs={{0,4},{4,8},{8,12},{12,14},{14,10},{10,6},{6,2},{2,0},{1,5},{5,9},... | collective-permute-start | bytes 2359304 | tf_op jit(solution)/shard_map/ppermute | solution.py:253
  4.3 0.0 collective-permute-start.4
  4.3 1.5 collective-permute-start.16
  5.8 0.9 collective-permute-start.11
  6.7 15.5 %collective-permute-done.refs_0_ = bf16[768,512]{1,0:T(8,128)(2,1)} collective-permute-done((bf16[768,512]{1,0:T(8,128)(2,1)S(1)}, bf16[768,512]{1,0:T(8,128)(2,1)}, u32[]{:S(2)}, u32[]{:S(2)}) %collective-permute-start) | collective-permute-done | bytes 786464 | tf_op jit(solution)/shard_map/ppermute | solution.py:253
  22.2 0.9 collective-permute-start.32
  23.1 0.1 collective-permute-done.4.refs_1_
  23.2 2.0 %collective-permute-start.33 = (bf16[768,512]{1,0:T(8,128)(2,1)}, bf16[768,512]{1,0:T(8,128)(2,1)}, u32[]{:S(2)}, u32[]{:S(2)}) collective-permute-start(bf16[768,512]{1,0:T(8,128)(2,1)} %collective-permute-done.4.refs_1_), channel_id=1, source_target_pairs={{0,1},{1,0},{2,3},{3,2},{4,5},{5,4},{6,7},{7,6},{8,9},{9,8},{10,11... | collective-permute-start | bytes 2359304 | tf_op jit(solution)/shard_map/ppermute | solution.py:243
  25.2 13.9 %collective-permute-done.16.refs_0_ = bf16[768,512]{1,0:T(8,128)(2,1)} collective-permute-done((bf16[768,512]{1,0:T(8,128)(2,1)S(1)}, bf16[768,512]{1,0:T(8,128)(2,1)}, u32[]{:S(2)}, u32[]{:S(2)}) %collective-permute-start.16) | collective-permute-done | bytes 786464 | tf_op jit(solution)/shard_map/ppermute | solution.py:253
  39.1 0.6 collective-permute-start.30
  39.7 0.0 collective-permute-done.11.refs_1_.refs_3_
  39.7 1.5 collective-permute-start.1
  41.3 0.5 collective-permute-start.31
  41.7 0.7 fusion.1
  42.4 0.7 fusion
  43.1 0.7 fusion.3
  43.8 0.0 collective-permute-done.33.refs_3_
  43.8 1.6 collective-permute-start.17
  45.4 0.7 broadcast_add_fusion
  46.1 13.1 %collective-permute-done.1.refs_0_ = bf16[768,512]{1,0:T(8,128)(2,1)} collective-permute-done((bf16[768,512]{1,0:T(8,128)(2,1)}, bf16[768,512]{1,0:T(8,128)(2,1)}, u32[]{:S(2)}, u32[]{:S(2)}) %collective-permute-start.1) | collective-permute-done | bytes 786464 | tf_op jit(solution)/shard_map/ppermute | solution.py:253
  59.1 1.3 collective-permute-start.28
  60.4 0.0 collective-permute-done.31.refs_3_
  60.4 1.5 collective-permute-start.2
  62.0 0.0 collective-permute-start.6
  62.0 0.2 broadcast_in_dim.26.refs_2_.refs_4_
  62.2 0.6 shard_map.172.refs_5_
  62.8 0.7 broadcast_select_fusion.coef
  63.5 0.7 add_multiply_fusion.1
  64.2 0.6 shard_map.173.refs_6_
  64.8 11.2 %collective-permute-done.17.refs_0_ = bf16[768,512]{1,0:T(8,128)(2,1)} collective-permute-done((bf16[768,512]{1,0:T(8,128)(2,1)}, bf16[768,512]{1,0:T(8,128)(2,1)}, u32[]{:S(2)}, u32[]{:S(2)}) %collective-permute-start.17) | collective-permute-done | bytes 786464 | tf_op jit(solution)/shard_map/ppermute | solution.py:253
  76.0 1.3 collective-permute-start.29
  77.3 0.0 collective-permute-done.20.refs_1_
  77.3 1.8 %collective-permute-start.26 = (bf16[768,512]{1,0:T(8,128)(2,1)}, bf16[768,512]{1,0:T(8,128)(2,1)S(1)}, u32[]{:S(2)}, u32[]{:S(2)}) collective-permute-start(bf16[768,512]{1,0:T(8,128)(2,1)} %collective-permute-done.17.refs_0_), channel_id=1, source_target_pairs={{0,1},{1,0},{2,3},{3,2},{4,5},{5,4},{6,7},{7,6},{8,9},{9,8},{10,11... | collective-permute-start | bytes 2359304 | tf_op jit(solution)/shard_map/ppermute | solution.py:243
  79.1 8.1 %shard_map.174.refs_8_ = f32[1,1024,8192]{2,1,0:T(8,128)} custom-call(s32[2]{0:T(128)S(1)} %add_multiply_fusion.columns, f32[2]{0:T(128)S(1)} %broadcast_select_fusion.coef, bf16[768,512]{1,0:T(8,128)(2,1)S(1)} %get-tuple-element.14.refs_0_, bf16[768,512]{1,0:T(8,128)(2,1)S(1)} %get-tuple-element.13.refs_1_, ...), custom_call_target="tpu_custom_call" | custom-call | flops 3221225472 | bytes 11534336 | tf_op jit(solution)/shard_map/pallas_call | solution.py:199
  87.2 1.3 collective-permute-start.18
  88.6 4.2 %collective-permute-done.2.refs_0_ = bf16[768,512]{1,0:T(8,128)(2,1)} collective-permute-done((bf16[768,512]{1,0:T(8,128)(2,1)}, bf16[768,512]{1,0:T(8,128)(2,1)}, u32[]{:S(2)}, u32[]{:S(2)}) %collective-permute-start.2) | collective-permute-done | bytes 786464 | tf_op jit(solution)/shard_map/ppermute | solution.py:253
  92.8 1.3 collective-permute-start.27
  94.1 1.5 collective-permute-start.21
  95.6 1.2 fusion.18
  96.8 1.2 fusion.17
  98.0 0.1 collective-permute-start.12
  98.1 1.4 collective-permute-start.13
  99.5 9.4 %shard_map.175.refs_8_ = f32[1,1024,8192]{2,1,0:T(8,128)} custom-call(s32[2]{0:T(128)S(1)} %get-tuple-element.5.columns, f32[2]{0:T(128)S(1)} %broadcast_select_fusion.coef, bf16[768,512]{1,0:T(8,128)(2,1)} %collective-permute-done.refs_0_, bf16[768,512]{1,0:T(8,128)(2,1)} %collective-permute-done.4.refs_1_, ...), custom_call_target="tpu_custom_call", output_to_operand_aliasing={{}: (10, {})} | custom-call | flops 3221225472 | bytes 11534336 | tf_op jit(solution)/shard_map/pallas_call | solution.py:199
  108.9 0.1 collective-permute-start.3
  109.0 0.5 collective-permute-done.18.refs_0_
  109.6 1.3 collective-permute-start.24
  110.9 1.9 %collective-permute-done.21.refs_1_ = bf16[768,512]{1,0:T(8,128)(2,1)S(1)} collective-permute-done((bf16[768,512]{1,0:T(8,128)(2,1)}, bf16[768,512]{1,0:T(8,128)(2,1)S(1)}, u32[]{:S(2)}, u32[]{:S(2)}) %collective-permute-start.21) | collective-permute-done | bytes 786464 | tf_op jit(solution)/shard_map/ppermute | solution.py:253
  112.8 3.0 %collective-permute-start.25 = (bf16[768,512]{1,0:T(8,128)(2,1)}, bf16[768,512]{1,0:T(8,128)(2,1)S(1)}, u32[]{:S(2)}, u32[]{:S(2)}) collective-permute-start(bf16[768,512]{1,0:T(8,128)(2,1)} %collective-permute-done.6.refs_1_), channel_id=1, source_target_pairs={{0,1},{1,0},{2,3},{3,2},{4,5},{5,4},{6,7},{7,6},{8,9},{9,8},{10,11... | collective-permute-start | bytes 2359304 | tf_op jit(solution)/shard_map/ppermute | solution.py:243
  115.9 9.4 %shard_map.176.refs_8_ = f32[1,1024,8192]{2,1,0:T(8,128)} custom-call(s32[2]{0:T(128)S(1)} %get-tuple-element.19.columns, f32[2]{0:T(128)S(1)} %broadcast_select_fusion.coef, bf16[768,512]{1,0:T(8,128)(2,1)} %collective-permute-done.16.refs_0_, bf16[768,512]{1,0:T(8,128)(2,1)} %collective-permute-done.19.refs_1_, ...), custom_call_target="tpu_custom_call", output_to_operand_aliasing={{}: (10, {})} | custom-call | flops 3221225472 | bytes 11534336 | tf_op jit(solution)/shard_map/pallas_call | solution.py:199
  125.3 0.1 collective-permute-start.22
  125.4 0.5 collective-permute-start.23
  125.9 9.3 %shard_map.177.refs_8_ = f32[1,1024,8192]{2,1,0:T(8,128)} custom-call(s32[2]{0:T(128)S(1)} %get-tuple-element.7.columns, f32[2]{0:T(128)S(1)} %broadcast_select_fusion.coef, bf16[768,512]{1,0:T(8,128)(2,1)} %collective-permute-done.1.refs_0_, bf16[768,512]{1,0:T(8,128)(2,1)} %collective-permute-done.5.refs_1_, ...), custom_call_target="tpu_custom_call", output_to_operand_aliasing={{}: (10, {})} | custom-call | flops 3221225472 | bytes 11534336 | tf_op jit(solution)/shard_map/pallas_call | solution.py:199
  135.2 0.4 collective-permute-start.7
  135.6 8.9 %shard_map.178.refs_8_ = f32[1,1024,8192]{2,1,0:T(8,128)} custom-call(s32[2]{0:T(128)S(1)} %get-tuple-element.21.columns, f32[2]{0:T(128)S(1)} %broadcast_select_fusion.coef, bf16[768,512]{1,0:T(8,128)(2,1)} %collective-permute-done.17.refs_0_, bf16[768,512]{1,0:T(8,128)(2,1)} %collective-permute-done.20.refs_1_, ...), custom_call_target="tpu_custom_call", output_to_operand_aliasing={{}: (10, {})} | custom-call | flops 3221225472 | bytes 11534336 | tf_op jit(solution)/shard_map/pallas_call | solution.py:199
  144.6 0.1 collective-permute-start.14
  144.7 0.5 collective-permute-start.15
  145.2 8.9 %shard_map.179.refs_8_ = f32[1,1024,8192]{2,1,0:T(8,128)} custom-call(s32[2]{0:T(128)S(1)} %get-tuple-element.9.columns, f32[2]{0:T(128)S(1)} %broadcast_select_fusion.coef, bf16[768,512]{1,0:T(8,128)(2,1)} %collective-permute-done.2.refs_0_, bf16[768,512]{1,0:T(8,128)(2,1)} %collective-permute-done.6.refs_1_, ...), custom_call_target="tpu_custom_call", output_to_operand_aliasing={{}: (10, {})} | custom-call | flops 3221225472 | bytes 11534336 | tf_op jit(solution)/shard_map/pallas_call | solution.py:199
  154.1 0.1 collective-permute-start.8
  154.2 0.5 collective-permute-start.9
  154.7 8.1 %shard_map.180.refs_8_ = f32[1,1024,8192]{2,1,0:T(8,128)} custom-call(s32[2]{0:T(128)S(1)} %get-tuple-element.20.columns, f32[2]{0:T(128)S(1)} %broadcast_select_fusion.coef, bf16[768,512]{1,0:T(8,128)(2,1)S(1)} %collective-permute-done.18.refs_0_, bf16[768,512]{1,0:T(8,128)(2,1)S(1)} %collective-permute-done.21.refs_1_, ...), custom_call_target="tpu_custom_call", output_to_operand_aliasing={{}: (10, {})} | custom-call | flops 3221225472 | bytes 11534336 | tf_op jit(solution)/shard_map/pallas_call | solution.py:199
  162.8 5.4 %shard_map.181.refs_8_ = f32[1,1024,8192]{2,1,0:T(8,128)} custom-call(s32[2]{0:T(128)S(1)} %get-tuple-element.12.columns, f32[2]{0:T(128)S(1)} %broadcast_select_fusion.coef, bf16[768,256]{1,0:T(8,128)(2,1)S(1)} %collective-permute-done.12.refs_0_, bf16[768,256]{1,0:T(8,128)(2,1)S(1)} %collective-permute-done.13.refs_1_, ...), custom_call_target="tpu_custom_call", output_to_operand_aliasing={{}: (10, {})} | custom-call | flops 1610612736 | bytes 5767168 | tf_op jit(solution)/shard_map/pallas_call | solution.py:199
  168.3 5.4 %shard_map.182 = f32[1,1024,8192]{2,1,0:T(8,128)} custom-call(s32[2]{0:T(128)S(1)} %get-tuple-element.11.columns, f32[2]{0:T(128)S(1)} %broadcast_select_fusion.coef, bf16[768,256]{1,0:T(8,128)(2,1)S(1)} %collective-permute-done.3.refs_0_, bf16[768,256]{1,0:T(8,128)(2,1)S(1)} %collective-permute-done.7.refs_1_, ...), custom_call_target="tpu_custom_call", output_to_operand_aliasing={{}: (10, {})} | custom-call | flops 1610612736 | bytes 5767168 | tf_op jit(solution)/shard_map/pallas_call | solution.py:199
  (27 shorter events, 0.1 us)
Async XLA Ops:
  1.5 5.2 %collective-permute-start.10 = (bf16[768,512]{1,0:T(8,128)(2,1)S(1)}, bf16[768,512]{1,0:T(8,128)(2,1)S(1)}, u32[]{:S(2)}, u32[]{:S(2)}) collective-permute-start(bf16[768,512]{1,0:T(8,128)(2,1)S(1)} %get-tuple-element.14.refs_0_), channel_id=1, source_target_pairs={{0,1},{1,0},{2,3},{3,2},{4,5},{5,4},{6,7},{7,6},{8,9},{9,8},{10,11... | collective-permute-start | bytes 2359304 | tf_op jit(solution)/shard_map/ppermute | solution.py:243
  1.6 20.6 %collective-permute-start = (bf16[768,512]{1,0:T(8,128)(2,1)S(1)}, bf16[768,512]{1,0:T(8,128)(2,1)}, u32[]{:S(2)}, u32[]{:S(2)}) collective-permute-start(bf16[768,512]{1,0:T(8,128)(2,1)S(1)} %get-tuple-element.14.refs_0_), channel_id=1, source_target_pairs={{0,4},{4,8},{8,12},{12,14},{14,10},{10,6},{6,2},{2,0},{1,5},{5,9},... | collective-permute-start | bytes 2359304 | tf_op jit(solution)/shard_map/ppermute | solution.py:253
  4.3 18.9 %collective-permute-start.4 = (bf16[768,512]{1,0:T(8,128)(2,1)S(1)}, bf16[768,512]{1,0:T(8,128)(2,1)}, u32[]{:S(2)}, u32[]{:S(2)}) collective-permute-start(bf16[768,512]{1,0:T(8,128)(2,1)S(1)} %get-tuple-element.13.refs_1_), channel_id=1, source_target_pairs={{4,0},{8,4},{12,8},{14,12},{10,14},{6,10},{2,6},{0,2},{5,1},{9,5},... | collective-permute-start | bytes 2359304 | tf_op jit(solution)/shard_map/ppermute | solution.py:253
  4.3 34.7 %collective-permute-start.16 = (bf16[768,512]{1,0:T(8,128)(2,1)S(1)}, bf16[768,512]{1,0:T(8,128)(2,1)}, u32[]{:S(2)}, u32[]{:S(2)}) collective-permute-start(bf16[768,512]{1,0:T(8,128)(2,1)S(1)} %get-tuple-element.13.refs_1_), channel_id=1, source_target_pairs={{0,4},{4,8},{8,12},{12,14},{14,10},{10,6},{6,2},{2,0},{1,5},{5,9},... | collective-permute-start | bytes 2359304 | tf_op jit(solution)/shard_map/ppermute | solution.py:253
  5.8 33.9 %collective-permute-start.11 = (bf16[768,512]{1,0:T(8,128)(2,1)S(1)}, bf16[768,512]{1,0:T(8,128)(2,1)S(1)}, u32[]{:S(2)}, u32[]{:S(2)}) collective-permute-start(bf16[768,512]{1,0:T(8,128)(2,1)S(1)} %get-tuple-element.13.refs_1_), channel_id=1, source_target_pairs={{0,1},{1,0},{2,3},{3,2},{4,5},{5,4},{6,7},{7,6},{8,9},{9,8},{10,11... | collective-permute-start | bytes 2359304 | tf_op jit(solution)/shard_map/ppermute | solution.py:243
  6.7 34.5 %collective-permute-start.19 = (bf16[768,512]{1,0:T(8,128)(2,1)S(1)}, bf16[768,512]{1,0:T(8,128)(2,1)}, u32[]{:S(2)}, u32[]{:S(2)}) collective-permute-start(bf16[768,512]{1,0:T(8,128)(2,1)S(1)} %get-tuple-element.14.refs_0_), channel_id=1, source_target_pairs={{4,0},{8,4},{12,8},{14,12},{10,14},{6,10},{2,6},{0,2},{5,1},{9,5},... | collective-permute-start | bytes 2359304 | tf_op jit(solution)/shard_map/ppermute | solution.py:253
  22.2 19.1 %collective-permute-start.32 = (bf16[768,512]{1,0:T(8,128)(2,1)}, bf16[768,512]{1,0:T(8,128)(2,1)}, u32[]{:S(2)}, u32[]{:S(2)}) collective-permute-start(bf16[768,512]{1,0:T(8,128)(2,1)} %collective-permute-done.refs_0_), channel_id=1, source_target_pairs={{0,1},{1,0},{2,3},{3,2},{4,5},{5,4},{6,7},{7,6},{8,9},{9,8},{10,11... | collective-permute-start | bytes 2359304 | tf_op jit(solution)/shard_map/ppermute | solution.py:243
  23.2 20.6 %collective-permute-start.33 = (bf16[768,512]{1,0:T(8,128)(2,1)}, bf16[768,512]{1,0:T(8,128)(2,1)}, u32[]{:S(2)}, u32[]{:S(2)}) collective-permute-start(bf16[768,512]{1,0:T(8,128)(2,1)} %collective-permute-done.4.refs_1_), channel_id=1, source_target_pairs={{0,1},{1,0},{2,3},{3,2},{4,5},{5,4},{6,7},{7,6},{8,9},{9,8},{10,11... | collective-permute-start | bytes 2359304 | tf_op jit(solution)/shard_map/ppermute | solution.py:243
  39.1 6.3 %collective-permute-start.30 = (bf16[768,512]{1,0:T(8,128)(2,1)}, bf16[768,512]{1,0:T(8,128)(2,1)}, u32[]{:S(2)}, u32[]{:S(2)}) collective-permute-start(bf16[768,512]{1,0:T(8,128)(2,1)} %collective-permute-done.16.refs_0_), channel_id=1, source_target_pairs={{0,1},{1,0},{2,3},{3,2},{4,5},{5,4},{6,7},{7,6},{8,9},{9,8},{10,11... | collective-permute-start | bytes 2359304 | tf_op jit(solution)/shard_map/ppermute | solution.py:243
  39.7 19.4 %collective-permute-start.1 = (bf16[768,512]{1,0:T(8,128)(2,1)}, bf16[768,512]{1,0:T(8,128)(2,1)}, u32[]{:S(2)}, u32[]{:S(2)}) collective-permute-start(bf16[768,512]{1,0:T(8,128)(2,1)} %collective-permute-done.refs_0_), channel_id=1, source_target_pairs={{0,4},{4,8},{8,12},{12,14},{14,10},{10,6},{6,2},{2,0},{1,5},{5,9},... | collective-permute-start | bytes 2359304 | tf_op jit(solution)/shard_map/ppermute | solution.py:253
  41.3 20.7 %collective-permute-start.5 = (bf16[768,512]{1,0:T(8,128)(2,1)}, bf16[768,512]{1,0:T(8,128)(2,1)}, u32[]{:S(2)}, u32[]{:S(2)}) collective-permute-start(bf16[768,512]{1,0:T(8,128)(2,1)} %collective-permute-done.4.refs_1_), channel_id=1, source_target_pairs={{4,0},{8,4},{12,8},{14,12},{10,14},{6,10},{2,6},{0,2},{5,1},{9,5},... | collective-permute-start | bytes 2359304 | tf_op jit(solution)/shard_map/ppermute | solution.py:253
  41.3 19.2 %collective-permute-start.31 = (bf16[768,512]{1,0:T(8,128)(2,1)}, bf16[768,512]{1,0:T(8,128)(2,1)}, u32[]{:S(2)}, u32[]{:S(2)}) collective-permute-start(bf16[768,512]{1,0:T(8,128)(2,1)} %collective-permute-done.19.refs_1_), channel_id=1, source_target_pairs={{0,1},{1,0},{2,3},{3,2},{4,5},{5,4},{6,7},{7,6},{8,9},{9,8},{10,11... | collective-permute-start | bytes 2359304 | tf_op jit(solution)/shard_map/ppermute | solution.py:243
  43.8 32.2 %collective-permute-start.17 = (bf16[768,512]{1,0:T(8,128)(2,1)}, bf16[768,512]{1,0:T(8,128)(2,1)}, u32[]{:S(2)}, u32[]{:S(2)}) collective-permute-start(bf16[768,512]{1,0:T(8,128)(2,1)} %collective-permute-done.16.refs_0_), channel_id=1, source_target_pairs={{0,4},{4,8},{8,12},{12,14},{14,10},{10,6},{6,2},{2,0},{1,5},{5,9},... | collective-permute-start | bytes 2359304 | tf_op jit(solution)/shard_map/ppermute | solution.py:253
  45.4 31.9 %collective-permute-start.20 = (bf16[768,512]{1,0:T(8,128)(2,1)}, bf16[768,512]{1,0:T(8,128)(2,1)}, u32[]{:S(2)}, u32[]{:S(2)}) collective-permute-start(bf16[768,512]{1,0:T(8,128)(2,1)} %collective-permute-done.19.refs_1_), channel_id=1, source_target_pairs={{4,0},{8,4},{12,8},{14,12},{10,14},{6,10},{2,6},{0,2},{5,1},{9,5},... | collective-permute-start | bytes 2359304 | tf_op jit(solution)/shard_map/ppermute | solution.py:253
  59.1 28.1 %collective-permute-start.28 = (bf16[768,512]{1,0:T(8,128)(2,1)}, bf16[768,512]{1,0:T(8,128)(2,1)}, u32[]{:S(2)}, u32[]{:S(2)}) collective-permute-start(bf16[768,512]{1,0:T(8,128)(2,1)} %collective-permute-done.1.refs_0_), channel_id=1, source_target_pairs={{0,1},{1,0},{2,3},{3,2},{4,5},{5,4},{6,7},{7,6},{8,9},{9,8},{10,11... | collective-permute-start | bytes 2359304 | tf_op jit(solution)/shard_map/ppermute | solution.py:243
  60.4 32.4 %collective-permute-start.2 = (bf16[768,512]{1,0:T(8,128)(2,1)}, bf16[768,512]{1,0:T(8,128)(2,1)}, u32[]{:S(2)}, u32[]{:S(2)}) collective-permute-start(bf16[768,512]{1,0:T(8,128)(2,1)} %collective-permute-done.1.refs_0_), channel_id=1, source_target_pairs={{0,4},{4,8},{8,12},{12,14},{14,10},{10,6},{6,2},{2,0},{1,5},{5,9},... | collective-permute-start | bytes 2359304 | tf_op jit(solution)/shard_map/ppermute | solution.py:253
  62.0 32.2 %collective-permute-start.6 = (bf16[768,512]{1,0:T(8,128)(2,1)}, bf16[768,512]{1,0:T(8,128)(2,1)}, u32[]{:S(2)}, u32[]{:S(2)}) collective-permute-start(bf16[768,512]{1,0:T(8,128)(2,1)} %collective-permute-done.5.refs_1_), channel_id=1, source_target_pairs={{4,0},{8,4},{12,8},{14,12},{10,14},{6,10},{2,6},{0,2},{5,1},{9,5},... | collective-permute-start | bytes 2359304 | tf_op jit(solution)/shard_map/ppermute | solution.py:253
  76.0 22.0 %collective-permute-start.29 = (bf16[768,512]{1,0:T(8,128)(2,1)}, bf16[768,512]{1,0:T(8,128)(2,1)S(1)}, u32[]{:S(2)}, u32[]{:S(2)}) collective-permute-start(bf16[768,512]{1,0:T(8,128)(2,1)} %collective-permute-done.5.refs_1_), channel_id=1, source_target_pairs={{0,1},{1,0},{2,3},{3,2},{4,5},{5,4},{6,7},{7,6},{8,9},{9,8},{10,11... | collective-permute-start | bytes 2359304 | tf_op jit(solution)/shard_map/ppermute | solution.py:243
  77.3 20.8 %collective-permute-start.26 = (bf16[768,512]{1,0:T(8,128)(2,1)}, bf16[768,512]{1,0:T(8,128)(2,1)S(1)}, u32[]{:S(2)}, u32[]{:S(2)}) collective-permute-start(bf16[768,512]{1,0:T(8,128)(2,1)} %collective-permute-done.17.refs_0_), channel_id=1, source_target_pairs={{0,1},{1,0},{2,3},{3,2},{4,5},{5,4},{6,7},{7,6},{8,9},{9,8},{10,11... | collective-permute-start | bytes 2359304 | tf_op jit(solution)/shard_map/ppermute | solution.py:243
  87.2 22.3 %collective-permute-start.18 = (bf16[768,512]{1,0:T(8,128)(2,1)}, bf16[768,512]{1,0:T(8,128)(2,1)S(1)}, u32[]{:S(2)}, u32[]{:S(2)}) collective-permute-start(bf16[768,512]{1,0:T(8,128)(2,1)} %collective-permute-done.17.refs_0_), channel_id=1, source_target_pairs={{0,4},{4,8},{8,12},{12,14},{14,10},{10,6},{6,2},{2,0},{1,5},{5,9},... | collective-permute-start | bytes 2359304 | tf_op jit(solution)/shard_map/ppermute | solution.py:253
  92.8 16.1 %collective-permute-start.27 = (bf16[768,512]{1,0:T(8,128)(2,1)}, bf16[768,512]{1,0:T(8,128)(2,1)S(1)}, u32[]{:S(2)}, u32[]{:S(2)}) collective-permute-start(bf16[768,512]{1,0:T(8,128)(2,1)} %collective-permute-done.20.refs_1_), channel_id=1, source_target_pairs={{0,1},{1,0},{2,3},{3,2},{4,5},{5,4},{6,7},{7,6},{8,9},{9,8},{10,11... | collective-permute-start | bytes 2359304 | tf_op jit(solution)/shard_map/ppermute | solution.py:243
  94.1 18.7 %collective-permute-start.21 = (bf16[768,512]{1,0:T(8,128)(2,1)}, bf16[768,512]{1,0:T(8,128)(2,1)S(1)}, u32[]{:S(2)}, u32[]{:S(2)}) collective-permute-start(bf16[768,512]{1,0:T(8,128)(2,1)} %collective-permute-done.20.refs_1_), channel_id=1, source_target_pairs={{4,0},{8,4},{12,8},{14,12},{10,14},{6,10},{2,6},{0,2},{5,1},{9,5},... | collective-permute-start | bytes 2359304 | tf_op jit(solution)/shard_map/ppermute | solution.py:253
  98.0 27.3 %collective-permute-start.12 = (bf16[768,256]{1,0:T(8,128)(2,1)S(1)}, bf16[768,256]{1,0:T(8,128)(2,1)S(1)}, u32[]{:S(2)}, u32[]{:S(2)}) collective-permute-start(bf16[768,256]{1,0:T(8,128)(2,1)S(1)} %get-tuple-element.17), channel_id=1, source_target_pairs={{0,4},{4,8},{8,12},{12,14},{14,10},{10,6},{6,2},{2,0},{1,5},{5,9},... | collective-permute-start | bytes 1179656 | tf_op jit(solution)/shard_map/ppermute | solution.py:253
  98.1 27.3 %collective-permute-start.13 = (bf16[768,256]{1,0:T(8,128)(2,1)S(1)}, bf16[768,256]{1,0:T(8,128)(2,1)S(1)}, u32[]{:S(2)}, u32[]{:S(2)}) collective-permute-start(bf16[768,256]{1,0:T(8,128)(2,1)S(1)} %get-tuple-element.15), channel_id=1, source_target_pairs={{4,0},{8,4},{12,8},{14,12},{10,14},{6,10},{2,6},{0,2},{5,1},{9,5},... | collective-permute-start | bytes 1179656 | tf_op jit(solution)/shard_map/ppermute | solution.py:253
  108.9 26.3 %collective-permute-start.3 = (bf16[768,256]{1,0:T(8,128)(2,1)S(1)}, bf16[768,256]{1,0:T(8,128)(2,1)S(1)}, u32[]{:S(2)}, u32[]{:S(2)}) collective-permute-start(bf16[768,256]{1,0:T(8,128)(2,1)S(1)} %get-tuple-element.18), channel_id=1, source_target_pairs={{0,4},{4,8},{8,12},{12,14},{14,10},{10,6},{6,2},{2,0},{1,5},{5,9},... | collective-permute-start | bytes 1179656 | tf_op jit(solution)/shard_map/ppermute | solution.py:253
  109.6 35.0 %collective-permute-start.24 = (bf16[768,512]{1,0:T(8,128)(2,1)}, bf16[768,512]{1,0:T(8,128)(2,1)S(1)}, u32[]{:S(2)}, u32[]{:S(2)}) collective-permute-start(bf16[768,512]{1,0:T(8,128)(2,1)} %collective-permute-done.2.refs_0_), channel_id=1, source_target_pairs={{0,1},{1,0},{2,3},{3,2},{4,5},{5,4},{6,7},{7,6},{8,9},{9,8},{10,11... | collective-permute-start | bytes 2359304 | tf_op jit(solution)/shard_map/ppermute | solution.py:243
  112.8 31.9 %collective-permute-start.25 = (bf16[768,512]{1,0:T(8,128)(2,1)}, bf16[768,512]{1,0:T(8,128)(2,1)S(1)}, u32[]{:S(2)}, u32[]{:S(2)}) collective-permute-start(bf16[768,512]{1,0:T(8,128)(2,1)} %collective-permute-done.6.refs_1_), channel_id=1, source_target_pairs={{0,1},{1,0},{2,3},{3,2},{4,5},{5,4},{6,7},{7,6},{8,9},{9,8},{10,11... | collective-permute-start | bytes 2359304 | tf_op jit(solution)/shard_map/ppermute | solution.py:243
  125.3 28.9 %collective-permute-start.22 = (bf16[768,512]{1,0:T(8,128)(2,1)S(1)}, bf16[768,512]{1,0:T(8,128)(2,1)S(1)}, u32[]{:S(2)}, u32[]{:S(2)}) collective-permute-start(bf16[768,512]{1,0:T(8,128)(2,1)S(1)} %collective-permute-done.18.refs_0_), channel_id=1, source_target_pairs={{0,1},{1,0},{2,3},{3,2},{4,5},{5,4},{6,7},{7,6},{8,9},{9,8},{10,11... | collective-permute-start | bytes 2359304 | tf_op jit(solution)/shard_map/ppermute | solution.py:243
  125.4 29.3 %collective-permute-start.23 = (bf16[768,512]{1,0:T(8,128)(2,1)S(1)}, bf16[768,512]{1,0:T(8,128)(2,1)S(1)}, u32[]{:S(2)}, u32[]{:S(2)}) collective-permute-start(bf16[768,512]{1,0:T(8,128)(2,1)S(1)} %collective-permute-done.21.refs_1_), channel_id=1, source_target_pairs={{0,1},{1,0},{2,3},{3,2},{4,5},{5,4},{6,7},{7,6},{8,9},{9,8},{10,11... | collective-permute-start | bytes 2359304 | tf_op jit(solution)/shard_map/ppermute | solution.py:243
  135.2 18.9 %collective-permute-start.7 = (bf16[768,256]{1,0:T(8,128)(2,1)S(1)}, bf16[768,256]{1,0:T(8,128)(2,1)S(1)}, u32[]{:S(2)}, u32[]{:S(2)}) collective-permute-start(bf16[768,256]{1,0:T(8,128)(2,1)S(1)} %get-tuple-element.16), channel_id=1, source_target_pairs={{4,0},{8,4},{12,8},{14,12},{10,14},{6,10},{2,6},{0,2},{5,1},{9,5},... | collective-permute-start | bytes 1179656 | tf_op jit(solution)/shard_map/ppermute | solution.py:253
  144.6 18.2 %collective-permute-start.14 = (bf16[768,256]{1,0:T(8,128)(2,1)S(1)}, bf16[768,256]{1,0:T(8,128)(2,1)S(1)}, u32[]{:S(2)}, u32[]{:S(2)}) collective-permute-start(bf16[768,256]{1,0:T(8,128)(2,1)S(1)} %collective-permute-done.12.refs_0_), channel_id=1, source_target_pairs={{0,1},{1,0},{2,3},{3,2},{4,5},{5,4},{6,7},{7,6},{8,9},{9,8},{10,11... | collective-permute-start | bytes 1179656 | tf_op jit(solution)/shard_map/ppermute | solution.py:243
  144.7 18.1 %collective-permute-start.15 = (bf16[768,256]{1,0:T(8,128)(2,1)S(1)}, bf16[768,256]{1,0:T(8,128)(2,1)S(1)}, u32[]{:S(2)}, u32[]{:S(2)}) collective-permute-start(bf16[768,256]{1,0:T(8,128)(2,1)S(1)} %collective-permute-done.13.refs_1_), channel_id=1, source_target_pairs={{0,1},{1,0},{2,3},{3,2},{4,5},{5,4},{6,7},{7,6},{8,9},{9,8},{10,11... | collective-permute-start | bytes 1179656 | tf_op jit(solution)/shard_map/ppermute | solution.py:243
  154.1 14.1 %collective-permute-start.8 = (bf16[768,256]{1,0:T(8,128)(2,1)S(1)}, bf16[768,256]{1,0:T(8,128)(2,1)S(1)}, u32[]{:S(2)}, u32[]{:S(2)}) collective-permute-start(bf16[768,256]{1,0:T(8,128)(2,1)S(1)} %collective-permute-done.3.refs_0_), channel_id=1, source_target_pairs={{0,1},{1,0},{2,3},{3,2},{4,5},{5,4},{6,7},{7,6},{8,9},{9,8},{10,11... | collective-permute-start | bytes 1179656 | tf_op jit(solution)/shard_map/ppermute | solution.py:243
  154.2 14.1 %collective-permute-start.9 = (bf16[768,256]{1,0:T(8,128)(2,1)S(1)}, bf16[768,256]{1,0:T(8,128)(2,1)S(1)}, u32[]{:S(2)}, u32[]{:S(2)}) collective-permute-start(bf16[768,256]{1,0:T(8,128)(2,1)S(1)} %collective-permute-done.7.refs_1_), channel_id=1, source_target_pairs={{0,1},{1,0},{2,3},{3,2},{4,5},{5,4},{6,7},{7,6},{8,9},{9,8},{10,11... | collective-permute-start | bytes 1179656 | tf_op jit(solution)/shard_map/ppermute | solution.py:243

commit v2 on v0

--- a/solution.py
+++ b/solution.py
@@ -9,6 +9,8 @@
 
 
 LANES = 128
+GRANT = 34 * 2**20
+LAST_HOPS = 2
 
 
 def weights(minutes):
@@ -64,10 +66,73 @@
     return (factor * (before + reach[0] * prior) + tile)[None]
 
 
+def split_kernel(returns, weight, *refs):
+    parts, (box, sem) = refs[:-2], refs[-2:]
+    width = parts[0].shape[1]
+    copies = []
+    for k in range(len(parts)):
+        at = slice(k * width, (k + 1) * width)
+        copies.append(pltpu.make_async_copy(returns.at[:, at], box.at[:, at], sem.at[k]))
+        copies[-1].start()
+    for k, part in enumerate(parts):
+        copies[k].wait()
+        for lane in range(0, width, LANES):
+            source = box[:, k * width + lane : k * width + lane + LANES]
+            part[:, lane : lane + LANES] = (
+                source.astype(jnp.float32) * weight[...]
+            ).astype(jnp.bfloat16)
+
+
+def split_call(returns, weight, count):
+    minutes, width = returns.shape
+    near = pl.BlockSpec(memory_space=pltpu.VMEM)
+    part = jax.ShapeDtypeStruct((minutes, width // count), jnp.bfloat16)
+    return pl.pallas_call(
+        split_kernel,
+        out_shape=[part] * count,
+        in_specs=[pl.BlockSpec(memory_space=pltpu.HBM), near],
+        out_specs=[near] * count,
+        scratch_shapes=[
+            pltpu.VMEM((minutes, width), jnp.bfloat16),
+            pltpu.SemaphoreType.DMA((count,)),
+        ],
+        compiler_params=pltpu.CompilerParams(vmem_limit_bytes=GRANT),
+        cost_estimate=pl.CostEstimate(
+            flops=minutes * width, bytes_accessed=4 * minutes * width, transcendentals=0
+        ),
+    )(returns, weight)
+
+
+def turn_kernel(*refs):
+    parts, out = refs[:-1], refs[-1]
+    width = parts[0].shape[1]
+    for k, part in enumerate(parts):
+        for lane in range(0, width, LANES):
+            at = slice(k * width + lane, k * width + lane + LANES)
+            out[at, :] = part[:, lane : lane + LANES].T
+
+
+def turn_call(parts):
+    minutes, width = parts[0].shape
+    near = pl.BlockSpec(memory_space=pltpu.VMEM)
+    return pl.pallas_call(
+        turn_kernel,
+        out_shape=jax.ShapeDtypeStruct((len(parts) * width, minutes), jnp.bfloat16),
+        in_specs=[near] * len(parts),
+        out_specs=near,
+        compiler_params=pltpu.CompilerParams(vmem_limit_bytes=GRANT),
+        cost_estimate=pl.CostEstimate(
+            flops=len(parts) * minutes * width,
+            bytes_accessed=4 * len(parts) * minutes * width,
+            transcendentals=0,
+        ),
+    )(*parts)
+
+
 def tile_kernel(count, rows, columns, coef, *refs):
     own, other = refs[:count], refs[count : 2 * count]
-    weight, left_own, left_other, prior = refs[2 * count : 2 * count + 4]
-    out, x_own, x_other, box, x_sem, in_sem, out_sem = refs[-7:]
+    left_own, left_other, prior = refs[2 * count : 2 * count + 3]
+    out, box, in_sem, out_sem = refs[-4:]
     width = own[0].shape[1]
     tiles = prior.shape[0] // rows
     earlier = coef[1] != 0.0
@@ -76,111 +141,56 @@
     def place(k):
         return pl.ds(pl.multiple_of(columns[k] * LANES, LANES), width)
 
-    def inside(k):
-        return pl.ds(k * width, width)
-
-    def take(part, x, side, k):
-        return copy(part[k], x.at[:, inside(k)], x_sem.at[side, k])
-
     def fetch(k, i):
         at = pl.ds(i * rows, rows)
-        return copy(prior.at[at, place(k)], box.at[at, inside(k)], in_sem.at[k, i])
+        return copy(prior.at[at, place(k)], box.at[k, at], in_sem.at[k, i])
 
     def flush(k, i):
         at = pl.ds(i * rows, rows)
-        return copy(box.at[at, inside(k)], out.at[0, at, place(k)], out_sem.at[k, i])
-
-    def scale_in_place(ref, k):
-        for lane in range(k * width, (k + 1) * width, LANES):
-            at = slice(lane, lane + LANES)
-            ref[:, at] = (ref[:, at].astype(jnp.float32) * weight[...]).astype(jnp.bfloat16)
+        return copy(box.at[k, at], out.at[0, at, place(k)], out_sem.at[k, i])
 
     for k in range(count):
-        take(own, x_own, 0, k).start()
-
-        @pl.when(earlier)
-        def _():
-            take(other, x_other, 1, k).start()
-
-    for i in range(tiles):
-        for k in range(count):
+        for i in range(tiles):
             fetch(k, i).start()
 
     for k in range(count):
-        take(own, x_own, 0, k).wait()
-        scale_in_place(x_own, k)
-
-        @pl.when(earlier)
-        def _():
-            take(other, x_other, 1, k).wait()
-            scale_in_place(x_other, k)
-
-    @pl.loop(0, tiles)
-    def _(i):
-        at = pl.ds(pl.multiple_of(i * rows, rows), rows)
-        for k in range(count):
+
+        @pl.loop(0, tiles)
+        def _(i):
+            at = pl.ds(pl.multiple_of(i * rows, rows), rows)
             fetch(k, i).wait()
-        base = coef[0] * box[at] + jnp.dot(
-            left_own[at], x_own[...], preferred_element_type=jnp.float32
-        )
-
-        @pl.when(earlier)
-        def _():
-            box[at] = base + coef[1] * jnp.dot(
-                left_other[at], x_other[...], preferred_element_type=jnp.float32
-            )
-
-        @pl.when(jnp.logical_not(earlier))
-        def _():
-            box[at] = base
-
-        for k in range(count):
+
+            @pl.when(earlier)
+            def _():
+                box[k, at] = (
+                    coef[0] * box[k, at]
+                    + jnp.dot(left_own[at], own[k][...], preferred_element_type=jnp.float32)
+                    + coef[1]
+                    * jnp.dot(left_other[at], other[k][...], preferred_element_type=jnp.float32)
+                )
+
+            @pl.when(jnp.logical_not(earlier))
+            def _():
+                box[k, at] = coef[0] * box[k, at] + jnp.dot(
+                    left_own[at], own[k][...], preferred_element_type=jnp.float32
+                )
+
             flush(k, i).start()
 
-    for i in range(tiles):
-        for k in range(count):
+    for k in range(count):
+        for i in range(tiles):
             flush(k, i).wait()
 
 
-def turn_kernel(count, *refs):
-    weight, out = refs[count], refs[-1]
-    for k in range(count):
-
-        @pl.when(pl.program_id(0) == k)
-        def _():
-            for lane in range(0, refs[k].shape[1], LANES):
-                part = refs[k][:, lane : lane + LANES].astype(jnp.float32) * weight[...]
-                out[lane : lane + LANES, :] = part.T.astype(jnp.bfloat16)
-
-
-def turn_call(pieces, weight):
-    count = len(pieces)
-    minutes, width = pieces[0].shape
-    return pl.pallas_call(
-        functools.partial(turn_kernel, count),
-        out_shape=jax.ShapeDtypeStruct((count * width, minutes), jnp.bfloat16),
-        grid=(count,),
-        in_specs=[pl.BlockSpec((minutes, width), lambda k: (0, 0))] * count
-        + [pl.BlockSpec((minutes, LANES), lambda k: (0, 0))],
-        out_specs=pl.BlockSpec((width, minutes), lambda k: (k, 0)),
-        cost_estimate=pl.CostEstimate(
-            flops=count * minutes * width,
-            bytes_accessed=4 * count * minutes * width,
-            transcendentals=0,
-        ),
-    )(*pieces, weight)
-
-
-def tile_call(out, columns, coef, own, other, weight, left_own, left_other, prior, rows):
+def tile_call(out, columns, coef, own, other, left_own, left_other, prior, rows):
     count = len(own)
     minutes, width = own[0].shape
     height, total = prior.shape
-    tiles = height // rows
     near = pl.BlockSpec(memory_space=pltpu.VMEM)
-    far = pl.BlockSpec(memory_space=pl.ANY)
+    far = pl.BlockSpec(memory_space=pltpu.HBM)
     scalar = pl.BlockSpec(memory_space=pltpu.SMEM)
-    args = [columns, coef, *own, *other, weight, left_own, left_other, prior]
-    in_specs = [scalar] * 2 + [far] * (2 * count) + [near] * 3 + [far]
+    args = [columns, coef, *own, *other, left_own, left_other, prior]
+    in_specs = [scalar] * 2 + [near] * (2 * count + 2) + [far]
     aliases = {}
     if out is not None:
         aliases = {len(args): 0}
@@ -192,15 +202,12 @@
         in_specs=in_specs,
         out_specs=far,
         scratch_shapes=[
-            pltpu.VMEM((minutes, count * width), jnp.bfloat16),
-            pltpu.VMEM((minutes, count * width), jnp.bfloat16),
-            pltpu.VMEM((height, count * width), jnp.float32),
-            pltpu.SemaphoreType.DMA((2, count)),
-            pltpu.SemaphoreType.DMA((count, tiles)),
-            pltpu.SemaphoreType.DMA((count, tiles)),
+            pltpu.VMEM((count, height, width), jnp.float32),
+            pltpu.SemaphoreType.DMA((count, height // rows)),
+            pltpu.SemaphoreType.DMA((count, height // rows)),
         ],
         input_output_aliases=aliases,
-        compiler_params=pltpu.CompilerParams(vmem_limit_bytes=24 * 2**20),
+        compiler_params=pltpu.CompilerParams(vmem_limit_bytes=GRANT),
         cost_estimate=pl.CostEstimate(
             flops=4 * count * minutes * width * height,
             bytes_accessed=count * (8 * width * height + 4 * width * minutes),
@@ -210,7 +217,7 @@
 
 
 def last_cuts(half):
-    return (half // 2, half // 4, half // 4)
+    return (half // LAST_HOPS,) * LAST_HOPS
 
 
 def local_ring(returns, prior):
@@ -245,7 +252,7 @@
             moved.append(lax.ppermute(parts[way], "assets", pairs))
         return moved
 
-    halves = [returns[:, :half], returns[:, half:]]
+    halves = split_call(returns, wide, 2)
     flight = [halves, halves[::-1]]
     arrived = []
     for k in range(n - 2):
@@ -258,10 +265,10 @@
         start = start + part
 
     own_other = swap(halves)
-    left_own = turn_call(halves, wide)
-    left_other = turn_call(own_other, wide)
-
-    common = (wide, left_own, left_other, prior, rows)
+    left_own = turn_call(halves)
+    left_other = turn_call(own_other)
+
+    common = (left_own, left_other, prior, rows)
     unit = half // LANES
     columns = (2 * me + jnp.arange(2, dtype=jnp.int32)) * unit
     out = tile_call(None, columns, coef, halves, own_other, *common)

time: 183 us -> 168 us (0.918)
  the two profiles are of different devices: /device:TPU:0 before, /device:TPU:1 now
where the time goes in v2:
time: 168 us; the launch traced here: 167 us
  Pallas kernels  63.1 us (38%)
  waiting for transfers between devices  61.3 us (36%)
  starting transfers between devices  30.9 us (18%)
  local copies, waits for them, and re-layouts  7.51 us (4%)
  other arithmetic  4.04 us (2%)
    pallas_call x9, Pallas kernels, tile_call(): pl.pallas_call(functools.partial(tile_kernel, count, rows), out_shape=jax...  61.6 us
    ppermute x16, waiting for transfers between devices, hop(): moved.append(lax.ppermute(parts[way], 'assets', pairs))  61.3 us
    ppermute x18, starting transfers between devices, swap(): moved.append(lax.ppermute(part, 'tm', [(0, 1), (1, 0)]))  17.3 us
    ppermute x16, starting transfers between devices, hop(): moved.append(lax.ppermute(parts[way], 'assets', pairs))  13.6 us
    unnamed x18, local copies, waits for them, and re-layouts  7.24 us
  transfers between devices with their start and end apart: 34, of which 10 were waited for; matrix products, arithmetic and copies ran while one was open for 2% of the time, Pallas kernels for 34%

profile of v2, /device:TPU:1, one launch (start us, length us, event | category | flops | bytes accessed | tf_op | source)
XLA Modules:
  0.0 167.4 jit_solution(17376076047802563755)
XLA Ops:
  0.0 0.2 broadcast_in_dim.2.weight
  0.2 1.4 copy-done.4
  1.6 0.6 shard_map.172
  2.2 0.1 collective-permute-start.10
  2.3 2.8 %collective-permute-start = (bf16[768,512]{1,0:T(8,128)(2,1)S(1)}, bf16[768,512]{1,0:T(8,128)(2,1)S(1)}, u32[]{:S(2)}, u32[]{:S(2)}) collective-permute-start(bf16[768,512]{1,0:T(8,128)(2,1)S(1)} %get-tuple-element.7.refs_0_), channel_id=1, source_target_pairs={{0,4},{4,8},{8,12},{12,14},{14,10},{10,6},{6,2},{2,0},{1,5},{5,9},... | collective-permute-start | bytes 2359304 | tf_op jit(solution)/shard_map/ppermute | solution.py:252
  5.1 1.5 collective-permute-start.16
  6.6 0.9 collective-permute-start.11
  7.5 0.9 copy-done
  8.4 14.6 %collective-permute-done.refs_0_ = bf16[768,512]{1,0:T(8,128)(2,1)S(1)} collective-permute-done((bf16[768,512]{1,0:T(8,128)(2,1)S(1)}, bf16[768,512]{1,0:T(8,128)(2,1)S(1)}, u32[]{:S(2)}, u32[]{:S(2)}) %collective-permute-start) | collective-permute-done | bytes 786464 | tf_op jit(solution)/shard_map/ppermute | solution.py:252
  23.0 0.8 collective-permute-start.32
  23.8 0.2 collective-permute-done.4.refs_1_
  24.0 2.0 %collective-permute-start.33 = (bf16[768,512]{1,0:T(8,128)(2,1)}, bf16[768,512]{1,0:T(8,128)(2,1)}, u32[]{:S(2)}, u32[]{:S(2)}) collective-permute-start(bf16[768,512]{1,0:T(8,128)(2,1)} %collective-permute-done.4.refs_1_), channel_id=1, source_target_pairs={{0,1},{1,0},{2,3},{3,2},{4,5},{5,4},{6,7},{7,6},{8,9},{9,8},{10,11... | collective-permute-start | bytes 2359304 | tf_op jit(solution)/shard_map/ppermute | solution.py:242
  26.0 13.9 %collective-permute-done.16.refs_0_ = bf16[768,512]{1,0:T(8,128)(2,1)} collective-permute-done((bf16[768,512]{1,0:T(8,128)(2,1)S(1)}, bf16[768,512]{1,0:T(8,128)(2,1)}, u32[]{:S(2)}, u32[]{:S(2)}) %collective-permute-start.16) | collective-permute-done | bytes 786464 | tf_op jit(solution)/shard_map/ppermute | solution.py:252
  39.8 0.6 collective-permute-start.30
  40.5 0.9 copy-done.2
  41.4 1.5 collective-permute-start.1
  42.9 0.9 copy-done.5
  43.8 0.5 collective-permute-start.31
  44.3 0.7 fusion.1
  45.0 0.7 fusion.3
  45.6 1.6 collective-permute-start.17
  47.3 0.7 fusion
  47.9 0.7 broadcast_add_fusion
  48.6 12.0 %collective-permute-done.1.refs_0_ = bf16[768,512]{1,0:T(8,128)(2,1)} collective-permute-done((bf16[768,512]{1,0:T(8,128)(2,1)S(1)}, bf16[768,512]{1,0:T(8,128)(2,1)}, u32[]{:S(2)}, u32[]{:S(2)}) %collective-permute-start.1) | collective-permute-done | bytes 786464 | tf_op jit(solution)/shard_map/ppermute | solution.py:252
  60.6 1.3 collective-permute-start.28
  61.9 0.9 copy-done.7
  62.8 1.5 collective-permute-start.2
  64.3 0.5 shard_map.173.refs_4_
  64.8 0.7 broadcast_select_fusion.coef
  65.5 0.7 add_multiply_fusion.1
  66.1 1.1 copy-done.1
  67.3 1.1 copy-done.3
  68.4 0.5 shard_map.174.refs_5_
  68.9 8.5 %collective-permute-done.17.refs_0_ = bf16[768,512]{1,0:T(8,128)(2,1)} collective-permute-done((bf16[768,512]{1,0:T(8,128)(2,1)}, bf16[768,512]{1,0:T(8,128)(2,1)}, u32[]{:S(2)}, u32[]{:S(2)}) %collective-permute-start.17) | collective-permute-done | bytes 786464 | tf_op jit(solution)/shard_map/ppermute | solution.py:252
  77.4 1.3 collective-permute-start.29
  78.7 1.1 collective-permute-done.20.refs_1_
  79.8 1.9 %collective-permute-start.26 = (bf16[768,512]{1,0:T(8,128)(2,1)}, bf16[768,512]{1,0:T(8,128)(2,1)S(1)}, u32[]{:S(2)}, u32[]{:S(2)}) collective-permute-start(bf16[768,512]{1,0:T(8,128)(2,1)} %collective-permute-done.17.refs_0_), channel_id=1, source_target_pairs={{0,1},{1,0},{2,3},{3,2},{4,5},{5,4},{6,7},{7,6},{8,9},{9,8},{10,11... | collective-permute-start | bytes 2359304 | tf_op jit(solution)/shard_map/ppermute | solution.py:242
  81.7 6.8 %shard_map.175.refs_7_ = f32[1,1024,8192]{2,1,0:T(8,128)} custom-call(s32[2]{0:T(128)S(1)} %add_multiply_fusion.columns, f32[2]{0:T(128)S(1)} %broadcast_select_fusion.coef, bf16[768,512]{1,0:T(8,128)(2,1)S(1)} %get-tuple-element.7.refs_0_, bf16[768,512]{1,0:T(8,128)(2,1)S(1)} %get-tuple-element.8.refs_1_, bf16[768,512]{1,0:T(8,128)(2,1)S(1)} %copy-done.1, ...), custom_call_target="tpu_custom_call" | custom-call | flops 3221225472 | bytes 11534336 | tf_op jit(solution)/shard_map/pallas_call | solution.py:199
  88.5 1.3 collective-permute-start.18
  89.9 4.3 %collective-permute-done.2.refs_0_ = bf16[768,512]{1,0:T(8,128)(2,1)S(1)} collective-permute-done((bf16[768,512]{1,0:T(8,128)(2,1)}, bf16[768,512]{1,0:T(8,128)(2,1)S(1)}, u32[]{:S(2)}, u32[]{:S(2)}) %collective-permute-start.2) | collective-permute-done | bytes 786464 | tf_op jit(solution)/shard_map/ppermute | solution.py:252
  94.2 1.3 collective-permute-start.27
  95.5 1.1 collective-permute-done.6.refs_1_
  96.6 0.4 collective-permute-start.21
  97.1 1.1 collective-permute-start.12
  98.2 0.4 collective-permute-start.13
  98.6 8.0 %shard_map.176.refs_7_ = f32[1,1024,8192]{2,1,0:T(8,128)} custom-call(s32[2]{0:T(128)S(1)} %get-tuple-element.9.columns, f32[2]{0:T(128)S(1)} %broadcast_select_fusion.coef, bf16[768,512]{1,0:T(8,128)(2,1)S(1)} %copy-done.6, bf16[768,512]{1,0:T(8,128)(2,1)} %collective-permute-done.4.refs_1_, ...), custom_call_target="tpu_custom_call", output_to_operand_aliasing={{}: (9, {})} | custom-call | flops 3221225472 | bytes 11534336 | tf_op jit(solution)/shard_map/pallas_call | solution.py:199
  106.6 1.1 collective-permute-start.3
  107.7 3.3 %collective-permute-done.18.refs_0_ = bf16[768,512]{1,0:T(8,128)(2,1)S(1)} collective-permute-done((bf16[768,512]{1,0:T(8,128)(2,1)}, bf16[768,512]{1,0:T(8,128)(2,1)S(1)}, u32[]{:S(2)}, u32[]{:S(2)}) %collective-permute-start.18) | collective-permute-done | bytes 786464 | tf_op jit(solution)/shard_map/ppermute | solution.py:252
  111.0 1.3 collective-permute-start.24
  112.3 2.4 %collective-permute-done.21.refs_1_ = bf16[768,512]{1,0:T(8,128)(2,1)S(1)} collective-permute-done((bf16[768,512]{1,0:T(8,128)(2,1)}, bf16[768,512]{1,0:T(8,128)(2,1)S(1)}, u32[]{:S(2)}, u32[]{:S(2)}) %collective-permute-start.21) | collective-permute-done | bytes 786464 | tf_op jit(solution)/shard_map/ppermute | solution.py:252
  114.7 3.6 %collective-permute-start.25 = (bf16[768,512]{1,0:T(8,128)(2,1)S(1)}, bf16[768,512]{1,0:T(8,128)(2,1)S(1)}, u32[]{:S(2)}, u32[]{:S(2)}) collective-permute-start(bf16[768,512]{1,0:T(8,128)(2,1)S(1)} %collective-permute-done.6.refs_1_), channel_id=1, source_target_pairs={{0,1},{1,0},{2,3},{3,2},{4,5},{5,4},{6,7},{7,6},{8,9},{9,8},{10,11... | collective-permute-start | bytes 2359304 | tf_op jit(solution)/shard_map/ppermute | solution.py:242
  118.3 7.9 %shard_map.177.refs_7_ = f32[1,1024,8192]{2,1,0:T(8,128)} custom-call(s32[2]{0:T(128)S(1)} %get-tuple-element.21.columns, f32[2]{0:T(128)S(1)} %broadcast_select_fusion.coef, bf16[768,512]{1,0:T(8,128)(2,1)} %collective-permute-done.16.refs_0_, bf16[768,512]{1,0:T(8,128)(2,1)} %collective-permute-done.19.refs_1_, ...), custom_call_target="tpu_custom_call", output_to_operand_aliasing={{}: (9, {})} | custom-call | flops 3221225472 | bytes 11534336 | tf_op jit(solution)/shard_map/pallas_call | solution.py:199
  126.2 0.1 collective-permute-start.22
  126.3 0.5 collective-permute-start.23
  126.8 7.9 %shard_map.178.refs_7_ = f32[1,1024,8192]{2,1,0:T(8,128)} custom-call(s32[2]{0:T(128)S(1)} %get-tuple-element.11.columns, f32[2]{0:T(128)S(1)} %broadcast_select_fusion.coef, bf16[768,512]{1,0:T(8,128)(2,1)} %collective-permute-done.1.refs_0_, bf16[768,512]{1,0:T(8,128)(2,1)} %collective-permute-done.5.refs_1_, ...), custom_call_target="tpu_custom_call", output_to_operand_aliasing={{}: (9, {})} | custom-call | flops 3221225472 | bytes 11534336 | tf_op jit(solution)/shard_map/pallas_call | solution.py:199
  134.7 0.2 collective-permute-start.7
  135.0 7.7 %shard_map.179.refs_7_ = f32[1,1024,8192]{2,1,0:T(8,128)} custom-call(s32[2]{0:T(128)S(1)} %get-tuple-element.23.columns, f32[2]{0:T(128)S(1)} %broadcast_select_fusion.coef, bf16[768,512]{1,0:T(8,128)(2,1)} %collective-permute-done.17.refs_0_, bf16[768,512]{1,0:T(8,128)(2,1)} %collective-permute-done.20.refs_1_, ...), custom_call_target="tpu_custom_call", output_to_operand_aliasing={{}: (9, {})} | custom-call | flops 3221225472 | bytes 11534336 | tf_op jit(solution)/shard_map/pallas_call | solution.py:199
  142.8 0.5 collective-permute-start.15
  143.2 6.8 %shard_map.180.refs_7_ = f32[1,1024,8192]{2,1,0:T(8,128)} custom-call(s32[2]{0:T(128)S(1)} %get-tuple-element.13.columns, f32[2]{0:T(128)S(1)} %broadcast_select_fusion.coef, bf16[768,512]{1,0:T(8,128)(2,1)S(1)} %collective-permute-done.2.refs_0_, bf16[768,512]{1,0:T(8,128)(2,1)S(1)} %collective-permute-done.6.refs_1_, ...), custom_call_target="tpu_custom_call", output_to_operand_aliasing={{}: (9, {})} | custom-call | flops 3221225472 | bytes 11534336 | tf_op jit(solution)/shard_map/pallas_call | solution.py:199
  150.1 0.1 collective-permute-start.8
  150.2 0.5 collective-permute-start.9
  150.7 6.8 %shard_map.181.refs_7_ = f32[1,1024,8192]{2,1,0:T(8,128)} custom-call(s32[2]{0:T(128)S(1)} %get-tuple-element.22.columns, f32[2]{0:T(128)S(1)} %broadcast_select_fusion.coef, bf16[768,512]{1,0:T(8,128)(2,1)S(1)} %collective-permute-done.18.refs_0_, bf16[768,512]{1,0:T(8,128)(2,1)S(1)} %collective-permute-done.21.refs_1_, ...), custom_call_target="tpu_custom_call", output_to_operand_aliasing={{}: (9, {})} | custom-call | flops 3221225472 | bytes 11534336 | tf_op jit(solution)/shard_map/pallas_call | solution.py:199
  157.5 4.9 %shard_map.182.refs_7_ = f32[1,1024,8192]{2,1,0:T(8,128)} custom-call(s32[2]{0:T(128)S(1)} %get-tuple-element.16.columns, f32[2]{0:T(128)S(1)} %broadcast_select_fusion.coef, bf16[768,256]{1,0:T(8,128)(2,1)S(1)} %collective-permute-done.12.refs_0_, bf16[768,256]{1,0:T(8,128)(2,1)S(1)} %collective-permute-done.13.refs_1_, ...), custom_call_target="tpu_custom_call", output_to_operand_aliasing={{}: (9, {})} | custom-call | flops 1610612736 | bytes 5767168 | tf_op jit(solution)/shard_map/pallas_call | solution.py:199
  162.4 4.8 %shard_map.183 = f32[1,1024,8192]{2,1,0:T(8,128)} custom-call(s32[2]{0:T(128)S(1)} %get-tuple-element.15.columns, f32[2]{0:T(128)S(1)} %broadcast_select_fusion.coef, bf16[768,256]{1,0:T(8,128)(2,1)S(1)} %collective-permute-done.3.refs_0_, bf16[768,256]{1,0:T(8,128)(2,1)S(1)} %collective-permute-done.7.refs_1_, ...), custom_call_target="tpu_custom_call", output_to_operand_aliasing={{}: (9, {})} | custom-call | flops 1610612736 | bytes 5767168 | tf_op jit(solution)/shard_map/pallas_call | solution.py:199
  (45 shorter events, 0.3 us)
Async XLA Ops:
  0.2 1.4 copy-start.4
  2.2 5.2 %collective-permute-start.10 = (bf16[768,512]{1,0:T(8,128)(2,1)S(1)}, bf16[768,512]{1,0:T(8,128)(2,1)S(1)}, u32[]{:S(2)}, u32[]{:S(2)}) collective-permute-start(bf16[768,512]{1,0:T(8,128)(2,1)S(1)} %get-tuple-element.7.refs_0_), channel_id=1, source_target_pairs={{0,1},{1,0},{2,3},{3,2},{4,5},{5,4},{6,7},{7,6},{8,9},{9,8},{10,11... | collective-permute-start | bytes 2359304 | tf_op jit(solution)/shard_map/ppermute | solution.py:242
  2.3 20.6 %collective-permute-start = (bf16[768,512]{1,0:T(8,128)(2,1)S(1)}, bf16[768,512]{1,0:T(8,128)(2,1)S(1)}, u32[]{:S(2)}, u32[]{:S(2)}) collective-permute-start(bf16[768,512]{1,0:T(8,128)(2,1)S(1)} %get-tuple-element.7.refs_0_), channel_id=1, source_target_pairs={{0,4},{4,8},{8,12},{12,14},{14,10},{10,6},{6,2},{2,0},{1,5},{5,9},... | collective-permute-start | bytes 2359304 | tf_op jit(solution)/shard_map/ppermute | solution.py:252
  5.1 18.9 %collective-permute-start.4 = (bf16[768,512]{1,0:T(8,128)(2,1)S(1)}, bf16[768,512]{1,0:T(8,128)(2,1)}, u32[]{:S(2)}, u32[]{:S(2)}) collective-permute-start(bf16[768,512]{1,0:T(8,128)(2,1)S(1)} %get-tuple-element.8.refs_1_), channel_id=1, source_target_pairs={{4,0},{8,4},{12,8},{14,12},{10,14},{6,10},{2,6},{0,2},{5,1},{9,5},... | collective-permute-start | bytes 2359304 | tf_op jit(solution)/shard_map/ppermute | solution.py:252
  5.1 34.7 %collective-permute-start.16 = (bf16[768,512]{1,0:T(8,128)(2,1)S(1)}, bf16[768,512]{1,0:T(8,128)(2,1)}, u32[]{:S(2)}, u32[]{:S(2)}) collective-permute-start(bf16[768,512]{1,0:T(8,128)(2,1)S(1)} %get-tuple-element.8.refs_1_), channel_id=1, source_target_pairs={{0,4},{4,8},{8,12},{12,14},{14,10},{10,6},{6,2},{2,0},{1,5},{5,9},... | collective-permute-start | bytes 2359304 | tf_op jit(solution)/shard_map/ppermute | solution.py:252
  6.6 33.9 %collective-permute-start.11 = (bf16[768,512]{1,0:T(8,128)(2,1)S(1)}, bf16[768,512]{1,0:T(8,128)(2,1)S(1)}, u32[]{:S(2)}, u32[]{:S(2)}) collective-permute-start(bf16[768,512]{1,0:T(8,128)(2,1)S(1)} %get-tuple-element.8.refs_1_), channel_id=1, source_target_pairs={{0,1},{1,0},{2,3},{3,2},{4,5},{5,4},{6,7},{7,6},{8,9},{9,8},{10,11... | collective-permute-start | bytes 2359304 | tf_op jit(solution)/shard_map/ppermute | solution.py:242
  7.5 0.9 copy-start
  8.4 35.5 %collective-permute-start.19 = (bf16[768,512]{1,0:T(8,128)(2,1)S(1)}, bf16[768,512]{1,0:T(8,128)(2,1)}, u32[]{:S(2)}, u32[]{:S(2)}) collective-permute-start(bf16[768,512]{1,0:T(8,128)(2,1)S(1)} %get-tuple-element.7.refs_0_), channel_id=1, source_target_pairs={{4,0},{8,4},{12,8},{14,12},{10,14},{6,10},{2,6},{0,2},{5,1},{9,5},... | collective-permute-start | bytes 2359304 | tf_op jit(solution)/shard_map/ppermute | solution.py:252
  23.0 20.9 %collective-permute-start.32 = (bf16[768,512]{1,0:T(8,128)(2,1)S(1)}, bf16[768,512]{1,0:T(8,128)(2,1)}, u32[]{:S(2)}, u32[]{:S(2)}) collective-permute-start(bf16[768,512]{1,0:T(8,128)(2,1)S(1)} %collective-permute-done.refs_0_), channel_id=1, source_target_pairs={{0,1},{1,0},{2,3},{3,2},{4,5},{5,4},{6,7},{7,6},{8,9},{9,8},{10,11... | collective-permute-start | bytes 2359304 | tf_op jit(solution)/shard_map/ppermute | solution.py:242
  24.0 21.7 %collective-permute-start.33 = (bf16[768,512]{1,0:T(8,128)(2,1)}, bf16[768,512]{1,0:T(8,128)(2,1)}, u32[]{:S(2)}, u32[]{:S(2)}) collective-permute-start(bf16[768,512]{1,0:T(8,128)(2,1)} %collective-permute-done.4.refs_1_), channel_id=1, source_target_pairs={{0,1},{1,0},{2,3},{3,2},{4,5},{5,4},{6,7},{7,6},{8,9},{9,8},{10,11... | collective-permute-start | bytes 2359304 | tf_op jit(solution)/shard_map/ppermute | solution.py:242
  39.8 7.4 %collective-permute-start.30 = (bf16[768,512]{1,0:T(8,128)(2,1)}, bf16[768,512]{1,0:T(8,128)(2,1)}, u32[]{:S(2)}, u32[]{:S(2)}) collective-permute-start(bf16[768,512]{1,0:T(8,128)(2,1)} %collective-permute-done.16.refs_0_), channel_id=1, source_target_pairs={{0,1},{1,0},{2,3},{3,2},{4,5},{5,4},{6,7},{7,6},{8,9},{9,8},{10,11... | collective-permute-start | bytes 2359304 | tf_op jit(solution)/shard_map/ppermute | solution.py:242
  40.5 0.9 copy-start.2
  41.4 19.2 %collective-permute-start.1 = (bf16[768,512]{1,0:T(8,128)(2,1)S(1)}, bf16[768,512]{1,0:T(8,128)(2,1)}, u32[]{:S(2)}, u32[]{:S(2)}) collective-permute-start(bf16[768,512]{1,0:T(8,128)(2,1)S(1)} %collective-permute-done.refs_0_), channel_id=1, source_target_pairs={{0,4},{4,8},{8,12},{12,14},{14,10},{10,6},{6,2},{2,0},{1,5},{5,9},... | collective-permute-start | bytes 2359304 | tf_op jit(solution)/shard_map/ppermute | solution.py:252
  42.9 0.9 copy-start.5
  43.8 20.5 %collective-permute-start.5 = (bf16[768,512]{1,0:T(8,128)(2,1)}, bf16[768,512]{1,0:T(8,128)(2,1)}, u32[]{:S(2)}, u32[]{:S(2)}) collective-permute-start(bf16[768,512]{1,0:T(8,128)(2,1)} %collective-permute-done.4.refs_1_), channel_id=1, source_target_pairs={{4,0},{8,4},{12,8},{14,12},{10,14},{6,10},{2,6},{0,2},{5,1},{9,5},... | collective-permute-start | bytes 2359304 | tf_op jit(solution)/shard_map/ppermute | solution.py:252
  43.8 18.1 %collective-permute-start.31 = (bf16[768,512]{1,0:T(8,128)(2,1)}, bf16[768,512]{1,0:T(8,128)(2,1)S(1)}, u32[]{:S(2)}, u32[]{:S(2)}) collective-permute-start(bf16[768,512]{1,0:T(8,128)(2,1)} %collective-permute-done.19.refs_1_), channel_id=1, source_target_pairs={{0,1},{1,0},{2,3},{3,2},{4,5},{5,4},{6,7},{7,6},{8,9},{9,8},{10,11... | collective-permute-start | bytes 2359304 | tf_op jit(solution)/shard_map/ppermute | solution.py:242
  45.6 31.8 %collective-permute-start.17 = (bf16[768,512]{1,0:T(8,128)(2,1)}, bf16[768,512]{1,0:T(8,128)(2,1)}, u32[]{:S(2)}, u32[]{:S(2)}) collective-permute-start(bf16[768,512]{1,0:T(8,128)(2,1)} %collective-permute-done.16.refs_0_), channel_id=1, source_target_pairs={{0,4},{4,8},{8,12},{12,14},{14,10},{10,6},{6,2},{2,0},{1,5},{5,9},... | collective-permute-start | bytes 2359304 | tf_op jit(solution)/shard_map/ppermute | solution.py:252
  47.3 32.6 %collective-permute-start.20 = (bf16[768,512]{1,0:T(8,128)(2,1)}, bf16[768,512]{1,0:T(8,128)(2,1)}, u32[]{:S(2)}, u32[]{:S(2)}) collective-permute-start(bf16[768,512]{1,0:T(8,128)(2,1)} %collective-permute-done.19.refs_1_), channel_id=1, source_target_pairs={{4,0},{8,4},{12,8},{14,12},{10,14},{6,10},{2,6},{0,2},{5,1},{9,5},... | collective-permute-start | bytes 2359304 | tf_op jit(solution)/shard_map/ppermute | solution.py:252
  60.6 28.0 %collective-permute-start.28 = (bf16[768,512]{1,0:T(8,128)(2,1)}, bf16[768,512]{1,0:T(8,128)(2,1)}, u32[]{:S(2)}, u32[]{:S(2)}) collective-permute-start(bf16[768,512]{1,0:T(8,128)(2,1)} %collective-permute-done.1.refs_0_), channel_id=1, source_target_pairs={{0,1},{1,0},{2,3},{3,2},{4,5},{5,4},{6,7},{7,6},{8,9},{9,8},{10,11... | collective-permute-start | bytes 2359304 | tf_op jit(solution)/shard_map/ppermute | solution.py:242
  61.9 0.9 copy-start.7
  62.8 31.4 %collective-permute-start.2 = (bf16[768,512]{1,0:T(8,128)(2,1)}, bf16[768,512]{1,0:T(8,128)(2,1)S(1)}, u32[]{:S(2)}, u32[]{:S(2)}) collective-permute-start(bf16[768,512]{1,0:T(8,128)(2,1)} %collective-permute-done.1.refs_0_), channel_id=1, source_target_pairs={{0,4},{4,8},{8,12},{12,14},{14,10},{10,6},{6,2},{2,0},{1,5},{5,9},... | collective-permute-start | bytes 2359304 | tf_op jit(solution)/shard_map/ppermute | solution.py:252
  64.3 32.2 %collective-permute-start.6 = (bf16[768,512]{1,0:T(8,128)(2,1)}, bf16[768,512]{1,0:T(8,128)(2,1)S(1)}, u32[]{:S(2)}, u32[]{:S(2)}) collective-permute-start(bf16[768,512]{1,0:T(8,128)(2,1)} %collective-permute-done.5.refs_1_), channel_id=1, source_target_pairs={{4,0},{8,4},{12,8},{14,12},{10,14},{6,10},{2,6},{0,2},{5,1},{9,5},... | collective-permute-start | bytes 2359304 | tf_op jit(solution)/shard_map/ppermute | solution.py:252
  66.1 1.1 copy-start.1
  67.3 1.1 copy-start.3
  68.9 29.7 %copy-start.6 = (bf16[768,512]{1,0:T(8,128)(2,1)S(1)}, bf16[768,512]{1,0:T(8,128)(2,1)}, u32[]{:S(2)}) copy-start(bf16[768,512]{1,0:T(8,128)(2,1)} %copy-done.5) | copy-start | bytes 2359300
  77.4 19.7 %collective-permute-start.29 = (bf16[768,512]{1,0:T(8,128)(2,1)}, bf16[768,512]{1,0:T(8,128)(2,1)S(1)}, u32[]{:S(2)}, u32[]{:S(2)}) collective-permute-start(bf16[768,512]{1,0:T(8,128)(2,1)} %collective-permute-done.5.refs_1_), channel_id=1, source_target_pairs={{0,1},{1,0},{2,3},{3,2},{4,5},{5,4},{6,7},{7,6},{8,9},{9,8},{10,11... | collective-permute-start | bytes 2359304 | tf_op jit(solution)/shard_map/ppermute | solution.py:242
  79.8 18.4 %collective-permute-start.26 = (bf16[768,512]{1,0:T(8,128)(2,1)}, bf16[768,512]{1,0:T(8,128)(2,1)S(1)}, u32[]{:S(2)}, u32[]{:S(2)}) collective-permute-start(bf16[768,512]{1,0:T(8,128)(2,1)} %collective-permute-done.17.refs_0_), channel_id=1, source_target_pairs={{0,1},{1,0},{2,3},{3,2},{4,5},{5,4},{6,7},{7,6},{8,9},{9,8},{10,11... | collective-permute-start | bytes 2359304 | tf_op jit(solution)/shard_map/ppermute | solution.py:242
  88.5 22.5 %collective-permute-start.18 = (bf16[768,512]{1,0:T(8,128)(2,1)}, bf16[768,512]{1,0:T(8,128)(2,1)S(1)}, u32[]{:S(2)}, u32[]{:S(2)}) collective-permute-start(bf16[768,512]{1,0:T(8,128)(2,1)} %collective-permute-done.17.refs_0_), channel_id=1, source_target_pairs={{0,4},{4,8},{8,12},{12,14},{14,10},{10,6},{6,2},{2,0},{1,5},{5,9},... | collective-permute-start | bytes 2359304 | tf_op jit(solution)/shard_map/ppermute | solution.py:252
  94.2 12.4 %collective-permute-start.27 = (bf16[768,512]{1,0:T(8,128)(2,1)}, bf16[768,512]{1,0:T(8,128)(2,1)S(1)}, u32[]{:S(2)}, u32[]{:S(2)}) collective-permute-start(bf16[768,512]{1,0:T(8,128)(2,1)} %collective-permute-done.20.refs_1_), channel_id=1, source_target_pairs={{0,1},{1,0},{2,3},{3,2},{4,5},{5,4},{6,7},{7,6},{8,9},{9,8},{10,11... | collective-permute-start | bytes 2359304 | tf_op jit(solution)/shard_map/ppermute | solution.py:242
  96.6 18.2 %collective-permute-start.21 = (bf16[768,512]{1,0:T(8,128)(2,1)}, bf16[768,512]{1,0:T(8,128)(2,1)S(1)}, u32[]{:S(2)}, u32[]{:S(2)}) collective-permute-start(bf16[768,512]{1,0:T(8,128)(2,1)} %collective-permute-done.20.refs_1_), channel_id=1, source_target_pairs={{4,0},{8,4},{12,8},{14,12},{10,14},{6,10},{2,6},{0,2},{5,1},{9,5},... | collective-permute-start | bytes 2359304 | tf_op jit(solution)/shard_map/ppermute | solution.py:252
  97.1 29.1 %collective-permute-start.12 = (bf16[768,256]{1,0:T(8,128)(2,1)S(1)}, bf16[768,256]{1,0:T(8,128)(2,1)S(1)}, u32[]{:S(2)}, u32[]{:S(2)}) collective-permute-start(bf16[768,256]{1,0:T(8,128)(2,1)S(1)} %get-tuple-element.19), channel_id=1, source_target_pairs={{0,4},{4,8},{8,12},{12,14},{14,10},{10,6},{6,2},{2,0},{1,5},{5,9},... | collective-permute-start | bytes 1179656 | tf_op jit(solution)/shard_map/ppermute | solution.py:252
  98.2 28.1 %collective-permute-start.13 = (bf16[768,256]{1,0:T(8,128)(2,1)S(1)}, bf16[768,256]{1,0:T(8,128)(2,1)S(1)}, u32[]{:S(2)}, u32[]{:S(2)}) collective-permute-start(bf16[768,256]{1,0:T(8,128)(2,1)S(1)} %get-tuple-element.17), channel_id=1, source_target_pairs={{4,0},{8,4},{12,8},{14,12},{10,14},{6,10},{2,6},{0,2},{5,1},{9,5},... | collective-permute-start | bytes 1179656 | tf_op jit(solution)/shard_map/ppermute | solution.py:252
  98.6 19.7 %copy-start.8 = (bf16[768,512]{1,0:T(8,128)(2,1)S(1)}, bf16[768,512]{1,0:T(8,128)(2,1)}, u32[]{:S(2)}) copy-start(bf16[768,512]{1,0:T(8,128)(2,1)} %copy-done.7) | copy-start | bytes 2359300
  106.6 28.1 %collective-permute-start.3 = (bf16[768,256]{1,0:T(8,128)(2,1)S(1)}, bf16[768,256]{1,0:T(8,128)(2,1)S(1)}, u32[]{:S(2)}, u32[]{:S(2)}) collective-permute-start(bf16[768,256]{1,0:T(8,128)(2,1)S(1)} %get-tuple-element.20), channel_id=1, source_target_pairs={{0,4},{4,8},{8,12},{12,14},{14,10},{10,6},{6,2},{2,0},{1,5},{5,9},... | collective-permute-start | bytes 1179656 | tf_op jit(solution)/shard_map/ppermute | solution.py:252
  111.0 31.6 %collective-permute-start.24 = (bf16[768,512]{1,0:T(8,128)(2,1)S(1)}, bf16[768,512]{1,0:T(8,128)(2,1)S(1)}, u32[]{:S(2)}, u32[]{:S(2)}) collective-permute-start(bf16[768,512]{1,0:T(8,128)(2,1)S(1)} %collective-permute-done.2.refs_0_), channel_id=1, source_target_pairs={{0,1},{1,0},{2,3},{3,2},{4,5},{5,4},{6,7},{7,6},{8,9},{9,8},{10,11... | collective-permute-start | bytes 2359304 | tf_op jit(solution)/shard_map/ppermute | solution.py:242
  114.7 28.0 %collective-permute-start.25 = (bf16[768,512]{1,0:T(8,128)(2,1)S(1)}, bf16[768,512]{1,0:T(8,128)(2,1)S(1)}, u32[]{:S(2)}, u32[]{:S(2)}) collective-permute-start(bf16[768,512]{1,0:T(8,128)(2,1)S(1)} %collective-permute-done.6.refs_1_), channel_id=1, source_target_pairs={{0,1},{1,0},{2,3},{3,2},{4,5},{5,4},{6,7},{7,6},{8,9},{9,8},{10,11... | collective-permute-start | bytes 2359304 | tf_op jit(solution)/shard_map/ppermute | solution.py:242
  126.2 23.9 %collective-permute-start.22 = (bf16[768,512]{1,0:T(8,128)(2,1)S(1)}, bf16[768,512]{1,0:T(8,128)(2,1)S(1)}, u32[]{:S(2)}, u32[]{:S(2)}) collective-permute-start(bf16[768,512]{1,0:T(8,128)(2,1)S(1)} %collective-permute-done.18.refs_0_), channel_id=1, source_target_pairs={{0,1},{1,0},{2,3},{3,2},{4,5},{5,4},{6,7},{7,6},{8,9},{9,8},{10,11... | collective-permute-start | bytes 2359304 | tf_op jit(solution)/shard_map/ppermute | solution.py:242
  126.3 24.3 %collective-permute-start.23 = (bf16[768,512]{1,0:T(8,128)(2,1)S(1)}, bf16[768,512]{1,0:T(8,128)(2,1)S(1)}, u32[]{:S(2)}, u32[]{:S(2)}) collective-permute-start(bf16[768,512]{1,0:T(8,128)(2,1)S(1)} %collective-permute-done.21.refs_1_), channel_id=1, source_target_pairs={{0,1},{1,0},{2,3},{3,2},{4,5},{5,4},{6,7},{7,6},{8,9},{9,8},{10,11... | collective-permute-start | bytes 2359304 | tf_op jit(solution)/shard_map/ppermute | solution.py:242
  134.7 15.4 %collective-permute-start.7 = (bf16[768,256]{1,0:T(8,128)(2,1)S(1)}, bf16[768,256]{1,0:T(8,128)(2,1)S(1)}, u32[]{:S(2)}, u32[]{:S(2)}) collective-permute-start(bf16[768,256]{1,0:T(8,128)(2,1)S(1)} %get-tuple-element.18), channel_id=1, source_target_pairs={{4,0},{8,4},{12,8},{14,12},{10,14},{6,10},{2,6},{0,2},{5,1},{9,5},... | collective-permute-start | bytes 1179656 | tf_op jit(solution)/shard_map/ppermute | solution.py:252
  142.7 14.8 %collective-permute-start.14 = (bf16[768,256]{1,0:T(8,128)(2,1)S(1)}, bf16[768,256]{1,0:T(8,128)(2,1)S(1)}, u32[]{:S(2)}, u32[]{:S(2)}) collective-permute-start(bf16[768,256]{1,0:T(8,128)(2,1)S(1)} %collective-permute-done.12.refs_0_), channel_id=1, source_target_pairs={{0,1},{1,0},{2,3},{3,2},{4,5},{5,4},{6,7},{7,6},{8,9},{9,8},{10,11... | collective-permute-start | bytes 1179656 | tf_op jit(solution)/shard_map/ppermute | solution.py:242
  142.8 14.8 %collective-permute-start.15 = (bf16[768,256]{1,0:T(8,128)(2,1)S(1)}, bf16[768,256]{1,0:T(8,128)(2,1)S(1)}, u32[]{:S(2)}, u32[]{:S(2)}) collective-permute-start(bf16[768,256]{1,0:T(8,128)(2,1)S(1)} %collective-permute-done.13.refs_1_), channel_id=1, source_target_pairs={{0,1},{1,0},{2,3},{3,2},{4,5},{5,4},{6,7},{7,6},{8,9},{9,8},{10,11... | collective-permute-start | bytes 1179656 | tf_op jit(solution)/shard_map/ppermute | solution.py:242
  150.1 12.3 %collective-permute-start.8 = (bf16[768,256]{1,0:T(8,128)(2,1)S(1)}, bf16[768,256]{1,0:T(8,128)(2,1)S(1)}, u32[]{:S(2)}, u32[]{:S(2)}) collective-permute-start(bf16[768,256]{1,0:T(8,128)(2,1)S(1)} %collective-permute-done.3.refs_0_), channel_id=1, source_target_pairs={{0,1},{1,0},{2,3},{3,2},{4,5},{5,4},{6,7},{7,6},{8,9},{9,8},{10,11... | collective-permute-start | bytes 1179656 | tf_op jit(solution)/shard_map/ppermute | solution.py:242
  150.2 12.2 %collective-permute-start.9 = (bf16[768,256]{1,0:T(8,128)(2,1)S(1)}, bf16[768,256]{1,0:T(8,128)(2,1)S(1)}, u32[]{:S(2)}, u32[]{:S(2)}) collective-permute-start(bf16[768,256]{1,0:T(8,128)(2,1)S(1)} %collective-permute-done.7.refs_1_), channel_id=1, source_target_pairs={{0,1},{1,0},{2,3},{3,2},{4,5},{5,4},{6,7},{7,6},{8,9},{9,8},{10,11... | collective-permute-start | bytes 1179656 | tf_op jit(solution)/shard_map/ppermute | solution.py:242

commit v3 on v2

--- a/solution.py
+++ b/solution.py
@@ -10,6 +10,7 @@
 
 LANES = 128
 GRANT = 34 * 2**20
+SPLIT_GRANT = 123 * 2**19
 LAST_HOPS = 2
 
 
@@ -70,16 +71,16 @@
     parts, (box, sem) = refs[:-2], refs[-2:]
     width = parts[0].shape[1]
     copies = []
-    for k in range(len(parts)):
-        at = slice(k * width, (k + 1) * width)
+    for k in range(sem.shape[0]):
+        at = slice(k * 2 * LANES, (k + 1) * 2 * LANES)
         copies.append(pltpu.make_async_copy(returns.at[:, at], box.at[:, at], sem.at[k]))
         copies[-1].start()
-    for k, part in enumerate(parts):
-        copies[k].wait()
-        for lane in range(0, width, LANES):
-            source = box[:, k * width + lane : k * width + lane + LANES]
-            part[:, lane : lane + LANES] = (
-                source.astype(jnp.float32) * weight[...]
+    for k, copy in enumerate(copies):
+        copy.wait()
+        for lane in range(k * 2 * LANES, (k + 1) * 2 * LANES, LANES):
+            part, start = parts[lane // width], lane % width
+            part[:, start : start + LANES] = (
+                box[:, lane : lane + LANES].astype(jnp.float32) * weight[...]
             ).astype(jnp.bfloat16)
 
 
@@ -94,9 +95,9 @@
         out_specs=[near] * count,
         scratch_shapes=[
             pltpu.VMEM((minutes, width), jnp.bfloat16),
-            pltpu.SemaphoreType.DMA((count,)),
+            pltpu.SemaphoreType.DMA((width // (2 * LANES),)),
         ],
-        compiler_params=pltpu.CompilerParams(vmem_limit_bytes=GRANT),
+        compiler_params=pltpu.CompilerParams(vmem_limit_bytes=SPLIT_GRANT),
         cost_estimate=pl.CostEstimate(
             flops=minutes * width, bytes_accessed=4 * minutes * width, transcendentals=0
         ),
@@ -158,22 +159,20 @@
         @pl.loop(0, tiles)
         def _(i):
             at = pl.ds(pl.multiple_of(i * rows, rows), rows)
-            fetch(k, i).wait()
+            first = jnp.dot(left_own[at], own[k][...], preferred_element_type=jnp.float32)
 
             @pl.when(earlier)
             def _():
-                box[k, at] = (
-                    coef[0] * box[k, at]
-                    + jnp.dot(left_own[at], own[k][...], preferred_element_type=jnp.float32)
-                    + coef[1]
-                    * jnp.dot(left_other[at], other[k][...], preferred_element_type=jnp.float32)
+                both = first + coef[1] * jnp.dot(
+                    left_other[at], other[k][...], preferred_element_type=jnp.float32
                 )
+                fetch(k, i).wait()
+                box[k, at] = coef[0] * box[k, at] + both
 
             @pl.when(jnp.logical_not(earlier))
             def _():
-                box[k, at] = coef[0] * box[k, at] + jnp.dot(
-                    left_own[at], own[k][...], preferred_element_type=jnp.float32
-                )
+                fetch(k, i).wait()
+                box[k, at] = coef[0] * box[k, at] + first
 
             flush(k, i).start()
 
@@ -216,6 +215,111 @@
     )(*args)
 
 
+def decayed_kernel(columns, coef, prior, out, sem):
+    count, _, width = out.shape
+
+    def fetch(k):
+        at = pl.ds(pl.multiple_of(columns[k] * LANES, LANES), width)
+        return pltpu.make_async_copy(prior.at[:, at], out.at[k], sem.at[k])
+
+    for k in range(count):
+        fetch(k).start()
+    for k in range(count):
+        fetch(k).wait()
+        out[k] = coef[0] * out[k]
+
+
+def own_kernel(count, *refs):
+    own, left, base, out = refs[:count], *refs[count:]
+    for k in range(count):
+        out[k] = base[k] + jnp.dot(left[...], own[k][...], preferred_element_type=jnp.float32)
+
+
+def other_kernel(count, rows, columns, coef, *refs):
+    other, left, base = refs[:count], *refs[count : count + 2]
+    out, box, sem = refs[-3:]
+    height, width = box.shape[1:]
+    earlier = coef[1] != 0.0
+
+    def flush(source, k, i):
+        at = pl.ds(i * rows, rows)
+        across = pl.ds(pl.multiple_of(columns[k] * LANES, LANES), width)
+        return pltpu.make_async_copy(source.at[k, at], out.at[0, at, across], sem.at[k, i])
+
+    for k in range(count):
+
+        @pl.loop(0, height // rows)
+        def _(i):
+            at = pl.ds(pl.multiple_of(i * rows, rows), rows)
+
+            @pl.when(earlier)
+            def _():
+                box[k, at] = base[k, at] + coef[1] * jnp.dot(
+                    left[at], other[k][...], preferred_element_type=jnp.float32
+                )
+                flush(box, k, i).start()
+
+            @pl.when(jnp.logical_not(earlier))
+            def _():
+                flush(base, k, i).start()
+
+    for k in range(count):
+        for i in range(height // rows):
+            flush(box, k, i).wait()
+
+
+def last_calls(columns, coef, own, left_own, left_other, prior, rows):
+    count = len(own)
+    minutes, width = own[0].shape
+    height, _ = prior.shape
+    near = pl.BlockSpec(memory_space=pltpu.VMEM)
+    far = pl.BlockSpec(memory_space=pltpu.HBM)
+    scalar = pl.BlockSpec(memory_space=pltpu.SMEM)
+    small = jax.ShapeDtypeStruct((count, height, width), jnp.float32)
+    grant = pltpu.CompilerParams(vmem_limit_bytes=GRANT)
+    size = 4 * count * height * width
+
+    def cost(flops, bytes_accessed):
+        return pl.CostEstimate(flops=flops, bytes_accessed=bytes_accessed, transcendentals=0)
+
+    base = pl.pallas_call(
+        decayed_kernel,
+        out_shape=small,
+        in_specs=[scalar, scalar, far],
+        out_specs=near,
+        scratch_shapes=[pltpu.SemaphoreType.DMA((count,))],
+        compiler_params=grant,
+        cost_estimate=cost(size // 4, size),
+    )(columns, coef, prior)
+    flops = 2 * count * minutes * width * height
+    base = pl.pallas_call(
+        functools.partial(own_kernel, count),
+        out_shape=small,
+        in_specs=[near] * (count + 2),
+        out_specs=near,
+        compiler_params=grant,
+        cost_estimate=cost(flops, 2 * size),
+    )(*own, left_own, base)
+
+    def finish(out, other):
+        args = [columns, coef, *other, left_other, base, out]
+        return pl.pallas_call(
+            functools.partial(other_kernel, count, rows),
+            out_shape=jax.ShapeDtypeStruct(out.shape, out.dtype),
+            in_specs=[scalar, scalar] + [near] * (count + 2) + [far],
+            out_specs=far,
+            scratch_shapes=[
+                pltpu.VMEM(small.shape, small.dtype),
+                pltpu.SemaphoreType.DMA((count, height // rows)),
+            ],
+            input_output_aliases={len(args) - 1: 0},
+            compiler_params=grant,
+            cost_estimate=cost(flops, 2 * size),
+        )(*args)
+
+    return finish
+
+
 def last_cuts(half):
     return (half // LAST_HOPS,) * LAST_HOPS
 
@@ -272,12 +376,14 @@
     unit = half // LANES
     columns = (2 * me + jnp.arange(2, dtype=jnp.int32)) * unit
     out = tile_call(None, columns, coef, halves, own_other, *common)
-    for pair, step, sides, start in arrived:
+    for k, (pair, step, sides, start) in enumerate(arrived):
         block = owner(jnp.array([step, -step], jnp.int32))
         columns = (2 * block + jnp.array(sides, jnp.int32)) * unit + start // LANES
+        if k == len(arrived) - 1:
+            finish = last_calls(columns, coef, pair, *common)
+            return finish(out, swap(pair))
         other = swap(pair)
         out = tile_call(out, columns, coef, pair, other, *common)
-    return out
 
 
 def solution(mesh):

time: 168 us -> 172 us (1.024)
  waiting for transfers between devices: 61.3 us -> 70 us
  local copies, waits for them, and re-layouts: 7.51 us -> 1.04 us
  Pallas kernels: 63.1 us -> 66.7 us
    ppermute x16, waiting for transfers between devices: 61.3 us -> 70 us  [hop(): moved.append(lax.ppermute(parts[way], 'assets', pairs))]
    unnamed x18 -> x8, local copies, waits for them, and re-layouts: 7.24 us -> 0.02 us
    pallas_call x0 -> x3, Pallas kernels: none -> 6.07 us  [the longest x1 2.91 us: finish(): pl.pallas_call(functools.partial(other_kernel, count, rows), out_shape=ja...]
    pallas_call x9 -> x8, Pallas kernels: 61.6 us -> 56.2 us  [tile_call(): pl.pallas_call(functools.partial(tile_kernel, count, rows), out_shape=jax...]
    pallas_call x1, Pallas kernels: 0.64 us -> 3.55 us  [split_call(): pl.pallas_call(split_kernel, out_shape=[part] * count, in_specs=[pl.Block...]
  transfers between devices with their start and end apart: 34 -> 34, of which waited for: 10 -> 8; matrix products, arithmetic and copies ran while one was open for 2% -> 2% of each run, Pallas kernels for 34% -> 35%
where the time goes in v3:
time: 172 us; the launch traced here: 171 us
  waiting for transfers between devices  70 us (41%)
  Pallas kernels  66.7 us (39%)
  starting transfers between devices  30.5 us (18%)
  other arithmetic  2.73 us (2%)
    ppermute x16, waiting for transfers between devices, hop(): moved.append(lax.ppermute(parts[way], 'assets', pairs))  70 us
    pallas_call x8, Pallas kernels, tile_call(): pl.pallas_call(functools.partial(tile_kernel, count, rows), out_shape=jax...  56.2 us
    ppermute x18, starting transfers between devices, swap(): moved.append(lax.ppermute(part, 'tm', [(0, 1), (1, 0)]))  16.8 us
    ppermute x16, starting transfers between devices, hop(): moved.append(lax.ppermute(parts[way], 'assets', pairs))  13.7 us
    pallas_call x1, Pallas kernels, split_call(): pl.pallas_call(split_kernel, out_shape=[part] * count, in_specs=[pl.Block...  3.55 us
  transfers between devices with their start and end apart: 34, of which 8 were waited for; matrix products, arithmetic and copies ran while one was open for 2% of the time, Pallas kernels for 35%

profile of v3, /device:TPU:1, one launch (start us, length us, event | category | flops | bytes accessed | tf_op | source)
XLA Modules:
  0.0 171.4 jit_solution(9687370224660616624)
XLA Ops:
  0.0 0.9 broadcast_in_dim.2.weight
  0.9 3.5 %shard_map.172 = (bf16[768,512]{1,0:T(8,128)(2,1)}, bf16[768,512]{1,0:T(8,128)(2,1)}) custom-call(bf16[768,1024]{1,0:T(8,128)(2,1)} %returns.1, f32[768,128]{1,0:T(8,128)} %broadcast_in_dim.2.weight), custom_call_target="tpu_custom_call" | custom-call | flops 786432 | bytes 3145728 | tf_op jit(solution)/shard_map/pallas_call | solution.py:91
  4.5 0.0 copy-start
  4.5 0.1 collective-permute-start.10
  4.6 2.8 %collective-permute-start = (bf16[768,512]{1,0:T(8,128)(2,1)}, bf16[768,512]{1,0:T(8,128)(2,1)}, u32[]{:S(2)}, u32[]{:S(2)}) collective-permute-start(bf16[768,512]{1,0:T(8,128)(2,1)} %get-tuple-element.7.refs_0_), channel_id=1, source_target_pairs={{0,4},{4,8},{8,12},{12,14},{14,10},{10,6},{6,2},{2,0},{1,5},{5,9},... | collective-permute-start | bytes 2359304 | tf_op jit(solution)/shard_map/ppermute | solution.py:356
  7.4 0.0 collective-permute-start.5
  7.4 1.5 collective-permute-start.16
  8.8 0.9 collective-permute-start.11
  9.7 0.0 collective-permute-done.10.refs_0_.refs_2_
  9.8 0.0 collective-permute-start.19
  9.8 15.7 %collective-permute-done.refs_0_ = bf16[768,512]{1,0:T(8,128)(2,1)} collective-permute-done((bf16[768,512]{1,0:T(8,128)(2,1)}, bf16[768,512]{1,0:T(8,128)(2,1)}, u32[]{:S(2)}, u32[]{:S(2)}) %collective-permute-start) | collective-permute-done | bytes 786464 | tf_op jit(solution)/shard_map/ppermute | solution.py:356
  25.5 0.9 collective-permute-start.32
  26.3 0.1 collective-permute-done.5.refs_1_
  26.4 2.0 %collective-permute-start.33 = (bf16[768,512]{1,0:T(8,128)(2,1)}, bf16[768,512]{1,0:T(8,128)(2,1)}, u32[]{:S(2)}, u32[]{:S(2)}) collective-permute-start(bf16[768,512]{1,0:T(8,128)(2,1)} %collective-permute-done.5.refs_1_), channel_id=1, source_target_pairs={{0,1},{1,0},{2,3},{3,2},{4,5},{5,4},{6,7},{7,6},{8,9},{9,8},{10,11... | collective-permute-start | bytes 2359304 | tf_op jit(solution)/shard_map/ppermute | solution.py:346
  28.4 13.9 %collective-permute-done.16.refs_0_ = bf16[768,512]{1,0:T(8,128)(2,1)} collective-permute-done((bf16[768,512]{1,0:T(8,128)(2,1)}, bf16[768,512]{1,0:T(8,128)(2,1)}, u32[]{:S(2)}, u32[]{:S(2)}) %collective-permute-start.16) | collective-permute-done | bytes 786464 | tf_op jit(solution)/shard_map/ppermute | solution.py:356
  42.3 0.6 collective-permute-start.30
  43.0 0.0 collective-permute-done.11.refs_1_.refs_3_
  43.0 1.5 collective-permute-start.1
  44.5 0.0 collective-permute-done.19.refs_1_
  44.5 0.5 collective-permute-start.31
  45.0 0.7 fusion.1
  45.7 0.7 fusion.3
  46.3 0.0 collective-permute-done.33.refs_3_
  46.3 1.6 collective-permute-start.17
  47.9 14.4 %collective-permute-done.1.refs_0_ = bf16[768,512]{1,0:T(8,128)(2,1)} collective-permute-done((bf16[768,512]{1,0:T(8,128)(2,1)}, bf16[768,512]{1,0:T(8,128)(2,1)}, u32[]{:S(2)}, u32[]{:S(2)}) %collective-permute-start.1) | collective-permute-done | bytes 786464 | tf_op jit(solution)/shard_map/ppermute | solution.py:356
  62.4 1.3 collective-permute-start.28
  63.7 0.7 broadcast_add_fusion
  64.4 0.7 broadcast_select_fusion.coef
  65.0 1.5 collective-permute-start.2
  66.6 2.2 %shard_map.175.refs_3_ = f32[2,1024,256]{2,1,0:T(8,128)S(1)} custom-call(s32[2]{0:T(128)S(1)} %get-tuple-element.15.columns, f32[2]{0:T(128)S(1)} %broadcast_select_fusion.coef, f32[1024,8192]{1,0:T(8,128)} %refs_6_.15), custom_call_target="tpu_custom_call" | custom-call | flops 524288 | bytes 2097152 | tf_op jit(solution)/shard_map/pallas_call | solution.py:285
  68.8 0.5 shard_map.174.refs_2_.refs_4_
  69.3 0.5 shard_map.173.refs_5_.refs_2_
  69.8 9.4 %collective-permute-done.17.refs_0_ = bf16[768,512]{1,0:T(8,128)(2,1)} collective-permute-done((bf16[768,512]{1,0:T(8,128)(2,1)}, bf16[768,512]{1,0:T(8,128)(2,1)}, u32[]{:S(2)}, u32[]{:S(2)}) %collective-permute-start.17) | collective-permute-done | bytes 786464 | tf_op jit(solution)/shard_map/ppermute | solution.py:356
  79.2 1.3 collective-permute-start.29
  80.5 1.8 %collective-permute-start.26 = (bf16[768,512]{1,0:T(8,128)(2,1)}, bf16[768,512]{1,0:T(8,128)(2,1)S(1)}, u32[]{:S(2)}, u32[]{:S(2)}) collective-permute-start(bf16[768,512]{1,0:T(8,128)(2,1)} %collective-permute-done.17.refs_0_), channel_id=1, source_target_pairs={{0,1},{1,0},{2,3},{3,2},{4,5},{5,4},{6,7},{7,6},{8,9},{9,8},{10,11... | collective-permute-start | bytes 2359304 | tf_op jit(solution)/shard_map/ppermute | solution.py:346
  82.4 0.0 collective-permute-start.27
  82.4 6.7 %shard_map.177.refs_7_ = f32[1,1024,8192]{2,1,0:T(8,128)} custom-call(s32[2]{0:T(128)S(1)} %add_multiply_fusion.columns, f32[2]{0:T(128)S(1)} %broadcast_select_fusion.coef, bf16[768,512]{1,0:T(8,128)(2,1)S(1)} %copy-done, bf16[768,512]{1,0:T(8,128)(2,1)S(1)} %copy-done.1, bf16[768,512]{1,0:T(8,128)(2,1)S(1)} %collective-permute-done.10.refs_0_.refs_2_, ...), custom_call_target="tpu_custom_call" | custom-call | flops 3221225472 | bytes 11534336 | tf_op jit(solution)/shard_map/pallas_call | solution.py:198
  89.1 6.9 %collective-permute-done.2.refs_0_ = bf16[768,512]{1,0:T(8,128)(2,1)S(1)} collective-permute-done((bf16[768,512]{1,0:T(8,128)(2,1)}, bf16[768,512]{1,0:T(8,128)(2,1)S(1)}, u32[]{:S(2)}, u32[]{:S(2)}) %collective-permute-start.2) | collective-permute-done | bytes 786464 | tf_op jit(solution)/shard_map/ppermute | solution.py:356
  96.0 1.5 collective-permute-start.18
  97.5 0.1 fusion.17
  97.6 0.1 fusion.16
  97.7 1.5 collective-permute-start.12
  99.2 1.3 collective-permute-start.3
  100.5 0.2 collective-permute-start.8
  100.6 8.0 %shard_map.178.refs_7_ = f32[1,1024,8192]{2,1,0:T(8,128)} custom-call(s32[2]{0:T(128)S(1)} %get-tuple-element.9.columns, f32[2]{0:T(128)S(1)} %broadcast_select_fusion.coef, bf16[768,512]{1,0:T(8,128)(2,1)} %collective-permute-done.refs_0_, bf16[768,512]{1,0:T(8,128)(2,1)} %collective-permute-done.5.refs_1_, ...), custom_call_target="tpu_custom_call", output_to_operand_aliasing={{}: (9, {})} | custom-call | flops 3221225472 | bytes 11534336 | tf_op jit(solution)/shard_map/pallas_call | solution.py:198
  108.6 5.8 %collective-permute-done.18.refs_0_ = bf16[768,512]{1,0:T(8,128)(2,1)S(1)} collective-permute-done((bf16[768,512]{1,0:T(8,128)(2,1)}, bf16[768,512]{1,0:T(8,128)(2,1)S(1)}, u32[]{:S(2)}, u32[]{:S(2)}) %collective-permute-start.18) | collective-permute-done | bytes 786464 | tf_op jit(solution)/shard_map/ppermute | solution.py:356
  114.4 3.0 %collective-permute-start.24 = (bf16[768,512]{1,0:T(8,128)(2,1)S(1)}, bf16[768,512]{1,0:T(8,128)(2,1)S(1)}, u32[]{:S(2)}, u32[]{:S(2)}) collective-permute-start(bf16[768,512]{1,0:T(8,128)(2,1)S(1)} %collective-permute-done.2.refs_0_), channel_id=1, source_target_pairs={{0,1},{1,0},{2,3},{3,2},{4,5},{5,4},{6,7},{7,6},{8,9},{9,8},{10,11... | collective-permute-start | bytes 2359304 | tf_op jit(solution)/shard_map/ppermute | solution.py:346
  117.5 1.8 %collective-permute-start.25 = (bf16[768,512]{1,0:T(8,128)(2,1)S(1)}, bf16[768,512]{1,0:T(8,128)(2,1)S(1)}, u32[]{:S(2)}, u32[]{:S(2)}) collective-permute-start(bf16[768,512]{1,0:T(8,128)(2,1)S(1)} %collective-permute-done.7.refs_1_), channel_id=1, source_target_pairs={{0,1},{1,0},{2,3},{3,2},{4,5},{5,4},{6,7},{7,6},{8,9},{9,8},{10,11... | collective-permute-start | bytes 2359304 | tf_op jit(solution)/shard_map/ppermute | solution.py:346
  119.3 8.0 %shard_map.179.refs_7_ = f32[1,1024,8192]{2,1,0:T(8,128)} custom-call(s32[2]{0:T(128)S(1)} %get-tuple-element.21.columns, f32[2]{0:T(128)S(1)} %broadcast_select_fusion.coef, bf16[768,512]{1,0:T(8,128)(2,1)} %collective-permute-done.16.refs_0_, bf16[768,512]{1,0:T(8,128)(2,1)} %collective-permute-done.19.refs_1_, ...), custom_call_target="tpu_custom_call", output_to_operand_aliasing={{}: (9, {})} | custom-call | flops 3221225472 | bytes 11534336 | tf_op jit(solution)/shard_map/pallas_call | solution.py:198
  127.3 0.2 collective-permute-start.13
  127.5 3.7 %collective-permute-done.3.refs_0_ = bf16[768,256]{1,0:T(8,128)(2,1)S(1)} collective-permute-done((bf16[768,256]{1,0:T(8,128)(2,1)S(1)}, bf16[768,256]{1,0:T(8,128)(2,1)S(1)}, u32[]{:S(2)}, u32[]{:S(2)}) %collective-permute-start.3) | collective-permute-done | bytes 393248 | tf_op jit(solution)/shard_map/ppermute | solution.py:356
  131.3 1.7 %collective-permute-start.22 = (bf16[768,512]{1,0:T(8,128)(2,1)S(1)}, bf16[768,512]{1,0:T(8,128)(2,1)S(1)}, u32[]{:S(2)}, u32[]{:S(2)}) collective-permute-start(bf16[768,512]{1,0:T(8,128)(2,1)S(1)} %collective-permute-done.18.refs_0_), channel_id=1, source_target_pairs={{0,1},{1,0},{2,3},{3,2},{4,5},{5,4},{6,7},{7,6},{8,9},{9,8},{10,11... | collective-permute-start | bytes 2359304 | tf_op jit(solution)/shard_map/ppermute | solution.py:346
  133.0 0.0 collective-permute-start.23
  133.0 7.7 %shard_map.180.refs_7_ = f32[1,1024,8192]{2,1,0:T(8,128)} custom-call(s32[2]{0:T(128)S(1)} %get-tuple-element.11.columns, f32[2]{0:T(128)S(1)} %broadcast_select_fusion.coef, bf16[768,512]{1,0:T(8,128)(2,1)} %collective-permute-done.1.refs_0_, bf16[768,512]{1,0:T(8,128)(2,1)} %collective-permute-done.6.refs_1_, ...), custom_call_target="tpu_custom_call", output_to_operand_aliasing={{}: (9, {})} | custom-call | flops 3221225472 | bytes 11534336 | tf_op jit(solution)/shard_map/pallas_call | solution.py:198
  140.7 7.5 %shard_map.181.refs_7_ = f32[1,1024,8192]{2,1,0:T(8,128)} custom-call(s32[2]{0:T(128)S(1)} %get-tuple-element.23.columns, f32[2]{0:T(128)S(1)} %broadcast_select_fusion.coef, bf16[768,512]{1,0:T(8,128)(2,1)} %collective-permute-done.17.refs_0_, bf16[768,512]{1,0:T(8,128)(2,1)} %collective-permute-done.20.refs_1_, ...), custom_call_target="tpu_custom_call", output_to_operand_aliasing={{}: (9, {})} | custom-call | flops 3221225472 | bytes 11534336 | tf_op jit(solution)/shard_map/pallas_call | solution.py:198
  148.3 1.0 shard_map.176.refs_3_
  149.3 0.1 collective-permute-start.4
  149.4 0.5 collective-permute-start.14
  149.8 0.1 collective-permute-start.15
  149.9 6.7 %shard_map.182.refs_7_ = f32[1,1024,8192]{2,1,0:T(8,128)} custom-call(s32[2]{0:T(128)S(1)} %get-tuple-element.13.columns, f32[2]{0:T(128)S(1)} %broadcast_select_fusion.coef, bf16[768,512]{1,0:T(8,128)(2,1)S(1)} %collective-permute-done.2.refs_0_, bf16[768,512]{1,0:T(8,128)(2,1)S(1)} %collective-permute-done.7.refs_1_, ...), custom_call_target="tpu_custom_call", output_to_operand_aliasing={{}: (9, {})} | custom-call | flops 3221225472 | bytes 11534336 | tf_op jit(solution)/shard_map/pallas_call | solution.py:198
  156.6 0.1 collective-permute-start.9
  156.7 6.7 %shard_map.183.refs_7_ = f32[1,1024,8192]{2,1,0:T(8,128)} custom-call(s32[2]{0:T(128)S(1)} %get-tuple-element.22.columns, f32[2]{0:T(128)S(1)} %broadcast_select_fusion.coef, bf16[768,512]{1,0:T(8,128)(2,1)S(1)} %collective-permute-done.18.refs_0_, bf16[768,512]{1,0:T(8,128)(2,1)S(1)} %collective-permute-done.21.refs_1_, ...), custom_call_target="tpu_custom_call", output_to_operand_aliasing={{}: (9, {})} | custom-call | flops 3221225472 | bytes 11534336 | tf_op jit(solution)/shard_map/pallas_call | solution.py:198
  163.4 4.9 %shard_map.184.refs_4_ = f32[1,1024,8192]{2,1,0:T(8,128)} custom-call(s32[2]{0:T(128)S(1)} %get-tuple-element.16.columns, f32[2]{0:T(128)S(1)} %broadcast_select_fusion.coef, bf16[768,256]{1,0:T(8,128)(2,1)S(1)} %collective-permute-done.12.refs_0_, bf16[768,256]{1,0:T(8,128)(2,1)S(1)} %collective-permute-done.13.refs_1_, ...), custom_call_target="tpu_custom_call", output_to_operand_aliasing={{}: (9, {})} | custom-call | flops 1610612736 | bytes 5767168 | tf_op jit(solution)/shard_map/pallas_call | solution.py:198
  168.4 2.9 %shard_map.185 = f32[1,1024,8192]{2,1,0:T(8,128)} custom-call(s32[2]{0:T(128)S(1)} %get-tuple-element.15.columns, f32[2]{0:T(128)S(1)} %broadcast_select_fusion.coef, bf16[768,256]{1,0:T(8,128)(2,1)S(1)} %collective-permute-done.4.refs_0_, bf16[768,256]{1,0:T(8,128)(2,1)S(1)} %collective-permute-done.9.refs_1_, ...), custom_call_target="tpu_custom_call", output_to_operand_aliasing={{}: (6, {})} | custom-call | flops 805306368 | bytes 4194304 | tf_op jit(solution)/shard_map/pallas_call | solution.py:306
  (37 shorter events, 0.1 us)
Async XLA Ops:
  0.0 69.3 %copy-start.3 = (s32[2]{0:T(128)S(1)}, s32[2]{0:T(128)}, u32[]{:S(2)}) copy-start(s32[2]{0:T(128)} %constant.96) | copy-start | bytes 28
  0.0 69.3 %copy-start.2 = (s32[2]{0:T(128)S(1)}, s32[2]{0:T(128)}, u32[]{:S(2)}) copy-start(s32[2]{0:T(128)} %constant.91.clone) | copy-start | bytes 28
  4.5 64.3 %copy-start = (bf16[768,512]{1,0:T(8,128)(2,1)S(1)}, bf16[768,512]{1,0:T(8,128)(2,1)}, u32[]{:S(2)}) copy-start(bf16[768,512]{1,0:T(8,128)(2,1)} %get-tuple-element.7.refs_0_) | copy-start | bytes 2359300
  4.5 64.3 %copy-start.1 = (bf16[768,512]{1,0:T(8,128)(2,1)S(1)}, bf16[768,512]{1,0:T(8,128)(2,1)}, u32[]{:S(2)}) copy-start(bf16[768,512]{1,0:T(8,128)(2,1)} %get-tuple-element.8.refs_1_) | copy-start | bytes 2359300
  4.5 5.2 %collective-permute-start.10 = (bf16[768,512]{1,0:T(8,128)(2,1)}, bf16[768,512]{1,0:T(8,128)(2,1)S(1)}, u32[]{:S(2)}, u32[]{:S(2)}) collective-permute-start(bf16[768,512]{1,0:T(8,128)(2,1)} %get-tuple-element.7.refs_0_), channel_id=1, source_target_pairs={{0,1},{1,0},{2,3},{3,2},{4,5},{5,4},{6,7},{7,6},{8,9},{9,8},{10,11... | collective-permute-start | bytes 2359304 | tf_op jit(solution)/shard_map/ppermute | solution.py:346
  4.6 20.8 %collective-permute-start = (bf16[768,512]{1,0:T(8,128)(2,1)}, bf16[768,512]{1,0:T(8,128)(2,1)}, u32[]{:S(2)}, u32[]{:S(2)}) collective-permute-start(bf16[768,512]{1,0:T(8,128)(2,1)} %get-tuple-element.7.refs_0_), channel_id=1, source_target_pairs={{0,4},{4,8},{8,12},{12,14},{14,10},{10,6},{6,2},{2,0},{1,5},{5,9},... | collective-permute-start | bytes 2359304 | tf_op jit(solution)/shard_map/ppermute | solution.py:356
  7.4 19.1 %collective-permute-start.5 = (bf16[768,512]{1,0:T(8,128)(2,1)}, bf16[768,512]{1,0:T(8,128)(2,1)}, u32[]{:S(2)}, u32[]{:S(2)}) collective-permute-start(bf16[768,512]{1,0:T(8,128)(2,1)} %get-tuple-element.8.refs_1_), channel_id=1, source_target_pairs={{4,0},{8,4},{12,8},{14,12},{10,14},{6,10},{2,6},{0,2},{5,1},{9,5},... | collective-permute-start | bytes 2359304 | tf_op jit(solution)/shard_map/ppermute | solution.py:356
  7.4 34.9 %collective-permute-start.16 = (bf16[768,512]{1,0:T(8,128)(2,1)}, bf16[768,512]{1,0:T(8,128)(2,1)}, u32[]{:S(2)}, u32[]{:S(2)}) collective-permute-start(bf16[768,512]{1,0:T(8,128)(2,1)} %get-tuple-element.8.refs_1_), channel_id=1, source_target_pairs={{0,4},{4,8},{8,12},{12,14},{14,10},{10,6},{6,2},{2,0},{1,5},{5,9},... | collective-permute-start | bytes 2359304 | tf_op jit(solution)/shard_map/ppermute | solution.py:356
  8.8 34.1 %collective-permute-start.11 = (bf16[768,512]{1,0:T(8,128)(2,1)}, bf16[768,512]{1,0:T(8,128)(2,1)S(1)}, u32[]{:S(2)}, u32[]{:S(2)}) collective-permute-start(bf16[768,512]{1,0:T(8,128)(2,1)} %get-tuple-element.8.refs_1_), channel_id=1, source_target_pairs={{0,1},{1,0},{2,3},{3,2},{4,5},{5,4},{6,7},{7,6},{8,9},{9,8},{10,11... | collective-permute-start | bytes 2359304 | tf_op jit(solution)/shard_map/ppermute | solution.py:346
  9.8 34.8 %collective-permute-start.19 = (bf16[768,512]{1,0:T(8,128)(2,1)}, bf16[768,512]{1,0:T(8,128)(2,1)}, u32[]{:S(2)}, u32[]{:S(2)}) collective-permute-start(bf16[768,512]{1,0:T(8,128)(2,1)} %get-tuple-element.7.refs_0_), channel_id=1, source_target_pairs={{4,0},{8,4},{12,8},{14,12},{10,14},{6,10},{2,6},{0,2},{5,1},{9,5},... | collective-permute-start | bytes 2359304 | tf_op jit(solution)/shard_map/ppermute | solution.py:356
  25.5 19.1 %collective-permute-start.32 = (bf16[768,512]{1,0:T(8,128)(2,1)}, bf16[768,512]{1,0:T(8,128)(2,1)}, u32[]{:S(2)}, u32[]{:S(2)}) collective-permute-start(bf16[768,512]{1,0:T(8,128)(2,1)} %collective-permute-done.refs_0_), channel_id=1, source_target_pairs={{0,1},{1,0},{2,3},{3,2},{4,5},{5,4},{6,7},{7,6},{8,9},{9,8},{10,11... | collective-permute-start | bytes 2359304 | tf_op jit(solution)/shard_map/ppermute | solution.py:346
  26.4 19.9 %collective-permute-start.33 = (bf16[768,512]{1,0:T(8,128)(2,1)}, bf16[768,512]{1,0:T(8,128)(2,1)}, u32[]{:S(2)}, u32[]{:S(2)}) collective-permute-start(bf16[768,512]{1,0:T(8,128)(2,1)} %collective-permute-done.5.refs_1_), channel_id=1, source_target_pairs={{0,1},{1,0},{2,3},{3,2},{4,5},{5,4},{6,7},{7,6},{8,9},{9,8},{10,11... | collective-permute-start | bytes 2359304 | tf_op jit(solution)/shard_map/ppermute | solution.py:346
  42.3 5.6 %collective-permute-start.30 = (bf16[768,512]{1,0:T(8,128)(2,1)}, bf16[768,512]{1,0:T(8,128)(2,1)}, u32[]{:S(2)}, u32[]{:S(2)}) collective-permute-start(bf16[768,512]{1,0:T(8,128)(2,1)} %collective-permute-done.16.refs_0_), channel_id=1, source_target_pairs={{0,1},{1,0},{2,3},{3,2},{4,5},{5,4},{6,7},{7,6},{8,9},{9,8},{10,11... | collective-permute-start | bytes 2359304 | tf_op jit(solution)/shard_map/ppermute | solution.py:346
  43.0 19.4 %collective-permute-start.1 = (bf16[768,512]{1,0:T(8,128)(2,1)}, bf16[768,512]{1,0:T(8,128)(2,1)}, u32[]{:S(2)}, u32[]{:S(2)}) collective-permute-start(bf16[768,512]{1,0:T(8,128)(2,1)} %collective-permute-done.refs_0_), channel_id=1, source_target_pairs={{0,4},{4,8},{8,12},{12,14},{14,10},{10,6},{6,2},{2,0},{1,5},{5,9},... | collective-permute-start | bytes 2359304 | tf_op jit(solution)/shard_map/ppermute | solution.py:356
  44.5 22.1 %collective-permute-start.6 = (bf16[768,512]{1,0:T(8,128)(2,1)}, bf16[768,512]{1,0:T(8,128)(2,1)}, u32[]{:S(2)}, u32[]{:S(2)}) collective-permute-start(bf16[768,512]{1,0:T(8,128)(2,1)} %collective-permute-done.5.refs_1_), channel_id=1, source_target_pairs={{4,0},{8,4},{12,8},{14,12},{10,14},{6,10},{2,6},{0,2},{5,1},{9,5},... | collective-permute-start | bytes 2359304 | tf_op jit(solution)/shard_map/ppermute | solution.py:356
  44.5 20.5 %collective-permute-start.31 = (bf16[768,512]{1,0:T(8,128)(2,1)}, bf16[768,512]{1,0:T(8,128)(2,1)}, u32[]{:S(2)}, u32[]{:S(2)}) collective-permute-start(bf16[768,512]{1,0:T(8,128)(2,1)} %collective-permute-done.19.refs_1_), channel_id=1, source_target_pairs={{0,1},{1,0},{2,3},{3,2},{4,5},{5,4},{6,7},{7,6},{8,9},{9,8},{10,11... | collective-permute-start | bytes 2359304 | tf_op jit(solution)/shard_map/ppermute | solution.py:346
  46.3 32.9 %collective-permute-start.17 = (bf16[768,512]{1,0:T(8,128)(2,1)}, bf16[768,512]{1,0:T(8,128)(2,1)}, u32[]{:S(2)}, u32[]{:S(2)}) collective-permute-start(bf16[768,512]{1,0:T(8,128)(2,1)} %collective-permute-done.16.refs_0_), channel_id=1, source_target_pairs={{0,4},{4,8},{8,12},{12,14},{14,10},{10,6},{6,2},{2,0},{1,5},{5,9},... | collective-permute-start | bytes 2359304 | tf_op jit(solution)/shard_map/ppermute | solution.py:356
  47.9 32.6 %collective-permute-start.20 = (bf16[768,512]{1,0:T(8,128)(2,1)}, bf16[768,512]{1,0:T(8,128)(2,1)}, u32[]{:S(2)}, u32[]{:S(2)}) collective-permute-start(bf16[768,512]{1,0:T(8,128)(2,1)} %collective-permute-done.19.refs_1_), channel_id=1, source_target_pairs={{4,0},{8,4},{12,8},{14,12},{10,14},{6,10},{2,6},{0,2},{5,1},{9,5},... | collective-permute-start | bytes 2359304 | tf_op jit(solution)/shard_map/ppermute | solution.py:356
  62.4 20.0 %collective-permute-start.28 = (bf16[768,512]{1,0:T(8,128)(2,1)}, bf16[768,512]{1,0:T(8,128)(2,1)}, u32[]{:S(2)}, u32[]{:S(2)}) collective-permute-start(bf16[768,512]{1,0:T(8,128)(2,1)} %collective-permute-done.1.refs_0_), channel_id=1, source_target_pairs={{0,1},{1,0},{2,3},{3,2},{4,5},{5,4},{6,7},{7,6},{8,9},{9,8},{10,11... | collective-permute-start | bytes 2359304 | tf_op jit(solution)/shard_map/ppermute | solution.py:346
  65.0 30.9 %collective-permute-start.2 = (bf16[768,512]{1,0:T(8,128)(2,1)}, bf16[768,512]{1,0:T(8,128)(2,1)S(1)}, u32[]{:S(2)}, u32[]{:S(2)}) collective-permute-start(bf16[768,512]{1,0:T(8,128)(2,1)} %collective-permute-done.1.refs_0_), channel_id=1, source_target_pairs={{0,4},{4,8},{8,12},{12,14},{14,10},{10,6},{6,2},{2,0},{1,5},{5,9},... | collective-permute-start | bytes 2359304 | tf_op jit(solution)/shard_map/ppermute | solution.py:356
  66.6 30.9 %collective-permute-start.7 = (bf16[768,512]{1,0:T(8,128)(2,1)}, bf16[768,512]{1,0:T(8,128)(2,1)S(1)}, u32[]{:S(2)}, u32[]{:S(2)}) collective-permute-start(bf16[768,512]{1,0:T(8,128)(2,1)} %collective-permute-done.6.refs_1_), channel_id=1, source_target_pairs={{4,0},{8,4},{12,8},{14,12},{10,14},{6,10},{2,6},{0,2},{5,1},{9,5},... | collective-permute-start | bytes 2359304 | tf_op jit(solution)/shard_map/ppermute | solution.py:356
  79.2 18.4 %collective-permute-start.29 = (bf16[768,512]{1,0:T(8,128)(2,1)}, bf16[768,512]{1,0:T(8,128)(2,1)S(1)}, u32[]{:S(2)}, u32[]{:S(2)}) collective-permute-start(bf16[768,512]{1,0:T(8,128)(2,1)} %collective-permute-done.6.refs_1_), channel_id=1, source_target_pairs={{0,1},{1,0},{2,3},{3,2},{4,5},{5,4},{6,7},{7,6},{8,9},{9,8},{10,11... | collective-permute-start | bytes 2359304 | tf_op jit(solution)/shard_map/ppermute | solution.py:346
  80.5 18.6 %collective-permute-start.26 = (bf16[768,512]{1,0:T(8,128)(2,1)}, bf16[768,512]{1,0:T(8,128)(2,1)S(1)}, u32[]{:S(2)}, u32[]{:S(2)}) collective-permute-start(bf16[768,512]{1,0:T(8,128)(2,1)} %collective-permute-done.17.refs_0_), channel_id=1, source_target_pairs={{0,1},{1,0},{2,3},{3,2},{4,5},{5,4},{6,7},{7,6},{8,9},{9,8},{10,11... | collective-permute-start | bytes 2359304 | tf_op jit(solution)/shard_map/ppermute | solution.py:346
  82.4 18.1 %collective-permute-start.27 = (bf16[768,512]{1,0:T(8,128)(2,1)}, bf16[768,512]{1,0:T(8,128)(2,1)S(1)}, u32[]{:S(2)}, u32[]{:S(2)}) collective-permute-start(bf16[768,512]{1,0:T(8,128)(2,1)} %collective-permute-done.20.refs_1_), channel_id=1, source_target_pairs={{0,1},{1,0},{2,3},{3,2},{4,5},{5,4},{6,7},{7,6},{8,9},{9,8},{10,11... | collective-permute-start | bytes 2359304 | tf_op jit(solution)/shard_map/ppermute | solution.py:346
  96.0 18.4 %collective-permute-start.18 = (bf16[768,512]{1,0:T(8,128)(2,1)}, bf16[768,512]{1,0:T(8,128)(2,1)S(1)}, u32[]{:S(2)}, u32[]{:S(2)}) collective-permute-start(bf16[768,512]{1,0:T(8,128)(2,1)} %collective-permute-done.17.refs_0_), channel_id=1, source_target_pairs={{0,4},{4,8},{8,12},{12,14},{14,10},{10,6},{6,2},{2,0},{1,5},{5,9},... | collective-permute-start | bytes 2359304 | tf_op jit(solution)/shard_map/ppermute | solution.py:356
  97.5 19.9 %collective-permute-start.21 = (bf16[768,512]{1,0:T(8,128)(2,1)}, bf16[768,512]{1,0:T(8,128)(2,1)S(1)}, u32[]{:S(2)}, u32[]{:S(2)}) collective-permute-start(bf16[768,512]{1,0:T(8,128)(2,1)} %collective-permute-done.20.refs_1_), channel_id=1, source_target_pairs={{4,0},{8,4},{12,8},{14,12},{10,14},{6,10},{2,6},{0,2},{5,1},{9,5},... | collective-permute-start | bytes 2359304 | tf_op jit(solution)/shard_map/ppermute | solution.py:356
  97.7 29.6 %collective-permute-start.12 = (bf16[768,256]{1,0:T(8,128)(2,1)S(1)}, bf16[768,256]{1,0:T(8,128)(2,1)S(1)}, u32[]{:S(2)}, u32[]{:S(2)}) collective-permute-start(bf16[768,256]{1,0:T(8,128)(2,1)S(1)} %get-tuple-element.19), channel_id=1, source_target_pairs={{0,4},{4,8},{8,12},{12,14},{14,10},{10,6},{6,2},{2,0},{1,5},{5,9},... | collective-permute-start | bytes 1179656 | tf_op jit(solution)/shard_map/ppermute | solution.py:356
  99.2 32.1 %collective-permute-start.3 = (bf16[768,256]{1,0:T(8,128)(2,1)S(1)}, bf16[768,256]{1,0:T(8,128)(2,1)S(1)}, u32[]{:S(2)}, u32[]{:S(2)}) collective-permute-start(bf16[768,256]{1,0:T(8,128)(2,1)S(1)} %get-tuple-element.20), channel_id=1, source_target_pairs={{0,4},{4,8},{8,12},{12,14},{14,10},{10,6},{6,2},{2,0},{1,5},{5,9},... | collective-permute-start | bytes 1179656 | tf_op jit(solution)/shard_map/ppermute | solution.py:356
  100.5 32.5 %collective-permute-start.8 = (bf16[768,256]{1,0:T(8,128)(2,1)S(1)}, bf16[768,256]{1,0:T(8,128)(2,1)S(1)}, u32[]{:S(2)}, u32[]{:S(2)}) collective-permute-start(bf16[768,256]{1,0:T(8,128)(2,1)S(1)} %get-tuple-element.18), channel_id=1, source_target_pairs={{4,0},{8,4},{12,8},{14,12},{10,14},{6,10},{2,6},{0,2},{5,1},{9,5},... | collective-permute-start | bytes 1179656 | tf_op jit(solution)/shard_map/ppermute | solution.py:356
  114.4 34.9 %collective-permute-start.24 = (bf16[768,512]{1,0:T(8,128)(2,1)S(1)}, bf16[768,512]{1,0:T(8,128)(2,1)S(1)}, u32[]{:S(2)}, u32[]{:S(2)}) collective-permute-start(bf16[768,512]{1,0:T(8,128)(2,1)S(1)} %collective-permute-done.2.refs_0_), channel_id=1, source_target_pairs={{0,1},{1,0},{2,3},{3,2},{4,5},{5,4},{6,7},{7,6},{8,9},{9,8},{10,11... | collective-permute-start | bytes 2359304 | tf_op jit(solution)/shard_map/ppermute | solution.py:346
  117.5 32.4 %collective-permute-start.25 = (bf16[768,512]{1,0:T(8,128)(2,1)S(1)}, bf16[768,512]{1,0:T(8,128)(2,1)S(1)}, u32[]{:S(2)}, u32[]{:S(2)}) collective-permute-start(bf16[768,512]{1,0:T(8,128)(2,1)S(1)} %collective-permute-done.7.refs_1_), channel_id=1, source_target_pairs={{0,1},{1,0},{2,3},{3,2},{4,5},{5,4},{6,7},{7,6},{8,9},{9,8},{10,11... | collective-permute-start | bytes 2359304 | tf_op jit(solution)/shard_map/ppermute | solution.py:346
  127.3 22.0 %collective-permute-start.13 = (bf16[768,256]{1,0:T(8,128)(2,1)S(1)}, bf16[768,256]{1,0:T(8,128)(2,1)S(1)}, u32[]{:S(2)}, u32[]{:S(2)}) collective-permute-start(bf16[768,256]{1,0:T(8,128)(2,1)S(1)} %get-tuple-element.17), channel_id=1, source_target_pairs={{4,0},{8,4},{12,8},{14,12},{10,14},{6,10},{2,6},{0,2},{5,1},{9,5},... | collective-permute-start | bytes 1179656 | tf_op jit(solution)/shard_map/ppermute | solution.py:356
  131.3 25.3 %collective-permute-start.22 = (bf16[768,512]{1,0:T(8,128)(2,1)S(1)}, bf16[768,512]{1,0:T(8,128)(2,1)S(1)}, u32[]{:S(2)}, u32[]{:S(2)}) collective-permute-start(bf16[768,512]{1,0:T(8,128)(2,1)S(1)} %collective-permute-done.18.refs_0_), channel_id=1, source_target_pairs={{0,1},{1,0},{2,3},{3,2},{4,5},{5,4},{6,7},{7,6},{8,9},{9,8},{10,11... | collective-permute-start | bytes 2359304 | tf_op jit(solution)/shard_map/ppermute | solution.py:346
  133.0 23.7 %collective-permute-start.23 = (bf16[768,512]{1,0:T(8,128)(2,1)S(1)}, bf16[768,512]{1,0:T(8,128)(2,1)S(1)}, u32[]{:S(2)}, u32[]{:S(2)}) collective-permute-start(bf16[768,512]{1,0:T(8,128)(2,1)S(1)} %collective-permute-done.21.refs_1_), channel_id=1, source_target_pairs={{0,1},{1,0},{2,3},{3,2},{4,5},{5,4},{6,7},{7,6},{8,9},{9,8},{10,11... | collective-permute-start | bytes 2359304 | tf_op jit(solution)/shard_map/ppermute | solution.py:346
  149.3 19.1 %collective-permute-start.4 = (bf16[768,256]{1,0:T(8,128)(2,1)S(1)}, bf16[768,256]{1,0:T(8,128)(2,1)S(1)}, u32[]{:S(2)}, u32[]{:S(2)}) collective-permute-start(bf16[768,256]{1,0:T(8,128)(2,1)S(1)} %collective-permute-done.3.refs_0_), channel_id=1, source_target_pairs={{0,1},{1,0},{2,3},{3,2},{4,5},{5,4},{6,7},{7,6},{8,9},{9,8},{10,11... | collective-permute-start | bytes 1179656 | tf_op jit(solution)/shard_map/ppermute | solution.py:346
  149.4 14.0 %collective-permute-start.14 = (bf16[768,256]{1,0:T(8,128)(2,1)S(1)}, bf16[768,256]{1,0:T(8,128)(2,1)S(1)}, u32[]{:S(2)}, u32[]{:S(2)}) collective-permute-start(bf16[768,256]{1,0:T(8,128)(2,1)S(1)} %collective-permute-done.12.refs_0_), channel_id=1, source_target_pairs={{0,1},{1,0},{2,3},{3,2},{4,5},{5,4},{6,7},{7,6},{8,9},{9,8},{10,11... | collective-permute-start | bytes 1179656 | tf_op jit(solution)/shard_map/ppermute | solution.py:346
  149.8 13.6 %collective-permute-start.15 = (bf16[768,256]{1,0:T(8,128)(2,1)S(1)}, bf16[768,256]{1,0:T(8,128)(2,1)S(1)}, u32[]{:S(2)}, u32[]{:S(2)}) collective-permute-start(bf16[768,256]{1,0:T(8,128)(2,1)S(1)} %collective-permute-done.13.refs_1_), channel_id=1, source_target_pairs={{0,1},{1,0},{2,3},{3,2},{4,5},{5,4},{6,7},{7,6},{8,9},{9,8},{10,11... | collective-permute-start | bytes 1179656 | tf_op jit(solution)/shard_map/ppermute | solution.py:346
  156.6 11.7 %collective-permute-start.9 = (bf16[768,256]{1,0:T(8,128)(2,1)S(1)}, bf16[768,256]{1,0:T(8,128)(2,1)S(1)}, u32[]{:S(2)}, u32[]{:S(2)}) collective-permute-start(bf16[768,256]{1,0:T(8,128)(2,1)S(1)} %collective-permute-done.8.refs_1_), channel_id=1, source_target_pairs={{0,1},{1,0},{2,3},{3,2},{4,5},{5,4},{6,7},{7,6},{8,9},{9,8},{10,11... | collective-permute-start | bytes 1179656 | tf_op jit(solution)/shard_map/ppermute | solution.py:346

commit v4 on v3

--- a/solution.py
+++ b/solution.py
@@ -2,6 +2,7 @@
 
 import jax
 import jax.numpy as jnp
+import numpy as np
 from jax import lax
 from jax.experimental import pallas as pl
 from jax.experimental.pallas import tpu as pltpu
@@ -9,8 +10,7 @@
 
 
 LANES = 128
-GRANT = 34 * 2**20
-SPLIT_GRANT = 123 * 2**19
+GRANT = 16 * 2**20
 LAST_HOPS = 2
 
 
@@ -21,6 +21,15 @@
         (jnp.float32(1.0) - lam) * jnp.power(lam, jnp.float32(minutes - 1) - position)
     )
     return weight, jnp.power(lam, jnp.float32(minutes))
+
+
+def constants(minutes):
+    lam = np.float32(0.9995)
+    position = np.arange(minutes, dtype=np.float32)
+    weight = np.sqrt(
+        (np.float32(1.0) - lam) * np.power(lam, np.float32(minutes - 1) - position)
+    )
+    return weight.astype(np.float32), np.power(lam, np.float32(minutes))
 
 
 def scale(part, weight):
@@ -67,27 +76,52 @@
     return (factor * (before + reach[0] * prior) + tile)[None]
 
 
+def owner(step):
+    n, me = lax.axis_size("assets"), lax.axis_index("assets")
+    place = jnp.where(me % 2 == 0, me // 2, n - 1 - me // 2)
+    at = lax.rem(place - step + 2 * n, n)
+    return jnp.where(at < n // 2, 2 * at, 2 * (n - 1 - at) + 1)
+
+
+def columns_of(where, k, width):
+    step, block, offset = where[k]
+    return pl.ds(pl.multiple_of(owner(step) * block + offset, LANES), width)
+
+
+def decay(factor):
+    first = lax.axis_index("tm") == 0
+    return jnp.where(first, factor, factor * factor), jnp.logical_not(first)
+
+
+def in_hbm(x):
+    return pltpu.with_memory_space_constraint(x, pltpu.HBM)
+
+
 def split_kernel(returns, weight, *refs):
-    parts, (box, sem) = refs[:-2], refs[-2:]
+    parts, (box, wide, sem) = refs[:-3], refs[-3:]
     width = parts[0].shape[1]
     copies = []
     for k in range(sem.shape[0]):
         at = slice(k * 2 * LANES, (k + 1) * 2 * LANES)
         copies.append(pltpu.make_async_copy(returns.at[:, at], box.at[:, at], sem.at[k]))
         copies[-1].start()
+    for k in range(weight.shape[0]):
+        wide[k * LANES : (k + 1) * LANES, :] = jnp.broadcast_to(
+            weight[k : k + 1, :], (LANES, LANES)
+        ).T
     for k, copy in enumerate(copies):
         copy.wait()
         for lane in range(k * 2 * LANES, (k + 1) * 2 * LANES, LANES):
             part, start = parts[lane // width], lane % width
             part[:, start : start + LANES] = (
-                box[:, lane : lane + LANES].astype(jnp.float32) * weight[...]
+                box[:, lane : lane + LANES].astype(jnp.float32) * wide[...]
             ).astype(jnp.bfloat16)
 
 
 def split_call(returns, weight, count):
     minutes, width = returns.shape
     near = pl.BlockSpec(memory_space=pltpu.VMEM)
-    part = jax.ShapeDtypeStruct((minutes, width // count), jnp.bfloat16)
+    part = pltpu.VMEM((minutes, width // count), jnp.bfloat16)
     return pl.pallas_call(
         split_kernel,
         out_shape=[part] * count,
@@ -95,13 +129,14 @@
         out_specs=[near] * count,
         scratch_shapes=[
             pltpu.VMEM((minutes, width), jnp.bfloat16),
+            pltpu.VMEM((minutes, LANES), jnp.float32),
             pltpu.SemaphoreType.DMA((width // (2 * LANES),)),
         ],
-        compiler_params=pltpu.CompilerParams(vmem_limit_bytes=SPLIT_GRANT),
+        compiler_params=pltpu.CompilerParams(vmem_limit_bytes=GRANT),
         cost_estimate=pl.CostEstimate(
             flops=minutes * width, bytes_accessed=4 * minutes * width, transcendentals=0
         ),
-    )(returns, weight)
+    )(in_hbm(returns), weight)
 
 
 def turn_kernel(*refs):
@@ -118,7 +153,7 @@
     near = pl.BlockSpec(memory_space=pltpu.VMEM)
     return pl.pallas_call(
         turn_kernel,
-        out_shape=jax.ShapeDtypeStruct((len(parts) * width, minutes), jnp.bfloat16),
+        out_shape=pltpu.VMEM((len(parts) * width, minutes), jnp.bfloat16),
         in_specs=[near] * len(parts),
         out_specs=near,
         compiler_params=pltpu.CompilerParams(vmem_limit_bytes=GRANT),
@@ -130,17 +165,18 @@
     )(*parts)
 
 
-def tile_kernel(count, rows, columns, coef, *refs):
+def tile_kernel(where, rows, factor, *refs):
+    count = len(where)
     own, other = refs[:count], refs[count : 2 * count]
     left_own, left_other, prior = refs[2 * count : 2 * count + 3]
     out, box, in_sem, out_sem = refs[-4:]
     width = own[0].shape[1]
     tiles = prior.shape[0] // rows
-    earlier = coef[1] != 0.0
+    kept, earlier = decay(factor)
     copy = pltpu.make_async_copy
 
     def place(k):
-        return pl.ds(pl.multiple_of(columns[k] * LANES, LANES), width)
+        return columns_of(where, k, width)
 
     def fetch(k, i):
         at = pl.ds(i * rows, rows)
@@ -163,16 +199,16 @@
 
             @pl.when(earlier)
             def _():
-                both = first + coef[1] * jnp.dot(
+                both = first + factor * jnp.dot(
                     left_other[at], other[k][...], preferred_element_type=jnp.float32
                 )
                 fetch(k, i).wait()
-                box[k, at] = coef[0] * box[k, at] + both
+                box[k, at] = kept * box[k, at] + both
 
             @pl.when(jnp.logical_not(earlier))
             def _():
                 fetch(k, i).wait()
-                box[k, at] = coef[0] * box[k, at] + first
+                box[k, at] = kept * box[k, at] + first
 
             flush(k, i).start()
 
@@ -181,23 +217,22 @@
             flush(k, i).wait()
 
 
-def tile_call(out, columns, coef, own, other, left_own, left_other, prior, rows):
+def tile_call(out, where, own, other, left_own, left_other, prior, rows, factor):
     count = len(own)
     minutes, width = own[0].shape
     height, total = prior.shape
     near = pl.BlockSpec(memory_space=pltpu.VMEM)
     far = pl.BlockSpec(memory_space=pltpu.HBM)
-    scalar = pl.BlockSpec(memory_space=pltpu.SMEM)
-    args = [columns, coef, *own, *other, left_own, left_other, prior]
-    in_specs = [scalar] * 2 + [near] * (2 * count + 2) + [far]
+    args = [*own, *other, left_own, left_other, prior]
+    in_specs = [near] * (2 * count + 2) + [far]
     aliases = {}
     if out is not None:
         aliases = {len(args): 0}
         in_specs.append(far)
         args.append(out)
     return pl.pallas_call(
-        functools.partial(tile_kernel, count, rows),
-        out_shape=jax.ShapeDtypeStruct((1, height, total), jnp.float32),
+        functools.partial(tile_kernel, where, rows, factor),
+        out_shape=pltpu.HBM((1, height, total), jnp.float32),
         in_specs=in_specs,
         out_specs=far,
         scratch_shapes=[
@@ -215,18 +250,19 @@
     )(*args)
 
 
-def decayed_kernel(columns, coef, prior, out, sem):
+def decayed_kernel(where, factor, prior, out, sem):
     count, _, width = out.shape
+    kept, _ = decay(factor)
 
     def fetch(k):
-        at = pl.ds(pl.multiple_of(columns[k] * LANES, LANES), width)
+        at = columns_of(where, k, width)
         return pltpu.make_async_copy(prior.at[:, at], out.at[k], sem.at[k])
 
     for k in range(count):
         fetch(k).start()
     for k in range(count):
         fetch(k).wait()
-        out[k] = coef[0] * out[k]
+        out[k] = kept * out[k]
 
 
 def own_kernel(count, *refs):
@@ -235,15 +271,16 @@
         out[k] = base[k] + jnp.dot(left[...], own[k][...], preferred_element_type=jnp.float32)
 
 
-def other_kernel(count, rows, columns, coef, *refs):
+def other_kernel(where, rows, factor, *refs):
+    count = len(where)
     other, left, base = refs[:count], *refs[count : count + 2]
     out, box, sem = refs[-3:]
     height, width = box.shape[1:]
-    earlier = coef[1] != 0.0
+    _, earlier = decay(factor)
 
     def flush(source, k, i):
         at = pl.ds(i * rows, rows)
-        across = pl.ds(pl.multiple_of(columns[k] * LANES, LANES), width)
+        across = columns_of(where, k, width)
         return pltpu.make_async_copy(source.at[k, at], out.at[0, at, across], sem.at[k, i])
 
     for k in range(count):
@@ -254,7 +291,7 @@
 
             @pl.when(earlier)
             def _():
-                box[k, at] = base[k, at] + coef[1] * jnp.dot(
+                box[k, at] = base[k, at] + factor * jnp.dot(
                     left[at], other[k][...], preferred_element_type=jnp.float32
                 )
                 flush(box, k, i).start()
@@ -268,14 +305,13 @@
             flush(box, k, i).wait()
 
 
-def last_calls(columns, coef, own, left_own, left_other, prior, rows):
+def last_calls(where, own, left_own, left_other, prior, rows, factor):
     count = len(own)
     minutes, width = own[0].shape
     height, _ = prior.shape
     near = pl.BlockSpec(memory_space=pltpu.VMEM)
     far = pl.BlockSpec(memory_space=pltpu.HBM)
-    scalar = pl.BlockSpec(memory_space=pltpu.SMEM)
-    small = jax.ShapeDtypeStruct((count, height, width), jnp.float32)
+    small = pltpu.VMEM((count, height, width), jnp.float32)
     grant = pltpu.CompilerParams(vmem_limit_bytes=GRANT)
     size = 4 * count * height * width
 
@@ -283,14 +319,14 @@
         return pl.CostEstimate(flops=flops, bytes_accessed=bytes_accessed, transcendentals=0)
 
     base = pl.pallas_call(
-        decayed_kernel,
+        functools.partial(decayed_kernel, where, factor),
         out_shape=small,
-        in_specs=[scalar, scalar, far],
+        in_specs=[far],
         out_specs=near,
         scratch_shapes=[pltpu.SemaphoreType.DMA((count,))],
         compiler_params=grant,
         cost_estimate=cost(size // 4, size),
-    )(columns, coef, prior)
+    )(prior)
     flops = 2 * count * minutes * width * height
     base = pl.pallas_call(
         functools.partial(own_kernel, count),
@@ -302,11 +338,11 @@
     )(*own, left_own, base)
 
     def finish(out, other):
-        args = [columns, coef, *other, left_other, base, out]
+        args = [*other, left_other, base, out]
         return pl.pallas_call(
-            functools.partial(other_kernel, count, rows),
-            out_shape=jax.ShapeDtypeStruct(out.shape, out.dtype),
-            in_specs=[scalar, scalar] + [near] * (count + 2) + [far],
+            functools.partial(other_kernel, where, rows, factor),
+            out_shape=pltpu.HBM(out.shape, out.dtype),
+            in_specs=[near] * (count + 2) + [far],
             out_specs=far,
             scratch_shapes=[
                 pltpu.VMEM(small.shape, small.dtype),
@@ -327,18 +363,12 @@
 def local_ring(returns, prior):
     minutes, width = returns.shape
     n = lax.axis_size("assets")
-    me, slab = lax.axis_index("assets"), lax.axis_index("tm")
     half = width // 2
     rows = min(prior.shape[0], 512)
 
     cycle = list(range(0, n, 2)) + list(range(n - 1, 0, -2))
     forward = [(cycle[k], cycle[(k + 1) % n]) for k in range(n)]
     backward = [(b, a) for a, b in forward]
-    place = jnp.where(me % 2 == 0, me // 2, n - 1 - me // 2)
-
-    def owner(step):
-        at = lax.rem(place - step + 2 * n, n)
-        return jnp.where(at < n // 2, 2 * at, 2 * (n - 1 - at) + 1)
 
     def swap(pieces):
         moved = []
@@ -346,9 +376,7 @@
             moved.append(lax.ppermute(part, "tm", [(0, 1), (1, 0)]))
         return moved
 
-    weight, factor = weights(minutes)
-    wide = jnp.broadcast_to(weight[:, None], (minutes, LANES))
-    coef = jnp.where(slab == 0, jnp.stack([factor, 0.0]), jnp.stack([factor * factor, factor]))
+    weight, factor = constants(minutes)
 
     def hop(parts):
         moved = []
@@ -356,7 +384,7 @@
             moved.append(lax.ppermute(parts[way], "assets", pairs))
         return moved
 
-    halves = split_call(returns, wide, 2)
+    halves = split_call(returns, jnp.asarray(weight.reshape(-1, LANES)), 2)
     flight = [halves, halves[::-1]]
     arrived = []
     for k in range(n - 2):
@@ -372,28 +400,31 @@
     left_own = turn_call(halves)
     left_other = turn_call(own_other)
 
-    common = (left_own, left_other, prior, rows)
-    unit = half // LANES
-    columns = (2 * me + jnp.arange(2, dtype=jnp.int32)) * unit
-    out = tile_call(None, columns, coef, halves, own_other, *common)
+    prior = in_hbm(prior)
+    common = (left_own, left_other, prior, rows, factor)
+    where = tuple((0, width, k * half) for k in (0, 1))
+    out = tile_call(None, where, halves, own_other, *common)
     for k, (pair, step, sides, start) in enumerate(arrived):
-        block = owner(jnp.array([step, -step], jnp.int32))
-        columns = (2 * block + jnp.array(sides, jnp.int32)) * unit + start // LANES
+        where = tuple(
+            (way_step, width, side * half + start)
+            for way_step, side in zip((step, -step), sides, strict=True)
+        )
         if k == len(arrived) - 1:
-            finish = last_calls(columns, coef, pair, *common)
+            finish = last_calls(where, pair, *common)
             return finish(out, swap(pair))
         other = swap(pair)
-        out = tile_call(out, columns, coef, pair, other, *common)
+        out = tile_call(out, where, pair, other, *common)
 
 
 def solution(mesh):
     n, slabs = mesh.shape["assets"], mesh.shape["tm"]
 
-    def rings(width):
-        return slabs == 2 and n % 2 == 0 and 4 <= n <= 16 and width % (8 * LANES) == 0
+    def rings(minutes, width):
+        even = slabs == 2 and n % 2 == 0 and 4 <= n <= 16
+        return even and minutes % LANES == 0 and width % (8 * LANES) == 0
 
     def local(returns, prior):
-        if not rings(returns.shape[1]):
+        if not rings(*returns.shape):
             return local_any(returns, prior)
         return local_ring(returns, prior)
 

time: 172 us -> 163 us (0.948)
  Pallas kernels: 66.7 us -> 54.6 us
  waiting for transfers between devices: 70 us -> 77.2 us
  other arithmetic: 2.73 us -> 0 us
    pallas_call x12, Pallas kernels: 62.2 us -> 52.2 us  [the longest x8 47.2 us: tile_call(): pl.pallas_call(functools.partial(tile_kernel, where, rows, factor), out_s...]
    ppermute x16, waiting for transfers between devices: 70 us -> 77.2 us  [hop(): moved.append(lax.ppermute(parts[way], 'assets', pairs))]
    pallas_call x1, Pallas kernels: 3.55 us -> 1.51 us  [split_call(): pl.pallas_call(split_kernel, out_shape=[part] * count, in_specs=[pl.Block...]
  transfers between devices with their start and end apart: 34 -> 34, of which waited for: 8 -> 10; matrix products, arithmetic and copies ran while one was open for 2% -> 0% of each run, Pallas kernels for 35% -> 31%
where the time goes in v4:
time: 163 us
  waiting for transfers between devices  77.2 us (47%)
  Pallas kernels  54.6 us (33%)
  starting transfers between devices  30.2 us (19%)
    ppermute x16, waiting for transfers between devices, hop(): moved.append(lax.ppermute(parts[way], 'assets', pairs))  77.2 us
    pallas_call x8, Pallas kernels, tile_call(): pl.pallas_call(functools.partial(tile_kernel, where, rows, factor), out_s...  47.2 us
    ppermute x18, starting transfers between devices, swap(): moved.append(lax.ppermute(part, 'tm', [(0, 1), (1, 0)]))  16.5 us
    ppermute x16, starting transfers between devices, hop(): moved.append(lax.ppermute(parts[way], 'assets', pairs))  13.6 us
  transfers between devices with their start and end apart: 34, of which 10 were waited for; matrix products, arithmetic and copies ran while one was open for 0% of the time, Pallas kernels for 31%

profile of v4, /device:TPU:1, one launch (start us, length us, event | category | flops | bytes accessed | tf_op | source)
XLA Modules:
  0.0 163.2 jit_solution(13430003736051416286)
XLA Ops:
  0.0 0.7 copy-done
  0.7 1.5 shard_map.37
  2.2 0.1 collective-permute-start.10
  2.3 2.8 %collective-permute-start = (bf16[768,512]{1,0:T(8,128)(2,1)S(1)}, bf16[768,512]{1,0:T(8,128)(2,1)S(1)}, u32[]{:S(2)}, u32[]{:S(2)}) collective-permute-start(bf16[768,512]{1,0:T(8,128)(2,1)S(1)} %get-tuple-element.7.refs_0_), channel_id=1, source_target_pairs={{0,4},{4,8},{8,12},{12,14},{14,10},{10,6},{6,2},{2,0},{1,5},{5,9},... | collective-permute-start | bytes 2359304 | tf_op jit(solution)/shard_map/ppermute | solution.py:384
  5.1 0.0 collective-permute-start.5
  5.1 1.5 collective-permute-start.16
  6.5 0.9 collective-permute-start.11
  7.4 15.4 %collective-permute-done.refs_0_ = bf16[768,512]{1,0:T(8,128)(2,1)S(1)} collective-permute-done((bf16[768,512]{1,0:T(8,128)(2,1)S(1)}, bf16[768,512]{1,0:T(8,128)(2,1)S(1)}, u32[]{:S(2)}, u32[]{:S(2)}) %collective-permute-start) | collective-permute-done | bytes 786464 | tf_op jit(solution)/shard_map/ppermute | solution.py:384
  22.8 0.9 collective-permute-start.32
  23.7 0.1 collective-permute-done.5.refs_1_
  23.8 2.0 %collective-permute-start.33 = (bf16[768,512]{1,0:T(8,128)(2,1)S(1)}, bf16[768,512]{1,0:T(8,128)(2,1)S(1)}, u32[]{:S(2)}, u32[]{:S(2)}) collective-permute-start(bf16[768,512]{1,0:T(8,128)(2,1)S(1)} %collective-permute-done.5.refs_1_), channel_id=1, source_target_pairs={{0,1},{1,0},{2,3},{3,2},{4,5},{5,4},{6,7},{7,6},{8,9},{9,8},{10,11... | collective-permute-start | bytes 2359304 | tf_op jit(solution)/shard_map/ppermute | solution.py:376
  25.8 13.9 %collective-permute-done.16.refs_0_ = bf16[768,512]{1,0:T(8,128)(2,1)S(1)} collective-permute-done((bf16[768,512]{1,0:T(8,128)(2,1)S(1)}, bf16[768,512]{1,0:T(8,128)(2,1)S(1)}, u32[]{:S(2)}, u32[]{:S(2)}) %collective-permute-start.16) | collective-permute-done | bytes 786464 | tf_op jit(solution)/shard_map/ppermute | solution.py:384
  39.7 0.6 collective-permute-start.30
  40.3 0.0 collective-permute-done.11.refs_1_.refs_3_
  40.3 1.5 collective-permute-start.1
  41.9 0.3 collective-permute-start.31
  42.2 0.0 collective-permute-done.32.refs_2_
  42.2 0.0 collective-permute-start.6
  42.2 0.0 collective-permute-done.33.refs_3_
  42.2 1.5 collective-permute-start.17
  43.6 0.1 collective-permute-start.20
  43.7 15.7 %collective-permute-done.1.refs_0_ = bf16[768,512]{1,0:T(8,128)(2,1)S(1)} collective-permute-done((bf16[768,512]{1,0:T(8,128)(2,1)S(1)}, bf16[768,512]{1,0:T(8,128)(2,1)S(1)}, u32[]{:S(2)}, u32[]{:S(2)}) %collective-permute-start.1) | collective-permute-done | bytes 786464 | tf_op jit(solution)/shard_map/ppermute | solution.py:384
  59.4 1.3 collective-permute-start.28
  60.7 1.5 collective-permute-start.2
  62.3 1.6 %shard_map.40.refs_3_ = f32[2,1024,256]{2,1,0:T(8,128)S(1)} custom-call(f32[1024,8192]{1,0:T(8,128)} %refs_6_.15), custom_call_target="tpu_custom_call" | custom-call | flops 524288 | bytes 2097152 | tf_op jit(solution)/shard_map/pallas_call | solution.py:321
  63.9 0.5 shard_map.39.refs_2_.refs_4_
  64.4 0.5 shard_map.38.refs_5_.refs_2_
  64.9 11.4 %collective-permute-done.17.refs_0_ = bf16[768,512]{1,0:T(8,128)(2,1)S(1)} collective-permute-done((bf16[768,512]{1,0:T(8,128)(2,1)S(1)}, bf16[768,512]{1,0:T(8,128)(2,1)S(1)}, u32[]{:S(2)}, u32[]{:S(2)}) %collective-permute-start.17) | collective-permute-done | bytes 786464 | tf_op jit(solution)/shard_map/ppermute | solution.py:384
  76.3 1.3 collective-permute-start.29
  77.6 0.3 collective-permute-done.20.refs_1_
  77.9 1.8 %collective-permute-start.26 = (bf16[768,512]{1,0:T(8,128)(2,1)S(1)}, bf16[768,512]{1,0:T(8,128)(2,1)S(1)}, u32[]{:S(2)}, u32[]{:S(2)}) collective-permute-start(bf16[768,512]{1,0:T(8,128)(2,1)S(1)} %collective-permute-done.17.refs_0_), channel_id=1, source_target_pairs={{0,1},{1,0},{2,3},{3,2},{4,5},{5,4},{6,7},{7,6},{8,9},{9,8},{10,11... | collective-permute-start | bytes 2359304 | tf_op jit(solution)/shard_map/ppermute | solution.py:376
  79.7 0.0 collective-permute-done.28.refs_2_
  79.7 0.0 collective-permute-start.27
  79.7 6.1 %shard_map.42.refs_7_ = f32[1,1024,8192]{2,1,0:T(8,128)} custom-call(bf16[768,512]{1,0:T(8,128)(2,1)S(1)} %get-tuple-element.7.refs_0_, bf16[768,512]{1,0:T(8,128)(2,1)S(1)} %get-tuple-element.8.refs_1_, bf16[768,512]{1,0:T(8,128)(2,1)S(1)} %collective-permute-done.10.refs_0_.refs_2_, bf16[768,512]{1,0:T(8,128)(2,1)S(1)} %collective-permute-done.11.refs_1_.refs_3_, ...), custom_call_target="tpu_custom_call" | custom-call | flops 3221225472 | bytes 11534336 | tf_op jit(solution)/shard_map/pallas_call | solution.py:233
  85.8 7.3 %collective-permute-done.2.refs_0_ = bf16[768,512]{1,0:T(8,128)(2,1)S(1)} collective-permute-done((bf16[768,512]{1,0:T(8,128)(2,1)S(1)}, bf16[768,512]{1,0:T(8,128)(2,1)S(1)}, u32[]{:S(2)}, u32[]{:S(2)}) %collective-permute-start.2) | collective-permute-done | bytes 786464 | tf_op jit(solution)/shard_map/ppermute | solution.py:384
  93.1 1.5 collective-permute-start.18
  94.7 0.1 collective-permute-done.7.refs_1_
  94.7 0.0 collective-permute-start.21
  94.8 0.1 fusion.1
  94.8 0.1 fusion
  94.9 1.5 collective-permute-start.12
  96.4 0.0 collective-permute-done.26.refs_2_
  96.4 1.3 collective-permute-start.3
  97.7 0.2 collective-permute-start.8
  97.9 6.1 %shard_map.43.refs_7_ = f32[1,1024,8192]{2,1,0:T(8,128)} custom-call(bf16[768,512]{1,0:T(8,128)(2,1)S(1)} %collective-permute-done.refs_0_, bf16[768,512]{1,0:T(8,128)(2,1)S(1)} %collective-permute-done.5.refs_1_, bf16[768,512]{1,0:T(8,128)(2,1)S(1)} %collective-permute-done.32.refs_2_, ...), custom_call_target="tpu_custom_call", output_to_operand_aliasing={{}: (7, {})} | custom-call | flops 3221225472 | bytes 11534336 | tf_op jit(solution)/shard_map/pallas_call | solution.py:233
  104.0 7.4 %collective-permute-done.18.refs_0_ = bf16[768,512]{1,0:T(8,128)(2,1)S(1)} collective-permute-done((bf16[768,512]{1,0:T(8,128)(2,1)S(1)}, bf16[768,512]{1,0:T(8,128)(2,1)S(1)}, u32[]{:S(2)}, u32[]{:S(2)}) %collective-permute-start.18) | collective-permute-done | bytes 786464 | tf_op jit(solution)/shard_map/ppermute | solution.py:384
  111.4 3.0 %collective-permute-start.24 = (bf16[768,512]{1,0:T(8,128)(2,1)S(1)}, bf16[768,512]{1,0:T(8,128)(2,1)S(1)}, u32[]{:S(2)}, u32[]{:S(2)}) collective-permute-start(bf16[768,512]{1,0:T(8,128)(2,1)S(1)} %collective-permute-done.2.refs_0_), channel_id=1, source_target_pairs={{0,1},{1,0},{2,3},{3,2},{4,5},{5,4},{6,7},{7,6},{8,9},{9,8},{10,11... | collective-permute-start | bytes 2359304 | tf_op jit(solution)/shard_map/ppermute | solution.py:376
  114.4 1.8 %collective-permute-start.25 = (bf16[768,512]{1,0:T(8,128)(2,1)S(1)}, bf16[768,512]{1,0:T(8,128)(2,1)S(1)}, u32[]{:S(2)}, u32[]{:S(2)}) collective-permute-start(bf16[768,512]{1,0:T(8,128)(2,1)S(1)} %collective-permute-done.7.refs_1_), channel_id=1, source_target_pairs={{0,1},{1,0},{2,3},{3,2},{4,5},{5,4},{6,7},{7,6},{8,9},{9,8},{10,11... | collective-permute-start | bytes 2359304 | tf_op jit(solution)/shard_map/ppermute | solution.py:376
  116.2 6.1 %shard_map.44.refs_7_ = f32[1,1024,8192]{2,1,0:T(8,128)} custom-call(bf16[768,512]{1,0:T(8,128)(2,1)S(1)} %collective-permute-done.16.refs_0_, bf16[768,512]{1,0:T(8,128)(2,1)S(1)} %collective-permute-done.19.refs_1_, bf16[768,512]{1,0:T(8,128)(2,1)S(1)} %collective-permute-done.30.refs_2_, ...), custom_call_target="tpu_custom_call", output_to_operand_aliasing={{}: (7, {})} | custom-call | flops 3221225472 | bytes 11534336 | tf_op jit(solution)/shard_map/pallas_call | solution.py:233
  122.4 0.2 collective-permute-start.13
  122.6 5.6 %collective-permute-done.3.refs_0_ = bf16[768,256]{1,0:T(8,128)(2,1)S(1)} collective-permute-done((bf16[768,256]{1,0:T(8,128)(2,1)S(1)}, bf16[768,256]{1,0:T(8,128)(2,1)S(1)}, u32[]{:S(2)}, u32[]{:S(2)}) %collective-permute-start.3) | collective-permute-done | bytes 393248 | tf_op jit(solution)/shard_map/ppermute | solution.py:384
  128.2 1.7 %collective-permute-start.22 = (bf16[768,512]{1,0:T(8,128)(2,1)S(1)}, bf16[768,512]{1,0:T(8,128)(2,1)S(1)}, u32[]{:S(2)}, u32[]{:S(2)}) collective-permute-start(bf16[768,512]{1,0:T(8,128)(2,1)S(1)} %collective-permute-done.18.refs_0_), channel_id=1, source_target_pairs={{0,1},{1,0},{2,3},{3,2},{4,5},{5,4},{6,7},{7,6},{8,9},{9,8},{10,11... | collective-permute-start | bytes 2359304 | tf_op jit(solution)/shard_map/ppermute | solution.py:376
  129.9 0.0 collective-permute-start.23
  129.9 6.1 %shard_map.45.refs_7_ = f32[1,1024,8192]{2,1,0:T(8,128)} custom-call(bf16[768,512]{1,0:T(8,128)(2,1)S(1)} %collective-permute-done.1.refs_0_, bf16[768,512]{1,0:T(8,128)(2,1)S(1)} %collective-permute-done.6.refs_1_, bf16[768,512]{1,0:T(8,128)(2,1)S(1)} %collective-permute-done.28.refs_2_, ...), custom_call_target="tpu_custom_call", output_to_operand_aliasing={{}: (7, {})} | custom-call | flops 3221225472 | bytes 11534336 | tf_op jit(solution)/shard_map/pallas_call | solution.py:233
  136.1 6.1 %shard_map.46.refs_7_ = f32[1,1024,8192]{2,1,0:T(8,128)} custom-call(bf16[768,512]{1,0:T(8,128)(2,1)S(1)} %collective-permute-done.17.refs_0_, bf16[768,512]{1,0:T(8,128)(2,1)S(1)} %collective-permute-done.20.refs_1_, bf16[768,512]{1,0:T(8,128)(2,1)S(1)} %collective-permute-done.26.refs_2_, ...), custom_call_target="tpu_custom_call", output_to_operand_aliasing={{}: (7, {})} | custom-call | flops 3221225472 | bytes 11534336 | tf_op jit(solution)/shard_map/pallas_call | solution.py:233
  142.2 1.0 shard_map.41.refs_3_
  143.2 0.1 collective-permute-start.4
  143.3 0.5 collective-permute-start.14
  143.8 0.1 collective-permute-start.15
  143.9 6.1 %shard_map.47.refs_7_ = f32[1,1024,8192]{2,1,0:T(8,128)} custom-call(bf16[768,512]{1,0:T(8,128)(2,1)S(1)} %collective-permute-done.2.refs_0_, bf16[768,512]{1,0:T(8,128)(2,1)S(1)} %collective-permute-done.7.refs_1_, bf16[768,512]{1,0:T(8,128)(2,1)S(1)} %collective-permute-done.24.refs_2_, ...), custom_call_target="tpu_custom_call", output_to_operand_aliasing={{}: (7, {})} | custom-call | flops 3221225472 | bytes 11534336 | tf_op jit(solution)/shard_map/pallas_call | solution.py:233
  150.0 0.1 collective-permute-start.9
  150.1 6.1 %shard_map.48.refs_7_ = f32[1,1024,8192]{2,1,0:T(8,128)} custom-call(bf16[768,512]{1,0:T(8,128)(2,1)S(1)} %collective-permute-done.18.refs_0_, bf16[768,512]{1,0:T(8,128)(2,1)S(1)} %collective-permute-done.21.refs_1_, bf16[768,512]{1,0:T(8,128)(2,1)S(1)} %collective-permute-done.22.refs_2_, ...), custom_call_target="tpu_custom_call", output_to_operand_aliasing={{}: (7, {})} | custom-call | flops 3221225472 | bytes 11534336 | tf_op jit(solution)/shard_map/pallas_call | solution.py:233
  156.3 4.4 %shard_map.49.refs_4_ = f32[1,1024,8192]{2,1,0:T(8,128)} custom-call(bf16[768,256]{1,0:T(8,128)(2,1)S(1)} %collective-permute-done.12.refs_0_, bf16[768,256]{1,0:T(8,128)(2,1)S(1)} %collective-permute-done.13.refs_1_, bf16[768,256]{1,0:T(8,128)(2,1)S(1)} %collective-permute-done.14.refs_2_, ...), custom_call_target="tpu_custom_call", output_to_operand_aliasing={{}: (7, {})} | custom-call | flops 1610612736 | bytes 5767168 | tf_op jit(solution)/shard_map/pallas_call | solution.py:233
  160.7 2.4 %shard_map.50 = f32[1,1024,8192]{2,1,0:T(8,128)} custom-call(bf16[768,256]{1,0:T(8,128)(2,1)S(1)} %collective-permute-done.4.refs_0_, bf16[768,256]{1,0:T(8,128)(2,1)S(1)} %collective-permute-done.9.refs_1_, bf16[1024,768]{1,0:T(8,128)(2,1)S(1)} %shard_map.38.refs_5_.refs_2_, f32[2,1024,256]{2,1,0:T(8,128)S(1)} %shard_map.41.refs_3_, ...), custom_call_target="tpu_custom_call", output_to_operand_aliasing={{}: (4, {})} | custom-call | flops 805306368 | bytes 4194304 | tf_op jit(solution)/shard_map/pallas_call | solution.py:342
  (22 shorter events, 0.1 us)
Async XLA Ops:
  0.0 0.7 copy-start
  2.2 5.2 %collective-permute-start.10 = (bf16[768,512]{1,0:T(8,128)(2,1)S(1)}, bf16[768,512]{1,0:T(8,128)(2,1)S(1)}, u32[]{:S(2)}, u32[]{:S(2)}) collective-permute-start(bf16[768,512]{1,0:T(8,128)(2,1)S(1)} %get-tuple-element.7.refs_0_), channel_id=1, source_target_pairs={{0,1},{1,0},{2,3},{3,2},{4,5},{5,4},{6,7},{7,6},{8,9},{9,8},{10,11... | collective-permute-start | bytes 2359304 | tf_op jit(solution)/shard_map/ppermute | solution.py:376
  2.3 20.5 %collective-permute-start = (bf16[768,512]{1,0:T(8,128)(2,1)S(1)}, bf16[768,512]{1,0:T(8,128)(2,1)S(1)}, u32[]{:S(2)}, u32[]{:S(2)}) collective-permute-start(bf16[768,512]{1,0:T(8,128)(2,1)S(1)} %get-tuple-element.7.refs_0_), channel_id=1, source_target_pairs={{0,4},{4,8},{8,12},{12,14},{14,10},{10,6},{6,2},{2,0},{1,5},{5,9},... | collective-permute-start | bytes 2359304 | tf_op jit(solution)/shard_map/ppermute | solution.py:384
  5.1 18.8 %collective-permute-start.5 = (bf16[768,512]{1,0:T(8,128)(2,1)S(1)}, bf16[768,512]{1,0:T(8,128)(2,1)S(1)}, u32[]{:S(2)}, u32[]{:S(2)}) collective-permute-start(bf16[768,512]{1,0:T(8,128)(2,1)S(1)} %get-tuple-element.8.refs_1_), channel_id=1, source_target_pairs={{4,0},{8,4},{12,8},{14,12},{10,14},{6,10},{2,6},{0,2},{5,1},{9,5},... | collective-permute-start | bytes 2359304 | tf_op jit(solution)/shard_map/ppermute | solution.py:384
  5.1 34.6 %collective-permute-start.16 = (bf16[768,512]{1,0:T(8,128)(2,1)S(1)}, bf16[768,512]{1,0:T(8,128)(2,1)S(1)}, u32[]{:S(2)}, u32[]{:S(2)}) collective-permute-start(bf16[768,512]{1,0:T(8,128)(2,1)S(1)} %get-tuple-element.8.refs_1_), channel_id=1, source_target_pairs={{0,4},{4,8},{8,12},{12,14},{14,10},{10,6},{6,2},{2,0},{1,5},{5,9},... | collective-permute-start | bytes 2359304 | tf_op jit(solution)/shard_map/ppermute | solution.py:384
  6.5 33.8 %collective-permute-start.11 = (bf16[768,512]{1,0:T(8,128)(2,1)S(1)}, bf16[768,512]{1,0:T(8,128)(2,1)S(1)}, u32[]{:S(2)}, u32[]{:S(2)}) collective-permute-start(bf16[768,512]{1,0:T(8,128)(2,1)S(1)} %get-tuple-element.8.refs_1_), channel_id=1, source_target_pairs={{0,1},{1,0},{2,3},{3,2},{4,5},{5,4},{6,7},{7,6},{8,9},{9,8},{10,11... | collective-permute-start | bytes 2359304 | tf_op jit(solution)/shard_map/ppermute | solution.py:376
  7.4 34.4 %collective-permute-start.19 = (bf16[768,512]{1,0:T(8,128)(2,1)S(1)}, bf16[768,512]{1,0:T(8,128)(2,1)S(1)}, u32[]{:S(2)}, u32[]{:S(2)}) collective-permute-start(bf16[768,512]{1,0:T(8,128)(2,1)S(1)} %get-tuple-element.7.refs_0_), channel_id=1, source_target_pairs={{4,0},{8,4},{12,8},{14,12},{10,14},{6,10},{2,6},{0,2},{5,1},{9,5},... | collective-permute-start | bytes 2359304 | tf_op jit(solution)/shard_map/ppermute | solution.py:384
  22.8 19.3 %collective-permute-start.32 = (bf16[768,512]{1,0:T(8,128)(2,1)S(1)}, bf16[768,512]{1,0:T(8,128)(2,1)S(1)}, u32[]{:S(2)}, u32[]{:S(2)}) collective-permute-start(bf16[768,512]{1,0:T(8,128)(2,1)S(1)} %collective-permute-done.refs_0_), channel_id=1, source_target_pairs={{0,1},{1,0},{2,3},{3,2},{4,5},{5,4},{6,7},{7,6},{8,9},{9,8},{10,11... | collective-permute-start | bytes 2359304 | tf_op jit(solution)/shard_map/ppermute | solution.py:376
  23.8 18.4 %collective-permute-start.33 = (bf16[768,512]{1,0:T(8,128)(2,1)S(1)}, bf16[768,512]{1,0:T(8,128)(2,1)S(1)}, u32[]{:S(2)}, u32[]{:S(2)}) collective-permute-start(bf16[768,512]{1,0:T(8,128)(2,1)S(1)} %collective-permute-done.5.refs_1_), channel_id=1, source_target_pairs={{0,1},{1,0},{2,3},{3,2},{4,5},{5,4},{6,7},{7,6},{8,9},{9,8},{10,11... | collective-permute-start | bytes 2359304 | tf_op jit(solution)/shard_map/ppermute | solution.py:376
  39.7 4.0 %collective-permute-start.30 = (bf16[768,512]{1,0:T(8,128)(2,1)S(1)}, bf16[768,512]{1,0:T(8,128)(2,1)S(1)}, u32[]{:S(2)}, u32[]{:S(2)}) collective-permute-start(bf16[768,512]{1,0:T(8,128)(2,1)S(1)} %collective-permute-done.16.refs_0_), channel_id=1, source_target_pairs={{0,1},{1,0},{2,3},{3,2},{4,5},{5,4},{6,7},{7,6},{8,9},{9,8},{10,11... | collective-permute-start | bytes 2359304 | tf_op jit(solution)/shard_map/ppermute | solution.py:376
  40.3 19.1 %collective-permute-start.1 = (bf16[768,512]{1,0:T(8,128)(2,1)S(1)}, bf16[768,512]{1,0:T(8,128)(2,1)S(1)}, u32[]{:S(2)}, u32[]{:S(2)}) collective-permute-start(bf16[768,512]{1,0:T(8,128)(2,1)S(1)} %collective-permute-done.refs_0_), channel_id=1, source_target_pairs={{0,4},{4,8},{8,12},{12,14},{14,10},{10,6},{6,2},{2,0},{1,5},{5,9},... | collective-permute-start | bytes 2359304 | tf_op jit(solution)/shard_map/ppermute | solution.py:384
  41.9 18.9 %collective-permute-start.31 = (bf16[768,512]{1,0:T(8,128)(2,1)S(1)}, bf16[768,512]{1,0:T(8,128)(2,1)S(1)}, u32[]{:S(2)}, u32[]{:S(2)}) collective-permute-start(bf16[768,512]{1,0:T(8,128)(2,1)S(1)} %collective-permute-done.19.refs_1_), channel_id=1, source_target_pairs={{0,1},{1,0},{2,3},{3,2},{4,5},{5,4},{6,7},{7,6},{8,9},{9,8},{10,11... | collective-permute-start | bytes 2359304 | tf_op jit(solution)/shard_map/ppermute | solution.py:376
  42.2 20.1 %collective-permute-start.6 = (bf16[768,512]{1,0:T(8,128)(2,1)S(1)}, bf16[768,512]{1,0:T(8,128)(2,1)S(1)}, u32[]{:S(2)}, u32[]{:S(2)}) collective-permute-start(bf16[768,512]{1,0:T(8,128)(2,1)S(1)} %collective-permute-done.5.refs_1_), channel_id=1, source_target_pairs={{4,0},{8,4},{12,8},{14,12},{10,14},{6,10},{2,6},{0,2},{5,1},{9,5},... | collective-permute-start | bytes 2359304 | tf_op jit(solution)/shard_map/ppermute | solution.py:384
  42.2 34.1 %collective-permute-start.17 = (bf16[768,512]{1,0:T(8,128)(2,1)S(1)}, bf16[768,512]{1,0:T(8,128)(2,1)S(1)}, u32[]{:S(2)}, u32[]{:S(2)}) collective-permute-start(bf16[768,512]{1,0:T(8,128)(2,1)S(1)} %collective-permute-done.16.refs_0_), channel_id=1, source_target_pairs={{0,4},{4,8},{8,12},{12,14},{14,10},{10,6},{6,2},{2,0},{1,5},{5,9},... | collective-permute-start | bytes 2359304 | tf_op jit(solution)/shard_map/ppermute | solution.py:384
  43.6 34.2 %collective-permute-start.20 = (bf16[768,512]{1,0:T(8,128)(2,1)S(1)}, bf16[768,512]{1,0:T(8,128)(2,1)S(1)}, u32[]{:S(2)}, u32[]{:S(2)}) collective-permute-start(bf16[768,512]{1,0:T(8,128)(2,1)S(1)} %collective-permute-done.19.refs_1_), channel_id=1, source_target_pairs={{4,0},{8,4},{12,8},{14,12},{10,14},{6,10},{2,6},{0,2},{5,1},{9,5},... | collective-permute-start | bytes 2359304 | tf_op jit(solution)/shard_map/ppermute | solution.py:384
  59.4 20.2 %collective-permute-start.28 = (bf16[768,512]{1,0:T(8,128)(2,1)S(1)}, bf16[768,512]{1,0:T(8,128)(2,1)S(1)}, u32[]{:S(2)}, u32[]{:S(2)}) collective-permute-start(bf16[768,512]{1,0:T(8,128)(2,1)S(1)} %collective-permute-done.1.refs_0_), channel_id=1, source_target_pairs={{0,1},{1,0},{2,3},{3,2},{4,5},{5,4},{6,7},{7,6},{8,9},{9,8},{10,11... | collective-permute-start | bytes 2359304 | tf_op jit(solution)/shard_map/ppermute | solution.py:376
  60.7 32.4 %collective-permute-start.2 = (bf16[768,512]{1,0:T(8,128)(2,1)S(1)}, bf16[768,512]{1,0:T(8,128)(2,1)S(1)}, u32[]{:S(2)}, u32[]{:S(2)}) collective-permute-start(bf16[768,512]{1,0:T(8,128)(2,1)S(1)} %collective-permute-done.1.refs_0_), channel_id=1, source_target_pairs={{0,4},{4,8},{8,12},{12,14},{14,10},{10,6},{6,2},{2,0},{1,5},{5,9},... | collective-permute-start | bytes 2359304 | tf_op jit(solution)/shard_map/ppermute | solution.py:384
  62.3 32.4 %collective-permute-start.7 = (bf16[768,512]{1,0:T(8,128)(2,1)S(1)}, bf16[768,512]{1,0:T(8,128)(2,1)S(1)}, u32[]{:S(2)}, u32[]{:S(2)}) collective-permute-start(bf16[768,512]{1,0:T(8,128)(2,1)S(1)} %collective-permute-done.6.refs_1_), channel_id=1, source_target_pairs={{4,0},{8,4},{12,8},{14,12},{10,14},{6,10},{2,6},{0,2},{5,1},{9,5},... | collective-permute-start | bytes 2359304 | tf_op jit(solution)/shard_map/ppermute | solution.py:384
  76.3 18.6 %collective-permute-start.29 = (bf16[768,512]{1,0:T(8,128)(2,1)S(1)}, bf16[768,512]{1,0:T(8,128)(2,1)S(1)}, u32[]{:S(2)}, u32[]{:S(2)}) collective-permute-start(bf16[768,512]{1,0:T(8,128)(2,1)S(1)} %collective-permute-done.6.refs_1_), channel_id=1, source_target_pairs={{0,1},{1,0},{2,3},{3,2},{4,5},{5,4},{6,7},{7,6},{8,9},{9,8},{10,11... | collective-permute-start | bytes 2359304 | tf_op jit(solution)/shard_map/ppermute | solution.py:376
  77.9 18.5 %collective-permute-start.26 = (bf16[768,512]{1,0:T(8,128)(2,1)S(1)}, bf16[768,512]{1,0:T(8,128)(2,1)S(1)}, u32[]{:S(2)}, u32[]{:S(2)}) collective-permute-start(bf16[768,512]{1,0:T(8,128)(2,1)S(1)} %collective-permute-done.17.refs_0_), channel_id=1, source_target_pairs={{0,1},{1,0},{2,3},{3,2},{4,5},{5,4},{6,7},{7,6},{8,9},{9,8},{10,11... | collective-permute-start | bytes 2359304 | tf_op jit(solution)/shard_map/ppermute | solution.py:376
  79.7 18.0 %collective-permute-start.27 = (bf16[768,512]{1,0:T(8,128)(2,1)S(1)}, bf16[768,512]{1,0:T(8,128)(2,1)S(1)}, u32[]{:S(2)}, u32[]{:S(2)}) collective-permute-start(bf16[768,512]{1,0:T(8,128)(2,1)S(1)} %collective-permute-done.20.refs_1_), channel_id=1, source_target_pairs={{0,1},{1,0},{2,3},{3,2},{4,5},{5,4},{6,7},{7,6},{8,9},{9,8},{10,11... | collective-permute-start | bytes 2359304 | tf_op jit(solution)/shard_map/ppermute | solution.py:376
  93.1 18.2 %collective-permute-start.18 = (bf16[768,512]{1,0:T(8,128)(2,1)S(1)}, bf16[768,512]{1,0:T(8,128)(2,1)S(1)}, u32[]{:S(2)}, u32[]{:S(2)}) collective-permute-start(bf16[768,512]{1,0:T(8,128)(2,1)S(1)} %collective-permute-done.17.refs_0_), channel_id=1, source_target_pairs={{0,4},{4,8},{8,12},{12,14},{14,10},{10,6},{6,2},{2,0},{1,5},{5,9},... | collective-permute-start | bytes 2359304 | tf_op jit(solution)/shard_map/ppermute | solution.py:384
  94.7 19.7 %collective-permute-start.21 = (bf16[768,512]{1,0:T(8,128)(2,1)S(1)}, bf16[768,512]{1,0:T(8,128)(2,1)S(1)}, u32[]{:S(2)}, u32[]{:S(2)}) collective-permute-start(bf16[768,512]{1,0:T(8,128)(2,1)S(1)} %collective-permute-done.20.refs_1_), channel_id=1, source_target_pairs={{4,0},{8,4},{12,8},{14,12},{10,14},{6,10},{2,6},{0,2},{5,1},{9,5},... | collective-permute-start | bytes 2359304 | tf_op jit(solution)/shard_map/ppermute | solution.py:384
  94.9 27.5 %collective-permute-start.12 = (bf16[768,256]{1,0:T(8,128)(2,1)S(1)}, bf16[768,256]{1,0:T(8,128)(2,1)S(1)}, u32[]{:S(2)}, u32[]{:S(2)}) collective-permute-start(bf16[768,256]{1,0:T(8,128)(2,1)S(1)} %get-tuple-element.11), channel_id=1, source_target_pairs={{0,4},{4,8},{8,12},{12,14},{14,10},{10,6},{6,2},{2,0},{1,5},{5,9},... | collective-permute-start | bytes 1179656 | tf_op jit(solution)/shard_map/ppermute | solution.py:384
  96.4 31.8 %collective-permute-start.3 = (bf16[768,256]{1,0:T(8,128)(2,1)S(1)}, bf16[768,256]{1,0:T(8,128)(2,1)S(1)}, u32[]{:S(2)}, u32[]{:S(2)}) collective-permute-start(bf16[768,256]{1,0:T(8,128)(2,1)S(1)} %get-tuple-element.12), channel_id=1, source_target_pairs={{0,4},{4,8},{8,12},{12,14},{14,10},{10,6},{6,2},{2,0},{1,5},{5,9},... | collective-permute-start | bytes 1179656 | tf_op jit(solution)/shard_map/ppermute | solution.py:384
  97.7 32.2 %collective-permute-start.8 = (bf16[768,256]{1,0:T(8,128)(2,1)S(1)}, bf16[768,256]{1,0:T(8,128)(2,1)S(1)}, u32[]{:S(2)}, u32[]{:S(2)}) collective-permute-start(bf16[768,256]{1,0:T(8,128)(2,1)S(1)} %get-tuple-element.10), channel_id=1, source_target_pairs={{4,0},{8,4},{12,8},{14,12},{10,14},{6,10},{2,6},{0,2},{5,1},{9,5},... | collective-permute-start | bytes 1179656 | tf_op jit(solution)/shard_map/ppermute | solution.py:384
  111.4 31.9 %collective-permute-start.24 = (bf16[768,512]{1,0:T(8,128)(2,1)S(1)}, bf16[768,512]{1,0:T(8,128)(2,1)S(1)}, u32[]{:S(2)}, u32[]{:S(2)}) collective-permute-start(bf16[768,512]{1,0:T(8,128)(2,1)S(1)} %collective-permute-done.2.refs_0_), channel_id=1, source_target_pairs={{0,1},{1,0},{2,3},{3,2},{4,5},{5,4},{6,7},{7,6},{8,9},{9,8},{10,11... | collective-permute-start | bytes 2359304 | tf_op jit(solution)/shard_map/ppermute | solution.py:376
  114.4 29.4 %collective-permute-start.25 = (bf16[768,512]{1,0:T(8,128)(2,1)S(1)}, bf16[768,512]{1,0:T(8,128)(2,1)S(1)}, u32[]{:S(2)}, u32[]{:S(2)}) collective-permute-start(bf16[768,512]{1,0:T(8,128)(2,1)S(1)} %collective-permute-done.7.refs_1_), channel_id=1, source_target_pairs={{0,1},{1,0},{2,3},{3,2},{4,5},{5,4},{6,7},{7,6},{8,9},{9,8},{10,11... | collective-permute-start | bytes 2359304 | tf_op jit(solution)/shard_map/ppermute | solution.py:376
  122.4 20.8 %collective-permute-start.13 = (bf16[768,256]{1,0:T(8,128)(2,1)S(1)}, bf16[768,256]{1,0:T(8,128)(2,1)S(1)}, u32[]{:S(2)}, u32[]{:S(2)}) collective-permute-start(bf16[768,256]{1,0:T(8,128)(2,1)S(1)} %get-tuple-element.9), channel_id=1, source_target_pairs={{4,0},{8,4},{12,8},{14,12},{10,14},{6,10},{2,6},{0,2},{5,1},{9,5},... | collective-permute-start | bytes 1179656 | tf_op jit(solution)/shard_map/ppermute | solution.py:384
  128.2 21.8 %collective-permute-start.22 = (bf16[768,512]{1,0:T(8,128)(2,1)S(1)}, bf16[768,512]{1,0:T(8,128)(2,1)S(1)}, u32[]{:S(2)}, u32[]{:S(2)}) collective-permute-start(bf16[768,512]{1,0:T(8,128)(2,1)S(1)} %collective-permute-done.18.refs_0_), channel_id=1, source_target_pairs={{0,1},{1,0},{2,3},{3,2},{4,5},{5,4},{6,7},{7,6},{8,9},{9,8},{10,11... | collective-permute-start | bytes 2359304 | tf_op jit(solution)/shard_map/ppermute | solution.py:376
  129.9 20.1 %collective-permute-start.23 = (bf16[768,512]{1,0:T(8,128)(2,1)S(1)}, bf16[768,512]{1,0:T(8,128)(2,1)S(1)}, u32[]{:S(2)}, u32[]{:S(2)}) collective-permute-start(bf16[768,512]{1,0:T(8,128)(2,1)S(1)} %collective-permute-done.21.refs_1_), channel_id=1, source_target_pairs={{0,1},{1,0},{2,3},{3,2},{4,5},{5,4},{6,7},{7,6},{8,9},{9,8},{10,11... | collective-permute-start | bytes 2359304 | tf_op jit(solution)/shard_map/ppermute | solution.py:376
  143.2 17.4 %collective-permute-start.4 = (bf16[768,256]{1,0:T(8,128)(2,1)S(1)}, bf16[768,256]{1,0:T(8,128)(2,1)S(1)}, u32[]{:S(2)}, u32[]{:S(2)}) collective-permute-start(bf16[768,256]{1,0:T(8,128)(2,1)S(1)} %collective-permute-done.3.refs_0_), channel_id=1, source_target_pairs={{0,1},{1,0},{2,3},{3,2},{4,5},{5,4},{6,7},{7,6},{8,9},{9,8},{10,11... | collective-permute-start | bytes 1179656 | tf_op jit(solution)/shard_map/ppermute | solution.py:376
  143.3 12.9 %collective-permute-start.14 = (bf16[768,256]{1,0:T(8,128)(2,1)S(1)}, bf16[768,256]{1,0:T(8,128)(2,1)S(1)}, u32[]{:S(2)}, u32[]{:S(2)}) collective-permute-start(bf16[768,256]{1,0:T(8,128)(2,1)S(1)} %collective-permute-done.12.refs_0_), channel_id=1, source_target_pairs={{0,1},{1,0},{2,3},{3,2},{4,5},{5,4},{6,7},{7,6},{8,9},{9,8},{10,11... | collective-permute-start | bytes 1179656 | tf_op jit(solution)/shard_map/ppermute | solution.py:376
  143.8 12.5 %collective-permute-start.15 = (bf16[768,256]{1,0:T(8,128)(2,1)S(1)}, bf16[768,256]{1,0:T(8,128)(2,1)S(1)}, u32[]{:S(2)}, u32[]{:S(2)}) collective-permute-start(bf16[768,256]{1,0:T(8,128)(2,1)S(1)} %collective-permute-done.13.refs_1_), channel_id=1, source_target_pairs={{0,1},{1,0},{2,3},{3,2},{4,5},{5,4},{6,7},{7,6},{8,9},{9,8},{10,11... | collective-permute-start | bytes 1179656 | tf_op jit(solution)/shard_map/ppermute | solution.py:376
  150.0 10.7 %collective-permute-start.9 = (bf16[768,256]{1,0:T(8,128)(2,1)S(1)}, bf16[768,256]{1,0:T(8,128)(2,1)S(1)}, u32[]{:S(2)}, u32[]{:S(2)}) collective-permute-start(bf16[768,256]{1,0:T(8,128)(2,1)S(1)} %collective-permute-done.8.refs_1_), channel_id=1, source_target_pairs={{0,1},{1,0},{2,3},{3,2},{4,5},{5,4},{6,7},{7,6},{8,9},{9,8},{10,11... | collective-permute-start | bytes 1179656 | tf_op jit(solution)/shard_map/ppermute | solution.py:376

commit v5 on v4

--- a/solution.py
+++ b/solution.py
@@ -11,7 +11,7 @@
 
 LANES = 128
 GRANT = 16 * 2**20
-LAST_HOPS = 2
+LAST_HOPS = 3
 
 
 def weights(minutes):
@@ -98,16 +98,19 @@
 
 
 def split_kernel(returns, weight, *refs):
-    parts, (box, wide, sem) = refs[:-3], refs[-3:]
+    parts, (box, row, wide, sem, row_sem) = refs[:-5], refs[-5:]
     width = parts[0].shape[1]
     copies = []
+    row_copy = pltpu.make_async_copy(weight, row, row_sem)
+    row_copy.start()
     for k in range(sem.shape[0]):
         at = slice(k * 2 * LANES, (k + 1) * 2 * LANES)
         copies.append(pltpu.make_async_copy(returns.at[:, at], box.at[:, at], sem.at[k]))
         copies[-1].start()
-    for k in range(weight.shape[0]):
+    row_copy.wait()
+    for k in range(row.shape[0]):
         wide[k * LANES : (k + 1) * LANES, :] = jnp.broadcast_to(
-            weight[k : k + 1, :], (LANES, LANES)
+            row[k : k + 1, :], (LANES, LANES)
         ).T
     for k, copy in enumerate(copies):
         copy.wait()
@@ -125,18 +128,20 @@
     return pl.pallas_call(
         split_kernel,
         out_shape=[part] * count,
-        in_specs=[pl.BlockSpec(memory_space=pltpu.HBM), near],
+        in_specs=[pl.BlockSpec(memory_space=pltpu.HBM)] * 2,
         out_specs=[near] * count,
         scratch_shapes=[
             pltpu.VMEM((minutes, width), jnp.bfloat16),
+            pltpu.VMEM(weight.shape, weight.dtype),
             pltpu.VMEM((minutes, LANES), jnp.float32),
             pltpu.SemaphoreType.DMA((width // (2 * LANES),)),
+            pltpu.SemaphoreType.DMA,
         ],
         compiler_params=pltpu.CompilerParams(vmem_limit_bytes=GRANT),
         cost_estimate=pl.CostEstimate(
             flops=minutes * width, bytes_accessed=4 * minutes * width, transcendentals=0
         ),
-    )(in_hbm(returns), weight)
+    )(in_hbm(returns), in_hbm(weight))
 
 
 def turn_kernel(*refs):
@@ -165,89 +170,16 @@
     )(*parts)
 
 
-def tile_kernel(where, rows, factor, *refs):
-    count = len(where)
-    own, other = refs[:count], refs[count : 2 * count]
-    left_own, left_other, prior = refs[2 * count : 2 * count + 3]
-    out, box, in_sem, out_sem = refs[-4:]
-    width = own[0].shape[1]
-    tiles = prior.shape[0] // rows
-    kept, earlier = decay(factor)
-    copy = pltpu.make_async_copy
-
-    def place(k):
-        return columns_of(where, k, width)
-
-    def fetch(k, i):
-        at = pl.ds(i * rows, rows)
-        return copy(prior.at[at, place(k)], box.at[k, at], in_sem.at[k, i])
-
-    def flush(k, i):
-        at = pl.ds(i * rows, rows)
-        return copy(box.at[k, at], out.at[0, at, place(k)], out_sem.at[k, i])
-
-    for k in range(count):
-        for i in range(tiles):
-            fetch(k, i).start()
-
-    for k in range(count):
-
-        @pl.loop(0, tiles)
-        def _(i):
-            at = pl.ds(pl.multiple_of(i * rows, rows), rows)
-            first = jnp.dot(left_own[at], own[k][...], preferred_element_type=jnp.float32)
-
-            @pl.when(earlier)
-            def _():
-                both = first + factor * jnp.dot(
-                    left_other[at], other[k][...], preferred_element_type=jnp.float32
-                )
-                fetch(k, i).wait()
-                box[k, at] = kept * box[k, at] + both
-
-            @pl.when(jnp.logical_not(earlier))
-            def _():
-                fetch(k, i).wait()
-                box[k, at] = kept * box[k, at] + first
-
-            flush(k, i).start()
-
-    for k in range(count):
-        for i in range(tiles):
-            flush(k, i).wait()
-
-
-def tile_call(out, where, own, other, left_own, left_other, prior, rows, factor):
-    count = len(own)
-    minutes, width = own[0].shape
-    height, total = prior.shape
-    near = pl.BlockSpec(memory_space=pltpu.VMEM)
-    far = pl.BlockSpec(memory_space=pltpu.HBM)
-    args = [*own, *other, left_own, left_other, prior]
-    in_specs = [near] * (2 * count + 2) + [far]
-    aliases = {}
-    if out is not None:
-        aliases = {len(args): 0}
-        in_specs.append(far)
-        args.append(out)
-    return pl.pallas_call(
-        functools.partial(tile_kernel, where, rows, factor),
-        out_shape=pltpu.HBM((1, height, total), jnp.float32),
-        in_specs=in_specs,
-        out_specs=far,
-        scratch_shapes=[
-            pltpu.VMEM((count, height, width), jnp.float32),
-            pltpu.SemaphoreType.DMA((count, height // rows)),
-            pltpu.SemaphoreType.DMA((count, height // rows)),
-        ],
-        input_output_aliases=aliases,
-        compiler_params=pltpu.CompilerParams(vmem_limit_bytes=GRANT),
-        cost_estimate=pl.CostEstimate(
-            flops=4 * count * minutes * width * height,
-            bytes_accessed=count * (8 * width * height + 4 * width * minutes),
-            transcendentals=0,
-        ),
-    )(*args)
+def products(left, parts, at):
+    width = parts[0].shape[1]
+    if width >= 2 * LANES:
+        for part in parts:
+            yield jnp.dot(left[at], part[...], preferred_element_type=jnp.float32)
+    else:
+        joined = jnp.concatenate([part[...] for part in parts], axis=1)
+        result = jnp.dot(left[at], joined, preferred_element_type=jnp.float32)
+        for k in range(len(parts)):
+            yield result[:, k * width : (k + 1) * width]
 
 
 def decayed_kernel(where, factor, prior, out, sem):
@@ -255,8 +187,9 @@
     kept, _ = decay(factor)
 
     def fetch(k):
-        at = columns_of(where, k, width)
-        return pltpu.make_async_copy(prior.at[:, at], out.at[k], sem.at[k])
+        return pltpu.make_async_copy(
+            prior.at[:, columns_of(where, k, width)], out.at[k], sem.at[k]
+        )
 
     for k in range(count):
         fetch(k).start()
@@ -265,10 +198,38 @@
         out[k] = kept * out[k]
 
 
-def own_kernel(count, *refs):
+def own_kernel(where, rows, factor, *refs):
+    count = len(where)
+    own, left, prior, out, sem = refs[:count], *refs[count:]
+    height, width = out.shape[1:]
+    kept, _ = decay(factor)
+
+    def fetch(k, i):
+        at = pl.ds(i * rows, rows)
+        return pltpu.make_async_copy(
+            prior.at[at, columns_of(where, k, width)], out.at[k, at], sem.at[k, i]
+        )
+
+    for i in range(height // rows):
+        for k in range(count):
+            fetch(k, i).start()
+
+    @pl.loop(0, height // rows)
+    def _(i):
+        at = pl.ds(pl.multiple_of(i * rows, rows), rows)
+        for k, product in enumerate(products(left, own, at)):
+            fetch(k, i).wait()
+            out[k, at] = kept * out[k, at] + product
+
+
+def own_late_kernel(count, rows, *refs):
     own, left, base, out = refs[:count], *refs[count:]
-    for k in range(count):
-        out[k] = base[k] + jnp.dot(left[...], own[k][...], preferred_element_type=jnp.float32)
+
+    @pl.loop(0, out.shape[1] // rows)
+    def _(i):
+        at = pl.ds(pl.multiple_of(i * rows, rows), rows)
+        for k, product in enumerate(products(left, own, at)):
+            out[k, at] = base[k, at] + product
 
 
 def other_kernel(where, rows, factor, *refs):
@@ -280,75 +241,92 @@
 
     def flush(source, k, i):
         at = pl.ds(i * rows, rows)
-        across = columns_of(where, k, width)
-        return pltpu.make_async_copy(source.at[k, at], out.at[0, at, across], sem.at[k, i])
-
-    for k in range(count):
-
-        @pl.loop(0, height // rows)
-        def _(i):
-            at = pl.ds(pl.multiple_of(i * rows, rows), rows)
-
-            @pl.when(earlier)
-            def _():
-                box[k, at] = base[k, at] + factor * jnp.dot(
-                    left[at], other[k][...], preferred_element_type=jnp.float32
-                )
+        return pltpu.make_async_copy(
+            source.at[k, at], out.at[0, at, columns_of(where, k, width)], sem.at[k, i]
+        )
+
+    @pl.loop(0, height // rows)
+    def _(i):
+        at = pl.ds(pl.multiple_of(i * rows, rows), rows)
+
+        @pl.when(earlier)
+        def _():
+            for k, product in enumerate(products(left, other, at)):
+                box[k, at] = base[k, at] + factor * product
                 flush(box, k, i).start()
 
-            @pl.when(jnp.logical_not(earlier))
-            def _():
+        @pl.when(jnp.logical_not(earlier))
+        def _():
+            for k in range(count):
                 flush(base, k, i).start()
 
-    for k in range(count):
-        for i in range(height // rows):
+    for i in range(height // rows):
+        for k in range(count):
             flush(box, k, i).wait()
 
 
-def last_calls(where, own, left_own, left_other, prior, rows, factor):
+def tile_calls(where, own, left_own, left_other, prior, rows, factor, early):
     count = len(own)
     minutes, width = own[0].shape
-    height, _ = prior.shape
+    height, total = prior.shape
+    tiles = height // rows
     near = pl.BlockSpec(memory_space=pltpu.VMEM)
     far = pl.BlockSpec(memory_space=pltpu.HBM)
     small = pltpu.VMEM((count, height, width), jnp.float32)
     grant = pltpu.CompilerParams(vmem_limit_bytes=GRANT)
     size = 4 * count * height * width
+    flops = 2 * count * minutes * width * height
 
     def cost(flops, bytes_accessed):
         return pl.CostEstimate(flops=flops, bytes_accessed=bytes_accessed, transcendentals=0)
 
-    base = pl.pallas_call(
-        functools.partial(decayed_kernel, where, factor),
-        out_shape=small,
-        in_specs=[far],
-        out_specs=near,
-        scratch_shapes=[pltpu.SemaphoreType.DMA((count,))],
-        compiler_params=grant,
-        cost_estimate=cost(size // 4, size),
-    )(prior)
-    flops = 2 * count * minutes * width * height
-    base = pl.pallas_call(
-        functools.partial(own_kernel, count),
-        out_shape=small,
-        in_specs=[near] * (count + 2),
-        out_specs=near,
-        compiler_params=grant,
-        cost_estimate=cost(flops, 2 * size),
-    )(*own, left_own, base)
+    if early:
+        base = pl.pallas_call(
+            functools.partial(decayed_kernel, where, factor),
+            out_shape=small,
+            in_specs=[far],
+            out_specs=near,
+            scratch_shapes=[pltpu.SemaphoreType.DMA((count,))],
+            compiler_params=grant,
+            cost_estimate=cost(size // 4, size),
+        )(prior)
+        base = pl.pallas_call(
+            functools.partial(own_late_kernel, count, rows),
+            out_shape=small,
+            in_specs=[near] * (count + 2),
+            out_specs=near,
+            compiler_params=grant,
+            cost_estimate=cost(flops, size),
+        )(*own, left_own, base)
+    else:
+        base = pl.pallas_call(
+            functools.partial(own_kernel, where, rows, factor),
+            out_shape=small,
+            in_specs=[near] * (count + 1) + [far],
+            out_specs=near,
+            scratch_shapes=[pltpu.SemaphoreType.DMA((count, tiles))],
+            compiler_params=grant,
+            cost_estimate=cost(flops, 2 * size),
+        )(*own, left_own, prior)
 
     def finish(out, other):
-        args = [*other, left_other, base, out]
+        args = [*other, left_other, base]
+        in_specs = [near] * (count + 2)
+        aliases = {}
+        if out is not None:
+            aliases = {len(args): 0}
+            args.append(out)
+            in_specs.append(far)
         return pl.pallas_call(
             functools.partial(other_kernel, where, rows, factor),
-            out_shape=pltpu.HBM(out.shape, out.dtype),
-            in_specs=[near] * (count + 2) + [far],
+            out_shape=pltpu.HBM((1, height, total), jnp.float32),
+            in_specs=in_specs,
             out_specs=far,
             scratch_shapes=[
                 pltpu.VMEM(small.shape, small.dtype),
-                pltpu.SemaphoreType.DMA((count, height // rows)),
+                pltpu.SemaphoreType.DMA((count, tiles)),
             ],
-            input_output_aliases={len(args) - 1: 0},
+            input_output_aliases=aliases,
             compiler_params=grant,
             cost_estimate=cost(flops, 2 * size),
         )(*args)
@@ -357,7 +335,8 @@
 
 
 def last_cuts(half):
-    return (half // LAST_HOPS,) * LAST_HOPS
+    rest = [half // 2**k for k in range(1, LAST_HOPS)]
+    return (*rest, rest[-1])
 
 
 def local_ring(returns, prior):
@@ -403,17 +382,15 @@
     prior = in_hbm(prior)
     common = (left_own, left_other, prior, rows, factor)
     where = tuple((0, width, k * half) for k in (0, 1))
-    out = tile_call(None, where, halves, own_other, *common)
+    out = tile_calls(where, halves, *common, False)(None, own_other)
     for k, (pair, step, sides, start) in enumerate(arrived):
         where = tuple(
             (way_step, width, side * half + start)
             for way_step, side in zip((step, -step), sides, strict=True)
         )
-        if k == len(arrived) - 1:
-            finish = last_calls(where, pair, *common)
-            return finish(out, swap(pair))
-        other = swap(pair)
-        out = tile_call(out, where, pair, other, *common)
+        finish = tile_calls(where, pair, *common, k >= n - 2)
+        out = finish(out, swap(pair))
+    return out
 
 
 def solution(mesh):

time: 163 us -> 161 us (0.988)
  the two profiles are of different devices: /device:TPU:1 before, /device:TPU:0 now
where the time goes in v5:
time: 161 us; the launch traced here: 158 us
  waiting for transfers between devices  78.9 us (49%)
  Pallas kernels  51.2 us (32%)
  starting transfers between devices  27.1 us (17%)
    ppermute x18, waiting for transfers between devices, hop(): moved.append(lax.ppermute(parts[way], 'assets', pairs))  78.9 us
    pallas_call x7, Pallas kernels, tile_calls(): pl.pallas_call(functools.partial(own_kernel, where, rows, factor), out_sh...  24 us
    ppermute x18, starting transfers between devices, hop(): moved.append(lax.ppermute(parts[way], 'assets', pairs))  20.8 us
    pallas_call x10, Pallas kernels, finish(): pl.pallas_call(functools.partial(other_kernel, where, rows, factor), out_...  17.8 us
    ppermute x20, starting transfers between devices, swap(): moved.append(lax.ppermute(part, 'tm', [(0, 1), (1, 0)]))  6.37 us
    pallas_call x3, Pallas kernels, tile_calls(): pl.pallas_call(functools.partial(decayed_kernel, where, factor), out_shap...  4.2 us
  transfers between devices with their start and end apart: 38, of which 12 were waited for; matrix products, arithmetic and copies ran while one was open for 0% of the time, Pallas kernels for 31%

profile of v5, /device:TPU:0, one launch (start us, length us, event | category | flops | bytes accessed | tf_op | source)
XLA Modules:
  0.0 157.8 jit_solution(11201255002872766637)
XLA Ops:
  0.0 1.7 %shard_map.37 = (bf16[768,512]{1,0:T(8,128)(2,1)S(1)}, bf16[768,512]{1,0:T(8,128)(2,1)S(1)}) custom-call(bf16[768,1024]{1,0:T(8,128)(2,1)} %returns.1, f32[6,128]{1,0:T(8,128)} %constant.2.clone.weight), custom_call_target="tpu_custom_call" | custom-call | flops 786432 | bytes 3145728 | tf_op jit(solution)/shard_map/pallas_call | solution.py:128
  1.7 0.6 collective-permute-start.10
  2.3 2.6 %collective-permute-start = (bf16[768,512]{1,0:T(8,128)(2,1)S(1)}, bf16[768,512]{1,0:T(8,128)(2,1)S(1)}, u32[]{:S(2)}, u32[]{:S(2)}) collective-permute-start(bf16[768,512]{1,0:T(8,128)(2,1)S(1)} %get-tuple-element.7.refs_0_), channel_id=1, source_target_pairs={{0,4},{4,8},{8,12},{12,14},{14,10},{10,6},{6,2},{2,0},{1,5},{5,9},... | collective-permute-start | bytes 2359304 | tf_op jit(solution)/shard_map/ppermute | solution.py:363
  4.9 2.0 %collective-permute-start.20 = (bf16[768,512]{1,0:T(8,128)(2,1)S(1)}, bf16[768,512]{1,0:T(8,128)(2,1)S(1)}, u32[]{:S(2)}, u32[]{:S(2)}) collective-permute-start(bf16[768,512]{1,0:T(8,128)(2,1)S(1)} %get-tuple-element.8.refs_1_), channel_id=1, source_target_pairs={{0,4},{4,8},{8,12},{12,14},{14,10},{10,6},{6,2},{2,0},{1,5},{5,9},... | collective-permute-start | bytes 2359304 | tf_op jit(solution)/shard_map/ppermute | solution.py:363
  6.9 0.1 collective-permute-start.24
  7.0 16.2 %collective-permute-done.refs_0_ = bf16[768,512]{1,0:T(8,128)(2,1)S(1)} collective-permute-done((bf16[768,512]{1,0:T(8,128)(2,1)S(1)}, bf16[768,512]{1,0:T(8,128)(2,1)S(1)}, u32[]{:S(2)}, u32[]{:S(2)}) %collective-permute-start) | collective-permute-done | bytes 786464 | tf_op jit(solution)/shard_map/ppermute | solution.py:363
  23.2 2.1 %collective-permute-done.5.refs_1_ = bf16[768,512]{1,0:T(8,128)(2,1)S(1)} collective-permute-done((bf16[768,512]{1,0:T(8,128)(2,1)S(1)}, bf16[768,512]{1,0:T(8,128)(2,1)S(1)}, u32[]{:S(2)}, u32[]{:S(2)}) %collective-permute-start.5) | collective-permute-done | bytes 786464 | tf_op jit(solution)/shard_map/ppermute | solution.py:363
  25.3 14.5 %collective-permute-done.20.refs_0_ = bf16[768,512]{1,0:T(8,128)(2,1)S(1)} collective-permute-done((bf16[768,512]{1,0:T(8,128)(2,1)S(1)}, bf16[768,512]{1,0:T(8,128)(2,1)S(1)}, u32[]{:S(2)}, u32[]{:S(2)}) %collective-permute-start.20) | collective-permute-done | bytes 786464 | tf_op jit(solution)/shard_map/ppermute | solution.py:363
  39.8 1.8 %collective-permute-start.1 = (bf16[768,512]{1,0:T(8,128)(2,1)S(1)}, bf16[768,512]{1,0:T(8,128)(2,1)S(1)}, u32[]{:S(2)}, u32[]{:S(2)}) collective-permute-start(bf16[768,512]{1,0:T(8,128)(2,1)S(1)} %collective-permute-done.refs_0_), channel_id=1, source_target_pairs={{0,4},{4,8},{8,12},{12,14},{14,10},{10,6},{6,2},{2,0},{1,5},{5,9},... | collective-permute-start | bytes 2359304 | tf_op jit(solution)/shard_map/ppermute | solution.py:363
  41.7 0.2 collective-permute-start.35
  41.9 0.3 collective-permute-start.6
  42.1 1.8 %collective-permute-start.21 = (bf16[768,512]{1,0:T(8,128)(2,1)S(1)}, bf16[768,512]{1,0:T(8,128)(2,1)S(1)}, u32[]{:S(2)}, u32[]{:S(2)}) collective-permute-start(bf16[768,512]{1,0:T(8,128)(2,1)S(1)} %collective-permute-done.20.refs_0_), channel_id=1, source_target_pairs={{0,4},{4,8},{8,12},{12,14},{14,10},{10,6},{6,2},{2,0},{1,5},{5,9},... | collective-permute-start | bytes 2359304 | tf_op jit(solution)/shard_map/ppermute | solution.py:363
  43.9 0.3 collective-permute-start.25
  44.2 16.1 %collective-permute-done.1.refs_0_ = bf16[768,512]{1,0:T(8,128)(2,1)S(1)} collective-permute-done((bf16[768,512]{1,0:T(8,128)(2,1)S(1)}, bf16[768,512]{1,0:T(8,128)(2,1)S(1)}, u32[]{:S(2)}, u32[]{:S(2)}) %collective-permute-start.1) | collective-permute-done | bytes 786464 | tf_op jit(solution)/shard_map/ppermute | solution.py:363
  60.2 1.8 %collective-permute-start.2 = (bf16[768,512]{1,0:T(8,128)(2,1)S(1)}, bf16[768,512]{1,0:T(8,128)(2,1)S(1)}, u32[]{:S(2)}, u32[]{:S(2)}) collective-permute-start(bf16[768,512]{1,0:T(8,128)(2,1)S(1)} %collective-permute-done.1.refs_0_), channel_id=1, source_target_pairs={{0,4},{4,8},{8,12},{12,14},{14,10},{10,6},{6,2},{2,0},{1,5},{5,9},... | collective-permute-start | bytes 2359304 | tf_op jit(solution)/shard_map/ppermute | solution.py:363
  62.1 0.2 collective-permute-done.6.refs_1_
  62.3 0.3 collective-permute-start.7
  62.6 1.3 shard_map.42.refs_3_
  63.8 1.3 shard_map.40.refs_3_
  65.1 1.7 %shard_map.44.refs_3_ = f32[2,1024,256]{2,1,0:T(8,128)S(1)} custom-call(f32[1024,8192]{1,0:T(8,128)} %refs_3_.13), custom_call_target="tpu_custom_call" | custom-call | flops 524288 | bytes 2097152 | tf_op jit(solution)/shard_map/pallas_call | solution.py:284
  66.8 0.5 shard_map.39.refs_2_
  67.2 3.4 %shard_map.52.refs_3_ = f32[2,1024,512]{2,1,0:T(8,128)S(1)} custom-call(bf16[768,512]{1,0:T(8,128)(2,1)S(1)} %get-tuple-element.7.refs_0_, bf16[768,512]{1,0:T(8,128)(2,1)S(1)} %get-tuple-element.8.refs_1_, bf16[1024,768]{1,0:T(8,128)(2,1)S(1)} %shard_map.39.refs_2_, f32[1024,8192]{1,0:T(8,128)} %refs_3_.13), custom_call_target="tpu_custom_call" | custom-call | flops 1610612736 | bytes 8388608 | tf_op jit(solution)/shard_map/pallas_call | solution.py:302
  70.7 3.4 %shard_map.51.refs_3_ = f32[2,1024,512]{2,1,0:T(8,128)S(1)} custom-call(bf16[768,512]{1,0:T(8,128)(2,1)S(1)} %collective-permute-done.refs_0_, bf16[768,512]{1,0:T(8,128)(2,1)S(1)} %collective-permute-done.5.refs_1_, bf16[1024,768]{1,0:T(8,128)(2,1)S(1)} %shard_map.39.refs_2_, f32[1024,8192]{1,0:T(8,128)} %refs_3_.13), custom_call_target="tpu_custom_call" | custom-call | flops 1610612736 | bytes 8388608 | tf_op jit(solution)/shard_map/pallas_call | solution.py:302
  74.1 3.0 %collective-permute-done.21.refs_0_ = bf16[768,512]{1,0:T(8,128)(2,1)S(1)} collective-permute-done((bf16[768,512]{1,0:T(8,128)(2,1)S(1)}, bf16[768,512]{1,0:T(8,128)(2,1)S(1)}, u32[]{:S(2)}, u32[]{:S(2)}) %collective-permute-start.21) | collective-permute-done | bytes 786464 | tf_op jit(solution)/shard_map/ppermute | solution.py:363
  77.1 2.1 %collective-permute-done.25.refs_1_ = bf16[768,512]{1,0:T(8,128)(2,1)S(1)} collective-permute-done((bf16[768,512]{1,0:T(8,128)(2,1)S(1)}, bf16[768,512]{1,0:T(8,128)(2,1)S(1)}, u32[]{:S(2)}, u32[]{:S(2)}) %collective-permute-start.25) | collective-permute-done | bytes 786464 | tf_op jit(solution)/shard_map/ppermute | solution.py:363
  79.2 0.5 collective-permute-start.31
  79.7 3.4 %shard_map.50.refs_3_ = f32[2,1024,512]{2,1,0:T(8,128)S(1)} custom-call(bf16[768,512]{1,0:T(8,128)(2,1)S(1)} %collective-permute-done.20.refs_0_, bf16[768,512]{1,0:T(8,128)(2,1)S(1)} %collective-permute-done.24.refs_1_, bf16[1024,768]{1,0:T(8,128)(2,1)S(1)} %shard_map.39.refs_2_, f32[1024,8192]{1,0:T(8,128)} %refs_3_.13), custom_call_target="tpu_custom_call" | custom-call | flops 1610612736 | bytes 8388608 | tf_op jit(solution)/shard_map/pallas_call | solution.py:302
  83.1 0.5 shard_map.38.refs_2_
  83.5 9.9 %collective-permute-done.2.refs_0_ = bf16[768,512]{1,0:T(8,128)(2,1)S(1)} collective-permute-done((bf16[768,512]{1,0:T(8,128)(2,1)S(1)}, bf16[768,512]{1,0:T(8,128)(2,1)S(1)}, u32[]{:S(2)}, u32[]{:S(2)}) %collective-permute-start.2) | collective-permute-done | bytes 786464 | tf_op jit(solution)/shard_map/ppermute | solution.py:363
  93.5 1.8 %collective-permute-start.22 = (bf16[768,512]{1,0:T(8,128)(2,1)S(1)}, bf16[768,512]{1,0:T(8,128)(2,1)S(1)}, u32[]{:S(2)}, u32[]{:S(2)}) collective-permute-start(bf16[768,512]{1,0:T(8,128)(2,1)S(1)} %collective-permute-done.21.refs_0_), channel_id=1, source_target_pairs={{0,4},{4,8},{8,12},{12,14},{14,10},{10,6},{6,2},{2,0},{1,5},{5,9},... | collective-permute-start | bytes 2359304 | tf_op jit(solution)/shard_map/ppermute | solution.py:363
  95.3 0.3 collective-permute-start.26
  95.6 2.0 %shard_map.53.refs_4_ = f32[1,1024,8192]{2,1,0:T(8,128)} custom-call(bf16[768,512]{1,0:T(8,128)(2,1)S(1)} %collective-permute-done.10.refs_0_, bf16[768,512]{1,0:T(8,128)(2,1)S(1)} %collective-permute-done.11.refs_1_, bf16[1024,768]{1,0:T(8,128)(2,1)S(1)} %shard_map.38.refs_2_, f32[2,1024,512]{2,1,0:T(8,128)S(1)} %shard_map.52.refs_3_), custom_call_target="tpu_custom_call" | custom-call | flops 1610612736 | bytes 8388608 | tf_op jit(solution)/shard_map/pallas_call | solution.py:320
  97.6 3.4 %shard_map.49.refs_3_ = f32[2,1024,512]{2,1,0:T(8,128)S(1)} custom-call(bf16[768,512]{1,0:T(8,128)(2,1)S(1)} %collective-permute-done.1.refs_0_, bf16[768,512]{1,0:T(8,128)(2,1)S(1)} %collective-permute-done.6.refs_1_, bf16[1024,768]{1,0:T(8,128)(2,1)S(1)} %shard_map.39.refs_2_, f32[1024,8192]{1,0:T(8,128)} %refs_3_.13), custom_call_target="tpu_custom_call" | custom-call | flops 1610612736 | bytes 8388608 | tf_op jit(solution)/shard_map/pallas_call | solution.py:302
  101.2 1.8 %collective-permute-start.16 = (bf16[768,256]{1,0:T(8,128)(2,1)S(1)}, bf16[768,256]{1,0:T(8,128)(2,1)S(1)}, u32[]{:S(2)}, u32[]{:S(2)}) collective-permute-start(bf16[768,256]{1,0:T(8,128)(2,1)S(1)} %slice.28), channel_id=1, source_target_pairs={{0,4},{4,8},{8,12},{12,14},{14,10},{10,6},{6,2},{2,0},{1,5},{5,9},... | collective-permute-start | bytes 1179656 | tf_op jit(solution)/shard_map/ppermute | solution.py:363
  103.0 1.6 collective-permute-start.12
  104.6 0.4 collective-permute-start.14
  105.0 3.4 %shard_map.48.refs_3_ = f32[2,1024,512]{2,1,0:T(8,128)S(1)} custom-call(bf16[768,512]{1,0:T(8,128)(2,1)S(1)} %collective-permute-done.21.refs_0_, bf16[768,512]{1,0:T(8,128)(2,1)S(1)} %collective-permute-done.25.refs_1_, bf16[1024,768]{1,0:T(8,128)(2,1)S(1)} %shard_map.39.refs_2_, f32[1024,8192]{1,0:T(8,128)} %refs_3_.13), custom_call_target="tpu_custom_call" | custom-call | flops 1610612736 | bytes 8388608 | tf_op jit(solution)/shard_map/pallas_call | solution.py:302
  108.5 5.4 %collective-permute-done.22.refs_0_ = bf16[768,512]{1,0:T(8,128)(2,1)S(1)} collective-permute-done((bf16[768,512]{1,0:T(8,128)(2,1)S(1)}, bf16[768,512]{1,0:T(8,128)(2,1)S(1)}, u32[]{:S(2)}, u32[]{:S(2)}) %collective-permute-start.22) | collective-permute-done | bytes 786464 | tf_op jit(solution)/shard_map/ppermute | solution.py:363
  113.9 1.8 %collective-permute-start.3 = (bf16[768,128]{1,0:T(8,128)(2,1)S(1)}, bf16[768,128]{1,0:T(8,128)(2,1)S(1)}, u32[]{:S(2)}, u32[]{:S(2)}) collective-permute-start(bf16[768,128]{1,0:T(8,128)(2,1)S(1)} %get-tuple-element.12), channel_id=1, source_target_pairs={{0,4},{4,8},{8,12},{12,14},{14,10},{10,6},{6,2},{2,0},{1,5},{5,9},... | collective-permute-start | bytes 589832 | tf_op jit(solution)/shard_map/ppermute | solution.py:363
  115.7 0.3 collective-permute-start.8
  116.0 2.0 %shard_map.54.refs_4_ = f32[1,1024,8192]{2,1,0:T(8,128)} custom-call(bf16[768,512]{1,0:T(8,128)(2,1)S(1)} %collective-permute-done.36.refs_0_, bf16[768,512]{1,0:T(8,128)(2,1)S(1)} %collective-permute-done.37.refs_1_, bf16[1024,768]{1,0:T(8,128)(2,1)S(1)} %shard_map.38.refs_2_, ...), custom_call_target="tpu_custom_call", output_to_operand_aliasing={{}: (4, {})} | custom-call | flops 1610612736 | bytes 8388608 | tf_op jit(solution)/shard_map/pallas_call | solution.py:320
  118.1 8.5 %collective-permute-done.12.refs_0_ = bf16[768,128]{1,0:T(8,128)(2,1)S(1)} collective-permute-done((bf16[768,128]{1,0:T(8,128)(2,1)S(1)}, bf16[768,128]{1,0:T(8,128)(2,1)S(1)}, u32[]{:S(2)}, u32[]{:S(2)}) %collective-permute-start.12) | collective-permute-done | bytes 196640 | tf_op jit(solution)/shard_map/ppermute | solution.py:363
  126.5 0.5 collective-permute-start.29
  127.0 2.0 %shard_map.55.refs_4_ = f32[1,1024,8192]{2,1,0:T(8,128)} custom-call(bf16[768,512]{1,0:T(8,128)(2,1)S(1)} %collective-permute-done.34.refs_0_, bf16[768,512]{1,0:T(8,128)(2,1)S(1)} %collective-permute-done.35.refs_1_, bf16[1024,768]{1,0:T(8,128)(2,1)S(1)} %shard_map.38.refs_2_, ...), custom_call_target="tpu_custom_call", output_to_operand_aliasing={{}: (4, {})} | custom-call | flops 1610612736 | bytes 8388608 | tf_op jit(solution)/shard_map/pallas_call | solution.py:320
  129.1 0.3 collective-permute-done.3.refs_0_
  129.4 1.7 %collective-permute-start.18 = (bf16[768,256]{1,0:T(8,128)(2,1)S(1)}, bf16[768,256]{1,0:T(8,128)(2,1)S(1)}, u32[]{:S(2)}, u32[]{:S(2)}) collective-permute-start(bf16[768,256]{1,0:T(8,128)(2,1)S(1)} %slice.29), channel_id=1, source_target_pairs={{4,0},{8,4},{12,8},{14,12},{10,14},{6,10},{2,6},{0,2},{5,1},{9,5},... | collective-permute-start | bytes 1179656 | tf_op jit(solution)/shard_map/ppermute | solution.py:363
  131.2 0.6 collective-permute-start.23
  131.8 3.4 %shard_map.47.refs_3_ = f32[2,1024,512]{2,1,0:T(8,128)S(1)} custom-call(bf16[768,512]{1,0:T(8,128)(2,1)S(1)} %collective-permute-done.2.refs_0_, bf16[768,512]{1,0:T(8,128)(2,1)S(1)} %collective-permute-done.7.refs_1_, bf16[1024,768]{1,0:T(8,128)(2,1)S(1)} %shard_map.39.refs_2_, f32[1024,8192]{1,0:T(8,128)} %refs_3_.13), custom_call_target="tpu_custom_call" | custom-call | flops 1610612736 | bytes 8388608 | tf_op jit(solution)/shard_map/pallas_call | solution.py:302
  135.3 3.4 %shard_map.46.refs_3_ = f32[2,1024,512]{2,1,0:T(8,128)S(1)} custom-call(bf16[768,512]{1,0:T(8,128)(2,1)S(1)} %collective-permute-done.22.refs_0_, bf16[768,512]{1,0:T(8,128)(2,1)S(1)} %collective-permute-done.26.refs_1_, bf16[1024,768]{1,0:T(8,128)(2,1)S(1)} %shard_map.39.refs_2_, f32[1024,8192]{1,0:T(8,128)} %refs_3_.13), custom_call_target="tpu_custom_call" | custom-call | flops 1610612736 | bytes 8388608 | tf_op jit(solution)/shard_map/pallas_call | solution.py:302
  138.7 2.1 %shard_map.56.refs_4_ = f32[1,1024,8192]{2,1,0:T(8,128)} custom-call(bf16[768,512]{1,0:T(8,128)(2,1)S(1)} %collective-permute-done.32.refs_0_, bf16[768,512]{1,0:T(8,128)(2,1)S(1)} %collective-permute-done.33.refs_1_, bf16[1024,768]{1,0:T(8,128)(2,1)S(1)} %shard_map.38.refs_2_, ...), custom_call_target="tpu_custom_call", output_to_operand_aliasing={{}: (4, {})} | custom-call | flops 1610612736 | bytes 8388608 | tf_op jit(solution)/shard_map/pallas_call | solution.py:320
  140.8 0.6 collective-permute-done.18.refs_1_
  141.4 0.8 collective-permute-start.17
  142.2 2.0 %shard_map.57.refs_4_ = f32[1,1024,8192]{2,1,0:T(8,128)} custom-call(bf16[768,512]{1,0:T(8,128)(2,1)S(1)} %collective-permute-done.30.refs_0_, bf16[768,512]{1,0:T(8,128)(2,1)S(1)} %collective-permute-done.31.refs_1_, bf16[1024,768]{1,0:T(8,128)(2,1)S(1)} %shard_map.38.refs_2_, ...), custom_call_target="tpu_custom_call", output_to_operand_aliasing={{}: (4, {})} | custom-call | flops 1610612736 | bytes 8388608 | tf_op jit(solution)/shard_map/pallas_call | solution.py:320
  144.3 0.7 shard_map.43.refs_3_
  145.0 1.0 collective-permute-start.19
  146.1 0.7 shard_map.41.refs_3_
  146.8 1.1 shard_map.45.refs_3_
  148.1 2.1 %shard_map.58.refs_4_ = f32[1,1024,8192]{2,1,0:T(8,128)} custom-call(bf16[768,512]{1,0:T(8,128)(2,1)S(1)} %collective-permute-done.28.refs_0_, bf16[768,512]{1,0:T(8,128)(2,1)S(1)} %collective-permute-done.29.refs_1_, bf16[1024,768]{1,0:T(8,128)(2,1)S(1)} %shard_map.38.refs_2_, ...), custom_call_target="tpu_custom_call", output_to_operand_aliasing={{}: (4, {})} | custom-call | flops 1610612736 | bytes 8388608 | tf_op jit(solution)/shard_map/pallas_call | solution.py:320
  150.1 1.5 collective-permute-start.15
  151.7 0.4 collective-permute-start.9
  152.1 2.0 %shard_map.59.refs_4_ = f32[1,1024,8192]{2,1,0:T(8,128)} custom-call(bf16[768,512]{1,0:T(8,128)(2,1)S(1)} %collective-permute-done.23.refs_0_, bf16[768,512]{1,0:T(8,128)(2,1)S(1)} %collective-permute-done.27.refs_1_, bf16[1024,768]{1,0:T(8,128)(2,1)S(1)} %shard_map.38.refs_2_, ...), custom_call_target="tpu_custom_call", output_to_operand_aliasing={{}: (4, {})} | custom-call | flops 1610612736 | bytes 8388608 | tf_op jit(solution)/shard_map/pallas_call | solution.py:320
  154.2 1.4 shard_map.60.refs_4_
  155.6 1.0 shard_map.61.refs_4_
  156.6 1.0 shard_map.62
  (42 shorter events, 0.5 us)
Async XLA Ops:
  1.7 5.2 %collective-permute-start.10 = (bf16[768,512]{1,0:T(8,128)(2,1)S(1)}, bf16[768,512]{1,0:T(8,128)(2,1)S(1)}, u32[]{:S(2)}, u32[]{:S(2)}) collective-permute-start(bf16[768,512]{1,0:T(8,128)(2,1)S(1)} %get-tuple-element.7.refs_0_), channel_id=1, source_target_pairs={{0,1},{1,0},{2,3},{3,2},{4,5},{5,4},{6,7},{7,6},{8,9},{9,8},{10,11... | collective-permute-start | bytes 2359304 | tf_op jit(solution)/shard_map/ppermute | solution.py:355
  2.3 20.9 %collective-permute-start = (bf16[768,512]{1,0:T(8,128)(2,1)S(1)}, bf16[768,512]{1,0:T(8,128)(2,1)S(1)}, u32[]{:S(2)}, u32[]{:S(2)}) collective-permute-start(bf16[768,512]{1,0:T(8,128)(2,1)S(1)} %get-tuple-element.7.refs_0_), channel_id=1, source_target_pairs={{0,4},{4,8},{8,12},{12,14},{14,10},{10,6},{6,2},{2,0},{1,5},{5,9},... | collective-permute-start | bytes 2359304 | tf_op jit(solution)/shard_map/ppermute | solution.py:363
  4.9 20.4 %collective-permute-start.5 = (bf16[768,512]{1,0:T(8,128)(2,1)S(1)}, bf16[768,512]{1,0:T(8,128)(2,1)S(1)}, u32[]{:S(2)}, u32[]{:S(2)}) collective-permute-start(bf16[768,512]{1,0:T(8,128)(2,1)S(1)} %get-tuple-element.8.refs_1_), channel_id=1, source_target_pairs={{4,0},{8,4},{12,8},{14,12},{10,14},{6,10},{2,6},{0,2},{5,1},{9,5},... | collective-permute-start | bytes 2359304 | tf_op jit(solution)/shard_map/ppermute | solution.py:363
  4.9 34.9 %collective-permute-start.20 = (bf16[768,512]{1,0:T(8,128)(2,1)S(1)}, bf16[768,512]{1,0:T(8,128)(2,1)S(1)}, u32[]{:S(2)}, u32[]{:S(2)}) collective-permute-start(bf16[768,512]{1,0:T(8,128)(2,1)S(1)} %get-tuple-element.8.refs_1_), channel_id=1, source_target_pairs={{0,4},{4,8},{8,12},{12,14},{14,10},{10,6},{6,2},{2,0},{1,5},{5,9},... | collective-permute-start | bytes 2359304 | tf_op jit(solution)/shard_map/ppermute | solution.py:363
  6.9 32.9 %collective-permute-start.11 = (bf16[768,512]{1,0:T(8,128)(2,1)S(1)}, bf16[768,512]{1,0:T(8,128)(2,1)S(1)}, u32[]{:S(2)}, u32[]{:S(2)}) collective-permute-start(bf16[768,512]{1,0:T(8,128)(2,1)S(1)} %get-tuple-element.8.refs_1_), channel_id=1, source_target_pairs={{0,1},{1,0},{2,3},{3,2},{4,5},{5,4},{6,7},{7,6},{8,9},{9,8},{10,11... | collective-permute-start | bytes 2359304 | tf_op jit(solution)/shard_map/ppermute | solution.py:355
  6.9 34.7 %collective-permute-start.24 = (bf16[768,512]{1,0:T(8,128)(2,1)S(1)}, bf16[768,512]{1,0:T(8,128)(2,1)S(1)}, u32[]{:S(2)}, u32[]{:S(2)}) collective-permute-start(bf16[768,512]{1,0:T(8,128)(2,1)S(1)} %get-tuple-element.7.refs_0_), channel_id=1, source_target_pairs={{4,0},{8,4},{12,8},{14,12},{10,14},{6,10},{2,6},{0,2},{5,1},{9,5},... | collective-permute-start | bytes 2359304 | tf_op jit(solution)/shard_map/ppermute | solution.py:363
  23.2 18.7 %collective-permute-start.36 = (bf16[768,512]{1,0:T(8,128)(2,1)S(1)}, bf16[768,512]{1,0:T(8,128)(2,1)S(1)}, u32[]{:S(2)}, u32[]{:S(2)}) collective-permute-start(bf16[768,512]{1,0:T(8,128)(2,1)S(1)} %collective-permute-done.refs_0_), channel_id=1, source_target_pairs={{0,1},{1,0},{2,3},{3,2},{4,5},{5,4},{6,7},{7,6},{8,9},{9,8},{10,11... | collective-permute-start | bytes 2359304 | tf_op jit(solution)/shard_map/ppermute | solution.py:355
  25.3 16.8 %collective-permute-start.37 = (bf16[768,512]{1,0:T(8,128)(2,1)S(1)}, bf16[768,512]{1,0:T(8,128)(2,1)S(1)}, u32[]{:S(2)}, u32[]{:S(2)}) collective-permute-start(bf16[768,512]{1,0:T(8,128)(2,1)S(1)} %collective-permute-done.5.refs_1_), channel_id=1, source_target_pairs={{0,1},{1,0},{2,3},{3,2},{4,5},{5,4},{6,7},{7,6},{8,9},{9,8},{10,11... | collective-permute-start | bytes 2359304 | tf_op jit(solution)/shard_map/ppermute | solution.py:355
  39.8 4.1 %collective-permute-start.34 = (bf16[768,512]{1,0:T(8,128)(2,1)S(1)}, bf16[768,512]{1,0:T(8,128)(2,1)S(1)}, u32[]{:S(2)}, u32[]{:S(2)}) collective-permute-start(bf16[768,512]{1,0:T(8,128)(2,1)S(1)} %collective-permute-done.20.refs_0_), channel_id=1, source_target_pairs={{0,1},{1,0},{2,3},{3,2},{4,5},{5,4},{6,7},{7,6},{8,9},{9,8},{10,11... | collective-permute-start | bytes 2359304 | tf_op jit(solution)/shard_map/ppermute | solution.py:355
  39.8 20.4 %collective-permute-start.1 = (bf16[768,512]{1,0:T(8,128)(2,1)S(1)}, bf16[768,512]{1,0:T(8,128)(2,1)S(1)}, u32[]{:S(2)}, u32[]{:S(2)}) collective-permute-start(bf16[768,512]{1,0:T(8,128)(2,1)S(1)} %collective-permute-done.refs_0_), channel_id=1, source_target_pairs={{0,4},{4,8},{8,12},{12,14},{14,10},{10,6},{6,2},{2,0},{1,5},{5,9},... | collective-permute-start | bytes 2359304 | tf_op jit(solution)/shard_map/ppermute | solution.py:363
  41.7 18.6 %collective-permute-start.35 = (bf16[768,512]{1,0:T(8,128)(2,1)S(1)}, bf16[768,512]{1,0:T(8,128)(2,1)S(1)}, u32[]{:S(2)}, u32[]{:S(2)}) collective-permute-start(bf16[768,512]{1,0:T(8,128)(2,1)S(1)} %collective-permute-done.24.refs_1_), channel_id=1, source_target_pairs={{0,1},{1,0},{2,3},{3,2},{4,5},{5,4},{6,7},{7,6},{8,9},{9,8},{10,11... | collective-permute-start | bytes 2359304 | tf_op jit(solution)/shard_map/ppermute | solution.py:355
  41.9 20.4 %collective-permute-start.6 = (bf16[768,512]{1,0:T(8,128)(2,1)S(1)}, bf16[768,512]{1,0:T(8,128)(2,1)S(1)}, u32[]{:S(2)}, u32[]{:S(2)}) collective-permute-start(bf16[768,512]{1,0:T(8,128)(2,1)S(1)} %collective-permute-done.5.refs_1_), channel_id=1, source_target_pairs={{4,0},{8,4},{12,8},{14,12},{10,14},{6,10},{2,6},{0,2},{5,1},{9,5},... | collective-permute-start | bytes 2359304 | tf_op jit(solution)/shard_map/ppermute | solution.py:363
  42.1 34.9 %collective-permute-start.21 = (bf16[768,512]{1,0:T(8,128)(2,1)S(1)}, bf16[768,512]{1,0:T(8,128)(2,1)S(1)}, u32[]{:S(2)}, u32[]{:S(2)}) collective-permute-start(bf16[768,512]{1,0:T(8,128)(2,1)S(1)} %collective-permute-done.20.refs_0_), channel_id=1, source_target_pairs={{0,4},{4,8},{8,12},{12,14},{14,10},{10,6},{6,2},{2,0},{1,5},{5,9},... | collective-permute-start | bytes 2359304 | tf_op jit(solution)/shard_map/ppermute | solution.py:363
  43.9 35.2 %collective-permute-start.25 = (bf16[768,512]{1,0:T(8,128)(2,1)S(1)}, bf16[768,512]{1,0:T(8,128)(2,1)S(1)}, u32[]{:S(2)}, u32[]{:S(2)}) collective-permute-start(bf16[768,512]{1,0:T(8,128)(2,1)S(1)} %collective-permute-done.24.refs_1_), channel_id=1, source_target_pairs={{4,0},{8,4},{12,8},{14,12},{10,14},{6,10},{2,6},{0,2},{5,1},{9,5},... | collective-permute-start | bytes 2359304 | tf_op jit(solution)/shard_map/ppermute | solution.py:363
  60.2 18.9 %collective-permute-start.32 = (bf16[768,512]{1,0:T(8,128)(2,1)S(1)}, bf16[768,512]{1,0:T(8,128)(2,1)S(1)}, u32[]{:S(2)}, u32[]{:S(2)}) collective-permute-start(bf16[768,512]{1,0:T(8,128)(2,1)S(1)} %collective-permute-done.1.refs_0_), channel_id=1, source_target_pairs={{0,1},{1,0},{2,3},{3,2},{4,5},{5,4},{6,7},{7,6},{8,9},{9,8},{10,11... | collective-permute-start | bytes 2359304 | tf_op jit(solution)/shard_map/ppermute | solution.py:355
  60.2 33.2 %collective-permute-start.2 = (bf16[768,512]{1,0:T(8,128)(2,1)S(1)}, bf16[768,512]{1,0:T(8,128)(2,1)S(1)}, u32[]{:S(2)}, u32[]{:S(2)}) collective-permute-start(bf16[768,512]{1,0:T(8,128)(2,1)S(1)} %collective-permute-done.1.refs_0_), channel_id=1, source_target_pairs={{0,4},{4,8},{8,12},{12,14},{14,10},{10,6},{6,2},{2,0},{1,5},{5,9},... | collective-permute-start | bytes 2359304 | tf_op jit(solution)/shard_map/ppermute | solution.py:363
  62.3 33.0 %collective-permute-start.7 = (bf16[768,512]{1,0:T(8,128)(2,1)S(1)}, bf16[768,512]{1,0:T(8,128)(2,1)S(1)}, u32[]{:S(2)}, u32[]{:S(2)}) collective-permute-start(bf16[768,512]{1,0:T(8,128)(2,1)S(1)} %collective-permute-done.6.refs_1_), channel_id=1, source_target_pairs={{4,0},{8,4},{12,8},{14,12},{10,14},{6,10},{2,6},{0,2},{5,1},{9,5},... | collective-permute-start | bytes 2359304 | tf_op jit(solution)/shard_map/ppermute | solution.py:363
  77.1 24.1 %collective-permute-start.33 = (bf16[768,512]{1,0:T(8,128)(2,1)S(1)}, bf16[768,512]{1,0:T(8,128)(2,1)S(1)}, u32[]{:S(2)}, u32[]{:S(2)}) collective-permute-start(bf16[768,512]{1,0:T(8,128)(2,1)S(1)} %collective-permute-done.6.refs_1_), channel_id=1, source_target_pairs={{0,1},{1,0},{2,3},{3,2},{4,5},{5,4},{6,7},{7,6},{8,9},{9,8},{10,11... | collective-permute-start | bytes 2359304 | tf_op jit(solution)/shard_map/ppermute | solution.py:355
  79.2 23.9 %collective-permute-start.30 = (bf16[768,512]{1,0:T(8,128)(2,1)S(1)}, bf16[768,512]{1,0:T(8,128)(2,1)S(1)}, u32[]{:S(2)}, u32[]{:S(2)}) collective-permute-start(bf16[768,512]{1,0:T(8,128)(2,1)S(1)} %collective-permute-done.21.refs_0_), channel_id=1, source_target_pairs={{0,1},{1,0},{2,3},{3,2},{4,5},{5,4},{6,7},{7,6},{8,9},{9,8},{10,11... | collective-permute-start | bytes 2359304 | tf_op jit(solution)/shard_map/ppermute | solution.py:355
  79.2 25.4 %collective-permute-start.31 = (bf16[768,512]{1,0:T(8,128)(2,1)S(1)}, bf16[768,512]{1,0:T(8,128)(2,1)S(1)}, u32[]{:S(2)}, u32[]{:S(2)}) collective-permute-start(bf16[768,512]{1,0:T(8,128)(2,1)S(1)} %collective-permute-done.25.refs_1_), channel_id=1, source_target_pairs={{0,1},{1,0},{2,3},{3,2},{4,5},{5,4},{6,7},{7,6},{8,9},{9,8},{10,11... | collective-permute-start | bytes 2359304 | tf_op jit(solution)/shard_map/ppermute | solution.py:355
  93.5 20.4 %collective-permute-start.22 = (bf16[768,512]{1,0:T(8,128)(2,1)S(1)}, bf16[768,512]{1,0:T(8,128)(2,1)S(1)}, u32[]{:S(2)}, u32[]{:S(2)}) collective-permute-start(bf16[768,512]{1,0:T(8,128)(2,1)S(1)} %collective-permute-done.21.refs_0_), channel_id=1, source_target_pairs={{0,4},{4,8},{8,12},{12,14},{14,10},{10,6},{6,2},{2,0},{1,5},{5,9},... | collective-permute-start | bytes 2359304 | tf_op jit(solution)/shard_map/ppermute | solution.py:363
  95.3 20.4 %collective-permute-start.26 = (bf16[768,512]{1,0:T(8,128)(2,1)S(1)}, bf16[768,512]{1,0:T(8,128)(2,1)S(1)}, u32[]{:S(2)}, u32[]{:S(2)}) collective-permute-start(bf16[768,512]{1,0:T(8,128)(2,1)S(1)} %collective-permute-done.25.refs_1_), channel_id=1, source_target_pairs={{4,0},{8,4},{12,8},{14,12},{10,14},{6,10},{2,6},{0,2},{5,1},{9,5},... | collective-permute-start | bytes 2359304 | tf_op jit(solution)/shard_map/ppermute | solution.py:363
  101.2 30.6 %collective-permute-start.16 = (bf16[768,256]{1,0:T(8,128)(2,1)S(1)}, bf16[768,256]{1,0:T(8,128)(2,1)S(1)}, u32[]{:S(2)}, u32[]{:S(2)}) collective-permute-start(bf16[768,256]{1,0:T(8,128)(2,1)S(1)} %slice.28), channel_id=1, source_target_pairs={{0,4},{4,8},{8,12},{12,14},{14,10},{10,6},{6,2},{2,0},{1,5},{5,9},... | collective-permute-start | bytes 1179656 | tf_op jit(solution)/shard_map/ppermute | solution.py:363
  103.0 23.5 %collective-permute-start.12 = (bf16[768,128]{1,0:T(8,128)(2,1)S(1)}, bf16[768,128]{1,0:T(8,128)(2,1)S(1)}, u32[]{:S(2)}, u32[]{:S(2)}) collective-permute-start(bf16[768,128]{1,0:T(8,128)(2,1)S(1)} %get-tuple-element.11), channel_id=1, source_target_pairs={{0,4},{4,8},{8,12},{12,14},{14,10},{10,6},{6,2},{2,0},{1,5},{5,9},... | collective-permute-start | bytes 589832 | tf_op jit(solution)/shard_map/ppermute | solution.py:363
  104.6 21.9 %collective-permute-start.14 = (bf16[768,128]{1,0:T(8,128)(2,1)S(1)}, bf16[768,128]{1,0:T(8,128)(2,1)S(1)}, u32[]{:S(2)}, u32[]{:S(2)}) collective-permute-start(bf16[768,128]{1,0:T(8,128)(2,1)S(1)} %get-tuple-element.9), channel_id=1, source_target_pairs={{4,0},{8,4},{12,8},{14,12},{10,14},{6,10},{2,6},{0,2},{5,1},{9,5},... | collective-permute-start | bytes 589832 | tf_op jit(solution)/shard_map/ppermute | solution.py:363
  113.9 15.5 %collective-permute-start.3 = (bf16[768,128]{1,0:T(8,128)(2,1)S(1)}, bf16[768,128]{1,0:T(8,128)(2,1)S(1)}, u32[]{:S(2)}, u32[]{:S(2)}) collective-permute-start(bf16[768,128]{1,0:T(8,128)(2,1)S(1)} %get-tuple-element.12), channel_id=1, source_target_pairs={{0,4},{4,8},{8,12},{12,14},{14,10},{10,6},{6,2},{2,0},{1,5},{5,9},... | collective-permute-start | bytes 589832 | tf_op jit(solution)/shard_map/ppermute | solution.py:363
  115.7 15.4 %collective-permute-start.8 = (bf16[768,128]{1,0:T(8,128)(2,1)S(1)}, bf16[768,128]{1,0:T(8,128)(2,1)S(1)}, u32[]{:S(2)}, u32[]{:S(2)}) collective-permute-start(bf16[768,128]{1,0:T(8,128)(2,1)S(1)} %get-tuple-element.10), channel_id=1, source_target_pairs={{4,0},{8,4},{12,8},{14,12},{10,14},{6,10},{2,6},{0,2},{5,1},{9,5},... | collective-permute-start | bytes 589832 | tf_op jit(solution)/shard_map/ppermute | solution.py:363
  126.5 18.5 %collective-permute-start.28 = (bf16[768,512]{1,0:T(8,128)(2,1)S(1)}, bf16[768,512]{1,0:T(8,128)(2,1)S(1)}, u32[]{:S(2)}, u32[]{:S(2)}) collective-permute-start(bf16[768,512]{1,0:T(8,128)(2,1)S(1)} %collective-permute-done.2.refs_0_), channel_id=1, source_target_pairs={{0,1},{1,0},{2,3},{3,2},{4,5},{5,4},{6,7},{7,6},{8,9},{9,8},{10,11... | collective-permute-start | bytes 2359304 | tf_op jit(solution)/shard_map/ppermute | solution.py:355
  126.5 21.4 %collective-permute-start.29 = (bf16[768,512]{1,0:T(8,128)(2,1)S(1)}, bf16[768,512]{1,0:T(8,128)(2,1)S(1)}, u32[]{:S(2)}, u32[]{:S(2)}) collective-permute-start(bf16[768,512]{1,0:T(8,128)(2,1)S(1)} %collective-permute-done.7.refs_1_), channel_id=1, source_target_pairs={{0,1},{1,0},{2,3},{3,2},{4,5},{5,4},{6,7},{7,6},{8,9},{9,8},{10,11... | collective-permute-start | bytes 2359304 | tf_op jit(solution)/shard_map/ppermute | solution.py:355
  129.4 12.0 %collective-permute-start.18 = (bf16[768,256]{1,0:T(8,128)(2,1)S(1)}, bf16[768,256]{1,0:T(8,128)(2,1)S(1)}, u32[]{:S(2)}, u32[]{:S(2)}) collective-permute-start(bf16[768,256]{1,0:T(8,128)(2,1)S(1)} %slice.29), channel_id=1, source_target_pairs={{4,0},{8,4},{12,8},{14,12},{10,14},{6,10},{2,6},{0,2},{5,1},{9,5},... | collective-permute-start | bytes 1179656 | tf_op jit(solution)/shard_map/ppermute | solution.py:363
  131.2 19.0 %collective-permute-start.23 = (bf16[768,512]{1,0:T(8,128)(2,1)S(1)}, bf16[768,512]{1,0:T(8,128)(2,1)S(1)}, u32[]{:S(2)}, u32[]{:S(2)}) collective-permute-start(bf16[768,512]{1,0:T(8,128)(2,1)S(1)} %collective-permute-done.22.refs_0_), channel_id=1, source_target_pairs={{0,1},{1,0},{2,3},{3,2},{4,5},{5,4},{6,7},{7,6},{8,9},{9,8},{10,11... | collective-permute-start | bytes 2359304 | tf_op jit(solution)/shard_map/ppermute | solution.py:355
  131.8 19.8 %collective-permute-start.27 = (bf16[768,512]{1,0:T(8,128)(2,1)S(1)}, bf16[768,512]{1,0:T(8,128)(2,1)S(1)}, u32[]{:S(2)}, u32[]{:S(2)}) collective-permute-start(bf16[768,512]{1,0:T(8,128)(2,1)S(1)} %collective-permute-done.26.refs_1_), channel_id=1, source_target_pairs={{0,1},{1,0},{2,3},{3,2},{4,5},{5,4},{6,7},{7,6},{8,9},{9,8},{10,11... | collective-permute-start | bytes 2359304 | tf_op jit(solution)/shard_map/ppermute | solution.py:355
  141.4 10.3 %collective-permute-start.17 = (bf16[768,256]{1,0:T(8,128)(2,1)S(1)}, bf16[768,256]{1,0:T(8,128)(2,1)S(1)}, u32[]{:S(2)}, u32[]{:S(2)}) collective-permute-start(bf16[768,256]{1,0:T(8,128)(2,1)S(1)} %collective-permute-done.16.refs_0_), channel_id=1, source_target_pairs={{0,1},{1,0},{2,3},{3,2},{4,5},{5,4},{6,7},{7,6},{8,9},{9,8},{10,11... | collective-permute-start | bytes 1179656 | tf_op jit(solution)/shard_map/ppermute | solution.py:355
  145.0 9.1 %collective-permute-start.19 = (bf16[768,256]{1,0:T(8,128)(2,1)S(1)}, bf16[768,256]{1,0:T(8,128)(2,1)S(1)}, u32[]{:S(2)}, u32[]{:S(2)}) collective-permute-start(bf16[768,256]{1,0:T(8,128)(2,1)S(1)} %collective-permute-done.18.refs_1_), channel_id=1, source_target_pairs={{0,1},{1,0},{2,3},{3,2},{4,5},{5,4},{6,7},{7,6},{8,9},{9,8},{10,11... | collective-permute-start | bytes 1179656 | tf_op jit(solution)/shard_map/ppermute | solution.py:355
  148.0 7.6 %collective-permute-start.13 = (bf16[768,128]{1,0:T(8,128)(2,1)S(1)}, bf16[768,128]{1,0:T(8,128)(2,1)S(1)}, u32[]{:S(2)}, u32[]{:S(2)}) collective-permute-start(bf16[768,128]{1,0:T(8,128)(2,1)S(1)} %collective-permute-done.12.refs_0_), channel_id=1, source_target_pairs={{0,1},{1,0},{2,3},{3,2},{4,5},{5,4},{6,7},{7,6},{8,9},{9,8},{10,11... | collective-permute-start | bytes 589832 | tf_op jit(solution)/shard_map/ppermute | solution.py:355
  150.1 5.4 %collective-permute-start.15 = (bf16[768,128]{1,0:T(8,128)(2,1)S(1)}, bf16[768,128]{1,0:T(8,128)(2,1)S(1)}, u32[]{:S(2)}, u32[]{:S(2)}) collective-permute-start(bf16[768,128]{1,0:T(8,128)(2,1)S(1)} %collective-permute-done.14.refs_1_), channel_id=1, source_target_pairs={{0,1},{1,0},{2,3},{3,2},{4,5},{5,4},{6,7},{7,6},{8,9},{9,8},{10,11... | collective-permute-start | bytes 589832 | tf_op jit(solution)/shard_map/ppermute | solution.py:355
  151.6 5.0 %collective-permute-start.4 = (bf16[768,128]{1,0:T(8,128)(2,1)S(1)}, bf16[768,128]{1,0:T(8,128)(2,1)S(1)}, u32[]{:S(2)}, u32[]{:S(2)}) collective-permute-start(bf16[768,128]{1,0:T(8,128)(2,1)S(1)} %collective-permute-done.3.refs_0_), channel_id=1, source_target_pairs={{0,1},{1,0},{2,3},{3,2},{4,5},{5,4},{6,7},{7,6},{8,9},{9,8},{10,11... | collective-permute-start | bytes 589832 | tf_op jit(solution)/shard_map/ppermute | solution.py:355
  151.7 4.9 %collective-permute-start.9 = (bf16[768,128]{1,0:T(8,128)(2,1)S(1)}, bf16[768,128]{1,0:T(8,128)(2,1)S(1)}, u32[]{:S(2)}, u32[]{:S(2)}) collective-permute-start(bf16[768,128]{1,0:T(8,128)(2,1)S(1)} %collective-permute-done.8.refs_1_), channel_id=1, source_target_pairs={{0,1},{1,0},{2,3},{3,2},{4,5},{5,4},{6,7},{7,6},{8,9},{9,8},{10,11... | collective-permute-start | bytes 589832 | tf_op jit(solution)/shard_map/ppermute | solution.py:355

commit v6 on v5

--- a/solution.py
+++ b/solution.py
@@ -11,7 +11,7 @@
 
 LANES = 128
 GRANT = 16 * 2**20
-LAST_HOPS = 3
+LAST_HOPS = 2
 
 
 def weights(minutes):
@@ -103,9 +103,10 @@
     copies = []
     row_copy = pltpu.make_async_copy(weight, row, row_sem)
     row_copy.start()
+    rows = returns.shape[0] // sem.shape[0]
     for k in range(sem.shape[0]):
-        at = slice(k * 2 * LANES, (k + 1) * 2 * LANES)
-        copies.append(pltpu.make_async_copy(returns.at[:, at], box.at[:, at], sem.at[k]))
+        at = slice(k * rows, (k + 1) * rows)
+        copies.append(pltpu.make_async_copy(returns.at[at], box.at[at], sem.at[k]))
         copies[-1].start()
     row_copy.wait()
     for k in range(row.shape[0]):
@@ -114,10 +115,11 @@
         ).T
     for k, copy in enumerate(copies):
         copy.wait()
-        for lane in range(k * 2 * LANES, (k + 1) * 2 * LANES, LANES):
+        at = slice(k * rows, (k + 1) * rows)
+        for lane in range(0, returns.shape[1], LANES):
             part, start = parts[lane // width], lane % width
-            part[:, start : start + LANES] = (
-                box[:, lane : lane + LANES].astype(jnp.float32) * wide[...]
+            part[at, start : start + LANES] = (
+                box[at, lane : lane + LANES].astype(jnp.float32) * wide[at]
             ).astype(jnp.bfloat16)
 
 
@@ -134,7 +136,7 @@
             pltpu.VMEM((minutes, width), jnp.bfloat16),
             pltpu.VMEM(weight.shape, weight.dtype),
             pltpu.VMEM((minutes, LANES), jnp.float32),
-            pltpu.SemaphoreType.DMA((width // (2 * LANES),)),
+            pltpu.SemaphoreType.DMA((max(1, minutes // (2 * LANES)),)),
             pltpu.SemaphoreType.DMA,
         ],
         compiler_params=pltpu.CompilerParams(vmem_limit_bytes=GRANT),
@@ -334,9 +336,106 @@
     return finish
 
 
-def last_cuts(half):
-    rest = [half // 2**k for k in range(1, LAST_HOPS)]
-    return (*rest, rest[-1])
+def early_kernel(count, rows, factor, *refs):
+    other, left, base, out = refs[:count], *refs[count:]
+    _, earlier = decay(factor)
+
+    @pl.loop(0, out.shape[1] // rows)
+    def _(i):
+        at = pl.ds(pl.multiple_of(i * rows, rows), rows)
+
+        @pl.when(earlier)
+        def _():
+            for k, product in enumerate(products(left, other, at)):
+                out[k, at] = base[k, at] + factor * product
+
+        @pl.when(jnp.logical_not(earlier))
+        def _():
+            for k in range(count):
+                out[k, at] = base[k, at]
+
+
+def final_kernel(where, rows, factor, *refs):
+    count = len(where)
+    choices = refs[:count], refs[count : 2 * count]
+    left, base = refs[2 * count : 2 * count + 2]
+    out, box, sem = refs[-3:]
+    height, width = box.shape[1:]
+    _, earlier = decay(factor)
+
+    def flush(k, i):
+        at = pl.ds(i * rows, rows)
+        return pltpu.make_async_copy(
+            box.at[k, at], out.at[0, at, columns_of(where, k, width)], sem.at[k, i]
+        )
+
+    @pl.loop(0, height // rows)
+    def _(i):
+        at = pl.ds(pl.multiple_of(i * rows, rows), rows)
+        for own, mine in zip(choices, (jnp.logical_not(earlier), earlier), strict=True):
+
+            @pl.when(mine)
+            def _():
+                for k, product in enumerate(products(left, own, at)):
+                    box[k, at] = base[k, at] + product
+                    flush(k, i).start()
+
+    for i in range(height // rows):
+        for k in range(count):
+            flush(k, i).wait()
+
+
+def last_calls(where, left_own, left_other, prior, rows, factor):
+    count = len(where)
+    height, total = prior.shape
+    near = pl.BlockSpec(memory_space=pltpu.VMEM)
+    far = pl.BlockSpec(memory_space=pltpu.HBM)
+    grant = pltpu.CompilerParams(vmem_limit_bytes=GRANT)
+    width = total // lax.axis_size("assets") // 2 // LAST_HOPS
+    small = pltpu.VMEM((count, height, width), jnp.float32)
+    size = 4 * count * height * width
+    flops = 2 * count * left_own.shape[1] * width * height
+
+    def cost(flops, bytes_accessed):
+        return pl.CostEstimate(flops=flops, bytes_accessed=bytes_accessed, transcendentals=0)
+
+    base = pl.pallas_call(
+        functools.partial(decayed_kernel, where, factor),
+        out_shape=small,
+        in_specs=[far],
+        out_specs=near,
+        scratch_shapes=[pltpu.SemaphoreType.DMA((count,))],
+        compiler_params=grant,
+        cost_estimate=cost(size // 4, size),
+    )(prior)
+
+    def early(other):
+        return pl.pallas_call(
+            functools.partial(early_kernel, count, rows, factor),
+            out_shape=small,
+            in_specs=[near] * (count + 2),
+            out_specs=near,
+            compiler_params=grant,
+            cost_estimate=cost(flops, size),
+        )(*other, left_other, base)
+
+    def final(out, first, second, base):
+        args = [*first, *second, left_own, base, out]
+        return pl.pallas_call(
+            functools.partial(final_kernel, where, rows, factor),
+            out_shape=pltpu.HBM(out.shape, out.dtype),
+            in_specs=[near] * (2 * count + 2) + [far],
+            out_specs=far,
+            scratch_shapes=[
+                pltpu.VMEM(small.shape, small.dtype),
+                pltpu.SemaphoreType.DMA((count, height // rows)),
+            ],
+            input_output_aliases={len(args) - 1: 0},
+            compiler_params=grant,
+            cost_estimate=cost(flops, 2 * size),
+        )(*args)
+
+    return early, final
 
 
 def local_ring(returns, prior):
@@ -369,11 +468,9 @@
     for k in range(n - 2):
         flight[k % 2] = hop(flight[k % 2])
         arrived.append((flight[k % 2], k // 2 + 1, (k % 2, 1 - k % 2), 0))
-    start = 0
-    for part in last_cuts(half):
-        cut = slice(start, start + part)
-        arrived.append((hop([f[:, cut] for f in flight[0]]), n // 2, (0, 1), start))
-        start = start + part
+    cut = half // LAST_HOPS
+    parts = [f[:, :cut] for f in flight[0]]
+    arrived.append((hop(parts), n // 2, (0, 1), 0))
 
     own_other = swap(halves)
     left_own = turn_call(halves)
@@ -389,8 +486,23 @@
             for way_step, side in zip((step, -step), sides, strict=True)
         )
         finish = tile_calls(where, pair, *common, k >= n - 2)
-        out = finish(out, swap(pair))
-    return out
+        other = swap(pair)
+        if k == n - 4:
+            crossed = [part[:, cut:] for part in other]
+        out = finish(out, other)
+
+    both = ("assets", "tm")
+    direct = {"p": [], "q": []}
+    for way, pairs in enumerate((forward, backward)):
+        for name, sender in (("p", 1), ("q", 0)):
+            links = [(2 * a + sender, 2 * b + 1) for a, b in pairs]
+            direct[name].append(lax.ppermute(crossed[way], both, links))
+    handed = []
+    for part in direct["p"]:
+        handed.append(lax.ppermute(part, "tm", [(0, 1), (1, 0)]))
+    where = tuple((s, width, side * half + cut) for s, side in ((n // 2, 0), (-(n // 2), 1)))
+    early, final = last_calls(where, *common)
+    return final(out, handed, direct["q"], early(direct["p"]))
 
 
 def solution(mesh):

time: 161 us -> 164 us (1.019)
  the two profiles are of different devices: /device:TPU:0 before, /device:TPU:1 now
where the time goes in v6:
time: 164 us
  waiting for transfers between devices  68.3 us (42%)
  Pallas kernels  57.5 us (35%)
  starting transfers between devices  36.4 us (22%)
    ppermute x14, waiting for transfers between devices, hop(): moved.append(lax.ppermute(parts[way], 'assets', pairs))  68.2 us
    pallas_call x7, Pallas kernels, tile_calls(): pl.pallas_call(functools.partial(own_kernel, where, rows, factor), out_sh...  24 us
    pallas_call x8, Pallas kernels, finish(): pl.pallas_call(functools.partial(other_kernel, where, rows, factor), out_...  23.1 us
    ppermute x14, starting transfers between devices, hop(): moved.append(lax.ppermute(parts[way], 'assets', pairs))  13.2 us
    ppermute x16, starting transfers between devices, swap(): moved.append(lax.ppermute(part, 'tm', [(0, 1), (1, 0)]))  12.3 us
    ppermute x4, starting transfers between devices, local_ring(): direct[name].append(lax.ppermute(crossed[way], both, links))  8.26 us
  transfers between devices with their start and end apart: 36, of which 6 were waited for; matrix products, arithmetic and copies ran while one was open for 0% of the time, Pallas kernels for 33%

profile of v6, /device:TPU:1, one launch (start us, length us, event | category | flops | bytes accessed | tf_op | source)
XLA Modules:
  0.0 163.8 jit_solution(13535585260784785106)
XLA Ops:
  0.0 1.5 shard_map.37
  1.6 0.1 collective-permute-start.14
  1.6 2.8 %collective-permute-start = (bf16[768,512]{1,0:T(8,128)(2,1)S(1)}, bf16[768,512]{1,0:T(8,128)(2,1)S(1)}, u32[]{:S(2)}, u32[]{:S(2)}) collective-permute-start(bf16[768,512]{1,0:T(8,128)(2,1)S(1)} %get-tuple-element.7.refs_0_), channel_id=1, source_target_pairs={{0,4},{4,8},{8,12},{12,14},{14,10},{10,6},{6,2},{2,0},{1,5},{5,9},... | collective-permute-start | bytes 2359304 | tf_op jit(solution)/shard_map/ppermute | solution.py:462
  4.4 1.5 collective-permute-start.20
  5.9 0.9 collective-permute-start.15
  6.8 0.0 collective-permute-done.14.refs_0_
  6.8 0.0 collective-permute-start.24
  6.8 15.4 %collective-permute-done.refs_0_ = bf16[768,512]{1,0:T(8,128)(2,1)S(1)} collective-permute-done((bf16[768,512]{1,0:T(8,128)(2,1)S(1)}, bf16[768,512]{1,0:T(8,128)(2,1)S(1)}, u32[]{:S(2)}, u32[]{:S(2)}) %collective-permute-start) | collective-permute-done | bytes 786464 | tf_op jit(solution)/shard_map/ppermute | solution.py:462
  22.2 0.9 collective-permute-start.34
  23.1 0.1 collective-permute-done.6.refs_1_
  23.2 2.0 %collective-permute-start.35 = (bf16[768,512]{1,0:T(8,128)(2,1)S(1)}, bf16[768,512]{1,0:T(8,128)(2,1)S(1)}, u32[]{:S(2)}, u32[]{:S(2)}) collective-permute-start(bf16[768,512]{1,0:T(8,128)(2,1)S(1)} %collective-permute-done.6.refs_1_), channel_id=1, source_target_pairs={{0,1},{1,0},{2,3},{3,2},{4,5},{5,4},{6,7},{7,6},{8,9},{9,8},{10,11... | collective-permute-start | bytes 2359304 | tf_op jit(solution)/shard_map/ppermute | solution.py:454
  25.2 13.9 %collective-permute-done.20.refs_0_ = bf16[768,512]{1,0:T(8,128)(2,1)S(1)} collective-permute-done((bf16[768,512]{1,0:T(8,128)(2,1)S(1)}, bf16[768,512]{1,0:T(8,128)(2,1)S(1)}, u32[]{:S(2)}, u32[]{:S(2)}) %collective-permute-start.20) | collective-permute-done | bytes 786464 | tf_op jit(solution)/shard_map/ppermute | solution.py:462
  39.0 0.6 collective-permute-start.32
  39.7 1.5 collective-permute-start.1
  41.2 0.0 collective-permute-done.24.refs_1_
  41.2 0.5 collective-permute-start.33
  41.7 1.5 collective-permute-start.21
  43.3 15.5 %collective-permute-done.1.refs_0_ = bf16[768,512]{1,0:T(8,128)(2,1)S(1)} collective-permute-done((bf16[768,512]{1,0:T(8,128)(2,1)S(1)}, bf16[768,512]{1,0:T(8,128)(2,1)S(1)}, u32[]{:S(2)}, u32[]{:S(2)}) %collective-permute-start.1) | collective-permute-done | bytes 786464 | tf_op jit(solution)/shard_map/ppermute | solution.py:462
  58.8 1.3 collective-permute-start.30
  60.1 1.8 %collective-permute-start.31 = (bf16[768,512]{1,0:T(8,128)(2,1)S(1)}, bf16[768,512]{1,0:T(8,128)(2,1)S(1)}, u32[]{:S(2)}, u32[]{:S(2)}) collective-permute-start(bf16[768,512]{1,0:T(8,128)(2,1)S(1)} %collective-permute-done.7.refs_1_), channel_id=1, source_target_pairs={{0,1},{1,0},{2,3},{3,2},{4,5},{5,4},{6,7},{7,6},{8,9},{9,8},{10,11... | collective-permute-start | bytes 2359304 | tf_op jit(solution)/shard_map/ppermute | solution.py:454
  61.9 1.3 collective-permute-start.2
  63.2 12.4 %collective-permute-done.21.refs_0_ = bf16[768,512]{1,0:T(8,128)(2,1)S(1)} collective-permute-done((bf16[768,512]{1,0:T(8,128)(2,1)S(1)}, bf16[768,512]{1,0:T(8,128)(2,1)S(1)}, u32[]{:S(2)}, u32[]{:S(2)}) %collective-permute-start.21) | collective-permute-done | bytes 786464 | tf_op jit(solution)/shard_map/ppermute | solution.py:462
  75.6 1.5 collective-permute-start.8
  77.1 1.6 collective-permute-start.28
  78.7 0.6 collective-permute-start.22
  79.3 0.5 shard_map.38.refs_2_.refs_4_
  79.8 0.9 copy-done.2
  80.7 0.8 collective-permute-start.26
  81.5 10.9 %collective-permute-done.2.refs_0_ = bf16[768,512]{1,0:T(8,128)(2,1)S(1)} collective-permute-done((bf16[768,512]{1,0:T(8,128)(2,1)S(1)}, bf16[768,512]{1,0:T(8,128)(2,1)S(1)}, u32[]{:S(2)}, u32[]{:S(2)}) %collective-permute-start.2) | collective-permute-done | bytes 786464 | tf_op jit(solution)/shard_map/ppermute | solution.py:462
  92.5 1.3 collective-permute-start.3
  93.8 3.4 %shard_map.50.refs_3_ = f32[2,1024,512]{2,1,0:T(8,128)S(1)} custom-call(bf16[768,512]{1,0:T(8,128)(2,1)S(1)} %get-tuple-element.7.refs_0_, bf16[768,512]{1,0:T(8,128)(2,1)S(1)} %get-tuple-element.8.refs_1_, bf16[1024,768]{1,0:T(8,128)(2,1)S(1)} %shard_map.38.refs_2_.refs_4_, f32[1024,8192]{1,0:T(8,128)} %refs_3_.13), custom_call_target="tpu_custom_call" | custom-call | flops 1610612736 | bytes 8388608 | tf_op jit(solution)/shard_map/pallas_call | solution.py:304
  97.2 1.7 %shard_map.42.refs_3_ = f32[2,1024,256]{2,1,0:T(8,128)S(1)} custom-call(f32[1024,8192]{1,0:T(8,128)} %refs_3_.13), custom_call_target="tpu_custom_call" | custom-call | flops 524288 | bytes 2097152 | tf_op jit(solution)/shard_map/pallas_call | solution.py:286
  98.9 1.7 %shard_map.40.refs_3_ = f32[2,1024,256]{2,1,0:T(8,128)S(1)} custom-call(f32[1024,8192]{1,0:T(8,128)} %refs_3_.13), custom_call_target="tpu_custom_call" | custom-call | flops 524288 | bytes 2097152 | tf_op jit(solution)/shard_map/pallas_call | solution.py:402
  100.6 0.1 collective-permute-start.9
  100.7 3.4 %shard_map.49.refs_3_ = f32[2,1024,512]{2,1,0:T(8,128)S(1)} custom-call(bf16[768,512]{1,0:T(8,128)(2,1)S(1)} %collective-permute-done.refs_0_, bf16[768,512]{1,0:T(8,128)(2,1)S(1)} %collective-permute-done.6.refs_1_, bf16[1024,768]{1,0:T(8,128)(2,1)S(1)} %shard_map.38.refs_2_.refs_4_, f32[1024,8192]{1,0:T(8,128)} %refs_3_.13), custom_call_target="tpu_custom_call" | custom-call | flops 1610612736 | bytes 8388608 | tf_op jit(solution)/shard_map/pallas_call | solution.py:304
  104.1 0.5 shard_map.39.refs_2_
  104.6 3.4 %shard_map.48.refs_3_ = f32[2,1024,512]{2,1,0:T(8,128)S(1)} custom-call(bf16[768,512]{1,0:T(8,128)(2,1)S(1)} %collective-permute-done.20.refs_0_, bf16[768,512]{1,0:T(8,128)(2,1)S(1)} %collective-permute-done.24.refs_1_, bf16[1024,768]{1,0:T(8,128)(2,1)S(1)} %shard_map.38.refs_2_.refs_4_, f32[1024,8192]{1,0:T(8,128)} %refs_3_.13), custom_call_target="tpu_custom_call" | custom-call | flops 1610612736 | bytes 8388608 | tf_op jit(solution)/shard_map/pallas_call | solution.py:304
  108.0 0.5 collective-permute-start.29
  108.6 3.0 %shard_map.51.refs_4_ = f32[1,1024,8192]{2,1,0:T(8,128)} custom-call(bf16[768,512]{1,0:T(8,128)(2,1)S(1)} %collective-permute-done.14.refs_0_, bf16[768,512]{1,0:T(8,128)(2,1)S(1)} %collective-permute-done.15.refs_1_, bf16[1024,768]{1,0:T(8,128)(2,1)S(1)} %shard_map.39.refs_2_, f32[2,1024,512]{2,1,0:T(8,128)S(1)} %shard_map.50.refs_3_), custom_call_target="tpu_custom_call" | custom-call | flops 1610612736 | bytes 8388608 | tf_op jit(solution)/shard_map/pallas_call | solution.py:322
  111.5 3.4 %shard_map.47.refs_3_ = f32[2,1024,512]{2,1,0:T(8,128)S(1)} custom-call(bf16[768,512]{1,0:T(8,128)(2,1)S(1)} %collective-permute-done.1.refs_0_, bf16[768,512]{1,0:T(8,128)(2,1)S(1)} %collective-permute-done.7.refs_1_, bf16[1024,768]{1,0:T(8,128)(2,1)S(1)} %shard_map.38.refs_2_.refs_4_, f32[1024,8192]{1,0:T(8,128)} %refs_3_.13), custom_call_target="tpu_custom_call" | custom-call | flops 1610612736 | bytes 8388608 | tf_op jit(solution)/shard_map/pallas_call | solution.py:304
  115.0 0.1 collective-permute-start.23
  115.1 3.4 %shard_map.46.refs_3_ = f32[2,1024,512]{2,1,0:T(8,128)S(1)} custom-call(bf16[768,512]{1,0:T(8,128)(2,1)S(1)} %collective-permute-done.21.refs_0_, bf16[768,512]{1,0:T(8,128)(2,1)S(1)} %collective-permute-done.25.refs_1_, bf16[1024,768]{1,0:T(8,128)(2,1)S(1)} %shard_map.38.refs_2_.refs_4_, f32[1024,8192]{1,0:T(8,128)} %refs_3_.13), custom_call_target="tpu_custom_call" | custom-call | flops 1610612736 | bytes 8388608 | tf_op jit(solution)/shard_map/pallas_call | solution.py:304
  118.6 1.6 collective-permute-start.16
  120.2 3.0 %shard_map.52.refs_4_ = f32[1,1024,8192]{2,1,0:T(8,128)} custom-call(bf16[768,512]{1,0:T(8,128)(2,1)S(1)} %collective-permute-done.34.refs_0_, bf16[768,512]{1,0:T(8,128)(2,1)S(1)} %collective-permute-done.35.refs_1_, bf16[1024,768]{1,0:T(8,128)(2,1)S(1)} %shard_map.39.refs_2_, ...), custom_call_target="tpu_custom_call", output_to_operand_aliasing={{}: (4, {})} | custom-call | flops 1610612736 | bytes 8388608 | tf_op jit(solution)/shard_map/pallas_call | solution.py:322
  123.2 0.1 collective-permute-start.27
  123.3 3.0 %shard_map.53.refs_4_ = f32[1,1024,8192]{2,1,0:T(8,128)} custom-call(bf16[768,512]{1,0:T(8,128)(2,1)S(1)} %collective-permute-done.32.refs_0_, bf16[768,512]{1,0:T(8,128)(2,1)S(1)} %collective-permute-done.33.refs_1_, bf16[1024,768]{1,0:T(8,128)(2,1)S(1)} %shard_map.39.refs_2_, ...), custom_call_target="tpu_custom_call", output_to_operand_aliasing={{}: (4, {})} | custom-call | flops 1610612736 | bytes 8388608 | tf_op jit(solution)/shard_map/pallas_call | solution.py:322
  126.3 3.4 %shard_map.45.refs_3_ = f32[2,1024,512]{2,1,0:T(8,128)S(1)} custom-call(bf16[768,512]{1,0:T(8,128)(2,1)S(1)} %collective-permute-done.2.refs_0_, bf16[768,512]{1,0:T(8,128)(2,1)S(1)} %collective-permute-done.8.refs_1_, bf16[1024,768]{1,0:T(8,128)(2,1)S(1)} %shard_map.38.refs_2_.refs_4_, f32[1024,8192]{1,0:T(8,128)} %refs_3_.13), custom_call_target="tpu_custom_call" | custom-call | flops 1610612736 | bytes 8388608 | tf_op jit(solution)/shard_map/pallas_call | solution.py:304
  129.8 0.4 collective-permute-start.17
  130.2 3.5 %collective-permute-start.10 = (bf16[768,256]{1,0:T(8,128)(2,1)S(1)}, bf16[768,256]{1,0:T(8,128)(2,1)S(1)}, u32[]{:S(2)}, u32[]{:S(2)}) collective-permute-start(bf16[768,256]{1,0:T(8,128)(2,1)S(1)} %slice.17), channel_id=1, source_target_pairs={{5,1},{9,5},{13,9},{15,13},{11,15},{7,11},{3,7},{1,3},{21,17},{25,... | collective-permute-start | bytes 1179656 | tf_op jit(solution)/shard_map/ppermute | solution.py:499
  133.7 2.2 %collective-permute-start.4 = (bf16[768,256]{1,0:T(8,128)(2,1)S(1)}, bf16[768,256]{1,0:T(8,128)(2,1)S(1)}, u32[]{:S(2)}, u32[]{:S(2)}) collective-permute-start(bf16[768,256]{1,0:T(8,128)(2,1)S(1)} %slice.16), channel_id=1, source_target_pairs={{1,5},{5,9},{9,13},{13,15},{15,11},{11,7},{7,3},{3,1},{17,21},{21,... | collective-permute-start | bytes 1179656 | tf_op jit(solution)/shard_map/ppermute | solution.py:499
  135.9 3.4 %shard_map.44.refs_3_ = f32[2,1024,512]{2,1,0:T(8,128)S(1)} custom-call(bf16[768,512]{1,0:T(8,128)(2,1)S(1)} %collective-permute-done.22.refs_0_, bf16[768,512]{1,0:T(8,128)(2,1)S(1)} %collective-permute-done.26.refs_1_, bf16[1024,768]{1,0:T(8,128)(2,1)S(1)} %shard_map.38.refs_2_.refs_4_, f32[1024,8192]{1,0:T(8,128)} %refs_3_.13), custom_call_target="tpu_custom_call" | custom-call | flops 1610612736 | bytes 8388608 | tf_op jit(solution)/shard_map/pallas_call | solution.py:304
  139.3 3.0 %shard_map.54.refs_4_ = f32[1,1024,8192]{2,1,0:T(8,128)} custom-call(bf16[768,512]{1,0:T(8,128)(2,1)S(1)} %copy-done.1, bf16[768,512]{1,0:T(8,128)(2,1)S(1)} %copy-done.3, bf16[1024,768]{1,0:T(8,128)(2,1)S(1)} %shard_map.39.refs_2_, f32[2,1024,512]{2,1,0:T(8,128)S(1)} %shard_map.47.refs_3_, ...), custom_call_target="tpu_custom_call", output_to_operand_aliasing={{}: (4, {})} | custom-call | flops 1610612736 | bytes 8388608 | tf_op jit(solution)/shard_map/pallas_call | solution.py:322
  142.3 0.1 collective-permute-start.19
  142.4 3.0 %shard_map.55.refs_4_ = f32[1,1024,8192]{2,1,0:T(8,128)} custom-call(bf16[768,512]{1,0:T(8,128)(2,1)S(1)} %collective-permute-done.28.refs_0_, bf16[768,512]{1,0:T(8,128)(2,1)S(1)} %collective-permute-done.29.refs_1_, bf16[1024,768]{1,0:T(8,128)(2,1)S(1)} %shard_map.39.refs_2_, ...), custom_call_target="tpu_custom_call", output_to_operand_aliasing={{}: (4, {})} | custom-call | flops 1610612736 | bytes 8388608 | tf_op jit(solution)/shard_map/pallas_call | solution.py:322
  145.4 1.1 shard_map.43.refs_3_
  146.6 1.3 collective-permute-start.12
  147.9 1.3 collective-permute-start.13
  149.2 2.6 %collective-permute-start.11 = (bf16[768,256]{1,0:T(8,128)(2,1)S(1)}, bf16[768,256]{1,0:T(8,128)(2,1)S(1)}, u32[]{:S(2)}, u32[]{:S(2)}) collective-permute-start(bf16[768,256]{1,0:T(8,128)(2,1)S(1)} %collective-permute-done.10.refs_1_), channel_id=1, source_target_pairs={{0,1},{1,0},{2,3},{3,2},{4,5},{5,4},{6,7},{7,6},{8,9},{9,8},{10,11... | collective-permute-start | bytes 1179656 | tf_op jit(solution)/shard_map/ppermute | solution.py:502
  151.8 0.1 collective-permute-start.5
  151.9 3.0 %shard_map.56.refs_4_ = f32[1,1024,8192]{2,1,0:T(8,128)} custom-call(bf16[768,512]{1,0:T(8,128)(2,1)S(1)} %collective-permute-done.3.refs_0_, bf16[768,512]{1,0:T(8,128)(2,1)S(1)} %collective-permute-done.9.refs_1_, bf16[1024,768]{1,0:T(8,128)(2,1)S(1)} %shard_map.39.refs_2_, f32[2,1024,512]{2,1,0:T(8,128)S(1)} %shard_map.45.refs_3_, ...), custom_call_target="tpu_custom_call", output_to_operand_aliasing={{}: (4, {})} | custom-call | flops 1610612736 | bytes 8388608 | tf_op jit(solution)/shard_map/pallas_call | solution.py:322
  154.8 3.0 %shard_map.57.refs_4_ = f32[1,1024,8192]{2,1,0:T(8,128)} custom-call(bf16[768,512]{1,0:T(8,128)(2,1)S(1)} %collective-permute-done.23.refs_0_, bf16[768,512]{1,0:T(8,128)(2,1)S(1)} %collective-permute-done.27.refs_1_, bf16[1024,768]{1,0:T(8,128)(2,1)S(1)} %shard_map.39.refs_2_, ...), custom_call_target="tpu_custom_call", output_to_operand_aliasing={{}: (4, {})} | custom-call | flops 1610612736 | bytes 8388608 | tf_op jit(solution)/shard_map/pallas_call | solution.py:322
  157.8 2.3 %shard_map.58.refs_6_ = f32[1,1024,8192]{2,1,0:T(8,128)} custom-call(bf16[768,256]{1,0:T(8,128)(2,1)S(1)} %collective-permute-done.17.refs_0_, bf16[768,256]{1,0:T(8,128)(2,1)S(1)} %collective-permute-done.19.refs_1_, bf16[1024,768]{1,0:T(8,128)(2,1)S(1)} %shard_map.39.refs_2_, ...), custom_call_target="tpu_custom_call", output_to_operand_aliasing={{}: (4, {})} | custom-call | flops 805306368 | bytes 4194304 | tf_op jit(solution)/shard_map/pallas_call | solution.py:322
  160.1 1.2 shard_map.41.refs_5_
  161.4 2.3 %shard_map.59 = f32[1,1024,8192]{2,1,0:T(8,128)} custom-call(bf16[768,256]{1,0:T(8,128)(2,1)S(1)} %collective-permute-done.5.refs_0_, bf16[768,256]{1,0:T(8,128)(2,1)S(1)} %collective-permute-done.11.refs_1_, bf16[768,256]{1,0:T(8,128)(2,1)S(1)} %collective-permute-done.12.refs_2_, ...), custom_call_target="tpu_custom_call", output_to_operand_aliasing={{}: (6, {})} | custom-call | flops 805306368 | bytes 4194304 | tf_op jit(solution)/shard_map/pallas_call | solution.py:424
  (43 shorter events, 0.2 us)
Async XLA Ops:
  1.6 5.2 %collective-permute-start.14 = (bf16[768,512]{1,0:T(8,128)(2,1)S(1)}, bf16[768,512]{1,0:T(8,128)(2,1)S(1)}, u32[]{:S(2)}, u32[]{:S(2)}) collective-permute-start(bf16[768,512]{1,0:T(8,128)(2,1)S(1)} %get-tuple-element.7.refs_0_), channel_id=1, source_target_pairs={{0,1},{1,0},{2,3},{3,2},{4,5},{5,4},{6,7},{7,6},{8,9},{9,8},{10,11... | collective-permute-start | bytes 2359304 | tf_op jit(solution)/shard_map/ppermute | solution.py:454
  1.6 20.5 %collective-permute-start = (bf16[768,512]{1,0:T(8,128)(2,1)S(1)}, bf16[768,512]{1,0:T(8,128)(2,1)S(1)}, u32[]{:S(2)}, u32[]{:S(2)}) collective-permute-start(bf16[768,512]{1,0:T(8,128)(2,1)S(1)} %get-tuple-element.7.refs_0_), channel_id=1, source_target_pairs={{0,4},{4,8},{8,12},{12,14},{14,10},{10,6},{6,2},{2,0},{1,5},{5,9},... | collective-permute-start | bytes 2359304 | tf_op jit(solution)/shard_map/ppermute | solution.py:462
  4.4 18.8 %collective-permute-start.6 = (bf16[768,512]{1,0:T(8,128)(2,1)S(1)}, bf16[768,512]{1,0:T(8,128)(2,1)S(1)}, u32[]{:S(2)}, u32[]{:S(2)}) collective-permute-start(bf16[768,512]{1,0:T(8,128)(2,1)S(1)} %get-tuple-element.8.refs_1_), channel_id=1, source_target_pairs={{4,0},{8,4},{12,8},{14,12},{10,14},{6,10},{2,6},{0,2},{5,1},{9,5},... | collective-permute-start | bytes 2359304 | tf_op jit(solution)/shard_map/ppermute | solution.py:462
  4.4 34.6 %collective-permute-start.20 = (bf16[768,512]{1,0:T(8,128)(2,1)S(1)}, bf16[768,512]{1,0:T(8,128)(2,1)S(1)}, u32[]{:S(2)}, u32[]{:S(2)}) collective-permute-start(bf16[768,512]{1,0:T(8,128)(2,1)S(1)} %get-tuple-element.8.refs_1_), channel_id=1, source_target_pairs={{0,4},{4,8},{8,12},{12,14},{14,10},{10,6},{6,2},{2,0},{1,5},{5,9},... | collective-permute-start | bytes 2359304 | tf_op jit(solution)/shard_map/ppermute | solution.py:462
  5.9 33.8 %collective-permute-start.15 = (bf16[768,512]{1,0:T(8,128)(2,1)S(1)}, bf16[768,512]{1,0:T(8,128)(2,1)S(1)}, u32[]{:S(2)}, u32[]{:S(2)}) collective-permute-start(bf16[768,512]{1,0:T(8,128)(2,1)S(1)} %get-tuple-element.8.refs_1_), channel_id=1, source_target_pairs={{0,1},{1,0},{2,3},{3,2},{4,5},{5,4},{6,7},{7,6},{8,9},{9,8},{10,11... | collective-permute-start | bytes 2359304 | tf_op jit(solution)/shard_map/ppermute | solution.py:454
  6.8 34.4 %collective-permute-start.24 = (bf16[768,512]{1,0:T(8,128)(2,1)S(1)}, bf16[768,512]{1,0:T(8,128)(2,1)S(1)}, u32[]{:S(2)}, u32[]{:S(2)}) collective-permute-start(bf16[768,512]{1,0:T(8,128)(2,1)S(1)} %get-tuple-element.7.refs_0_), channel_id=1, source_target_pairs={{4,0},{8,4},{12,8},{14,12},{10,14},{6,10},{2,6},{0,2},{5,1},{9,5},... | collective-permute-start | bytes 2359304 | tf_op jit(solution)/shard_map/ppermute | solution.py:462
  22.2 19.1 %collective-permute-start.34 = (bf16[768,512]{1,0:T(8,128)(2,1)S(1)}, bf16[768,512]{1,0:T(8,128)(2,1)S(1)}, u32[]{:S(2)}, u32[]{:S(2)}) collective-permute-start(bf16[768,512]{1,0:T(8,128)(2,1)S(1)} %collective-permute-done.refs_0_), channel_id=1, source_target_pairs={{0,1},{1,0},{2,3},{3,2},{4,5},{5,4},{6,7},{7,6},{8,9},{9,8},{10,11... | collective-permute-start | bytes 2359304 | tf_op jit(solution)/shard_map/ppermute | solution.py:454
  23.2 18.6 %collective-permute-start.35 = (bf16[768,512]{1,0:T(8,128)(2,1)S(1)}, bf16[768,512]{1,0:T(8,128)(2,1)S(1)}, u32[]{:S(2)}, u32[]{:S(2)}) collective-permute-start(bf16[768,512]{1,0:T(8,128)(2,1)S(1)} %collective-permute-done.6.refs_1_), channel_id=1, source_target_pairs={{0,1},{1,0},{2,3},{3,2},{4,5},{5,4},{6,7},{7,6},{8,9},{9,8},{10,11... | collective-permute-start | bytes 2359304 | tf_op jit(solution)/shard_map/ppermute | solution.py:454
  39.0 4.2 %collective-permute-start.32 = (bf16[768,512]{1,0:T(8,128)(2,1)S(1)}, bf16[768,512]{1,0:T(8,128)(2,1)S(1)}, u32[]{:S(2)}, u32[]{:S(2)}) collective-permute-start(bf16[768,512]{1,0:T(8,128)(2,1)S(1)} %collective-permute-done.20.refs_0_), channel_id=1, source_target_pairs={{0,1},{1,0},{2,3},{3,2},{4,5},{5,4},{6,7},{7,6},{8,9},{9,8},{10,11... | collective-permute-start | bytes 2359304 | tf_op jit(solution)/shard_map/ppermute | solution.py:454
  39.7 19.1 %collective-permute-start.1 = (bf16[768,512]{1,0:T(8,128)(2,1)S(1)}, bf16[768,512]{1,0:T(8,128)(2,1)S(1)}, u32[]{:S(2)}, u32[]{:S(2)}) collective-permute-start(bf16[768,512]{1,0:T(8,128)(2,1)S(1)} %collective-permute-done.refs_0_), channel_id=1, source_target_pairs={{0,4},{4,8},{8,12},{12,14},{14,10},{10,6},{6,2},{2,0},{1,5},{5,9},... | collective-permute-start | bytes 2359304 | tf_op jit(solution)/shard_map/ppermute | solution.py:462
  41.2 18.9 %collective-permute-start.7 = (bf16[768,512]{1,0:T(8,128)(2,1)S(1)}, bf16[768,512]{1,0:T(8,128)(2,1)S(1)}, u32[]{:S(2)}, u32[]{:S(2)}) collective-permute-start(bf16[768,512]{1,0:T(8,128)(2,1)S(1)} %collective-permute-done.6.refs_1_), channel_id=1, source_target_pairs={{4,0},{8,4},{12,8},{14,12},{10,14},{6,10},{2,6},{0,2},{5,1},{9,5},... | collective-permute-start | bytes 2359304 | tf_op jit(solution)/shard_map/ppermute | solution.py:462
  41.2 20.7 %collective-permute-start.33 = (bf16[768,512]{1,0:T(8,128)(2,1)S(1)}, bf16[768,512]{1,0:T(8,128)(2,1)S(1)}, u32[]{:S(2)}, u32[]{:S(2)}) collective-permute-start(bf16[768,512]{1,0:T(8,128)(2,1)S(1)} %collective-permute-done.24.refs_1_), channel_id=1, source_target_pairs={{0,1},{1,0},{2,3},{3,2},{4,5},{5,4},{6,7},{7,6},{8,9},{9,8},{10,11... | collective-permute-start | bytes 2359304 | tf_op jit(solution)/shard_map/ppermute | solution.py:454
  41.7 33.9 %collective-permute-start.21 = (bf16[768,512]{1,0:T(8,128)(2,1)S(1)}, bf16[768,512]{1,0:T(8,128)(2,1)S(1)}, u32[]{:S(2)}, u32[]{:S(2)}) collective-permute-start(bf16[768,512]{1,0:T(8,128)(2,1)S(1)} %collective-permute-done.20.refs_0_), channel_id=1, source_target_pairs={{0,4},{4,8},{8,12},{12,14},{14,10},{10,6},{6,2},{2,0},{1,5},{5,9},... | collective-permute-start | bytes 2359304 | tf_op jit(solution)/shard_map/ppermute | solution.py:462
  43.3 33.8 %collective-permute-start.25 = (bf16[768,512]{1,0:T(8,128)(2,1)S(1)}, bf16[768,512]{1,0:T(8,128)(2,1)S(1)}, u32[]{:S(2)}, u32[]{:S(2)}) collective-permute-start(bf16[768,512]{1,0:T(8,128)(2,1)S(1)} %collective-permute-done.24.refs_1_), channel_id=1, source_target_pairs={{4,0},{8,4},{12,8},{14,12},{10,14},{6,10},{2,6},{0,2},{5,1},{9,5},... | collective-permute-start | bytes 2359304 | tf_op jit(solution)/shard_map/ppermute | solution.py:462
  58.8 19.9 %collective-permute-start.30 = (bf16[768,512]{1,0:T(8,128)(2,1)S(1)}, bf16[768,512]{1,0:T(8,128)(2,1)S(1)}, u32[]{:S(2)}, u32[]{:S(2)}) collective-permute-start(bf16[768,512]{1,0:T(8,128)(2,1)S(1)} %collective-permute-done.1.refs_0_), channel_id=1, source_target_pairs={{0,1},{1,0},{2,3},{3,2},{4,5},{5,4},{6,7},{7,6},{8,9},{9,8},{10,11... | collective-permute-start | bytes 2359304 | tf_op jit(solution)/shard_map/ppermute | solution.py:454
  60.1 19.7 %collective-permute-start.31 = (bf16[768,512]{1,0:T(8,128)(2,1)S(1)}, bf16[768,512]{1,0:T(8,128)(2,1)S(1)}, u32[]{:S(2)}, u32[]{:S(2)}) collective-permute-start(bf16[768,512]{1,0:T(8,128)(2,1)S(1)} %collective-permute-done.7.refs_1_), channel_id=1, source_target_pairs={{0,1},{1,0},{2,3},{3,2},{4,5},{5,4},{6,7},{7,6},{8,9},{9,8},{10,11... | collective-permute-start | bytes 2359304 | tf_op jit(solution)/shard_map/ppermute | solution.py:454
  61.9 30.5 %collective-permute-start.2 = (bf16[768,512]{1,0:T(8,128)(2,1)S(1)}, bf16[768,512]{1,0:T(8,128)(2,1)S(1)}, u32[]{:S(2)}, u32[]{:S(2)}) collective-permute-start(bf16[768,512]{1,0:T(8,128)(2,1)S(1)} %collective-permute-done.1.refs_0_), channel_id=1, source_target_pairs={{0,4},{4,8},{8,12},{12,14},{14,10},{10,6},{6,2},{2,0},{1,5},{5,9},... | collective-permute-start | bytes 2359304 | tf_op jit(solution)/shard_map/ppermute | solution.py:462
  75.6 24.9 %collective-permute-start.8 = (bf16[768,512]{1,0:T(8,128)(2,1)S(1)}, bf16[768,512]{1,0:T(8,128)(2,1)S(1)}, u32[]{:S(2)}, u32[]{:S(2)}) collective-permute-start(bf16[768,512]{1,0:T(8,128)(2,1)S(1)} %collective-permute-done.7.refs_1_), channel_id=1, source_target_pairs={{4,0},{8,4},{12,8},{14,12},{10,14},{6,10},{2,6},{0,2},{5,1},{9,5},... | collective-permute-start | bytes 2359304 | tf_op jit(solution)/shard_map/ppermute | solution.py:462
  77.1 30.9 %collective-permute-start.28 = (bf16[768,512]{1,0:T(8,128)(2,1)S(1)}, bf16[768,512]{1,0:T(8,128)(2,1)S(1)}, u32[]{:S(2)}, u32[]{:S(2)}) collective-permute-start(bf16[768,512]{1,0:T(8,128)(2,1)S(1)} %collective-permute-done.21.refs_0_), channel_id=1, source_target_pairs={{0,1},{1,0},{2,3},{3,2},{4,5},{5,4},{6,7},{7,6},{8,9},{9,8},{10,11... | collective-permute-start | bytes 2359304 | tf_op jit(solution)/shard_map/ppermute | solution.py:454
  78.7 18.5 %copy-start = (bf16[768,512]{1,0:T(8,128)(2,1)}, bf16[768,512]{1,0:T(8,128)(2,1)S(1)}, u32[]{:S(2)}) copy-start(bf16[768,512]{1,0:T(8,128)(2,1)S(1)} %collective-permute-done.30.refs_0_) | copy-start | bytes 2359300
  78.7 36.3 %collective-permute-start.22 = (bf16[768,512]{1,0:T(8,128)(2,1)S(1)}, bf16[768,512]{1,0:T(8,128)(2,1)S(1)}, u32[]{:S(2)}, u32[]{:S(2)}) collective-permute-start(bf16[768,512]{1,0:T(8,128)(2,1)S(1)} %collective-permute-done.21.refs_0_), channel_id=1, source_target_pairs={{0,4},{4,8},{8,12},{12,14},{14,10},{10,6},{6,2},{2,0},{1,5},{5,9},... | collective-permute-start | bytes 2359304 | tf_op jit(solution)/shard_map/ppermute | solution.py:462
  79.8 0.9 copy-start.2
  80.7 37.9 %collective-permute-start.26 = (bf16[768,512]{1,0:T(8,128)(2,1)S(1)}, bf16[768,512]{1,0:T(8,128)(2,1)S(1)}, u32[]{:S(2)}, u32[]{:S(2)}) collective-permute-start(bf16[768,512]{1,0:T(8,128)(2,1)S(1)} %collective-permute-done.25.refs_1_), channel_id=1, source_target_pairs={{4,0},{8,4},{12,8},{14,12},{10,14},{6,10},{2,6},{0,2},{5,1},{9,5},... | collective-permute-start | bytes 2359304 | tf_op jit(solution)/shard_map/ppermute | solution.py:462
  92.5 27.7 %collective-permute-start.3 = (bf16[768,512]{1,0:T(8,128)(2,1)S(1)}, bf16[768,512]{1,0:T(8,128)(2,1)S(1)}, u32[]{:S(2)}, u32[]{:S(2)}) collective-permute-start(bf16[768,512]{1,0:T(8,128)(2,1)S(1)} %collective-permute-done.2.refs_0_), channel_id=1, source_target_pairs={{0,1},{1,0},{2,3},{3,2},{4,5},{5,4},{6,7},{7,6},{8,9},{9,8},{10,11... | collective-permute-start | bytes 2359304 | tf_op jit(solution)/shard_map/ppermute | solution.py:454
  100.6 22.6 %collective-permute-start.9 = (bf16[768,512]{1,0:T(8,128)(2,1)S(1)}, bf16[768,512]{1,0:T(8,128)(2,1)S(1)}, u32[]{:S(2)}, u32[]{:S(2)}) collective-permute-start(bf16[768,512]{1,0:T(8,128)(2,1)S(1)} %collective-permute-done.8.refs_1_), channel_id=1, source_target_pairs={{0,1},{1,0},{2,3},{3,2},{4,5},{5,4},{6,7},{7,6},{8,9},{9,8},{10,11... | collective-permute-start | bytes 2359304 | tf_op jit(solution)/shard_map/ppermute | solution.py:454
  108.0 22.2 %collective-permute-start.29 = (bf16[768,512]{1,0:T(8,128)(2,1)S(1)}, bf16[768,512]{1,0:T(8,128)(2,1)S(1)}, u32[]{:S(2)}, u32[]{:S(2)}) collective-permute-start(bf16[768,512]{1,0:T(8,128)(2,1)S(1)} %collective-permute-done.25.refs_1_), channel_id=1, source_target_pairs={{0,1},{1,0},{2,3},{3,2},{4,5},{5,4},{6,7},{7,6},{8,9},{9,8},{10,11... | collective-permute-start | bytes 2359304 | tf_op jit(solution)/shard_map/ppermute | solution.py:454
  115.0 27.4 %collective-permute-start.23 = (bf16[768,512]{1,0:T(8,128)(2,1)S(1)}, bf16[768,512]{1,0:T(8,128)(2,1)S(1)}, u32[]{:S(2)}, u32[]{:S(2)}) collective-permute-start(bf16[768,512]{1,0:T(8,128)(2,1)S(1)} %collective-permute-done.22.refs_0_), channel_id=1, source_target_pairs={{0,1},{1,0},{2,3},{3,2},{4,5},{5,4},{6,7},{7,6},{8,9},{9,8},{10,11... | collective-permute-start | bytes 2359304 | tf_op jit(solution)/shard_map/ppermute | solution.py:454
  118.6 11.2 %collective-permute-start.16 = (bf16[768,256]{1,0:T(8,128)(2,1)S(1)}, bf16[768,256]{1,0:T(8,128)(2,1)S(1)}, u32[]{:S(2)}, u32[]{:S(2)}) collective-permute-start(bf16[768,256]{1,0:T(8,128)(2,1)S(1)} %slice.18), channel_id=1, source_target_pairs={{0,4},{4,8},{8,12},{12,14},{14,10},{10,6},{6,2},{2,0},{1,5},{5,9},... | collective-permute-start | bytes 1179656 | tf_op jit(solution)/shard_map/ppermute | solution.py:462
  120.2 13.5 %collective-permute-start.18 = (bf16[768,256]{1,0:T(8,128)(2,1)S(1)}, bf16[768,256]{1,0:T(8,128)(2,1)S(1)}, u32[]{:S(2)}, u32[]{:S(2)}) collective-permute-start(bf16[768,256]{1,0:T(8,128)(2,1)S(1)} %slice.19), channel_id=1, source_target_pairs={{4,0},{8,4},{12,8},{14,12},{10,14},{6,10},{2,6},{0,2},{5,1},{9,5},... | collective-permute-start | bytes 1179656 | tf_op jit(solution)/shard_map/ppermute | solution.py:462
  123.2 23.4 %collective-permute-start.27 = (bf16[768,512]{1,0:T(8,128)(2,1)S(1)}, bf16[768,512]{1,0:T(8,128)(2,1)S(1)}, u32[]{:S(2)}, u32[]{:S(2)}) collective-permute-start(bf16[768,512]{1,0:T(8,128)(2,1)S(1)} %collective-permute-done.26.refs_1_), channel_id=1, source_target_pairs={{0,1},{1,0},{2,3},{3,2},{4,5},{5,4},{6,7},{7,6},{8,9},{9,8},{10,11... | collective-permute-start | bytes 2359304 | tf_op jit(solution)/shard_map/ppermute | solution.py:454
  129.8 9.6 %copy-start.1 = (bf16[768,512]{1,0:T(8,128)(2,1)S(1)}, bf16[768,512]{1,0:T(8,128)(2,1)}, u32[]{:S(2)}) copy-start(bf16[768,512]{1,0:T(8,128)(2,1)} %copy-done) | copy-start | bytes 2359300
  129.8 9.6 %copy-start.3 = (bf16[768,512]{1,0:T(8,128)(2,1)S(1)}, bf16[768,512]{1,0:T(8,128)(2,1)}, u32[]{:S(2)}) copy-start(bf16[768,512]{1,0:T(8,128)(2,1)} %copy-done.2) | copy-start | bytes 2359300
  129.8 18.1 %collective-permute-start.17 = (bf16[768,256]{1,0:T(8,128)(2,1)S(1)}, bf16[768,256]{1,0:T(8,128)(2,1)S(1)}, u32[]{:S(2)}, u32[]{:S(2)}) collective-permute-start(bf16[768,256]{1,0:T(8,128)(2,1)S(1)} %collective-permute-done.16.refs_0_), channel_id=1, source_target_pairs={{0,1},{1,0},{2,3},{3,2},{4,5},{5,4},{6,7},{7,6},{8,9},{9,8},{10,11... | collective-permute-start | bytes 1179656 | tf_op jit(solution)/shard_map/ppermute | solution.py:454
  130.2 19.0 %collective-permute-start.10 = (bf16[768,256]{1,0:T(8,128)(2,1)S(1)}, bf16[768,256]{1,0:T(8,128)(2,1)S(1)}, u32[]{:S(2)}, u32[]{:S(2)}) collective-permute-start(bf16[768,256]{1,0:T(8,128)(2,1)S(1)} %slice.17), channel_id=1, source_target_pairs={{5,1},{9,5},{13,9},{15,13},{11,15},{7,11},{3,7},{1,3},{21,17},{25,... | collective-permute-start | bytes 1179656 | tf_op jit(solution)/shard_map/ppermute | solution.py:499
  133.7 18.1 %collective-permute-start.4 = (bf16[768,256]{1,0:T(8,128)(2,1)S(1)}, bf16[768,256]{1,0:T(8,128)(2,1)S(1)}, u32[]{:S(2)}, u32[]{:S(2)}) collective-permute-start(bf16[768,256]{1,0:T(8,128)(2,1)S(1)} %slice.16), channel_id=1, source_target_pairs={{1,5},{5,9},{9,13},{13,15},{15,11},{11,7},{7,3},{3,1},{17,21},{21,... | collective-permute-start | bytes 1179656 | tf_op jit(solution)/shard_map/ppermute | solution.py:499
  142.3 15.5 %collective-permute-start.19 = (bf16[768,256]{1,0:T(8,128)(2,1)S(1)}, bf16[768,256]{1,0:T(8,128)(2,1)S(1)}, u32[]{:S(2)}, u32[]{:S(2)}) collective-permute-start(bf16[768,256]{1,0:T(8,128)(2,1)S(1)} %collective-permute-done.18.refs_1_), channel_id=1, source_target_pairs={{0,1},{1,0},{2,3},{3,2},{4,5},{5,4},{6,7},{7,6},{8,9},{9,8},{10,11... | collective-permute-start | bytes 1179656 | tf_op jit(solution)/shard_map/ppermute | solution.py:454
  146.6 14.7 %collective-permute-start.12 = (bf16[768,256]{1,0:T(8,128)(2,1)S(1)}, bf16[768,256]{1,0:T(8,128)(2,1)S(1)}, u32[]{:S(2)}, u32[]{:S(2)}) collective-permute-start(bf16[768,256]{1,0:T(8,128)(2,1)S(1)} %slice.16), channel_id=1, source_target_pairs={{0,5},{4,9},{8,13},{12,15},{14,11},{10,7},{6,3},{2,1},{16,21},{20,... | collective-permute-start | bytes 1179656 | tf_op jit(solution)/shard_map/ppermute | solution.py:499
  147.9 13.4 %collective-permute-start.13 = (bf16[768,256]{1,0:T(8,128)(2,1)S(1)}, bf16[768,256]{1,0:T(8,128)(2,1)S(1)}, u32[]{:S(2)}, u32[]{:S(2)}) collective-permute-start(bf16[768,256]{1,0:T(8,128)(2,1)S(1)} %slice.17), channel_id=1, source_target_pairs={{4,1},{8,5},{12,9},{14,13},{10,15},{6,11},{2,7},{0,3},{20,17},{24,... | collective-permute-start | bytes 1179656 | tf_op jit(solution)/shard_map/ppermute | solution.py:499
  149.2 12.1 %collective-permute-start.11 = (bf16[768,256]{1,0:T(8,128)(2,1)S(1)}, bf16[768,256]{1,0:T(8,128)(2,1)S(1)}, u32[]{:S(2)}, u32[]{:S(2)}) collective-permute-start(bf16[768,256]{1,0:T(8,128)(2,1)S(1)} %collective-permute-done.10.refs_1_), channel_id=1, source_target_pairs={{0,1},{1,0},{2,3},{3,2},{4,5},{5,4},{6,7},{7,6},{8,9},{9,8},{10,11... | collective-permute-start | bytes 1179656 | tf_op jit(solution)/shard_map/ppermute | solution.py:502
  151.8 9.6 %collective-permute-start.5 = (bf16[768,256]{1,0:T(8,128)(2,1)S(1)}, bf16[768,256]{1,0:T(8,128)(2,1)S(1)}, u32[]{:S(2)}, u32[]{:S(2)}) collective-permute-start(bf16[768,256]{1,0:T(8,128)(2,1)S(1)} %collective-permute-done.4.refs_0_), channel_id=1, source_target_pairs={{0,1},{1,0},{2,3},{3,2},{4,5},{5,4},{6,7},{7,6},{8,9},{9,8},{10,11... | collective-permute-start | bytes 1179656 | tf_op jit(solution)/shard_map/ppermute | solution.py:502

commit v7 on v6

--- a/solution.py
+++ b/solution.py
@@ -336,53 +336,83 @@
     return finish
 
 
-def early_kernel(count, rows, factor, *refs):
-    other, left, base, out = refs[:count], *refs[count:]
+def pick_kernel(first, second, out):
+    for source, mine in ((first, 0), (second, 1)):
+
+        @pl.when(lax.axis_index("tm") == mine)
+        def _():
+            out[...] = source[...]
+
+
+def pick_call(first, second):
+    near = pl.BlockSpec(memory_space=pltpu.VMEM)
+    return pl.pallas_call(
+        pick_kernel,
+        out_shape=pltpu.VMEM(first.shape, first.dtype),
+        in_specs=[near] * 2,
+        out_specs=near,
+        compiler_params=pltpu.CompilerParams(vmem_limit_bytes=GRANT),
+        cost_estimate=pl.CostEstimate(
+            flops=0, bytes_accessed=4 * first.size, transcendentals=0
+        ),
+    )(first, second)
+
+
+def early_kernel(rows, factor, mixed, straight, left_own, left_other, base, out):
     _, earlier = decay(factor)
 
     @pl.loop(0, out.shape[1] // rows)
     def _(i):
         at = pl.ds(pl.multiple_of(i * rows, rows), rows)
 
+        def times(left, part):
+            return jnp.dot(left[at], part[...], preferred_element_type=jnp.float32)
+
         @pl.when(earlier)
         def _():
-            for k, product in enumerate(products(left, other, at)):
-                out[k, at] = base[k, at] + factor * product
+            out[0, at] = base[0, at] + times(left_own, straight)
+            out[1, at] = base[1, at] + factor * times(left_other, mixed)
 
         @pl.when(jnp.logical_not(earlier))
         def _():
-            for k in range(count):
-                out[k, at] = base[k, at]
-
-
-def final_kernel(where, rows, factor, *refs):
-    count = len(where)
-    choices = refs[:count], refs[count : 2 * count]
-    left, base = refs[2 * count : 2 * count + 2]
-    out, box, sem = refs[-3:]
+            out[0, at] = base[0, at] + times(left_own, mixed)
+            out[1, at] = base[1, at]
+
+
+def final_kernel(where, rows, factor, handed, straight, left_own, left_other, base, _, *refs):
+    out, box, sem = refs
     height, width = box.shape[1:]
-    _, earlier = decay(factor)
-
-    def flush(k, i):
+    count, (_, earlier) = len(where), decay(factor)
+
+    def flush(source, k, i):
         at = pl.ds(i * rows, rows)
         return pltpu.make_async_copy(
-            box.at[k, at], out.at[0, at, columns_of(where, k, width)], sem.at[k, i]
+            source.at[k, at], out.at[0, at, columns_of(where, k, width)], sem.at[k, i]
         )
 
     @pl.loop(0, height // rows)
     def _(i):
         at = pl.ds(pl.multiple_of(i * rows, rows), rows)
-        for own, mine in zip(choices, (jnp.logical_not(earlier), earlier), strict=True):
-
-            @pl.when(mine)
-            def _():
-                for k, product in enumerate(products(left, own, at)):
-                    box[k, at] = base[k, at] + product
-                    flush(k, i).start()
+
+        def times(left, part):
+            return jnp.dot(left[at], part[...], preferred_element_type=jnp.float32)
+
+        @pl.when(earlier)
+        def _():
+            box[0, at] = base[0, at] + factor * times(left_other, handed)
+            flush(box, 0, i).start()
+            box[1, at] = base[1, at] + times(left_own, straight)
+            flush(box, 1, i).start()
+
+        @pl.when(jnp.logical_not(earlier))
+        def _():
+            flush(base, 0, i).start()
+            box[1, at] = base[1, at] + times(left_own, handed)
+            flush(box, 1, i).start()
 
     for i in range(height // rows):
         for k in range(count):
-            flush(k, i).wait()
+            flush(box, k, i).wait()
 
 
 def last_calls(where, left_own, left_other, prior, rows, factor):
@@ -409,22 +439,23 @@
         cost_estimate=cost(size // 4, size),
     )(prior)
 
-    def early(other):
+    def early(mixed, straight):
+        args = [mixed, straight, left_own, left_other, base]
         return pl.pallas_call(
-            functools.partial(early_kernel, count, rows, factor),
+            functools.partial(early_kernel, rows, factor),
             out_shape=small,
-            in_specs=[near] * (count + 2),
+            in_specs=[near] * len(args),
             out_specs=near,
             compiler_params=grant,
             cost_estimate=cost(flops, size),
-        )(*other, left_other, base)
-
-    def final(out, first, second, base):
-        args = [*first, *second, left_own, base, out]
+        )(*args)
+
+    def final(out, handed, straight, base):
+        args = [handed, straight, left_own, left_other, base, out]
         return pl.pallas_call(
             functools.partial(final_kernel, where, rows, factor),
             out_shape=pltpu.HBM(out.shape, out.dtype),
-            in_specs=[near] * (2 * count + 2) + [far],
+            in_specs=[near] * (len(args) - 1) + [far],
             out_specs=far,
             scratch_shapes=[
                 pltpu.VMEM(small.shape, small.dtype),
@@ -492,17 +523,16 @@
         out = finish(out, other)
 
     both = ("assets", "tm")
-    direct = {"p": [], "q": []}
-    for way, pairs in enumerate((forward, backward)):
-        for name, sender in (("p", 1), ("q", 0)):
-            links = [(2 * a + sender, 2 * b + 1) for a, b in pairs]
-            direct[name].append(lax.ppermute(crossed[way], both, links))
-    handed = []
-    for part in direct["p"]:
-        handed.append(lax.ppermute(part, "tm", [(0, 1), (1, 0)]))
+    plain = [f[:, cut:] for f in flight[0]]
+    mixed = pick_call(plain[0], crossed[1])
+    links = [(2 * a, 2 * b) for a, b in forward] + [(2 * a + 1, 2 * b + 1) for a, b in backward]
+    mixed = lax.ppermute(mixed, both, links)
+    ahead = lax.ppermute(plain[0], both, [(2 * a + 1, 2 * b + 1) for a, b in forward])
+    astern = lax.ppermute(crossed[1], both, [(2 * a, 2 * b + 1) for a, b in backward])
+    handed = swap([mixed])[0]
     where = tuple((s, width, side * half + cut) for s, side in ((n // 2, 0), (-(n // 2), 1)))
     early, final = last_calls(where, *common)
-    return final(out, handed, direct["q"], early(direct["p"]))
+    return final(out, handed, astern, early(mixed, ahead))
 
 
 def solution(mesh):

time: 164 us -> 158 us (0.963)
  waiting for transfers between devices: 68.3 us -> 65 us
  starting transfers between devices: 36.4 us -> 34.3 us
    ppermute x6 -> x3, starting transfers between devices: 10.9 us -> 4.9 us  [the longest x1 2.08 us: local_ring(): lax.ppermute(plain[0], both, [(2 * a + 1, 2 * b + 1) for a, b in forward])]
    ppermute x16 -> x17, starting transfers between devices: 12.3 us -> 16.1 us  [swap(): moved.append(lax.ppermute(part, 'tm', [(0, 1), (1, 0)]))]
    ppermute x14, waiting for transfers between devices: 68.2 us -> 64.9 us  [hop(): moved.append(lax.ppermute(parts[way], 'assets', pairs))]
  transfers between devices with their start and end apart: 36 -> 34, of which waited for: 6 -> 6; matrix products, arithmetic and copies ran while one was open for 0% -> 0% of each run, Pallas kernels for 33% -> 34%
where the time goes in v7:
time: 158 us; the launch traced here: 157 us
  waiting for transfers between devices  65 us (41%)
  Pallas kernels  57.5 us (36%)
  starting transfers between devices  34.3 us (22%)
    ppermute x14, waiting for transfers between devices, hop(): moved.append(lax.ppermute(parts[way], 'assets', pairs))  64.9 us
    pallas_call x7, Pallas kernels, tile_calls(): pl.pallas_call(functools.partial(own_kernel, where, rows, factor), out_sh...  23.9 us
    pallas_call x8, Pallas kernels, finish(): pl.pallas_call(functools.partial(other_kernel, where, rows, factor), out_...  23.1 us
    ppermute x17, starting transfers between devices, swap(): moved.append(lax.ppermute(part, 'tm', [(0, 1), (1, 0)]))  16.1 us
    ppermute x14, starting transfers between devices, hop(): moved.append(lax.ppermute(parts[way], 'assets', pairs))  13.3 us
  transfers between devices with their start and end apart: 34, of which 6 were waited for; matrix products, arithmetic and copies ran while one was open for 0% of the time, Pallas kernels for 34%

profile of v7, /device:TPU:1, one launch (start us, length us, event | category | flops | bytes accessed | tf_op | source)
XLA Modules:
  0.0 157.4 jit_solution(7369512673999372789)
XLA Ops:
  0.0 1.6 shard_map.37
  1.6 0.1 collective-permute-start.10
  1.7 2.8 %collective-permute-start = (bf16[768,512]{1,0:T(8,128)(2,1)S(1)}, bf16[768,512]{1,0:T(8,128)(2,1)S(1)}, u32[]{:S(2)}, u32[]{:S(2)}) collective-permute-start(bf16[768,512]{1,0:T(8,128)(2,1)S(1)} %get-tuple-element.7.refs_0_), channel_id=1, source_target_pairs={{0,4},{4,8},{8,12},{12,14},{14,10},{10,6},{6,2},{2,0},{1,5},{5,9},... | collective-permute-start | bytes 2359304 | tf_op jit(solution)/shard_map/ppermute | solution.py:493
  4.4 0.0 collective-permute-start.3
  4.4 1.5 collective-permute-start.17
  5.9 0.9 collective-permute-start.11
  6.8 15.4 %collective-permute-done.refs_0_ = bf16[768,512]{1,0:T(8,128)(2,1)S(1)} collective-permute-done((bf16[768,512]{1,0:T(8,128)(2,1)S(1)}, bf16[768,512]{1,0:T(8,128)(2,1)S(1)}, u32[]{:S(2)}, u32[]{:S(2)}) %collective-permute-start) | collective-permute-done | bytes 786464 | tf_op jit(solution)/shard_map/ppermute | solution.py:493
  22.2 0.9 collective-permute-start.32
  23.1 0.1 collective-permute-done.3.refs_1_
  23.2 2.0 %collective-permute-start.33 = (bf16[768,512]{1,0:T(8,128)(2,1)S(1)}, bf16[768,512]{1,0:T(8,128)(2,1)S(1)}, u32[]{:S(2)}, u32[]{:S(2)}) collective-permute-start(bf16[768,512]{1,0:T(8,128)(2,1)S(1)} %collective-permute-done.3.refs_1_), channel_id=1, source_target_pairs={{0,1},{1,0},{2,3},{3,2},{4,5},{5,4},{6,7},{7,6},{8,9},{9,8},{10,11... | collective-permute-start | bytes 2359304 | tf_op jit(solution)/shard_map/ppermute | solution.py:485
  25.2 13.9 %collective-permute-done.17.refs_0_ = bf16[768,512]{1,0:T(8,128)(2,1)S(1)} collective-permute-done((bf16[768,512]{1,0:T(8,128)(2,1)S(1)}, bf16[768,512]{1,0:T(8,128)(2,1)S(1)}, u32[]{:S(2)}, u32[]{:S(2)}) %collective-permute-start.17) | collective-permute-done | bytes 786464 | tf_op jit(solution)/shard_map/ppermute | solution.py:493
  39.0 0.6 collective-permute-start.30
  39.7 0.0 collective-permute-done.11.refs_1_
  39.7 1.5 collective-permute-start.1
  41.3 1.5 collective-permute-start.18
  42.7 0.0 collective-permute-done.33.refs_1_
  42.7 0.8 collective-permute-start.31
  43.6 0.0 collective-permute-done.30.refs_0_
  43.6 15.2 %collective-permute-done.1.refs_0_ = bf16[768,512]{1,0:T(8,128)(2,1)S(1)} collective-permute-done((bf16[768,512]{1,0:T(8,128)(2,1)S(1)}, bf16[768,512]{1,0:T(8,128)(2,1)S(1)}, u32[]{:S(2)}, u32[]{:S(2)}) %collective-permute-start.1) | collective-permute-done | bytes 786464 | tf_op jit(solution)/shard_map/ppermute | solution.py:493
  58.8 1.3 collective-permute-start.28
  60.1 1.8 %collective-permute-start.29 = (bf16[768,512]{1,0:T(8,128)(2,1)S(1)}, bf16[768,512]{1,0:T(8,128)(2,1)S(1)}, u32[]{:S(2)}, u32[]{:S(2)}) collective-permute-start(bf16[768,512]{1,0:T(8,128)(2,1)S(1)} %collective-permute-done.4.refs_1_), channel_id=1, source_target_pairs={{0,1},{1,0},{2,3},{3,2},{4,5},{5,4},{6,7},{7,6},{8,9},{9,8},{10,11... | collective-permute-start | bytes 2359304 | tf_op jit(solution)/shard_map/ppermute | solution.py:485
  61.9 13.7 %collective-permute-done.18.refs_0_ = bf16[768,512]{1,0:T(8,128)(2,1)S(1)} collective-permute-done((bf16[768,512]{1,0:T(8,128)(2,1)S(1)}, bf16[768,512]{1,0:T(8,128)(2,1)S(1)}, u32[]{:S(2)}, u32[]{:S(2)}) %collective-permute-start.18) | collective-permute-done | bytes 786464 | tf_op jit(solution)/shard_map/ppermute | solution.py:493
  75.6 0.9 collective-permute-start.26
  76.5 1.5 collective-permute-start.5
  78.0 0.5 shard_map.39.left_own.refs_2_
  78.4 0.1 collective-permute-start.2
  78.6 3.4 %shard_map.51.refs_3_ = f32[2,1024,512]{2,1,0:T(8,128)S(1)} custom-call(bf16[768,512]{1,0:T(8,128)(2,1)S(1)} %get-tuple-element.7.refs_0_, bf16[768,512]{1,0:T(8,128)(2,1)S(1)} %get-tuple-element.8.refs_1_, bf16[1024,768]{1,0:T(8,128)(2,1)S(1)} %shard_map.39.left_own.refs_2_, f32[1024,8192]{1,0:T(8,128)} %refs_3_.13), custom_call_target="tpu_custom_call" | custom-call | flops 1610612736 | bytes 8388608 | tf_op jit(solution)/shard_map/pallas_call | solution.py:304
  82.0 1.7 %shard_map.43.refs_3_ = f32[2,1024,256]{2,1,0:T(8,128)S(1)} custom-call(f32[1024,8192]{1,0:T(8,128)} %refs_3_.13), custom_call_target="tpu_custom_call" | custom-call | flops 524288 | bytes 2097152 | tf_op jit(solution)/shard_map/pallas_call | solution.py:286
  83.7 1.7 %shard_map.41.base = f32[2,1024,256]{2,1,0:T(8,128)S(1)} custom-call(f32[1024,8192]{1,0:T(8,128)} %refs_3_.13), custom_call_target="tpu_custom_call" | custom-call | flops 524288 | bytes 2097152 | tf_op jit(solution)/shard_map/pallas_call | solution.py:432
  85.3 0.5 shard_map.40.left_other.refs_2_
  85.8 3.4 %shard_map.50.refs_3_ = f32[2,1024,512]{2,1,0:T(8,128)S(1)} custom-call(bf16[768,512]{1,0:T(8,128)(2,1)S(1)} %collective-permute-done.refs_0_, bf16[768,512]{1,0:T(8,128)(2,1)S(1)} %collective-permute-done.3.refs_1_, bf16[1024,768]{1,0:T(8,128)(2,1)S(1)} %shard_map.39.left_own.refs_2_, f32[1024,8192]{1,0:T(8,128)} %refs_3_.13), custom_call_target="tpu_custom_call" | custom-call | flops 1610612736 | bytes 8388608 | tf_op jit(solution)/shard_map/pallas_call | solution.py:304
  89.3 1.5 collective-permute-start.19
  90.8 1.2 collective-permute-start.27
  91.9 3.4 %shard_map.49.refs_3_ = f32[2,1024,512]{2,1,0:T(8,128)S(1)} custom-call(bf16[768,512]{1,0:T(8,128)(2,1)S(1)} %collective-permute-done.17.refs_0_, bf16[768,512]{1,0:T(8,128)(2,1)S(1)} %collective-permute-done.21.refs_1_, bf16[1024,768]{1,0:T(8,128)(2,1)S(1)} %shard_map.39.left_own.refs_2_, f32[1024,8192]{1,0:T(8,128)} %refs_3_.13), custom_call_target="tpu_custom_call" | custom-call | flops 1610612736 | bytes 8388608 | tf_op jit(solution)/shard_map/pallas_call | solution.py:304
  95.4 0.2 collective-permute-start.23
  95.6 3.0 %shard_map.52.refs_4_ = f32[1,1024,8192]{2,1,0:T(8,128)} custom-call(bf16[768,512]{1,0:T(8,128)(2,1)S(1)} %collective-permute-done.10.refs_0_, bf16[768,512]{1,0:T(8,128)(2,1)S(1)} %collective-permute-done.11.refs_1_, bf16[1024,768]{1,0:T(8,128)(2,1)S(1)} %shard_map.40.left_other.refs_2_, f32[2,1024,512]{2,1,0:T(8,128)S(1)} %shard_map.51.refs_3_), custom_call_target="tpu_custom_call" | custom-call | flops 1610612736 | bytes 8388608 | tf_op jit(solution)/shard_map/pallas_call | solution.py:322
  98.6 0.1 collective-permute-start.6
  98.6 3.4 %shard_map.48.refs_3_ = f32[2,1024,512]{2,1,0:T(8,128)S(1)} custom-call(bf16[768,512]{1,0:T(8,128)(2,1)S(1)} %collective-permute-done.1.refs_0_, bf16[768,512]{1,0:T(8,128)(2,1)S(1)} %collective-permute-done.4.refs_1_, bf16[1024,768]{1,0:T(8,128)(2,1)S(1)} %shard_map.39.left_own.refs_2_, f32[1024,8192]{1,0:T(8,128)} %refs_3_.13), custom_call_target="tpu_custom_call" | custom-call | flops 1610612736 | bytes 8388608 | tf_op jit(solution)/shard_map/pallas_call | solution.py:304
  102.1 3.4 %shard_map.47.refs_3_ = f32[2,1024,512]{2,1,0:T(8,128)S(1)} custom-call(bf16[768,512]{1,0:T(8,128)(2,1)S(1)} %collective-permute-done.18.refs_0_, bf16[768,512]{1,0:T(8,128)(2,1)S(1)} %collective-permute-done.22.refs_1_, bf16[1024,768]{1,0:T(8,128)(2,1)S(1)} %shard_map.39.left_own.refs_2_, f32[1024,8192]{1,0:T(8,128)} %refs_3_.13), custom_call_target="tpu_custom_call" | custom-call | flops 1610612736 | bytes 8388608 | tf_op jit(solution)/shard_map/pallas_call | solution.py:304
  105.5 0.5 collective-permute-start.25
  106.1 0.1 fusion
  106.2 1.3 collective-permute-start.13
  107.5 6.7 %collective-permute-done.19.refs_0_ = bf16[768,512]{1,0:T(8,128)(2,1)S(1)} collective-permute-done((bf16[768,512]{1,0:T(8,128)(2,1)S(1)}, bf16[768,512]{1,0:T(8,128)(2,1)S(1)}, u32[]{:S(2)}, u32[]{:S(2)}) %collective-permute-start.19) | collective-permute-done | bytes 786464 | tf_op jit(solution)/shard_map/ppermute | solution.py:493
  114.2 1.9 %collective-permute-start.20 = (bf16[768,512]{1,0:T(8,128)(2,1)S(1)}, bf16[768,512]{1,0:T(8,128)(2,1)S(1)}, u32[]{:S(2)}, u32[]{:S(2)}) collective-permute-start(bf16[768,512]{1,0:T(8,128)(2,1)S(1)} %collective-permute-done.19.refs_0_), channel_id=1, source_target_pairs={{0,1},{1,0},{2,3},{3,2},{4,5},{5,4},{6,7},{7,6},{8,9},{9,8},{10,11... | collective-permute-start | bytes 2359304 | tf_op jit(solution)/shard_map/ppermute | solution.py:485
  116.0 3.0 %shard_map.53.refs_4_ = f32[1,1024,8192]{2,1,0:T(8,128)} custom-call(bf16[768,512]{1,0:T(8,128)(2,1)S(1)} %collective-permute-done.32.refs_0_, bf16[768,512]{1,0:T(8,128)(2,1)S(1)} %collective-permute-done.33.refs_1_, bf16[1024,768]{1,0:T(8,128)(2,1)S(1)} %shard_map.40.left_other.refs_2_, ...), custom_call_target="tpu_custom_call", output_to_operand_aliasing={{}: (4, {})} | custom-call | flops 1610612736 | bytes 8388608 | tf_op jit(solution)/shard_map/pallas_call | solution.py:322
  119.0 0.1 collective-permute-start.24
  119.1 3.0 %shard_map.54.refs_4_ = f32[1,1024,8192]{2,1,0:T(8,128)} custom-call(bf16[768,512]{1,0:T(8,128)(2,1)S(1)} %collective-permute-done.30.refs_0_, bf16[768,512]{1,0:T(8,128)(2,1)S(1)} %collective-permute-done.31.refs_1_, bf16[1024,768]{1,0:T(8,128)(2,1)S(1)} %shard_map.40.left_other.refs_2_, ...), custom_call_target="tpu_custom_call", output_to_operand_aliasing={{}: (4, {})} | custom-call | flops 1610612736 | bytes 8388608 | tf_op jit(solution)/shard_map/pallas_call | solution.py:322
  122.1 1.4 collective-permute-start.15
  123.5 3.4 %shard_map.46.refs_3_ = f32[2,1024,512]{2,1,0:T(8,128)S(1)} custom-call(bf16[768,512]{1,0:T(8,128)(2,1)S(1)} %collective-permute-done.2.refs_0_, bf16[768,512]{1,0:T(8,128)(2,1)S(1)} %collective-permute-done.5.refs_1_, bf16[1024,768]{1,0:T(8,128)(2,1)S(1)} %shard_map.39.left_own.refs_2_, f32[1024,8192]{1,0:T(8,128)} %refs_3_.13), custom_call_target="tpu_custom_call" | custom-call | flops 1610612736 | bytes 8388608 | tf_op jit(solution)/shard_map/pallas_call | solution.py:304
  127.0 1.5 collective-permute-start.7
  128.5 3.4 %shard_map.45.refs_3_ = f32[2,1024,512]{2,1,0:T(8,128)S(1)} custom-call(bf16[768,512]{1,0:T(8,128)(2,1)S(1)} %collective-permute-done.19.refs_0_, bf16[768,512]{1,0:T(8,128)(2,1)S(1)} %collective-permute-done.23.refs_1_, bf16[1024,768]{1,0:T(8,128)(2,1)S(1)} %shard_map.39.left_own.refs_2_, f32[1024,8192]{1,0:T(8,128)} %refs_3_.13), custom_call_target="tpu_custom_call" | custom-call | flops 1610612736 | bytes 8388608 | tf_op jit(solution)/shard_map/pallas_call | solution.py:304
  132.0 3.0 %shard_map.55.refs_4_ = f32[1,1024,8192]{2,1,0:T(8,128)} custom-call(bf16[768,512]{1,0:T(8,128)(2,1)S(1)} %collective-permute-done.28.refs_0_, bf16[768,512]{1,0:T(8,128)(2,1)S(1)} %collective-permute-done.29.refs_1_, bf16[1024,768]{1,0:T(8,128)(2,1)S(1)} %shard_map.40.left_other.refs_2_, ...), custom_call_target="tpu_custom_call", output_to_operand_aliasing={{}: (4, {})} | custom-call | flops 1610612736 | bytes 8388608 | tf_op jit(solution)/shard_map/pallas_call | solution.py:322
  135.0 0.1 collective-permute-start.14
  135.0 0.5 collective-permute-start.16
  135.5 3.0 %shard_map.56.refs_4_ = f32[1,1024,8192]{2,1,0:T(8,128)} custom-call(bf16[768,512]{1,0:T(8,128)(2,1)S(1)} %collective-permute-done.26.refs_0_, bf16[768,512]{1,0:T(8,128)(2,1)S(1)} %collective-permute-done.27.refs_1_, bf16[1024,768]{1,0:T(8,128)(2,1)S(1)} %shard_map.40.left_other.refs_2_, ...), custom_call_target="tpu_custom_call", output_to_operand_aliasing={{}: (4, {})} | custom-call | flops 1610612736 | bytes 8388608 | tf_op jit(solution)/shard_map/pallas_call | solution.py:322
  138.5 2.1 %collective-permute-start.12 = (bf16[768,256]{1,0:T(8,128)(2,1)S(1)}, bf16[768,256]{1,0:T(8,128)(2,1)S(1)}, u32[]{:S(2)}, u32[]{:S(2)}) collective-permute-start(bf16[768,256]{1,0:T(8,128)(2,1)S(1)} %get-tuple-element.10.first), channel_id=1, source_target_pairs={{1,5},{5,9},{9,13},{13,15},{15,11},{11,7},{7,3},{3,1},{17,21},{21,... | collective-permute-start | bytes 1179656 | tf_op jit(solution)/shard_map/ppermute | solution.py:530
  140.6 1.1 shard_map.44.refs_3_
  141.8 1.3 collective-permute-start.9
  143.1 2.4 %collective-permute-start.8 = (bf16[768,256]{1,0:T(8,128)(2,1)S(1)}, bf16[768,256]{1,0:T(8,128)(2,1)S(1)}, u32[]{:S(2)}, u32[]{:S(2)}) collective-permute-start(bf16[768,256]{1,0:T(8,128)(2,1)S(1)} %collective-permute-done.7.mixed), channel_id=1, source_target_pairs={{0,1},{1,0},{2,3},{3,2},{4,5},{5,4},{6,7},{7,6},{8,9},{9,8},{10,11... | collective-permute-start | bytes 1179656 | tf_op jit(solution)/shard_map/ppermute | solution.py:485
  145.5 3.0 %shard_map.57.refs_4_ = f32[1,1024,8192]{2,1,0:T(8,128)} custom-call(bf16[768,512]{1,0:T(8,128)(2,1)S(1)} %collective-permute-done.25.refs_0_, bf16[768,512]{1,0:T(8,128)(2,1)S(1)} %collective-permute-done.6.refs_1_, bf16[1024,768]{1,0:T(8,128)(2,1)S(1)} %shard_map.40.left_other.refs_2_, ...), custom_call_target="tpu_custom_call", output_to_operand_aliasing={{}: (4, {})} | custom-call | flops 1610612736 | bytes 8388608 | tf_op jit(solution)/shard_map/pallas_call | solution.py:322
  148.5 3.0 %shard_map.58.refs_4_ = f32[1,1024,8192]{2,1,0:T(8,128)} custom-call(bf16[768,512]{1,0:T(8,128)(2,1)S(1)} %collective-permute-done.20.refs_0_, bf16[768,512]{1,0:T(8,128)(2,1)S(1)} %collective-permute-done.24.refs_1_, bf16[1024,768]{1,0:T(8,128)(2,1)S(1)} %shard_map.40.left_other.refs_2_, ...), custom_call_target="tpu_custom_call", output_to_operand_aliasing={{}: (4, {})} | custom-call | flops 1610612736 | bytes 8388608 | tf_op jit(solution)/shard_map/pallas_call | solution.py:322
  151.5 2.3 %shard_map.59._ = f32[1,1024,8192]{2,1,0:T(8,128)} custom-call(bf16[768,256]{1,0:T(8,128)(2,1)S(1)} %collective-permute-done.14.refs_0_, bf16[768,256]{1,0:T(8,128)(2,1)S(1)} %collective-permute-done.16.refs_1_, bf16[1024,768]{1,0:T(8,128)(2,1)S(1)} %shard_map.40.left_other.refs_2_, ...), custom_call_target="tpu_custom_call", output_to_operand_aliasing={{}: (4, {})} | custom-call | flops 805306368 | bytes 4194304 | tf_op jit(solution)/shard_map/pallas_call | solution.py:322
  153.8 1.2 shard_map.42.base
  155.0 2.3 %shard_map.60 = f32[1,1024,8192]{2,1,0:T(8,128)} custom-call(bf16[768,256]{1,0:T(8,128)(2,1)S(1)} %collective-permute-done.8.handed, bf16[768,256]{1,0:T(8,128)(2,1)S(1)} %collective-permute-done.9.straight, bf16[1024,768]{1,0:T(8,128)(2,1)S(1)} %shard_map.39.left_own.refs_2_, ...), custom_call_target="tpu_custom_call", output_to_operand_aliasing={{}: (5, {})} | custom-call | flops 805306368 | bytes 4194304 | tf_op jit(solution)/shard_map/pallas_call | solution.py:455
  (31 shorter events, 0.2 us)
Async XLA Ops:
  1.6 5.2 %collective-permute-start.10 = (bf16[768,512]{1,0:T(8,128)(2,1)S(1)}, bf16[768,512]{1,0:T(8,128)(2,1)S(1)}, u32[]{:S(2)}, u32[]{:S(2)}) collective-permute-start(bf16[768,512]{1,0:T(8,128)(2,1)S(1)} %get-tuple-element.7.refs_0_), channel_id=1, source_target_pairs={{0,1},{1,0},{2,3},{3,2},{4,5},{5,4},{6,7},{7,6},{8,9},{9,8},{10,11... | collective-permute-start | bytes 2359304 | tf_op jit(solution)/shard_map/ppermute | solution.py:485
  1.7 20.5 %collective-permute-start = (bf16[768,512]{1,0:T(8,128)(2,1)S(1)}, bf16[768,512]{1,0:T(8,128)(2,1)S(1)}, u32[]{:S(2)}, u32[]{:S(2)}) collective-permute-start(bf16[768,512]{1,0:T(8,128)(2,1)S(1)} %get-tuple-element.7.refs_0_), channel_id=1, source_target_pairs={{0,4},{4,8},{8,12},{12,14},{14,10},{10,6},{6,2},{2,0},{1,5},{5,9},... | collective-permute-start | bytes 2359304 | tf_op jit(solution)/shard_map/ppermute | solution.py:493
  4.4 18.8 %collective-permute-start.3 = (bf16[768,512]{1,0:T(8,128)(2,1)S(1)}, bf16[768,512]{1,0:T(8,128)(2,1)S(1)}, u32[]{:S(2)}, u32[]{:S(2)}) collective-permute-start(bf16[768,512]{1,0:T(8,128)(2,1)S(1)} %get-tuple-element.8.refs_1_), channel_id=1, source_target_pairs={{4,0},{8,4},{12,8},{14,12},{10,14},{6,10},{2,6},{0,2},{5,1},{9,5},... | collective-permute-start | bytes 2359304 | tf_op jit(solution)/shard_map/ppermute | solution.py:493
  4.4 34.6 %collective-permute-start.17 = (bf16[768,512]{1,0:T(8,128)(2,1)S(1)}, bf16[768,512]{1,0:T(8,128)(2,1)S(1)}, u32[]{:S(2)}, u32[]{:S(2)}) collective-permute-start(bf16[768,512]{1,0:T(8,128)(2,1)S(1)} %get-tuple-element.8.refs_1_), channel_id=1, source_target_pairs={{0,4},{4,8},{8,12},{12,14},{14,10},{10,6},{6,2},{2,0},{1,5},{5,9},... | collective-permute-start | bytes 2359304 | tf_op jit(solution)/shard_map/ppermute | solution.py:493
  5.9 33.8 %collective-permute-start.11 = (bf16[768,512]{1,0:T(8,128)(2,1)S(1)}, bf16[768,512]{1,0:T(8,128)(2,1)S(1)}, u32[]{:S(2)}, u32[]{:S(2)}) collective-permute-start(bf16[768,512]{1,0:T(8,128)(2,1)S(1)} %get-tuple-element.8.refs_1_), channel_id=1, source_target_pairs={{0,1},{1,0},{2,3},{3,2},{4,5},{5,4},{6,7},{7,6},{8,9},{9,8},{10,11... | collective-permute-start | bytes 2359304 | tf_op jit(solution)/shard_map/ppermute | solution.py:485
  6.8 34.4 %collective-permute-start.21 = (bf16[768,512]{1,0:T(8,128)(2,1)S(1)}, bf16[768,512]{1,0:T(8,128)(2,1)S(1)}, u32[]{:S(2)}, u32[]{:S(2)}) collective-permute-start(bf16[768,512]{1,0:T(8,128)(2,1)S(1)} %get-tuple-element.7.refs_0_), channel_id=1, source_target_pairs={{4,0},{8,4},{12,8},{14,12},{10,14},{6,10},{2,6},{0,2},{5,1},{9,5},... | collective-permute-start | bytes 2359304 | tf_op jit(solution)/shard_map/ppermute | solution.py:493
  22.2 19.1 %collective-permute-start.32 = (bf16[768,512]{1,0:T(8,128)(2,1)S(1)}, bf16[768,512]{1,0:T(8,128)(2,1)S(1)}, u32[]{:S(2)}, u32[]{:S(2)}) collective-permute-start(bf16[768,512]{1,0:T(8,128)(2,1)S(1)} %collective-permute-done.refs_0_), channel_id=1, source_target_pairs={{0,1},{1,0},{2,3},{3,2},{4,5},{5,4},{6,7},{7,6},{8,9},{9,8},{10,11... | collective-permute-start | bytes 2359304 | tf_op jit(solution)/shard_map/ppermute | solution.py:485
  23.2 19.5 %collective-permute-start.33 = (bf16[768,512]{1,0:T(8,128)(2,1)S(1)}, bf16[768,512]{1,0:T(8,128)(2,1)S(1)}, u32[]{:S(2)}, u32[]{:S(2)}) collective-permute-start(bf16[768,512]{1,0:T(8,128)(2,1)S(1)} %collective-permute-done.3.refs_1_), channel_id=1, source_target_pairs={{0,1},{1,0},{2,3},{3,2},{4,5},{5,4},{6,7},{7,6},{8,9},{9,8},{10,11... | collective-permute-start | bytes 2359304 | tf_op jit(solution)/shard_map/ppermute | solution.py:485
  39.0 4.5 %collective-permute-start.30 = (bf16[768,512]{1,0:T(8,128)(2,1)S(1)}, bf16[768,512]{1,0:T(8,128)(2,1)S(1)}, u32[]{:S(2)}, u32[]{:S(2)}) collective-permute-start(bf16[768,512]{1,0:T(8,128)(2,1)S(1)} %collective-permute-done.17.refs_0_), channel_id=1, source_target_pairs={{0,1},{1,0},{2,3},{3,2},{4,5},{5,4},{6,7},{7,6},{8,9},{9,8},{10,11... | collective-permute-start | bytes 2359304 | tf_op jit(solution)/shard_map/ppermute | solution.py:485
  39.7 19.1 %collective-permute-start.1 = (bf16[768,512]{1,0:T(8,128)(2,1)S(1)}, bf16[768,512]{1,0:T(8,128)(2,1)S(1)}, u32[]{:S(2)}, u32[]{:S(2)}) collective-permute-start(bf16[768,512]{1,0:T(8,128)(2,1)S(1)} %collective-permute-done.refs_0_), channel_id=1, source_target_pairs={{0,4},{4,8},{8,12},{12,14},{14,10},{10,6},{6,2},{2,0},{1,5},{5,9},... | collective-permute-start | bytes 2359304 | tf_op jit(solution)/shard_map/ppermute | solution.py:493
  41.2 18.9 %collective-permute-start.4 = (bf16[768,512]{1,0:T(8,128)(2,1)S(1)}, bf16[768,512]{1,0:T(8,128)(2,1)S(1)}, u32[]{:S(2)}, u32[]{:S(2)}) collective-permute-start(bf16[768,512]{1,0:T(8,128)(2,1)S(1)} %collective-permute-done.3.refs_1_), channel_id=1, source_target_pairs={{4,0},{8,4},{12,8},{14,12},{10,14},{6,10},{2,6},{0,2},{5,1},{9,5},... | collective-permute-start | bytes 2359304 | tf_op jit(solution)/shard_map/ppermute | solution.py:493
  41.3 34.4 %collective-permute-start.18 = (bf16[768,512]{1,0:T(8,128)(2,1)S(1)}, bf16[768,512]{1,0:T(8,128)(2,1)S(1)}, u32[]{:S(2)}, u32[]{:S(2)}) collective-permute-start(bf16[768,512]{1,0:T(8,128)(2,1)S(1)} %collective-permute-done.17.refs_0_), channel_id=1, source_target_pairs={{0,4},{4,8},{8,12},{12,14},{14,10},{10,6},{6,2},{2,0},{1,5},{5,9},... | collective-permute-start | bytes 2359304 | tf_op jit(solution)/shard_map/ppermute | solution.py:493
  42.7 33.8 %collective-permute-start.31 = (bf16[768,512]{1,0:T(8,128)(2,1)S(1)}, bf16[768,512]{1,0:T(8,128)(2,1)S(1)}, u32[]{:S(2)}, u32[]{:S(2)}) collective-permute-start(bf16[768,512]{1,0:T(8,128)(2,1)S(1)} %collective-permute-done.21.refs_1_), channel_id=1, source_target_pairs={{0,1},{1,0},{2,3},{3,2},{4,5},{5,4},{6,7},{7,6},{8,9},{9,8},{10,11... | collective-permute-start | bytes 2359304 | tf_op jit(solution)/shard_map/ppermute | solution.py:485
  43.6 34.9 %collective-permute-start.22 = (bf16[768,512]{1,0:T(8,128)(2,1)S(1)}, bf16[768,512]{1,0:T(8,128)(2,1)S(1)}, u32[]{:S(2)}, u32[]{:S(2)}) collective-permute-start(bf16[768,512]{1,0:T(8,128)(2,1)S(1)} %collective-permute-done.21.refs_1_), channel_id=1, source_target_pairs={{4,0},{8,4},{12,8},{14,12},{10,14},{6,10},{2,6},{0,2},{5,1},{9,5},... | collective-permute-start | bytes 2359304 | tf_op jit(solution)/shard_map/ppermute | solution.py:493
  58.8 30.5 %collective-permute-start.28 = (bf16[768,512]{1,0:T(8,128)(2,1)S(1)}, bf16[768,512]{1,0:T(8,128)(2,1)S(1)}, u32[]{:S(2)}, u32[]{:S(2)}) collective-permute-start(bf16[768,512]{1,0:T(8,128)(2,1)S(1)} %collective-permute-done.1.refs_0_), channel_id=1, source_target_pairs={{0,1},{1,0},{2,3},{3,2},{4,5},{5,4},{6,7},{7,6},{8,9},{9,8},{10,11... | collective-permute-start | bytes 2359304 | tf_op jit(solution)/shard_map/ppermute | solution.py:485
  60.1 30.7 %collective-permute-start.29 = (bf16[768,512]{1,0:T(8,128)(2,1)S(1)}, bf16[768,512]{1,0:T(8,128)(2,1)S(1)}, u32[]{:S(2)}, u32[]{:S(2)}) collective-permute-start(bf16[768,512]{1,0:T(8,128)(2,1)S(1)} %collective-permute-done.4.refs_1_), channel_id=1, source_target_pairs={{0,1},{1,0},{2,3},{3,2},{4,5},{5,4},{6,7},{7,6},{8,9},{9,8},{10,11... | collective-permute-start | bytes 2359304 | tf_op jit(solution)/shard_map/ppermute | solution.py:485
  75.6 19.7 %collective-permute-start.26 = (bf16[768,512]{1,0:T(8,128)(2,1)S(1)}, bf16[768,512]{1,0:T(8,128)(2,1)S(1)}, u32[]{:S(2)}, u32[]{:S(2)}) collective-permute-start(bf16[768,512]{1,0:T(8,128)(2,1)S(1)} %collective-permute-done.18.refs_0_), channel_id=1, source_target_pairs={{0,1},{1,0},{2,3},{3,2},{4,5},{5,4},{6,7},{7,6},{8,9},{9,8},{10,11... | collective-permute-start | bytes 2359304 | tf_op jit(solution)/shard_map/ppermute | solution.py:485
  76.5 22.1 %collective-permute-start.5 = (bf16[768,512]{1,0:T(8,128)(2,1)S(1)}, bf16[768,512]{1,0:T(8,128)(2,1)S(1)}, u32[]{:S(2)}, u32[]{:S(2)}) collective-permute-start(bf16[768,512]{1,0:T(8,128)(2,1)S(1)} %collective-permute-done.4.refs_1_), channel_id=1, source_target_pairs={{4,0},{8,4},{12,8},{14,12},{10,14},{6,10},{2,6},{0,2},{5,1},{9,5},... | collective-permute-start | bytes 2359304 | tf_op jit(solution)/shard_map/ppermute | solution.py:493
  78.4 27.1 %collective-permute-start.2 = (bf16[768,512]{1,0:T(8,128)(2,1)S(1)}, bf16[768,512]{1,0:T(8,128)(2,1)S(1)}, u32[]{:S(2)}, u32[]{:S(2)}) collective-permute-start(bf16[768,512]{1,0:T(8,128)(2,1)S(1)} %collective-permute-done.1.refs_0_), channel_id=1, source_target_pairs={{0,4},{4,8},{8,12},{12,14},{14,10},{10,6},{6,2},{2,0},{1,5},{5,9},... | collective-permute-start | bytes 2359304 | tf_op jit(solution)/shard_map/ppermute | solution.py:493
  89.3 24.9 %collective-permute-start.19 = (bf16[768,512]{1,0:T(8,128)(2,1)S(1)}, bf16[768,512]{1,0:T(8,128)(2,1)S(1)}, u32[]{:S(2)}, u32[]{:S(2)}) collective-permute-start(bf16[768,512]{1,0:T(8,128)(2,1)S(1)} %collective-permute-done.18.refs_0_), channel_id=1, source_target_pairs={{0,4},{4,8},{8,12},{12,14},{14,10},{10,6},{6,2},{2,0},{1,5},{5,9},... | collective-permute-start | bytes 2359304 | tf_op jit(solution)/shard_map/ppermute | solution.py:493
  90.8 15.4 %collective-permute-start.27 = (bf16[768,512]{1,0:T(8,128)(2,1)S(1)}, bf16[768,512]{1,0:T(8,128)(2,1)S(1)}, u32[]{:S(2)}, u32[]{:S(2)}) collective-permute-start(bf16[768,512]{1,0:T(8,128)(2,1)S(1)} %collective-permute-done.22.refs_1_), channel_id=1, source_target_pairs={{0,1},{1,0},{2,3},{3,2},{4,5},{5,4},{6,7},{7,6},{8,9},{9,8},{10,11... | collective-permute-start | bytes 2359304 | tf_op jit(solution)/shard_map/ppermute | solution.py:485
  95.4 23.7 %collective-permute-start.23 = (bf16[768,512]{1,0:T(8,128)(2,1)S(1)}, bf16[768,512]{1,0:T(8,128)(2,1)S(1)}, u32[]{:S(2)}, u32[]{:S(2)}) collective-permute-start(bf16[768,512]{1,0:T(8,128)(2,1)S(1)} %collective-permute-done.22.refs_1_), channel_id=1, source_target_pairs={{4,0},{8,4},{12,8},{14,12},{10,14},{6,10},{2,6},{0,2},{5,1},{9,5},... | collective-permute-start | bytes 2359304 | tf_op jit(solution)/shard_map/ppermute | solution.py:493
  98.6 23.6 %collective-permute-start.6 = (bf16[768,512]{1,0:T(8,128)(2,1)S(1)}, bf16[768,512]{1,0:T(8,128)(2,1)S(1)}, u32[]{:S(2)}, u32[]{:S(2)}) collective-permute-start(bf16[768,512]{1,0:T(8,128)(2,1)S(1)} %collective-permute-done.5.refs_1_), channel_id=1, source_target_pairs={{0,1},{1,0},{2,3},{3,2},{4,5},{5,4},{6,7},{7,6},{8,9},{9,8},{10,11... | collective-permute-start | bytes 2359304 | tf_op jit(solution)/shard_map/ppermute | solution.py:485
  105.5 29.5 %collective-permute-start.25 = (bf16[768,512]{1,0:T(8,128)(2,1)S(1)}, bf16[768,512]{1,0:T(8,128)(2,1)S(1)}, u32[]{:S(2)}, u32[]{:S(2)}) collective-permute-start(bf16[768,512]{1,0:T(8,128)(2,1)S(1)} %collective-permute-done.2.refs_0_), channel_id=1, source_target_pairs={{0,1},{1,0},{2,3},{3,2},{4,5},{5,4},{6,7},{7,6},{8,9},{9,8},{10,11... | collective-permute-start | bytes 2359304 | tf_op jit(solution)/shard_map/ppermute | solution.py:485
  106.2 20.8 %collective-permute-start.13 = (bf16[768,256]{1,0:T(8,128)(2,1)S(1)}, bf16[768,256]{1,0:T(8,128)(2,1)S(1)}, u32[]{:S(2)}, u32[]{:S(2)}) collective-permute-start(bf16[768,256]{1,0:T(8,128)(2,1)S(1)} %get-tuple-element.9), channel_id=1, source_target_pairs={{0,4},{4,8},{8,12},{12,14},{14,10},{10,6},{6,2},{2,0},{1,5},{5,9},... | collective-permute-start | bytes 1179656 | tf_op jit(solution)/shard_map/ppermute | solution.py:493
  114.2 24.4 %collective-permute-start.20 = (bf16[768,512]{1,0:T(8,128)(2,1)S(1)}, bf16[768,512]{1,0:T(8,128)(2,1)S(1)}, u32[]{:S(2)}, u32[]{:S(2)}) collective-permute-start(bf16[768,512]{1,0:T(8,128)(2,1)S(1)} %collective-permute-done.19.refs_0_), channel_id=1, source_target_pairs={{0,1},{1,0},{2,3},{3,2},{4,5},{5,4},{6,7},{7,6},{8,9},{9,8},{10,11... | collective-permute-start | bytes 2359304 | tf_op jit(solution)/shard_map/ppermute | solution.py:485
  119.0 22.7 %collective-permute-start.24 = (bf16[768,512]{1,0:T(8,128)(2,1)S(1)}, bf16[768,512]{1,0:T(8,128)(2,1)S(1)}, u32[]{:S(2)}, u32[]{:S(2)}) collective-permute-start(bf16[768,512]{1,0:T(8,128)(2,1)S(1)} %collective-permute-done.23.refs_1_), channel_id=1, source_target_pairs={{0,1},{1,0},{2,3},{3,2},{4,5},{5,4},{6,7},{7,6},{8,9},{9,8},{10,11... | collective-permute-start | bytes 2359304 | tf_op jit(solution)/shard_map/ppermute | solution.py:485
  122.1 12.8 %collective-permute-start.15 = (bf16[768,256]{1,0:T(8,128)(2,1)S(1)}, bf16[768,256]{1,0:T(8,128)(2,1)S(1)}, u32[]{:S(2)}, u32[]{:S(2)}) collective-permute-start(bf16[768,256]{1,0:T(8,128)(2,1)S(1)} %slice.19), channel_id=1, source_target_pairs={{4,0},{8,4},{12,8},{14,12},{10,14},{6,10},{2,6},{0,2},{5,1},{9,5},... | collective-permute-start | bytes 1179656 | tf_op jit(solution)/shard_map/ppermute | solution.py:493
  127.0 16.1 %collective-permute-start.7 = (bf16[768,256]{1,0:T(8,128)(2,1)S(1)}, bf16[768,256]{1,0:T(8,128)(2,1)S(1)}, u32[]{:S(2)}, u32[]{:S(2)}) collective-permute-start(bf16[768,256]{1,0:T(8,128)(2,1)S(1)} %shard_map.38), channel_id=1, source_target_pairs={{0,4},{4,8},{8,12},{12,14},{14,10},{10,6},{6,2},{2,0},{5,1},{9,5},... | collective-permute-start | bytes 1179656 | tf_op jit(solution)/shard_map/ppermute | solution.py:529
  135.0 16.5 %collective-permute-start.14 = (bf16[768,256]{1,0:T(8,128)(2,1)S(1)}, bf16[768,256]{1,0:T(8,128)(2,1)S(1)}, u32[]{:S(2)}, u32[]{:S(2)}) collective-permute-start(bf16[768,256]{1,0:T(8,128)(2,1)S(1)} %collective-permute-done.13.refs_0_), channel_id=1, source_target_pairs={{0,1},{1,0},{2,3},{3,2},{4,5},{5,4},{6,7},{7,6},{8,9},{9,8},{10,11... | collective-permute-start | bytes 1179656 | tf_op jit(solution)/shard_map/ppermute | solution.py:485
  135.0 16.4 %collective-permute-start.16 = (bf16[768,256]{1,0:T(8,128)(2,1)S(1)}, bf16[768,256]{1,0:T(8,128)(2,1)S(1)}, u32[]{:S(2)}, u32[]{:S(2)}) collective-permute-start(bf16[768,256]{1,0:T(8,128)(2,1)S(1)} %collective-permute-done.15.refs_1_), channel_id=1, source_target_pairs={{0,1},{1,0},{2,3},{3,2},{4,5},{5,4},{6,7},{7,6},{8,9},{9,8},{10,11... | collective-permute-start | bytes 1179656 | tf_op jit(solution)/shard_map/ppermute | solution.py:485
  138.5 15.2 %collective-permute-start.12 = (bf16[768,256]{1,0:T(8,128)(2,1)S(1)}, bf16[768,256]{1,0:T(8,128)(2,1)S(1)}, u32[]{:S(2)}, u32[]{:S(2)}) collective-permute-start(bf16[768,256]{1,0:T(8,128)(2,1)S(1)} %get-tuple-element.10.first), channel_id=1, source_target_pairs={{1,5},{5,9},{9,13},{13,15},{15,11},{11,7},{7,3},{3,1},{17,21},{21,... | collective-permute-start | bytes 1179656 | tf_op jit(solution)/shard_map/ppermute | solution.py:530
  141.8 13.2 %collective-permute-start.9 = (bf16[768,256]{1,0:T(8,128)(2,1)S(1)}, bf16[768,256]{1,0:T(8,128)(2,1)S(1)}, u32[]{:S(2)}, u32[]{:S(2)}) collective-permute-start(bf16[768,256]{1,0:T(8,128)(2,1)S(1)} %slice.17.second), channel_id=1, source_target_pairs={{4,1},{8,5},{12,9},{14,13},{10,15},{6,11},{2,7},{0,3},{20,17},{24,... | collective-permute-start | bytes 1179656 | tf_op jit(solution)/shard_map/ppermute | solution.py:531
  143.1 11.9 %collective-permute-start.8 = (bf16[768,256]{1,0:T(8,128)(2,1)S(1)}, bf16[768,256]{1,0:T(8,128)(2,1)S(1)}, u32[]{:S(2)}, u32[]{:S(2)}) collective-permute-start(bf16[768,256]{1,0:T(8,128)(2,1)S(1)} %collective-permute-done.7.mixed), channel_id=1, source_target_pairs={{0,1},{1,0},{2,3},{3,2},{4,5},{5,4},{6,7},{7,6},{8,9},{9,8},{10,11... | collective-permute-start | bytes 1179656 | tf_op jit(solution)/shard_map/ppermute | solution.py:485
